TPU v7x, 128 devices: a whole 4x4x4 slice. The times are simulated.
128 devices in a mesh: dp: 64 (over y_lo, z, x, core), feat: 2 (over y_hi).
Axes of the slice: x: 4, y: 4 (y_hi: 2, y_lo: 2; y = y_hi * 2 + y_lo), z: 4, core: 2. Of those that a mesh axis runs over, the one named last changes fastest.
Arguments:
- grads: bfloat16 [32768, 4096], P('dp', 'feat'), may hold values from -16 to 16
- covariance: float32 [4096, 4096], P('dp', 'feat'), may hold values from -0.16 to 6, as said below
- test_grads: bfloat16 [512, 4096], P('feat', 'dp'), may hold values from -0.09375 to 0.09375
- inverse_factor: bfloat16 [4096, 4096], P('dp'), may hold values from -0.09375 to 0.09375
Outputs:
- scores: float32 [32768, 512], P('dp', 'feat')
- covariance_out: float32 [4096, 4096], P('dp', 'feat')
Inputs may be any that keep to these rules, and one draw needn't show every extreme that they name: covariance is symmetric.
All inputs are finite; a program needn't handle non-finite values.
Results may differ from a plain program's by a relative error of at most 0.0029.
Values may be sent and summed in bfloat16 or wider, within the bound.
No kernel may reach another device: no remote copies, remote signals or barrier semaphores. Data moves between devices by JAX's collectives and lax.ppermute only.
A program may use at most 192 MiB of HBM per device.

v0:
```python
import jax
import jax.numpy as jnp
from jax import lax
from jax.sharding import PartitionSpec as P


def on_device(grads, covariance, test_grads, inverse_factor):
    all_features = lax.all_gather(grads, "feat", axis=1, tiled=True)
    examples = grads.shape[0] * lax.axis_size("dp")
    partial_value = jnp.dot(test_grads, inverse_factor, preferred_element_type=jnp.float32)
    summed = lax.psum(partial_value, "dp")
    preconditioned = summed.astype(jnp.bfloat16)
    term = lax.psum_scatter(
        lax.dot_general(
            all_features, grads, (((0,), (0,)), ((), ())), preferred_element_type=jnp.float32
        ),
        "dp",
        scatter_dimension=0,
        tiled=True,
    )
    scores = lax.dot_general(
        all_features, preconditioned, (((1,), (1,)), ((), ())), preferred_element_type=jnp.float32
    )
    covariance_out = 0.9 * covariance + term / examples
    return (scores, covariance_out)


def solution(mesh):
    placed = (P("dp", "feat"), P("dp", "feat"), P("feat", "dp"), P("dp", None))
    return jax.shard_map(
        on_device,
        mesh=mesh,
        in_specs=placed,
        out_specs=(P("dp", "feat"), P("dp", "feat")),
        check_vma=False,
    )
```

profile of v0, /device:TPU:0, one launch (start us, length us, event | category | flops | bytes accessed | tf_op | source)
XLA Modules:
  0.0 444.9 jit_solution(6468622768820996146)
XLA Ops:
  7.2 0.0 copy-start
  7.2 0.0 all-gather.2.cloned.1.call-start
  7.2 0.7 all-gather.2.cloned.1.call-update
  7.9 0.0 reduce-scatter.2.cloned.1.call-start
  8.0 65.0 %all-gather.2.cloned.1.call-done = bf16[512,4096]{1,0:T(8,128)(2,1)} async-done(((bf16[512,2048]{1,0:T(8,128)(2,1)}), bf16[512,4096]{1,0:T(8,128)(2,1)}) %all-gather.2.cloned.1.call-update) | async-done | bytes 4194320 | tf_op jit(solution)/shard_map/all_gather | solution.py:8
  73.0 17.8 %fusion.6 = f32[4096,2048]{1,0:T(8,128)} fusion(bf16[512,4096]{1,0:T(8,128)(2,1)} %all-gather.2.cloned.1.call-done, bf16[512,2048]{1,0:T(8,128)(2,1)} %param.4), kind=kOutput, calls=%fused_computation.5 | convolution fusion | flops 8589934592 | bytes 39845888 | tf_op jit(solution)/shard_map/dot_general | solution.py:14
  90.8 0.0 copy-start.2
  90.8 0.0 reduce-scatter.2.cloned.1.call-update
  90.8 0.0 copy-done
  90.8 0.7 copy-done.2
  91.5 2.7 fusion.5
  94.2 335.5 %all-reduce.1 = bf16[256,4096]{1,0:T(8,128)(2,1)S(1)} all-reduce(f32[256,4096]{1,0:T(8,128)} %fusion.5), channel_id=1, replica_groups=mesh['dp'=64,'feat'=2] {'dp'}, use_global_device_ids=true, to_apply=%region_0.0 | all-reduce | flops 1048576 | bytes 6291456 | tf_op jit(solution)/shard_map/psum | solution.py:11
  429.8 0.0 copy-start.1
  429.8 4.3 fusion.2
  434.1 2.0 copy.6
  436.2 0.0 reduce-scatter.2.cloned.1.call-done
  436.2 0.0 copy-done.1
  436.2 1.9 multiply_add_fusion
Async XLA Ops:
  7.2 83.6 %copy-start = (bf16[64,4096]{1,0:T(8,128)(2,1)S(1)}, bf16[64,4096]{1,0:T(8,128)(2,1)}, u32[]{:S(2)}) copy-start(bf16[64,4096]{1,0:T(8,128)(2,1)} %param.7) | copy-start | bytes 1572868
  7.2 65.8 %all-gather.2.cloned.1.call-start = ((), (), s32[]{:S(2)}) async-start(), calls=%async_computation.1 | async-start | bytes 6291456 | tf_op jit(solution)/shard_map/all_gather | solution.py:8
  7.9 428.3 %reduce-scatter.2.cloned.1.call-start = ((), (), s32[]{:S(2)}) async-start(), calls=%async_computation.2 | async-start | bytes 34078720 | tf_op jit(solution)/shard_map/reduce_scatter | solution.py:13
  90.8 0.8 copy-start.2
  429.8 6.4 %copy-start.1 = (f32[64,2048]{1,0:T(8,128)S(1)}, f32[64,2048]{1,0:T(8,128)}, u32[]{:S(2)}) copy-start(f32[64,2048]{1,0:T(8,128)} %param.5) | copy-start | bytes 1572868
Sparse Core Ops, SparseCore 0:
  9.7 63.2 all-gather.1
  90.9 343.5 reduce-scatter.1
where the time goes:
time: 445 us
  blocking collectives  336 us (76%)
  waiting for transfers between devices  65.7 us (15%)
  matrix products  24.8 us (6%)
  between operations  14.1 us (3%)
    psum x1, blocking collectives, on_device(): summed = lax.psum(partial_value, 'dp')  336 us
    all_gather x1, waiting for transfers between devices, on_device(): all_features = lax.all_gather(grads, 'feat', axis=1, tiled=True)  65 us
    dot_general x1, matrix products, on_device(): lax.dot_general(all_features, grads, (((0,), (0,)), ((), ())), preferred_...  17.8 us
  transfers between devices with their start and end apart: 2, of which 1 were waited for; matrix products, arithmetic and copies ran while one was open for 2% of the time, Pallas kernels for 0%

commit v1 on v0

v1 whole, which is shorter than its diff:
```python
import functools

import jax
import jax.numpy as jnp
import numpy as np
from jax import lax
from jax.experimental import pallas as pl
from jax.experimental.pallas import tpu as pltpu
from jax.sharding import Mesh
from jax.sharding import PartitionSpec as P

AXES = ("yl", "z", "x", "c", "yh")
SIZES = (2, 4, 4, 2, 2)
DP = ("yl", "z", "x", "c")
bf16, f32 = jnp.bfloat16, jnp.float32


def send(value, move, only=None):
    pairs = []
    for i in range(int(np.prod(SIZES))):
        at = dict(zip(AXES, (int(v) for v in np.unravel_index(i, SIZES))))
        if only is None or only(at):
            to = {**at, **move(at)}
            pairs.append((i, int(np.ravel_multi_index([to[a] for a in AXES], SIZES))))
    return lax.ppermute(value, AXES, pairs)


def along(axis, k):
    return lambda at: {axis: (at[axis] + k) % 4}


def gram_kernel(stride, rows, at_ref, a1_ref, a2_ref, b1_ref, b2_ref, *outs):
    z, x, base = at_ref[0], at_ref[1], at_ref[2]
    n = outs[0].shape[1]
    for half in range(2):
        for k in range(4):
            picks1, picks2 = [], []
            for j in range(4):
                dx, dz = (k, j) if half == 0 else (j, k)
                block = lax.rem(z + dz, 4) * 4 + lax.rem(x + dx, 4)
                start = pl.ds(pl.multiple_of(block * stride + base, rows), rows)
                picks1.append(a1_ref[start, :])
                picks2.append(a2_ref[start, :])
            left1, left2 = jnp.concatenate(picks1), jnp.concatenate(picks2)
            cols = pl.ds(half * n, n)
            nt = (((1,), (1,)), ((), ()))
            acc = lax.dot_general(left1, b1_ref[cols, :], nt, preferred_element_type=f32)
            acc += lax.dot_general(left2, b2_ref[cols, :], nt, preferred_element_type=f32)
            outs[4 * half + k][...] = acc.astype(bf16)


def gram(at, a1, a2, b1, b2, stride, rows):
    n = b1.shape[0] // 2
    vmem = pl.BlockSpec(memory_space=pltpu.VMEM)
    flops = 4 * 16 * rows * b1.shape[0] * b1.shape[1]
    return pl.pallas_call(
        functools.partial(gram_kernel, stride, rows),
        out_shape=[jax.ShapeDtypeStruct((4 * rows, n), bf16)] * 8,
        in_specs=[pl.BlockSpec(memory_space=pltpu.SMEM)] + [vmem] * 4,
        out_specs=[vmem] * 8,
        cost_estimate=pl.CostEstimate(flops=flops, bytes_accessed=10 << 20, transcendentals=0),
    )(at, a1, a2, b1, b2)


def scatter_sum(parts, rows):
    got = []
    for half, axis in ((0, "x"), (1, "z")):
        got.append([send(parts[4 * half + k], along(axis, k)) for k in (1, 2, 3)])
    mids = []
    for half in range(2):
        mids.append([])
        for j in range(4):
            cut = lambda v: lax.slice_in_dim(v, j * rows, (j + 1) * rows).astype(f32)
            total = cut(parts[4 * half])
            for r in got[half]:
                total = total + cut(r)
            mids[half].append(total)
    sums = []
    for half, axis in ((0, "z"), (1, "x")):
        total = mids[half][0]
        rs = [send(mids[half][k].astype(bf16), along(axis, k)) for k in (1, 2, 3)]
        for r in rs:
            total = total + r.astype(f32)
        sums.append(total)
    return jnp.concatenate(sums, axis=1)


def on_device(grads, covariance, test_grads, inverse_factor):
    tokens, feats = grads.shape
    z, x, c = lax.axis_index("z"), lax.axis_index("x"), lax.axis_index("c")
    yl, h = lax.axis_index("yl"), lax.axis_index("yh")
    rows = feats // 32
    gt = grads.T
    blocks = gt.reshape(16, 2, rows, tokens)
    pick = lambda v, i: lax.dynamic_index_in_dim(v, i, 1, keepdims=False).reshape(16 * rows, tokens)
    mine, other = pick(blocks, c), pick(blocks, 1 - c)
    b_same = send(mine, lambda at: {"yh": 1 - at["yh"]})
    b_flip = send(other, lambda at: {"yh": 1 - at["yh"], "c": 1 - at["c"]})
    sib = send(gt, lambda at: {"c": 1 - at["c"]})

    tt = test_grads.T
    slots = inverse_factor.reshape(rows, 32, 2 * rows).transpose(1, 0, 2)
    slots = jnp.concatenate([slots, jnp.broadcast_to(tt[None], (32,) + tt.shape)], axis=2)
    slots = lax.all_to_all(slots, ("yl", "z", "x"), split_axis=0, concat_axis=0, tiled=True)
    slots = slots.reshape(32 * rows, -1)
    pt = lax.dot_general(
        slots[:, : 2 * rows], slots[:, 2 * rows :], (((0,), (0,)), ((), ())), preferred_element_type=f32
    )
    pt_keep = lax.dynamic_slice_in_dim(pt, c * rows, rows, 0)
    pt_give = lax.dynamic_slice_in_dim(pt, (1 - c) * rows, rows, 0)
    pt = (pt_keep + send(pt_give, lambda at: {"c": 1 - at["c"]})).astype(bf16)
    pt = jnp.broadcast_to(pt[None], (32,) + pt.shape)
    pt = lax.all_to_all(pt, ("yl", "z", "x"), split_axis=0, concat_axis=0, tiled=True)
    pt = pt.reshape(2, 16 * rows, -1)
    pt_own = lax.dynamic_index_in_dim(pt, h, 0, keepdims=False)
    pt_cross = lax.dynamic_index_in_dim(pt, 1 - h, 0, keepdims=False)

    at_own = jnp.stack([z, x, c * rows]).astype(jnp.int32)
    at_cross = jnp.stack([z, x, 0 * c]).astype(jnp.int32)
    own = scatter_sum(gram(at_own, gt, sib, gt, sib, 2 * rows, rows), rows)
    flip_yl = lambda at: {"yl": 1 - at["yl"]}
    own_in = send(own.astype(bf16), flip_yl, lambda at: at["yl"] != at["yh"])
    own = own + own_in.astype(f32)
    cross = scatter_sum(gram(at_cross, b_same, b_flip, gt, sib, rows, rows), rows)
    cross_in = send(cross.astype(bf16), flip_yl, lambda at: at["yl"] == at["yh"])
    cross = cross + cross_in.astype(f32)
    examples = tokens * 64
    covariance_out = 0.9 * covariance + jnp.where(yl == h, own, cross) / examples

    tn = (((0,), (0,)), ((), ()))
    dot = lambda a, b: lax.dot_general(a, b, tn, preferred_element_type=f32)
    sib_mine = pick(sib.reshape(16, 2, rows, tokens), c)
    s_keep = dot(mine, pt_own) + dot(b_same, pt_cross)
    s_give = dot(sib_mine, pt_own) + dot(b_flip, pt_cross)
    scores = s_keep + send(s_give, lambda at: {"c": 1 - at["c"]})
    return scores, covariance_out


def solution(mesh):
    grid = Mesh(mesh.devices.reshape(SIZES), AXES)
    return jax.shard_map(
        on_device,
        mesh=grid,
        in_specs=(P(DP, "yh"), P(DP, "yh"), P("yh", DP), P(DP, None)),
        out_specs=(P(DP, "yh"), P(DP, "yh")),
        check_vma=False,
    )
```

time: 445 us -> 194 us (0.44)
  blocking collectives: 336 us -> 0 us
  starting transfers between devices: 0.08 us -> 58 us
  waiting for transfers between devices: 65.7 us -> 89.7 us
  Pallas kernels: 0 us -> 17.8 us
  matrix products: 24.8 us -> 8.26 us
  between operations: 14.1 us -> 1.06 us
  other arithmetic: 1.91 us -> 9.71 us
  local copies, waits for them, and re-layouts: 2.78 us -> 8.74 us
    psum x1 -> x0, blocking collectives: 336 us -> none  [on_device(): summed = lax.psum(partial_value, 'dp')]
    ppermute x0 -> x31, waiting for transfers between devices: none -> 75.3 us  [send(): return lax.ppermute(value, AXES, pairs)]
    all_gather x1 -> x0, waiting for transfers between devices: 65 us -> none  [on_device(): all_features = lax.all_gather(grads, 'feat', axis=1, tiled=True)]
    ppermute x0 -> x31, starting transfers between devices: none -> 43.9 us  [send(): return lax.ppermute(value, AXES, pairs)]
    pallas_call x0 -> x2, Pallas kernels: none -> 17.8 us  [gram(): pl.pallas_call(functools.partial(gram_kernel, stride, rows), out_shape=[j...]
    dot_general x3 -> x5, matrix products: 24.8 us -> 8.26 us  [the longest x4 6.53 us: on_device(): dot = lambda a, b: lax.dot_general(a, b, tn, preferred_element_type=f32)]
    all_to_all x0 -> x2, waiting for transfers between devices: none -> 14.4 us  [the longest x1 14.4 us: on_device(): lax.all_to_all(slots, ('yl', 'z', 'x'), split_axis=0, concat_axis=0, tile...]
    all_to_all x0 -> x2, starting transfers between devices: none -> 14.1 us  [the longest x1 9.37 us: on_device(): lax.all_to_all(slots, ('yl', 'z', 'x'), split_axis=0, concat_axis=0, tile...]
  transfers between devices with their start and end apart: 2 -> 33, of which waited for: 1 -> 14; matrix products, arithmetic and copies ran while one was open for 2% -> 11% of each run, Pallas kernels for 0% -> 9%
where the time goes in v1:
time: 194 us; the launch traced here: 193 us
  waiting for transfers between devices  89.7 us (46%)
  starting transfers between devices  58 us (30%)
  Pallas kernels  17.8 us (9%)
  other arithmetic  9.71 us (5%)
  local copies, waits for them, and re-layouts  8.74 us (5%)
  matrix products  8.26 us (4%)
    ppermute x31, waiting for transfers between devices, send(): return lax.ppermute(value, AXES, pairs)  75.3 us
    ppermute x31, starting transfers between devices, send(): return lax.ppermute(value, AXES, pairs)  43.9 us
    pallas_call x2, Pallas kernels, gram(): pl.pallas_call(functools.partial(gram_kernel, stride, rows), out_shape=[j...  17.8 us
    all_to_all x1, waiting for transfers between devices, on_device(): lax.all_to_all(slots, ('yl', 'z', 'x'), split_axis=0, concat_axis=0, tile...  14.4 us
    all_to_all x1, starting transfers between devices, on_device(): lax.all_to_all(slots, ('yl', 'z', 'x'), split_axis=0, concat_axis=0, tile...  9.37 us
    dot_general x4, matrix products, on_device(): dot = lambda a, b: lax.dot_general(a, b, tn, preferred_element_type=f32)  6.53 us
    all_to_all x1, starting transfers between devices, on_device(): lax.all_to_all(pt, ('yl', 'z', 'x'), split_axis=0, concat_axis=0, tiled=T...  4.7 us
    unnamed x30, local copies, waits for them, and re-layouts  4.28 us
  transfers between devices with their start and end apart: 33, of which 14 were waited for; matrix products, arithmetic and copies ran while one was open for 11% of the time, Pallas kernels for 9%

profile of v1, /device:TPU:0, one launch (start us, length us, event | category | flops | bytes accessed | tf_op | source)
XLA Modules:
  0.0 193.2 jit_solution(8909964731495551820)
XLA Ops:
  0.6 1.1 copy.8
  2.1 1.4 pad_maximum_fusion
  3.5 9.4 %all-to-all-start = ((bf16[32,64,384]{2,1,0:T(8,128)(2,1)}), bf16[32,64,384]{2,1,0:T(8,128)(2,1)}, u32[]{:S(2)}, u32[]{:S(2)}) async-start(bf16[32,64,384]{2,1,0:T(8,128)(2,1)} %pad_maximum_fusion), calls=%async_computation | async-start | bytes 3145728 | tf_op jit(solution)/shard_map/all_to_all | solution.py:104
  12.9 2.9 %copy.6 = bf16[512,2048]{0,1:T(8,128)(2,1)S(1)} copy(bf16[512,2048]{1,0:T(8,128)(2,1)} %param.4) | data formatting | bytes 4194304 | tf_op args[0]
  15.9 1.7 constant_dynamic-slice_fusion.3
  17.8 2.6 %collective-permute-start.3 = (bf16[1024,512]{1,0:T(8,128)(2,1)}, bf16[1024,512]{1,0:T(8,128)(2,1)}, u32[]{:S(2)}, u32[]{:S(2)}) collective-permute-start(bf16[1024,512]{1,0:T(8,128)(2,1)} %bitcast.12), channel_id=1, source_target_pairs={{0,3},{1,2},{2,1},{3,0},{4,7},{5,6},{6,5},{7,4},{8,11},{9,10},{10,... | collective-permute-start | bytes 3145736 | tf_op jit(solution)/shard_map/ppermute | solution.py:25
  21.0 14.4 %all-to-all-done = bf16[32,64,384]{2,1,0:T(8,128)(2,1)} async-done(((bf16[32,64,384]{2,1,0:T(8,128)(2,1)}), bf16[32,64,384]{2,1,0:T(8,128)(2,1)}, u32[]{:S(2)}, u32[]{:S(2)}) %all-to-all-start) | async-done | bytes 1572896 | tf_op jit(solution)/shard_map/all_to_all | solution.py:104
  35.4 1.7 fusion.1
  38.5 1.1 broadcast_in_dim.5
  39.6 4.7 %all-to-all-start.1 = ((bf16[32,64,256]{2,1,0:T(8,128)(2,1)}), bf16[32,64,256]{2,1,0:T(8,128)(2,1)S(1)}, u32[]{:S(2)}, u32[]{:S(2)}) async-start(bf16[32,64,256]{2,1,0:T(8,128)(2,1)} %broadcast_in_dim.5), calls=%async_computation.1 | async-start | bytes 2097152 | tf_op jit(solution)/shard_map/all_to_all | solution.py:113
  45.0 18.9 %collective-permute-done.3.a2_ref = bf16[1024,512]{1,0:T(8,128)(2,1)} collective-permute-done((bf16[1024,512]{1,0:T(8,128)(2,1)}, bf16[1024,512]{1,0:T(8,128)(2,1)}, u32[]{:S(2)}, u32[]{:S(2)}) %collective-permute-start.3) | collective-permute-done | bytes 1048608 | tf_op jit(solution)/shard_map/ppermute | solution.py:25
  63.9 22.6 %collective-permute-done.1.a1_ref = bf16[1024,512]{1,0:T(8,128)(2,1)} collective-permute-done((bf16[1024,512]{1,0:T(8,128)(2,1)}, bf16[1024,512]{1,0:T(8,128)(2,1)}, u32[]{:S(2)}, u32[]{:S(2)}) %collective-permute-start.1) | collective-permute-done | bytes 1048608 | tf_op jit(solution)/shard_map/ppermute | solution.py:25
  86.5 8.6 %shard_map.60 = (bf16[256,1024]{1,0:T(8,128)(2,1)}, bf16[256,1024]{1,0:T(8,128)(2,1)}, bf16[256,1024]{1,0:T(8,128)(2,1)}, bf16[256,1024]{1,0:T(8,128)(2,1)}, bf1...) custom-call(s32[3]{0:T(128)} %pad_add_fusion.2.at_ref, ...), custom_call_target="tpu_custom_call" | custom-call | flops 4294967296 | bytes 10485760 | tf_op jit(solution)/shard_map/pallas_call | solution.py:56
  95.1 3.9 %collective-permute-start.26 = (bf16[256,1024]{1,0:T(8,128)(2,1)}, bf16[256,1024]{1,0:T(8,128)(2,1)S(1)}, u32[]{:S(2)}, u32[]{:S(2)}) collective-permute-start(bf16[256,1024]{1,0:T(8,128)(2,1)} %get-tuple-element.33), channel_id=1, source_target_pairs={{0,48},{1,49},{2,50},{3,51},{4,52},{5,53},{6,54},{7,55},{8,56},{9,... | collective-permute-start | bytes 1572872 | tf_op jit(solution)/shard_map/ppermute | solution.py:25
  99.8 0.9 collective-permute-start.24
  100.7 2.5 %collective-permute-start.20 = (bf16[256,1024]{1,0:T(8,128)(2,1)}, bf16[256,1024]{1,0:T(8,128)(2,1)S(1)}, u32[]{:S(2)}, u32[]{:S(2)}) collective-permute-start(bf16[256,1024]{1,0:T(8,128)(2,1)} %get-tuple-element.29), channel_id=1, source_target_pairs={{0,12},{1,13},{2,14},{3,15},{4,0},{5,1},{6,2},{7,3},{8,4},{9,5},{1... | collective-permute-start | bytes 1572872 | tf_op jit(solution)/shard_map/ppermute | solution.py:25
  103.2 1.0 collective-permute-start.19
  104.2 9.2 %shard_map.59 = (bf16[256,1024]{1,0:T(8,128)(2,1)}, bf16[256,1024]{1,0:T(8,128)(2,1)}, bf16[256,1024]{1,0:T(8,128)(2,1)}, bf16[256,1024]{1,0:T(8,128)(2,1)}, bf1...) custom-call(s32[3]{0:T(128)} %pad_add_fusion.at_ref, ...), custom_call_target="tpu_custom_call" | custom-call | flops 4294967296 | bytes 10485760 | tf_op jit(solution)/shard_map/pallas_call | solution.py:56
  113.3 1.3 constant_dynamic-slice_fusion.1
  114.7 5.3 %collective-permute-done.26 = bf16[256,1024]{1,0:T(8,128)(2,1)S(1)} collective-permute-done((bf16[256,1024]{1,0:T(8,128)(2,1)}, bf16[256,1024]{1,0:T(8,128)(2,1)S(1)}, u32[]{:S(2)}, u32[]{:S(2)}) %collective-permute-start.26) | collective-permute-done | bytes 524320 | tf_op jit(solution)/shard_map/ppermute | solution.py:25
  119.9 1.7 collective-permute-start.18
  121.6 3.6 %collective-permute-start.13 = (bf16[256,1024]{1,0:T(8,128)(2,1)}, bf16[256,1024]{1,0:T(8,128)(2,1)S(1)}, u32[]{:S(2)}, u32[]{:S(2)}) collective-permute-start(bf16[256,1024]{1,0:T(8,128)(2,1)} %get-tuple-element.25), channel_id=1, source_target_pairs={{0,48},{1,49},{2,50},{3,51},{4,52},{5,53},{6,54},{7,55},{8,56},{9,... | collective-permute-start | bytes 1572872 | tf_op jit(solution)/shard_map/ppermute | solution.py:25
  125.2 1.9 fusion.4
  128.6 2.6 %collective-permute-start.7 = (bf16[256,1024]{1,0:T(8,128)(2,1)S(1)}, bf16[256,1024]{1,0:T(8,128)(2,1)S(1)}, u32[]{:S(2)}, u32[]{:S(2)}) collective-permute-start(bf16[256,1024]{1,0:T(8,128)(2,1)S(1)} %copy-done.11), channel_id=1, source_target_pairs={{0,12},{1,13},{2,14},{3,15},{4,0},{5,1},{6,2},{7,3},{8,4},{9,5},{1... | collective-permute-start | bytes 1572872 | tf_op jit(solution)/shard_map/ppermute | solution.py:25
  131.2 1.9 collective-permute-start.6
  133.1 11.5 %collective-permute-done.13 = bf16[256,1024]{1,0:T(8,128)(2,1)S(1)} collective-permute-done((bf16[256,1024]{1,0:T(8,128)(2,1)}, bf16[256,1024]{1,0:T(8,128)(2,1)S(1)}, u32[]{:S(2)}, u32[]{:S(2)}) %collective-permute-start.13) | collective-permute-done | bytes 524320 | tf_op jit(solution)/shard_map/ppermute | solution.py:25
  144.6 1.5 add_convert_fusion.2
  146.1 1.5 add_convert_fusion.5
  147.7 2.4 %collective-permute-done.11 = bf16[256,1024]{1,0:T(8,128)(2,1)S(1)} collective-permute-done((bf16[256,1024]{1,0:T(8,128)(2,1)S(1)}, bf16[256,1024]{1,0:T(8,128)(2,1)S(1)}, u32[]{:S(2)}, u32[]{:S(2)}) %collective-permute-start.11) | collective-permute-done | bytes 524320 | tf_op jit(solution)/shard_map/ppermute | solution.py:25
  150.2 3.4 %collective-permute-start.29 = (bf16[64,1024]{1,0:T(8,128)(2,1)S(1)}, bf16[64,1024]{1,0:T(8,128)(2,1)S(1)}, u32[]{:S(2)}, u32[]{:S(2)}) collective-permute-start(bf16[64,1024]{1,0:T(8,128)(2,1)S(1)} %get-tuple-element.44), channel_id=1, source_target_pairs={{0,12},{1,13},{2,14},{3,15},{4,0},{5,1},{6,2},{7,3},{8,4},{9,5},{1... | collective-permute-start | bytes 393224 | tf_op jit(solution)/shard_map/ppermute | solution.py:25
  154.3 1.8 collective-permute-start.27
  156.1 2.9 %collective-permute-start.23 = (bf16[64,1024]{1,0:T(8,128)(2,1)S(1)}, bf16[64,1024]{1,0:T(8,128)(2,1)S(1)}, u32[]{:S(2)}, u32[]{:S(2)}) collective-permute-start(bf16[64,1024]{1,0:T(8,128)(2,1)S(1)} %get-tuple-element.41), channel_id=1, source_target_pairs={{0,48},{1,49},{2,50},{3,51},{4,52},{5,53},{6,54},{7,55},{8,56},{9,... | collective-permute-start | bytes 393224 | tf_op jit(solution)/shard_map/ppermute | solution.py:25
  159.3 1.6 collective-permute-start.22
  160.9 0.9 collective-permute-done.28
  162.0 1.4 collective-permute-done.27
  163.4 1.3 collective-permute-start.16
  164.7 1.1 convert_add_fusion
  165.9 1.3 collective-permute-done.22
  167.2 1.1 collective-permute-done.21
  168.3 1.6 collective-permute-start.10
  169.9 1.1 convert_add_fusion.1
  171.9 1.7 collective-permute-done.15
  174.5 4.4 %collective-permute-start.30 = (bf16[64,2048]{1,0:T(8,128)(2,1)S(1)}, bf16[64,2048]{1,0:T(8,128)(2,1)S(1)}, u32[]{:S(2)}, u32[]{:S(2)}) collective-permute-start(bf16[64,2048]{1,0:T(8,128)(2,1)S(1)} %fusion.14), channel_id=1, source_target_pairs={{0,64},{2,66},{4,68},{6,70},{8,72},{10,74},{12,76},{14,78},{16,80}... | collective-permute-start | bytes 786440 | tf_op jit(solution)/shard_map/ppermute | solution.py:25
  180.0 1.3 collective-permute-start.17
  181.3 1.7 fusion.8
  183.0 6.7 %collective-permute-done.17 = bf16[64,2048]{1,0:T(8,128)(2,1)S(1)} collective-permute-done((bf16[64,2048]{1,0:T(8,128)(2,1)S(1)}, bf16[64,2048]{1,0:T(8,128)(2,1)S(1)}, u32[]{:S(2)}, u32[]{:S(2)}) %collective-permute-start.17) | collective-permute-done | bytes 262176 | tf_op jit(solution)/shard_map/ppermute | solution.py:25
  189.7 0.9 multiply_add_fusion
  190.7 2.5 %fusion = f32[512,256]{1,0:T(8,128)} fusion(f32[512,256]{1,0:T(8,128)S(1)} %collective-permute-done.4, f32[512,256]{1,0:T(8,128)S(1)} %fusion.8, bf16[1024,512]{1,0:T(8,128)(2,1)} %collective-permute-done.1.a1_ref, bf16[2,1024,256]{2,1,0:T(8,128)(2,1)S(1)} %bitcast.40, s32[]{:T(128)S(6)} %select_n.33), kind=kOutput, calls=%fused_computation.3 | convolution fusion | flops 268697600 | bytes 3145732 | tf_op jit(solution)/shard_map/dot_general | solution.py:131
  (76 shorter events, 9.6 us)
Async XLA Ops:
  0.6 1.4 copy-start.8
  3.5 31.9 %all-to-all-start = ((bf16[32,64,384]{2,1,0:T(8,128)(2,1)}), bf16[32,64,384]{2,1,0:T(8,128)(2,1)}, u32[]{:S(2)}, u32[]{:S(2)}) async-start(bf16[32,64,384]{2,1,0:T(8,128)(2,1)} %pad_maximum_fusion), calls=%async_computation | async-start | bytes 3145728 | tf_op jit(solution)/shard_map/all_to_all | solution.py:104
  15.8 2.0 %copy-start = (bf16[512,2048]{0,1:T(8,128)(2,1)}, bf16[512,2048]{0,1:T(8,128)(2,1)S(1)}, u32[]{:S(2)}) copy-start(bf16[512,2048]{0,1:T(8,128)(2,1)S(1)} %copy.6) | copy-start | bytes 6291460
  15.8 70.7 %collective-permute-start.2 = (bf16[2048,512]{1,0:T(8,128)(2,1)S(1)}, bf16[2048,512]{1,0:T(8,128)(2,1)}, u32[]{:S(2)}, u32[]{:S(2)}) collective-permute-start(bf16[2048,512]{1,0:T(8,128)(2,1)S(1)} %bitcast.31), channel_id=1, source_target_pairs={{0,2},{1,3},{2,0},{3,1},{4,6},{5,7},{6,4},{7,5},{8,10},{9,11},{10,... | collective-permute-start | bytes 6291464 | tf_op jit(solution)/shard_map/ppermute | solution.py:25
  17.8 46.1 %collective-permute-start.3 = (bf16[1024,512]{1,0:T(8,128)(2,1)}, bf16[1024,512]{1,0:T(8,128)(2,1)}, u32[]{:S(2)}, u32[]{:S(2)}) collective-permute-start(bf16[1024,512]{1,0:T(8,128)(2,1)} %bitcast.12), channel_id=1, source_target_pairs={{0,3},{1,2},{2,1},{3,0},{4,7},{5,6},{6,5},{7,4},{8,11},{9,10},{10,... | collective-permute-start | bytes 3145736 | tf_op jit(solution)/shard_map/ppermute | solution.py:25
  20.4 66.1 %collective-permute-start.1 = (bf16[1024,512]{1,0:T(8,128)(2,1)}, bf16[1024,512]{1,0:T(8,128)(2,1)}, u32[]{:S(2)}, u32[]{:S(2)}) collective-permute-start(bf16[1024,512]{1,0:T(8,128)(2,1)} %bitcast.2), channel_id=1, source_target_pairs={{0,1},{1,0},{2,3},{3,2},{4,5},{5,4},{6,7},{7,6},{8,9},{9,8},{10,11... | collective-permute-start | bytes 3145736 | tf_op jit(solution)/shard_map/ppermute | solution.py:25
  37.2 1.3 collective-permute-start
  39.6 85.6 %all-to-all-start.1 = ((bf16[32,64,256]{2,1,0:T(8,128)(2,1)}), bf16[32,64,256]{2,1,0:T(8,128)(2,1)S(1)}, u32[]{:S(2)}, u32[]{:S(2)}) async-start(bf16[32,64,256]{2,1,0:T(8,128)(2,1)} %broadcast_in_dim.5), calls=%async_computation.1 | async-start | bytes 2097152 | tf_op jit(solution)/shard_map/all_to_all | solution.py:113
  95.1 24.8 %collective-permute-start.26 = (bf16[256,1024]{1,0:T(8,128)(2,1)}, bf16[256,1024]{1,0:T(8,128)(2,1)S(1)}, u32[]{:S(2)}, u32[]{:S(2)}) collective-permute-start(bf16[256,1024]{1,0:T(8,128)(2,1)} %get-tuple-element.33), channel_id=1, source_target_pairs={{0,48},{1,49},{2,50},{3,51},{4,52},{5,53},{6,54},{7,55},{8,56},{9,... | collective-permute-start | bytes 1572872 | tf_op jit(solution)/shard_map/ppermute | solution.py:25
  99.0 22.7 %collective-permute-start.25 = (bf16[256,1024]{1,0:T(8,128)(2,1)}, bf16[256,1024]{1,0:T(8,128)(2,1)}, u32[]{:S(2)}, u32[]{:S(2)}) collective-permute-start(bf16[256,1024]{1,0:T(8,128)(2,1)} %get-tuple-element.32), channel_id=1, source_target_pairs={{0,32},{1,33},{2,34},{3,35},{4,36},{5,37},{6,38},{7,39},{8,40},{9,... | collective-permute-start | bytes 1572872 | tf_op jit(solution)/shard_map/ppermute | solution.py:25
  99.8 27.3 %collective-permute-start.24 = (bf16[256,1024]{1,0:T(8,128)(2,1)}, bf16[256,1024]{1,0:T(8,128)(2,1)}, u32[]{:S(2)}, u32[]{:S(2)}) collective-permute-start(bf16[256,1024]{1,0:T(8,128)(2,1)} %get-tuple-element.31), channel_id=1, source_target_pairs={{0,16},{1,17},{2,18},{3,19},{4,20},{5,21},{6,22},{7,23},{8,24},{9,... | collective-permute-start | bytes 1572872 | tf_op jit(solution)/shard_map/ppermute | solution.py:25
  100.7 26.5 %collective-permute-start.20 = (bf16[256,1024]{1,0:T(8,128)(2,1)}, bf16[256,1024]{1,0:T(8,128)(2,1)S(1)}, u32[]{:S(2)}, u32[]{:S(2)}) collective-permute-start(bf16[256,1024]{1,0:T(8,128)(2,1)} %get-tuple-element.29), channel_id=1, source_target_pairs={{0,12},{1,13},{2,14},{3,15},{4,0},{5,1},{6,2},{7,3},{8,4},{9,5},{1... | collective-permute-start | bytes 1572872 | tf_op jit(solution)/shard_map/ppermute | solution.py:25
  103.2 25.4 %collective-permute-start.19 = (bf16[256,1024]{1,0:T(8,128)(2,1)}, bf16[256,1024]{1,0:T(8,128)(2,1)}, u32[]{:S(2)}, u32[]{:S(2)}) collective-permute-start(bf16[256,1024]{1,0:T(8,128)(2,1)} %get-tuple-element.28), channel_id=1, source_target_pairs={{0,8},{1,9},{2,10},{3,11},{4,12},{5,13},{6,14},{7,15},{8,0},{9,1},... | collective-permute-start | bytes 1572872 | tf_op jit(solution)/shard_map/ppermute | solution.py:25
  119.9 1.7 copy-start.6
  119.9 11.3 %collective-permute-start.18 = (bf16[256,1024]{1,0:T(8,128)(2,1)}, bf16[256,1024]{1,0:T(8,128)(2,1)}, u32[]{:S(2)}, u32[]{:S(2)}) collective-permute-start(bf16[256,1024]{1,0:T(8,128)(2,1)} %get-tuple-element.27), channel_id=1, source_target_pairs={{0,4},{1,5},{2,6},{3,7},{4,8},{5,9},{6,10},{7,11},{8,12},{9,13},{1... | collective-permute-start | bytes 1572872 | tf_op jit(solution)/shard_map/ppermute | solution.py:25
  121.6 23.0 %collective-permute-start.13 = (bf16[256,1024]{1,0:T(8,128)(2,1)}, bf16[256,1024]{1,0:T(8,128)(2,1)S(1)}, u32[]{:S(2)}, u32[]{:S(2)}) collective-permute-start(bf16[256,1024]{1,0:T(8,128)(2,1)} %get-tuple-element.25), channel_id=1, source_target_pairs={{0,48},{1,49},{2,50},{3,51},{4,52},{5,53},{6,54},{7,55},{8,56},{9,... | collective-permute-start | bytes 1572872 | tf_op jit(solution)/shard_map/ppermute | solution.py:25
  125.2 1.9 copy-start.13
  125.2 2.0 %copy-start.12 = (bf16[256,1024]{1,0:T(8,128)(2,1)S(1)}, bf16[256,1024]{1,0:T(8,128)(2,1)}, u32[]{:S(2)}) copy-start(bf16[256,1024]{1,0:T(8,128)(2,1)} %get-tuple-element.23) | copy-start | bytes 1572868
  125.2 3.4 %copy-start.11 = (bf16[256,1024]{1,0:T(8,128)(2,1)S(1)}, bf16[256,1024]{1,0:T(8,128)(2,1)}, u32[]{:S(2)}) copy-start(bf16[256,1024]{1,0:T(8,128)(2,1)} %get-tuple-element.21) | copy-start | bytes 1572868
  125.2 6.0 %copy-start.10 = (bf16[256,1024]{1,0:T(8,128)(2,1)S(1)}, bf16[256,1024]{1,0:T(8,128)(2,1)}, u32[]{:S(2)}) copy-start(bf16[256,1024]{1,0:T(8,128)(2,1)} %get-tuple-element.20) | copy-start | bytes 1572868
  125.2 19.4 %copy-start.9 = (bf16[256,1024]{1,0:T(8,128)(2,1)S(1)}, bf16[256,1024]{1,0:T(8,128)(2,1)}, u32[]{:S(2)}) copy-start(bf16[256,1024]{1,0:T(8,128)(2,1)} %get-tuple-element.19) | copy-start | bytes 1572868
  125.2 19.4 %copy-start.5 = (bf16[256,1024]{1,0:T(8,128)(2,1)S(1)}, bf16[256,1024]{1,0:T(8,128)(2,1)}, u32[]{:S(2)}) copy-start(bf16[256,1024]{1,0:T(8,128)(2,1)} %get-tuple-element.30) | copy-start | bytes 1572868
  125.2 19.4 %copy-start.7 = (bf16[256,1024]{1,0:T(8,128)(2,1)S(1)}, bf16[256,1024]{1,0:T(8,128)(2,1)}, u32[]{:S(2)}) copy-start(bf16[256,1024]{1,0:T(8,128)(2,1)} %copy-done.6) | copy-start | bytes 1572868
  127.1 20.5 %collective-permute-start.12 = (bf16[256,1024]{1,0:T(8,128)(2,1)S(1)}, bf16[256,1024]{1,0:T(8,128)(2,1)S(1)}, u32[]{:S(2)}, u32[]{:S(2)}) collective-permute-start(bf16[256,1024]{1,0:T(8,128)(2,1)S(1)} %copy-done.13), channel_id=1, source_target_pairs={{0,32},{1,33},{2,34},{3,35},{4,36},{5,37},{6,38},{7,39},{8,40},{9,... | collective-permute-start | bytes 1572872 | tf_op jit(solution)/shard_map/ppermute | solution.py:25
  127.2 22.9 %collective-permute-start.11 = (bf16[256,1024]{1,0:T(8,128)(2,1)S(1)}, bf16[256,1024]{1,0:T(8,128)(2,1)S(1)}, u32[]{:S(2)}, u32[]{:S(2)}) collective-permute-start(bf16[256,1024]{1,0:T(8,128)(2,1)S(1)} %copy-done.12), channel_id=1, source_target_pairs={{0,16},{1,17},{2,18},{3,19},{4,20},{5,21},{6,22},{7,23},{8,24},{9,... | collective-permute-start | bytes 1572872 | tf_op jit(solution)/shard_map/ppermute | solution.py:25
  128.1 18.0 %copy-start.4 = (bf16[256,1024]{1,0:T(8,128)(2,1)S(1)}, bf16[256,1024]{1,0:T(8,128)(2,1)}, u32[]{:S(2)}) copy-start(bf16[256,1024]{1,0:T(8,128)(2,1)} %get-tuple-element.26) | copy-start | bytes 1572868
  128.6 25.0 %copy-start.3 = (bf16[256,1024]{1,0:T(8,128)(2,1)S(1)}, bf16[256,1024]{1,0:T(8,128)(2,1)}, u32[]{:S(2)}) copy-start(bf16[256,1024]{1,0:T(8,128)(2,1)} %get-tuple-element.22) | copy-start | bytes 1572868
  128.6 25.2 %collective-permute-start.7 = (bf16[256,1024]{1,0:T(8,128)(2,1)S(1)}, bf16[256,1024]{1,0:T(8,128)(2,1)S(1)}, u32[]{:S(2)}, u32[]{:S(2)}) collective-permute-start(bf16[256,1024]{1,0:T(8,128)(2,1)S(1)} %copy-done.11), channel_id=1, source_target_pairs={{0,12},{1,13},{2,14},{3,15},{4,0},{5,1},{6,2},{7,3},{8,4},{9,5},{1... | collective-permute-start | bytes 1572872 | tf_op jit(solution)/shard_map/ppermute | solution.py:25
  131.2 23.1 %collective-permute-start.6 = (bf16[256,1024]{1,0:T(8,128)(2,1)S(1)}, bf16[256,1024]{1,0:T(8,128)(2,1)S(1)}, u32[]{:S(2)}, u32[]{:S(2)}) collective-permute-start(bf16[256,1024]{1,0:T(8,128)(2,1)S(1)} %copy-done.10), channel_id=1, source_target_pairs={{0,8},{1,9},{2,10},{3,11},{4,12},{5,13},{6,14},{7,15},{8,0},{9,1},... | collective-permute-start | bytes 1572872 | tf_op jit(solution)/shard_map/ppermute | solution.py:25
  144.6 11.5 %collective-permute-start.5 = (bf16[256,1024]{1,0:T(8,128)(2,1)S(1)}, bf16[256,1024]{1,0:T(8,128)(2,1)S(1)}, u32[]{:S(2)}, u32[]{:S(2)}) collective-permute-start(bf16[256,1024]{1,0:T(8,128)(2,1)S(1)} %copy-done.9), channel_id=1, source_target_pairs={{0,4},{1,5},{2,6},{3,7},{4,8},{5,9},{6,10},{7,11},{8,12},{9,13},{1... | collective-permute-start | bytes 1572872 | tf_op jit(solution)/shard_map/ppermute | solution.py:25
  146.1 12.9 %copy-start.2 = (bf16[256,1024]{1,0:T(8,128)(2,1)S(1)}, bf16[256,1024]{1,0:T(8,128)(2,1)}, u32[]{:S(2)}) copy-start(bf16[256,1024]{1,0:T(8,128)(2,1)} %get-tuple-element.18) | copy-start | bytes 1572868
  147.6 43.0 %collective-permute-start.4 = (f32[512,256]{1,0:T(8,128)S(1)}, f32[512,256]{1,0:T(8,128)S(1)}, u32[]{:S(2)}, u32[]{:S(2)}) collective-permute-start(f32[512,256]{1,0:T(8,128)S(1)} %convolution_add_fusion), channel_id=1, source_target_pairs={{0,2},{1,3},{2,0},{3,1},{4,6},{5,7},{6,4},{7,5},{8,10},{9,11},{10,... | collective-permute-start | bytes 1572872 | tf_op jit(solution)/shard_map/ppermute | solution.py:25
  150.2 9.2 %collective-permute-start.29 = (bf16[64,1024]{1,0:T(8,128)(2,1)S(1)}, bf16[64,1024]{1,0:T(8,128)(2,1)S(1)}, u32[]{:S(2)}, u32[]{:S(2)}) collective-permute-start(bf16[64,1024]{1,0:T(8,128)(2,1)S(1)} %get-tuple-element.44), channel_id=1, source_target_pairs={{0,12},{1,13},{2,14},{3,15},{4,0},{5,1},{6,2},{7,3},{8,4},{9,5},{1... | collective-permute-start | bytes 393224 | tf_op jit(solution)/shard_map/ppermute | solution.py:25
  153.9 8.0 %collective-permute-start.28 = (bf16[64,1024]{1,0:T(8,128)(2,1)S(1)}, bf16[64,1024]{1,0:T(8,128)(2,1)S(1)}, u32[]{:S(2)}, u32[]{:S(2)}) collective-permute-start(bf16[64,1024]{1,0:T(8,128)(2,1)S(1)} %get-tuple-element.45), channel_id=1, source_target_pairs={{0,8},{1,9},{2,10},{3,11},{4,12},{5,13},{6,14},{7,15},{8,0},{9,1},... | collective-permute-start | bytes 393224 | tf_op jit(solution)/shard_map/ppermute | solution.py:25
  154.3 9.1 %collective-permute-start.27 = (bf16[64,1024]{1,0:T(8,128)(2,1)S(1)}, bf16[64,1024]{1,0:T(8,128)(2,1)S(1)}, u32[]{:S(2)}, u32[]{:S(2)}) collective-permute-start(bf16[64,1024]{1,0:T(8,128)(2,1)S(1)} %get-tuple-element.43), channel_id=1, source_target_pairs={{0,4},{1,5},{2,6},{3,7},{4,8},{5,9},{6,10},{7,11},{8,12},{9,13},{1... | collective-permute-start | bytes 393224 | tf_op jit(solution)/shard_map/ppermute | solution.py:25
  156.1 9.7 %collective-permute-start.23 = (bf16[64,1024]{1,0:T(8,128)(2,1)S(1)}, bf16[64,1024]{1,0:T(8,128)(2,1)S(1)}, u32[]{:S(2)}, u32[]{:S(2)}) collective-permute-start(bf16[64,1024]{1,0:T(8,128)(2,1)S(1)} %get-tuple-element.41), channel_id=1, source_target_pairs={{0,48},{1,49},{2,50},{3,51},{4,52},{5,53},{6,54},{7,55},{8,56},{9,... | collective-permute-start | bytes 393224 | tf_op jit(solution)/shard_map/ppermute | solution.py:25
  159.3 7.9 %collective-permute-start.22 = (bf16[64,1024]{1,0:T(8,128)(2,1)S(1)}, bf16[64,1024]{1,0:T(8,128)(2,1)S(1)}, u32[]{:S(2)}, u32[]{:S(2)}) collective-permute-start(bf16[64,1024]{1,0:T(8,128)(2,1)S(1)} %get-tuple-element.42), channel_id=1, source_target_pairs={{0,32},{1,33},{2,34},{3,35},{4,36},{5,37},{6,38},{7,39},{8,40},{9,... | collective-permute-start | bytes 393224 | tf_op jit(solution)/shard_map/ppermute | solution.py:25
  161.9 6.5 %collective-permute-start.21 = (bf16[64,1024]{1,0:T(8,128)(2,1)S(1)}, bf16[64,1024]{1,0:T(8,128)(2,1)S(1)}, u32[]{:S(2)}, u32[]{:S(2)}) collective-permute-start(bf16[64,1024]{1,0:T(8,128)(2,1)S(1)} %get-tuple-element.40), channel_id=1, source_target_pairs={{0,16},{1,17},{2,18},{3,19},{4,20},{5,21},{6,22},{7,23},{8,24},{9,... | collective-permute-start | bytes 393224 | tf_op jit(solution)/shard_map/ppermute | solution.py:25
  163.4 7.7 %collective-permute-start.16 = (bf16[64,1024]{1,0:T(8,128)(2,1)S(1)}, bf16[64,1024]{1,0:T(8,128)(2,1)S(1)}, u32[]{:S(2)}, u32[]{:S(2)}) collective-permute-start(bf16[64,1024]{1,0:T(8,128)(2,1)S(1)} %get-tuple-element.38), channel_id=1, source_target_pairs={{0,12},{1,13},{2,14},{3,15},{4,0},{5,1},{6,2},{7,3},{8,4},{9,5},{1... | collective-permute-start | bytes 393224 | tf_op jit(solution)/shard_map/ppermute | solution.py:25
  165.8 7.8 %collective-permute-start.15 = (bf16[64,1024]{1,0:T(8,128)(2,1)S(1)}, bf16[64,1024]{1,0:T(8,128)(2,1)S(1)}, u32[]{:S(2)}, u32[]{:S(2)}) collective-permute-start(bf16[64,1024]{1,0:T(8,128)(2,1)S(1)} %get-tuple-element.39), channel_id=1, source_target_pairs={{0,8},{1,9},{2,10},{3,11},{4,12},{5,13},{6,14},{7,15},{8,0},{9,1},... | collective-permute-start | bytes 393224 | tf_op jit(solution)/shard_map/ppermute | solution.py:25
  167.2 7.3 %collective-permute-start.14 = (bf16[64,1024]{1,0:T(8,128)(2,1)S(1)}, bf16[64,1024]{1,0:T(8,128)(2,1)S(1)}, u32[]{:S(2)}, u32[]{:S(2)}) collective-permute-start(bf16[64,1024]{1,0:T(8,128)(2,1)S(1)} %get-tuple-element.37), channel_id=1, source_target_pairs={{0,4},{1,5},{2,6},{3,7},{4,8},{5,9},{6,10},{7,11},{8,12},{9,13},{1... | collective-permute-start | bytes 393224 | tf_op jit(solution)/shard_map/ppermute | solution.py:25
  168.3 10.8 %collective-permute-start.10 = (bf16[64,1024]{1,0:T(8,128)(2,1)S(1)}, bf16[64,1024]{1,0:T(8,128)(2,1)S(1)}, u32[]{:S(2)}, u32[]{:S(2)}) collective-permute-start(bf16[64,1024]{1,0:T(8,128)(2,1)S(1)} %get-tuple-element.35), channel_id=1, source_target_pairs={{0,48},{1,49},{2,50},{3,51},{4,52},{5,53},{6,54},{7,55},{8,56},{9,... | collective-permute-start | bytes 393224 | tf_op jit(solution)/shard_map/ppermute | solution.py:25
  171.1 8.1 %collective-permute-start.9 = (bf16[64,1024]{1,0:T(8,128)(2,1)S(1)}, bf16[64,1024]{1,0:T(8,128)(2,1)S(1)}, u32[]{:S(2)}, u32[]{:S(2)}) collective-permute-start(bf16[64,1024]{1,0:T(8,128)(2,1)S(1)} %get-tuple-element.36), channel_id=1, source_target_pairs={{0,32},{1,33},{2,34},{3,35},{4,36},{5,37},{6,38},{7,39},{8,40},{9,... | collective-permute-start | bytes 393224 | tf_op jit(solution)/shard_map/ppermute | solution.py:25
  173.6 6.2 %collective-permute-start.8 = (bf16[64,1024]{1,0:T(8,128)(2,1)S(1)}, bf16[64,1024]{1,0:T(8,128)(2,1)S(1)}, u32[]{:S(2)}, u32[]{:S(2)}) collective-permute-start(bf16[64,1024]{1,0:T(8,128)(2,1)S(1)} %get-tuple-element.34), channel_id=1, source_target_pairs={{0,16},{1,17},{2,18},{3,19},{4,20},{5,21},{6,22},{7,23},{8,24},{9,... | collective-permute-start | bytes 393224 | tf_op jit(solution)/shard_map/ppermute | solution.py:25
  174.5 8.5 %collective-permute-start.30 = (bf16[64,2048]{1,0:T(8,128)(2,1)S(1)}, bf16[64,2048]{1,0:T(8,128)(2,1)S(1)}, u32[]{:S(2)}, u32[]{:S(2)}) collective-permute-start(bf16[64,2048]{1,0:T(8,128)(2,1)S(1)} %fusion.14), channel_id=1, source_target_pairs={{0,64},{2,66},{4,68},{6,70},{8,72},{10,74},{12,76},{14,78},{16,80}... | collective-permute-start | bytes 786440 | tf_op jit(solution)/shard_map/ppermute | solution.py:25
  179.1 10.6 %copy-start.1 = (f32[64,2048]{1,0:T(8,128)S(1)}, f32[64,2048]{1,0:T(8,128)}, u32[]{:S(2)}) copy-start(f32[64,2048]{1,0:T(8,128)} %param.5) | copy-start | bytes 1572868
  180.0 9.8 %collective-permute-start.17 = (bf16[64,2048]{1,0:T(8,128)(2,1)S(1)}, bf16[64,2048]{1,0:T(8,128)(2,1)S(1)}, u32[]{:S(2)}, u32[]{:S(2)}) collective-permute-start(bf16[64,2048]{1,0:T(8,128)(2,1)S(1)} %fusion.15), channel_id=1, source_target_pairs={{1,65},{3,67},{5,69},{7,71},{9,73},{11,75},{13,77},{15,79},{17,81}... | collective-permute-start | bytes 786440 | tf_op jit(solution)/shard_map/ppermute | solution.py:25

commit v2 on v1

v2 whole, which is shorter than its diff:
```python
import functools

import jax
import jax.numpy as jnp
import numpy as np
from jax import lax
from jax.experimental import pallas as pl
from jax.experimental.pallas import tpu as pltpu
from jax.sharding import Mesh
from jax.sharding import PartitionSpec as P

AXES = ("yl", "z", "x", "c", "yh")
SIZES = (2, 4, 4, 2, 2)
DP = ("yl", "z", "x", "c")
CHUNKS = ((0, 32), (32, 64))
NT = (((1,), (1,)), ((), ()))
TN = (((0,), (0,)), ((), ()))
bf16, f32 = jnp.bfloat16, jnp.float32
VMEM = pl.BlockSpec(memory_space=pltpu.VMEM)
SMEM = pl.BlockSpec(memory_space=pltpu.SMEM)


def send(value, move, only=None):
    pairs = []
    for i in range(int(np.prod(SIZES))):
        at = dict(zip(AXES, (int(v) for v in np.unravel_index(i, SIZES))))
        if only is None or only(at):
            to = {**at, **move(at)}
            pairs.append((i, int(np.ravel_multi_index([to[a] for a in AXES], SIZES))))
    return lax.ppermute(value, AXES, pairs)


def along(axis, k):
    return lambda at: {axis: (at[axis] + k) % 4}


def flip(*axes):
    return lambda at: {a: 1 - at[a] for a in axes}


def cross_kernel(rows, at_ref, a1_ref, a2_ref, b1_ref, b2_ref, *outs):
    z, x = at_ref[0], at_ref[1]
    n = outs[0].shape[1]
    for half in range(2):
        for k in range(4):
            picks1, picks2 = [], []
            for j in range(4):
                dx, dz = (k, j) if half == 0 else (j, k)
                block = lax.rem(z + dz, 4) * 4 + lax.rem(x + dx, 4)
                start = pl.ds(pl.multiple_of(block * rows, rows), rows)
                picks1.append(a1_ref[start, :])
                picks2.append(a2_ref[start, :])
            left1, left2 = jnp.concatenate(picks1), jnp.concatenate(picks2)
            cols = pl.ds(half * n, n)
            acc = lax.dot_general(left1, b1_ref[cols, :], NT, preferred_element_type=f32)
            acc += lax.dot_general(left2, b2_ref[cols, :], NT, preferred_element_type=f32)
            outs[4 * half + k][...] = acc.astype(bf16)


def cross_gram(at, a1, a2, b1, b2, rows):
    n = b1.shape[0] // 2
    return pl.pallas_call(
        functools.partial(cross_kernel, rows),
        out_shape=[jax.ShapeDtypeStruct((4 * rows, n), bf16)] * 8,
        in_specs=[SMEM] + [VMEM] * 4,
        out_specs=[VMEM] * 8,
        cost_estimate=pl.CostEstimate(
            flops=4 * 16 * rows * b1.shape[0] * b1.shape[1], bytes_accessed=8 << 20, transcendentals=0
        ),
    )(at, a1, a2, b1, b2)


def own_kernel(at_ref, b1_ref, b2_ref, out_ref):
    base = at_ref[0]
    rows = out_ref.shape[1]
    wide = 2 * rows
    for g in range(4):
        starts = [pl.ds(pl.multiple_of((4 * g + i) * wide + base, rows), rows) for i in range(4)]
        left1 = jnp.concatenate([b1_ref[s, :] for s in starts])
        left2 = jnp.concatenate([b2_ref[s, :] for s in starts])
        for q in range(3):
            cols = pl.ds((g + q) % 4 * 4 * wide, 4 * wide)
            acc = lax.dot_general(left1, b1_ref[cols, :], NT, preferred_element_type=f32)
            acc += lax.dot_general(left2, b2_ref[cols, :], NT, preferred_element_type=f32)
            acc = acc.astype(bf16)
            for i in range(4):
                lo, hi = max(4 * q, i), min(4 * q + 4, i + 9)
                if lo < hi:
                    piece = acc[i * rows : (i + 1) * rows, (lo - 4 * q) * wide : (hi - 4 * q) * wide]
                    out_ref[4 * g + i, :, (lo - i) * wide : (hi - i) * wide] = piece


def own_gram(at, b1, b2, rows):
    return pl.pallas_call(
        own_kernel,
        out_shape=jax.ShapeDtypeStruct((16, rows, 18 * rows), bf16),
        in_specs=[SMEM, VMEM, VMEM],
        out_specs=VMEM,
        cost_estimate=pl.CostEstimate(
            flops=3 * 16 * rows * b1.shape[0] * b1.shape[1], bytes_accessed=6 << 20, transcendentals=0
        ),
    )(at, b1, b2)


def scatter_sum(parts, rows):
    got = []
    for half, axis in ((0, "x"), (1, "z")):
        got.append([send(parts[4 * half + k], along(axis, k)) for k in (1, 2, 3)])
    mids = []
    for half in range(2):
        mids.append([])
        for j in range(4):
            cut = lambda v: lax.slice_in_dim(v, j * rows, (j + 1) * rows).astype(f32)
            total = cut(parts[4 * half])
            for r in got[half]:
                total = total + cut(r)
            mids[half].append(total)
    sums = []
    for half, axis in ((0, "z"), (1, "x")):
        total = mids[half][0]
        rs = [send(mids[half][k].astype(bf16), along(axis, k)) for k in (1, 2, 3)]
        for r in rs:
            total = total + r.astype(f32)
        sums.append(total)
    return jnp.concatenate(sums, axis=1)


def gather_plane(block, z, x):
    zs = jnp.stack([block] + [send(block, along("z", -k)) for k in (1, 2, 3)])
    zs = jnp.roll(zs, z, axis=0)
    xs = jnp.stack([zs] + [send(zs, along("x", -k)) for k in (1, 2, 3)])
    xs = jnp.roll(xs, x, axis=0)
    return xs.transpose(1, 0, 2, 3).reshape((16,) + block.shape)


def on_device(grads, covariance, test_grads, inverse_factor):
    tokens, feats = grads.shape
    z, x, c = lax.axis_index("z"), lax.axis_index("x"), lax.axis_index("c")
    yl, h = lax.axis_index("yl"), lax.axis_index("yh")
    rows = feats // 32
    gt = grads.T
    pick = lambda v, i: lax.dynamic_index_in_dim(v.reshape(16, 2, rows, tokens), i, 1, keepdims=False)
    cut = lambda v, lo, hi: v[:, lo:hi].reshape(16 * (hi - lo), tokens)
    mine, other = pick(gt, c), pick(gt, 1 - c)
    sib = send(gt, flip("c"))
    arrived = []
    for lo, hi in CHUNKS:
        a, b = cut(mine, lo, hi), cut(other, lo, hi)
        if arrived:
            a, b, _ = lax.optimization_barrier((a, b, arrived[-1]))
        arrived.append((send(a, flip("yh")), send(b, flip("yh", "c"))))

    test_grads, inverse_factor, mine = lax.optimization_barrier((test_grads, inverse_factor, mine))
    tt = test_grads.T
    slots = inverse_factor.reshape(rows, 2, 16, 2 * rows).transpose(2, 0, 1, 3).reshape(16, rows, 4 * rows)
    slots = jnp.concatenate([slots, jnp.broadcast_to(tt[None], (16,) + tt.shape)], axis=2)
    slots = lax.all_to_all(slots, ("z", "x"), split_axis=0, concat_axis=0, tiled=True)
    slots = slots.reshape(16 * rows, -1)
    pt = lax.dot_general(slots[:, : 4 * rows], slots[:, 4 * rows :], TN, preferred_element_type=f32)
    pt = pt.reshape(4, rows, -1)
    at = lambda a, b: lax.dynamic_index_in_dim(pt, 2 * a + b, 0, keepdims=False)
    pt = (
        at(yl, c)
        + send(at(yl, 1 - c), flip("c"))
        + send(at(1 - yl, c), flip("yl"))
        + send(at(1 - yl, 1 - c), flip("yl", "c"))
    ).astype(bf16)
    far = send(pt, flip("yl"))
    pt = jnp.concatenate([jnp.where(yl == 0, pt, far), jnp.where(yl == 0, far, pt)], axis=0)
    pt = gather_plane(pt, z, x).reshape(16, 2, rows, -1)
    pt_own = lax.dynamic_index_in_dim(pt, h, 1, keepdims=False)
    pt_cross = lax.dynamic_index_in_dim(pt, 1 - h, 1, keepdims=False)

    own_parts = own_gram(jnp.stack([c * rows]).astype(jnp.int32), gt, sib, rows)
    token = own_parts[0, :8, :128]
    own = lax.all_to_all(own_parts, ("z", "x"), split_axis=0, concat_axis=0, tiled=True)
    own = own.astype(f32).sum(axis=0)
    own = own + send(own.astype(bf16), flip("yl"), lambda at: at["yl"] != at["yh"]).astype(f32)
    chip = z * 4 + x
    wide = jnp.concatenate([own, jnp.zeros((rows, 14 * rows), f32)], axis=1).reshape(rows, 16, 2 * rows)
    direct = jnp.roll(wide, chip, axis=1)
    mirror = direct.astype(bf16).transpose(1, 0, 2)
    mirror = lax.all_to_all(mirror, ("z", "x"), split_axis=0, concat_axis=0, tiled=True)
    mirror = mirror.reshape(16 * rows, 2 * rows).T
    keep = lax.dynamic_slice_in_dim(mirror, c * rows, rows, 0)
    give = lax.dynamic_slice_in_dim(mirror, (1 - c) * rows, rows, 0)
    far = send(give, flip("c"))
    both = [jnp.where(c == 0, keep, far), jnp.where(c == 0, far, keep)]
    both = jnp.stack([v.reshape(rows, 16, rows) for v in both], axis=2).reshape(rows, 16, 2 * rows)
    near = (lax.broadcasted_iota(jnp.int32, (rows, 16, 2 * rows), 1) - chip) % 16 <= 8
    own = jnp.where(near, direct, both.astype(f32)).reshape(rows, feats)

    at_zx = jnp.stack([z, x]).astype(jnp.int32)
    cross = []
    for (lo, hi), (a1, a2) in zip(CHUNKS, arrived):
        a1, a2, _ = lax.optimization_barrier((a1, a2, token))
        part = scatter_sum(cross_gram(at_zx, a1, a2, gt, sib, hi - lo), hi - lo)
        far = send(part.astype(bf16), flip("yl"), lambda at: at["yl"] == at["yh"])
        cross.append(part + far.astype(f32))
    cross = jnp.concatenate(cross, axis=0)
    examples = tokens * 64
    covariance_out = 0.9 * covariance + jnp.where(yl == h, own, cross) / examples

    dot = lambda a, b: lax.dot_general(a, b, TN, preferred_element_type=f32)
    flat = lambda v: v.reshape(-1, v.shape[-1])
    s_keep = dot(flat(mine), flat(pt_own))
    s_give = dot(flat(pick(sib, c)), flat(pt_own))
    for (lo, hi), (a1, a2) in zip(CHUNKS, arrived):
        s_keep += dot(a1, flat(pt_cross[:, lo:hi]))
        s_give += dot(a2, flat(pt_cross[:, lo:hi]))
    scores = s_keep + send(s_give, flip("c"))
    return scores, covariance_out


def solution(mesh):
    grid = Mesh(mesh.devices.reshape(SIZES), AXES)
    return jax.shard_map(
        on_device,
        mesh=grid,
        in_specs=(P(DP, "yh"), P(DP, "yh"), P("yh", DP), P(DP, None)),
        out_specs=(P(DP, "yh"), P(DP, "yh")),
        check_vma=False,
    )
```

time: 194 us -> 238 us (1.23)
  local copies, waits for them, and re-layouts: 8.74 us -> 24.9 us
  starting transfers between devices: 58 us -> 69.7 us
  Pallas kernels: 17.8 us -> 24.5 us
  other arithmetic: 9.71 us -> 16 us
  matrix products: 8.26 us -> 14 us
  waiting for transfers between devices: 89.7 us -> 85.2 us
    ppermute x31 -> x44, waiting for transfers between devices: 75.3 us -> 60.5 us  [send(): return lax.ppermute(value, AXES, pairs)]
    all_to_all x2 -> x3, waiting for transfers between devices: 14.4 us -> 24.7 us  [the longest x1 17.7 us: on_device(): lax.all_to_all(slots, ('z', 'x'), split_axis=0, concat_axis=0, tiled=True)]
    ppermute x31 -> x44, starting transfers between devices: 43.9 us -> 53.1 us  [send(): return lax.ppermute(value, AXES, pairs)]
    unnamed x30 -> x54, local copies, waits for them, and re-layouts: 4.28 us -> 11.9 us
    pallas_call x2 -> x3, Pallas kernels: 17.8 us -> 24.5 us  [the longest x2 17.5 us: cross_gram(): pl.pallas_call(functools.partial(cross_kernel, rows), out_shape=[jax.Shap...]
    dot_general x5 -> x7, matrix products: 8.26 us -> 14 us  [the longest x6 12.5 us: on_device(): dot = lambda a, b: lax.dot_general(a, b, TN, preferred_element_type=f32)]
    reshape x0 -> x2, local copies, waits for them, and re-layouts: none -> 3.43 us  [on_device(): inverse_factor.reshape(rows, 2, 16, 2 * rows).transpose(2, 0, 1, 3)]
    add x0 -> x3, other arithmetic: none -> 3.3 us  [the longest x2 3.27 us: on_device(): cross.append(part + far.astype(f32))]
  transfers between devices with their start and end apart: 33 -> 47, of which waited for: 14 -> 18; matrix products, arithmetic and copies ran while one was open for 11% -> 16% of each run, Pallas kernels for 9% -> 10%
where the time goes in v2:
time: 238 us; the launch traced here: 235 us
  waiting for transfers between devices  85.2 us (36%)
  starting transfers between devices  69.7 us (29%)
  local copies, waits for them, and re-layouts  24.9 us (10%)
  Pallas kernels  24.5 us (10%)
  other arithmetic  16 us (7%)
  matrix products  14 us (6%)
    ppermute x44, waiting for transfers between devices, send(): return lax.ppermute(value, AXES, pairs)  60.5 us
    ppermute x44, starting transfers between devices, send(): return lax.ppermute(value, AXES, pairs)  53.1 us
    all_to_all x1, waiting for transfers between devices, on_device(): lax.all_to_all(slots, ('z', 'x'), split_axis=0, concat_axis=0, tiled=True)  17.7 us
    pallas_call x2, Pallas kernels, cross_gram(): pl.pallas_call(functools.partial(cross_kernel, rows), out_shape=[jax.Shap...  17.5 us
    dot_general x6, matrix products, on_device(): dot = lambda a, b: lax.dot_general(a, b, TN, preferred_element_type=f32)  12.5 us
    unnamed x54, local copies, waits for them, and re-layouts  11.9 us
    all_to_all x1, starting transfers between devices, on_device(): lax.all_to_all(slots, ('z', 'x'), split_axis=0, concat_axis=0, tiled=True)  8.01 us
    pallas_call x1, Pallas kernels, own_gram(): pl.pallas_call(own_kernel, out_shape=jax.ShapeDtypeStruct((16, rows, 18 *...  7.06 us
  transfers between devices with their start and end apart: 47, of which 18 were waited for; matrix products, arithmetic and copies ran while one was open for 16% of the time, Pallas kernels for 10%

profile of v2, /device:TPU:0, one launch (start us, length us, event | category | flops | bytes accessed | tf_op | source)
XLA Modules:
  0.0 235.5 jit_solution(7088210482931975694)
XLA Ops:
  0.6 2.9 %copy.27 = bf16[512,2048]{0,1:T(8,128)(2,1)S(1)} copy(bf16[512,2048]{1,0:T(8,128)(2,1)} %param.4) | data formatting | bytes 4194304 | tf_op args[0]
  6.3 2.2 reshape.75
  8.5 2.1 pad_maximum_fusion
  10.7 8.0 %all-to-all-start = ((bf16[16,64,512]{2,1,0:T(8,128)(2,1)}), bf16[16,64,512]{2,1,0:T(8,128)(2,1)}, u32[]{:S(2)}, u32[]{:S(2)}) async-start(bf16[16,64,512]{2,1,0:T(8,128)(2,1)} %pad_maximum_fusion), calls=%async_computation | async-start | bytes 2097152 | tf_op jit(solution)/shard_map/all_to_all | solution.py:157
  18.7 17.7 %all-to-all-done = bf16[16,64,512]{2,1,0:T(8,128)(2,1)} async-done(((bf16[16,64,512]{2,1,0:T(8,128)(2,1)}), bf16[16,64,512]{2,1,0:T(8,128)(2,1)}, u32[]{:S(2)}, u32[]{:S(2)}) %all-to-all-start) | async-done | bytes 1048608 | tf_op jit(solution)/shard_map/all_to_all | solution.py:157
  38.6 1.7 collective-permute-start.2
  40.7 2.3 collective-permute-done.2
  43.0 1.7 collective-permute-done.1
  45.6 1.7 collective-permute-start.3
  47.3 2.6 %fusion.20 = (bf16[16,32,512]{2,1,0:T(8,128)(2,1)}, bf16[16,32,512]{2,1,0:T(8,128)(2,1)}, bf16[16,32,512]{2,1,0:T(8,128)(2,1)}, bf16[16,32,512]{2,1,0:T(8,128)(2,1)}) fusion(bf16[16,64,512]{2,1,0:T(8,128)(2,1)} %get-tuple-element.54, bf16[16,64,512]{2,1,0:T(8,128)(2,1)S(1)} %get-tuple-element.27), kind=kLoop, calls=%fused_computation.92 | loop fusion | bytes 4194304 | tf_op jit(solution)/shard_map/slice | solution.py:143
  49.8 1.7 collective-permute-start.11
  54.8 3.6 %collective-permute-done.4 = bf16[128,256]{1,0:T(8,128)(2,1)S(1)} collective-permute-done((bf16[128,256]{1,0:T(8,128)(2,1)S(1)}, bf16[128,256]{1,0:T(8,128)(2,1)S(1)}, u32[]{:S(2)}, u32[]{:S(2)}) %collective-permute-start.4) | collective-permute-done | bytes 65568 | tf_op jit(solution)/shard_map/ppermute | solution.py:30
  59.4 4.5 %collective-permute-done.6 = bf16[128,256]{1,0:T(8,128)(2,1)S(1)} collective-permute-done((bf16[128,256]{1,0:T(8,128)(2,1)S(1)}, bf16[128,256]{1,0:T(8,128)(2,1)S(1)}, u32[]{:S(2)}, u32[]{:S(2)}) %collective-permute-start.6) | collective-permute-done | bytes 65568 | tf_op jit(solution)/shard_map/ppermute | solution.py:30
  68.0 9.0 %collective-permute-done.10.a1_ref = bf16[512,512]{1,0:T(8,128)(2,1)} collective-permute-done((bf16[512,512]{1,0:T(8,128)(2,1)}, bf16[512,512]{1,0:T(8,128)(2,1)}, u32[]{:S(2)}, u32[]{:S(2)}) %collective-permute-start.10) | collective-permute-done | bytes 524320 | tf_op jit(solution)/shard_map/ppermute | solution.py:30
  77.0 1.8 collective-permute-start.12
  80.8 1.7 bitcast_dynamic-update-slice_fusion
  82.4 7.8 %collective-permute-done.9 = bf16[4,128,256]{2,1,0:T(8,128)(2,1)S(1)} collective-permute-done((bf16[4,128,256]{2,1,0:T(8,128)(2,1)}, bf16[4,128,256]{2,1,0:T(8,128)(2,1)S(1)}, u32[]{:S(2)}, u32[]{:S(2)}) %collective-permute-start.9) | collective-permute-done | bytes 262176 | tf_op jit(solution)/shard_map/ppermute | solution.py:30
  91.0 1.7 bitcast_dynamic-update-slice_fusion.7
  93.4 1.7 bitcast_dynamic-update-slice_fusion.1
  97.2 2.3 fusion.24
  100.0 2.2 convolution_add_fusion.1
  102.3 7.1 %shard_map.59 = bf16[16,64,1152]{2,1,0:T(8,128)(2,1)} custom-call(s32[1]{0:T(128)} %bitcast.41.at_ref, bf16[2048,512]{1,0:T(8,128)(2,1)} %bitcast.123, bf16[2048,512]{1,0:T(8,128)(2,1)} %collective-permute-done.13.b2_ref), custom_call_target="tpu_custom_call" | custom-call | flops 3221225472 | bytes 6291456 | tf_op jit(solution)/shard_map/pallas_call | solution.py:94
  109.3 8.7 %shard_map.60 = (bf16[128,1024]{1,0:T(8,128)(2,1)}, bf16[128,1024]{1,0:T(8,128)(2,1)}, bf16[128,1024]{1,0:T(8,128)(2,1)}, bf16[128,1024]{1,0:T(8,128)(2,1)}, bf1...) custom-call(s32[2]{0:T(128)} %pad_add_fusion.at_ref, ...), custom_call_target="tpu_custom_call" | custom-call | flops 2147483648 | bytes 8388608 | tf_op jit(solution)/shard_map/pallas_call | solution.py:62
  119.2 2.2 fusion.25
  121.4 4.7 %all-to-all-start.1 = ((bf16[16,64,1152]{2,1,0:T(8,128)(2,1)}), bf16[16,64,1152]{2,1,0:T(8,128)(2,1)S(1)}, u32[]{:S(2)}, u32[]{:S(2)}) async-start(bf16[16,64,1152]{2,1,0:T(8,128)(2,1)} %shard_map.59), calls=%async_computation.1 | async-start | bytes 4718592 | tf_op jit(solution)/shard_map/all_to_all | solution.py:176
  126.0 3.2 %collective-permute-start.20 = (bf16[128,1024]{1,0:T(8,128)(2,1)}, bf16[128,1024]{1,0:T(8,128)(2,1)}, u32[]{:S(2)}, u32[]{:S(2)}) collective-permute-start(bf16[128,1024]{1,0:T(8,128)(2,1)} %get-tuple-element.37), channel_id=1, source_target_pairs={{0,12},{1,13},{2,14},{3,15},{4,0},{5,1},{6,2},{7,3},{8,4},{9,5},{1... | collective-permute-start | bytes 786440 | tf_op jit(solution)/shard_map/ppermute | solution.py:30
  130.7 2.7 %collective-permute-start.25 = (bf16[128,1024]{1,0:T(8,128)(2,1)}, bf16[128,1024]{1,0:T(8,128)(2,1)}, u32[]{:S(2)}, u32[]{:S(2)}) collective-permute-start(bf16[128,1024]{1,0:T(8,128)(2,1)} %get-tuple-element.40), channel_id=1, source_target_pairs={{0,32},{1,33},{2,34},{3,35},{4,36},{5,37},{6,38},{7,39},{8,40},{9,... | collective-permute-start | bytes 786440 | tf_op jit(solution)/shard_map/ppermute | solution.py:30
  133.4 8.7 %shard_map.61 = (bf16[128,1024]{1,0:T(8,128)(2,1)}, bf16[128,1024]{1,0:T(8,128)(2,1)}, bf16[128,1024]{1,0:T(8,128)(2,1)}, bf16[128,1024]{1,0:T(8,128)(2,1)}, bf1...) custom-call(s32[2]{0:T(128)} %pad_add_fusion.at_ref, ...), custom_call_target="tpu_custom_call" | custom-call | flops 2147483648 | bytes 8388608 | tf_op jit(solution)/shard_map/pallas_call | solution.py:62
  142.1 1.6 collective-permute-done.18
  144.5 2.9 %fusion.2 = f32[512,256]{1,0:T(8,128)} fusion(f32[512,256]{1,0:T(8,128)} %fusion.25, f32[512,256]{1,0:T(8,128)S(1)} %copy-done.5, bf16[16,2,64,512]{3,2,1,0:T(8,128)(2,1)} %bitcast.37, s32[]{:T(128)S(6)} %select_n.109, bf16[16,1,64,256]{3,2,1,0:T(8,128)(2,1)} %copy-done.6), kind=kOutput, calls=%fused_computation.6 | convolution fusion | flops 268697600 | bytes 3145732 | tf_op jit(solution)/shard_map/dot_general | solution.py:204
  147.5 13.1 %collective-permute-done.20 = bf16[128,1024]{1,0:T(8,128)(2,1)} collective-permute-done((bf16[128,1024]{1,0:T(8,128)(2,1)}, bf16[128,1024]{1,0:T(8,128)(2,1)}, u32[]{:S(2)}, u32[]{:S(2)}) %collective-permute-start.20) | collective-permute-done | bytes 262176 | tf_op jit(solution)/shard_map/ppermute | solution.py:30
  166.5 2.0 collective-permute-start.38
  168.6 3.5 %collective-permute-start.39 = (bf16[128,1024]{1,0:T(8,128)(2,1)S(1)}, bf16[128,1024]{1,0:T(8,128)(2,1)S(1)}, u32[]{:S(2)}, u32[]{:S(2)}) collective-permute-start(bf16[128,1024]{1,0:T(8,128)(2,1)S(1)} %copy-done.14), channel_id=1, source_target_pairs={{0,48},{1,49},{2,50},{3,51},{4,52},{5,53},{6,54},{7,55},{8,56},{9,... | collective-permute-start | bytes 786440 | tf_op jit(solution)/shard_map/ppermute | solution.py:30
  173.9 3.1 %collective-permute-done.33 = bf16[128,1024]{1,0:T(8,128)(2,1)S(1)} collective-permute-done((bf16[128,1024]{1,0:T(8,128)(2,1)S(1)}, bf16[128,1024]{1,0:T(8,128)(2,1)S(1)}, u32[]{:S(2)}, u32[]{:S(2)}) %collective-permute-start.33) | collective-permute-done | bytes 262176 | tf_op jit(solution)/shard_map/ppermute | solution.py:30
  177.2 3.5 %collective-permute-done.37 = bf16[128,1024]{1,0:T(8,128)(2,1)S(1)} collective-permute-done((bf16[128,1024]{1,0:T(8,128)(2,1)S(1)}, bf16[128,1024]{1,0:T(8,128)(2,1)S(1)}, u32[]{:S(2)}, u32[]{:S(2)}) %collective-permute-start.37) | collective-permute-done | bytes 262176 | tf_op jit(solution)/shard_map/ppermute | solution.py:30
  183.7 2.2 collective-permute-start.29
  185.9 2.1 collective-permute-start.28
  189.5 2.7 %collective-permute-start.36 = (bf16[32,1024]{1,0:T(8,128)(2,1)S(1)}, bf16[32,1024]{1,0:T(8,128)(2,1)S(1)}, u32[]{:S(2)}, u32[]{:S(2)}) collective-permute-start(bf16[32,1024]{1,0:T(8,128)(2,1)S(1)} %get-tuple-element.63), channel_id=1, source_target_pairs={{0,48},{1,49},{2,50},{3,51},{4,52},{5,53},{6,54},{7,55},{8,56},{9,... | collective-permute-start | bytes 196616 | tf_op jit(solution)/shard_map/ppermute | solution.py:30
  195.3 2.7 %collective-permute-start.42 = (bf16[32,1024]{1,0:T(8,128)(2,1)S(1)}, bf16[32,1024]{1,0:T(8,128)(2,1)S(1)}, u32[]{:S(2)}, u32[]{:S(2)}) collective-permute-start(bf16[32,1024]{1,0:T(8,128)(2,1)S(1)} %get-tuple-element.66), channel_id=1, source_target_pairs={{0,12},{1,13},{2,14},{3,15},{4,0},{5,1},{6,2},{7,3},{8,4},{9,5},{1... | collective-permute-start | bytes 196616 | tf_op jit(solution)/shard_map/ppermute | solution.py:30
  198.7 2.2 collective-permute-start.30
  201.0 2.9 %collective-permute-done.41 = bf16[32,1024]{1,0:T(8,128)(2,1)S(1)} collective-permute-done((bf16[32,1024]{1,0:T(8,128)(2,1)S(1)}, bf16[32,1024]{1,0:T(8,128)(2,1)S(1)}, u32[]{:S(2)}, u32[]{:S(2)}) %collective-permute-start.41) | collective-permute-done | bytes 65568 | tf_op jit(solution)/shard_map/ppermute | solution.py:30
  204.6 2.3 collective-permute-start.43
  208.8 1.6 convert_add_fusion.2
  210.5 3.8 %collective-permute-done.16 = bf16[64,1152]{1,0:T(8,128)(2,1)S(1)} collective-permute-done((bf16[64,1152]{1,0:T(8,128)(2,1)S(1)}, bf16[64,1152]{1,0:T(8,128)(2,1)S(1)}, u32[]{:S(2)}, u32[]{:S(2)}) %collective-permute-start.16) | collective-permute-done | bytes 147488 | tf_op jit(solution)/shard_map/ppermute | solution.py:30
  215.4 3.9 %all-to-all-start.2 = ((bf16[16,64,128]{2,1,0:T(8,128)(2,1)}), bf16[16,64,128]{2,1,0:T(8,128)(2,1)S(1)}, u32[]{:S(2)}, u32[]{:S(2)}) async-start(bf16[16,64,128]{2,1,0:T(8,128)(2,1)} %copy.33), calls=%async_computation.2 | async-start | bytes 524288 | tf_op jit(solution)/shard_map/all_to_all | solution.py:183
  221.0 7.1 %all-to-all-done.2 = bf16[16,64,128]{2,1,0:T(8,128)(2,1)S(1)} async-done(((bf16[16,64,128]{2,1,0:T(8,128)(2,1)}), bf16[16,64,128]{2,1,0:T(8,128)(2,1)S(1)}, u32[]{:S(2)}, u32[]{:S(2)}) %all-to-all-start.2) | async-done | bytes 262176 | tf_op jit(solution)/shard_map/all_to_all | solution.py:183
  228.3 2.3 fusion
  233.4 2.1 fusion.7
  (156 shorter events, 48.3 us)
Async XLA Ops:
  3.5 49.3 %copy-start = (bf16[512,2048]{0,1:T(8,128)(2,1)}, bf16[512,2048]{0,1:T(8,128)(2,1)S(1)}, u32[]{:S(2)}) copy-start(bf16[512,2048]{0,1:T(8,128)(2,1)S(1)} %copy.27) | copy-start | bytes 6291460
  10.7 25.7 %all-to-all-start = ((bf16[16,64,512]{2,1,0:T(8,128)(2,1)}), bf16[16,64,512]{2,1,0:T(8,128)(2,1)}, u32[]{:S(2)}, u32[]{:S(2)}) async-start(bf16[16,64,512]{2,1,0:T(8,128)(2,1)} %pad_maximum_fusion), calls=%async_computation | async-start | bytes 2097152 | tf_op jit(solution)/shard_map/all_to_all | solution.py:157
  38.6 2.1 collective-permute-start
  38.6 4.5 %collective-permute-start.2 = (f32[64,256]{1,0:T(8,128)}, f32[64,256]{1,0:T(8,128)}, u32[]{:S(2)}, u32[]{:S(2)}) collective-permute-start(f32[64,256]{1,0:T(8,128)} %get-tuple-element.79), channel_id=1, source_target_pairs={{0,66},{1,67},{2,64},{3,65},{4,70},{5,71},{6,68},{7,69},{8,74},{9,... | collective-permute-start | bytes 196616 | tf_op jit(solution)/shard_map/ppermute | solution.py:30
  40.3 4.4 %collective-permute-start.1 = (f32[64,256]{1,0:T(8,128)S(1)}, f32[64,256]{1,0:T(8,128)}, u32[]{:S(2)}, u32[]{:S(2)}) collective-permute-start(f32[64,256]{1,0:T(8,128)S(1)} %get-tuple-element.80), channel_id=1, source_target_pairs={{0,64},{1,65},{2,66},{3,67},{4,68},{5,69},{6,70},{7,71},{8,72},{9,... | collective-permute-start | bytes 196616 | tf_op jit(solution)/shard_map/ppermute | solution.py:30
  45.6 7.6 %collective-permute-start.3 = (bf16[64,256]{1,0:T(8,128)(2,1)S(1)}, bf16[64,256]{1,0:T(8,128)(2,1)S(1)}, u32[]{:S(2)}, u32[]{:S(2)}) collective-permute-start(bf16[64,256]{1,0:T(8,128)(2,1)S(1)} %fusion.17), channel_id=1, source_target_pairs={{0,64},{1,65},{2,66},{3,67},{4,68},{5,69},{6,70},{7,71},{8,72},{9,... | collective-permute-start | bytes 98312 | tf_op jit(solution)/shard_map/ppermute | solution.py:30
  49.8 18.1 %collective-permute-start.11 = (bf16[512,512]{1,0:T(8,128)(2,1)}, bf16[512,512]{1,0:T(8,128)(2,1)}, u32[]{:S(2)}, u32[]{:S(2)}) collective-permute-start(bf16[512,512]{1,0:T(8,128)(2,1)} %bitcast.35), channel_id=1, source_target_pairs={{0,3},{1,2},{2,1},{3,0},{4,7},{5,6},{6,5},{7,4},{8,11},{9,10},{10,... | collective-permute-start | bytes 1572872 | tf_op jit(solution)/shard_map/ppermute | solution.py:30
  51.5 25.5 %collective-permute-start.10 = (bf16[512,512]{1,0:T(8,128)(2,1)}, bf16[512,512]{1,0:T(8,128)(2,1)}, u32[]{:S(2)}, u32[]{:S(2)}) collective-permute-start(bf16[512,512]{1,0:T(8,128)(2,1)} %bitcast.27), channel_id=1, source_target_pairs={{0,1},{1,0},{2,3},{3,2},{4,5},{5,4},{6,7},{7,6},{8,9},{9,8},{10,11... | collective-permute-start | bytes 1572872 | tf_op jit(solution)/shard_map/ppermute | solution.py:30
  52.8 49.5 %collective-permute-start.13 = (bf16[2048,512]{1,0:T(8,128)(2,1)S(1)}, bf16[2048,512]{1,0:T(8,128)(2,1)}, u32[]{:S(2)}, u32[]{:S(2)}) collective-permute-start(bf16[2048,512]{1,0:T(8,128)(2,1)S(1)} %bitcast.122), channel_id=1, source_target_pairs={{0,2},{1,3},{2,0},{3,1},{4,6},{5,7},{6,4},{7,5},{8,10},{9,11},{10,... | collective-permute-start | bytes 6291464 | tf_op jit(solution)/shard_map/ppermute | solution.py:30
  53.2 6.1 %collective-permute-start.5 = (bf16[128,256]{1,0:T(8,128)(2,1)S(1)}, bf16[128,256]{1,0:T(8,128)(2,1)S(1)}, u32[]{:S(2)}, u32[]{:S(2)}) collective-permute-start(bf16[128,256]{1,0:T(8,128)(2,1)S(1)} %pad_maximum_fusion.3), channel_id=1, source_target_pairs={{0,32},{1,33},{2,34},{3,35},{4,36},{5,37},{6,38},{7,39},{8,40},{9,... | collective-permute-start | bytes 196616 | tf_op jit(solution)/shard_map/ppermute | solution.py:30
  54.2 4.3 %collective-permute-start.4 = (bf16[128,256]{1,0:T(8,128)(2,1)S(1)}, bf16[128,256]{1,0:T(8,128)(2,1)S(1)}, u32[]{:S(2)}, u32[]{:S(2)}) collective-permute-start(bf16[128,256]{1,0:T(8,128)(2,1)S(1)} %pad_maximum_fusion.3), channel_id=1, source_target_pairs={{0,48},{1,49},{2,50},{3,51},{4,52},{5,53},{6,54},{7,55},{8,56},{9,... | collective-permute-start | bytes 196616 | tf_op jit(solution)/shard_map/ppermute | solution.py:30
  58.4 5.5 %collective-permute-start.6 = (bf16[128,256]{1,0:T(8,128)(2,1)S(1)}, bf16[128,256]{1,0:T(8,128)(2,1)S(1)}, u32[]{:S(2)}, u32[]{:S(2)}) collective-permute-start(bf16[128,256]{1,0:T(8,128)(2,1)S(1)} %pad_maximum_fusion.3), channel_id=1, source_target_pairs={{0,16},{1,17},{2,18},{3,19},{4,20},{5,21},{6,22},{7,23},{8,24},{9,... | collective-permute-start | bytes 196616 | tf_op jit(solution)/shard_map/ppermute | solution.py:30
  64.8 15.2 %collective-permute-start.7 = (bf16[4,128,256]{2,1,0:T(8,128)(2,1)}, bf16[4,128,256]{2,1,0:T(8,128)(2,1)S(1)}, u32[]{:S(2)}, u32[]{:S(2)}) collective-permute-start(bf16[4,128,256]{2,1,0:T(8,128)(2,1)} %get-tuple-element.53), channel_id=1, source_target_pairs={{0,12},{1,13},{2,14},{3,15},{4,0},{5,1},{6,2},{7,3},{8,4},{9,5},{1... | collective-permute-start | bytes 786440 | tf_op jit(solution)/shard_map/ppermute | solution.py:30
  65.7 15.1 %collective-permute-start.8 = (bf16[4,128,256]{2,1,0:T(8,128)(2,1)}, bf16[4,128,256]{2,1,0:T(8,128)(2,1)}, u32[]{:S(2)}, u32[]{:S(2)}) collective-permute-start(bf16[4,128,256]{2,1,0:T(8,128)(2,1)} %get-tuple-element.53), channel_id=1, source_target_pairs={{0,8},{1,9},{2,10},{3,11},{4,12},{5,13},{6,14},{7,15},{8,0},{9,1},... | collective-permute-start | bytes 786440 | tf_op jit(solution)/shard_map/ppermute | solution.py:30
  77.0 49.0 %collective-permute-start.12 = (bf16[512,512]{1,0:T(8,128)(2,1)}, bf16[512,512]{1,0:T(8,128)(2,1)}, u32[]{:S(2)}, u32[]{:S(2)}) collective-permute-start(bf16[512,512]{1,0:T(8,128)(2,1)} %bitcast.143), channel_id=1, source_target_pairs={{0,1},{1,0},{2,3},{3,2},{4,5},{5,4},{6,7},{7,6},{8,9},{9,8},{10,11... | collective-permute-start | bytes 1572872 | tf_op jit(solution)/shard_map/ppermute | solution.py:30
  78.8 40.4 %collective-permute-start.14 = (bf16[512,512]{1,0:T(8,128)(2,1)}, bf16[512,512]{1,0:T(8,128)(2,1)}, u32[]{:S(2)}, u32[]{:S(2)}) collective-permute-start(bf16[512,512]{1,0:T(8,128)(2,1)} %bitcast.144), channel_id=1, source_target_pairs={{0,3},{1,2},{2,1},{3,0},{4,7},{5,6},{6,5},{7,4},{8,11},{9,10},{10,... | collective-permute-start | bytes 1572872 | tf_op jit(solution)/shard_map/ppermute | solution.py:30
  80.0 10.3 %collective-permute-start.9 = (bf16[4,128,256]{2,1,0:T(8,128)(2,1)}, bf16[4,128,256]{2,1,0:T(8,128)(2,1)S(1)}, u32[]{:S(2)}, u32[]{:S(2)}) collective-permute-start(bf16[4,128,256]{2,1,0:T(8,128)(2,1)} %get-tuple-element.53), channel_id=1, source_target_pairs={{0,4},{1,5},{2,6},{3,7},{4,8},{5,9},{6,10},{7,11},{8,12},{9,13},{1... | collective-permute-start | bytes 786440 | tf_op jit(solution)/shard_map/ppermute | solution.py:30
  118.1 25.7 %collective-permute-start.18 = (bf16[128,1024]{1,0:T(8,128)(2,1)}, bf16[128,1024]{1,0:T(8,128)(2,1)S(1)}, u32[]{:S(2)}, u32[]{:S(2)}) collective-permute-start(bf16[128,1024]{1,0:T(8,128)(2,1)} %get-tuple-element.35), channel_id=1, source_target_pairs={{0,4},{1,5},{2,6},{3,7},{4,8},{5,9},{6,10},{7,11},{8,12},{9,13},{1... | collective-permute-start | bytes 786440 | tf_op jit(solution)/shard_map/ppermute | solution.py:30
  118.1 26.1 %collective-permute-start.19 = (bf16[128,1024]{1,0:T(8,128)(2,1)}, bf16[128,1024]{1,0:T(8,128)(2,1)}, u32[]{:S(2)}, u32[]{:S(2)}) collective-permute-start(bf16[128,1024]{1,0:T(8,128)(2,1)} %get-tuple-element.36), channel_id=1, source_target_pairs={{0,8},{1,9},{2,10},{3,11},{4,12},{5,13},{6,14},{7,15},{8,0},{9,1},... | collective-permute-start | bytes 786440 | tf_op jit(solution)/shard_map/ppermute | solution.py:30
  121.4 85.5 %all-to-all-start.1 = ((bf16[16,64,1152]{2,1,0:T(8,128)(2,1)}), bf16[16,64,1152]{2,1,0:T(8,128)(2,1)S(1)}, u32[]{:S(2)}, u32[]{:S(2)}) async-start(bf16[16,64,1152]{2,1,0:T(8,128)(2,1)} %shard_map.59), calls=%async_computation.1 | async-start | bytes 4718592 | tf_op jit(solution)/shard_map/all_to_all | solution.py:176
  126.0 34.6 %collective-permute-start.20 = (bf16[128,1024]{1,0:T(8,128)(2,1)}, bf16[128,1024]{1,0:T(8,128)(2,1)}, u32[]{:S(2)}, u32[]{:S(2)}) collective-permute-start(bf16[128,1024]{1,0:T(8,128)(2,1)} %get-tuple-element.37), channel_id=1, source_target_pairs={{0,12},{1,13},{2,14},{3,15},{4,0},{5,1},{6,2},{7,3},{8,4},{9,5},{1... | collective-permute-start | bytes 786440 | tf_op jit(solution)/shard_map/ppermute | solution.py:30
  129.3 33.7 %collective-permute-start.24 = (bf16[128,1024]{1,0:T(8,128)(2,1)}, bf16[128,1024]{1,0:T(8,128)(2,1)}, u32[]{:S(2)}, u32[]{:S(2)}) collective-permute-start(bf16[128,1024]{1,0:T(8,128)(2,1)} %get-tuple-element.39), channel_id=1, source_target_pairs={{0,16},{1,17},{2,18},{3,19},{4,20},{5,21},{6,22},{7,23},{8,24},{9,... | collective-permute-start | bytes 786440 | tf_op jit(solution)/shard_map/ppermute | solution.py:30
  130.7 35.3 %collective-permute-start.25 = (bf16[128,1024]{1,0:T(8,128)(2,1)}, bf16[128,1024]{1,0:T(8,128)(2,1)}, u32[]{:S(2)}, u32[]{:S(2)}) collective-permute-start(bf16[128,1024]{1,0:T(8,128)(2,1)} %get-tuple-element.40), channel_id=1, source_target_pairs={{0,32},{1,33},{2,34},{3,35},{4,36},{5,37},{6,38},{7,39},{8,40},{9,... | collective-permute-start | bytes 786440 | tf_op jit(solution)/shard_map/ppermute | solution.py:30
  143.8 22.8 %collective-permute-start.26 = (bf16[128,1024]{1,0:T(8,128)(2,1)}, bf16[128,1024]{1,0:T(8,128)(2,1)S(1)}, u32[]{:S(2)}, u32[]{:S(2)}) collective-permute-start(bf16[128,1024]{1,0:T(8,128)(2,1)} %get-tuple-element.41), channel_id=1, source_target_pairs={{0,48},{1,49},{2,50},{3,51},{4,52},{5,53},{6,54},{7,55},{8,56},{9,... | collective-permute-start | bytes 786440 | tf_op jit(solution)/shard_map/ppermute | solution.py:30
  144.2 24.4 %collective-permute-start.31 = (bf16[128,1024]{1,0:T(8,128)(2,1)}, bf16[128,1024]{1,0:T(8,128)(2,1)S(1)}, u32[]{:S(2)}, u32[]{:S(2)}) collective-permute-start(bf16[128,1024]{1,0:T(8,128)(2,1)} %get-tuple-element.45), channel_id=1, source_target_pairs={{0,4},{1,5},{2,6},{3,7},{4,8},{5,9},{6,10},{7,11},{8,12},{9,13},{1... | collective-permute-start | bytes 786440 | tf_op jit(solution)/shard_map/ppermute | solution.py:30
  160.6 13.3 %collective-permute-start.32 = (bf16[128,1024]{1,0:T(8,128)(2,1)S(1)}, bf16[128,1024]{1,0:T(8,128)(2,1)S(1)}, u32[]{:S(2)}, u32[]{:S(2)}) collective-permute-start(bf16[128,1024]{1,0:T(8,128)(2,1)S(1)} %copy-done.18), channel_id=1, source_target_pairs={{0,8},{1,9},{2,10},{3,11},{4,12},{5,13},{6,14},{7,15},{8,0},{9,1},... | collective-permute-start | bytes 786440 | tf_op jit(solution)/shard_map/ppermute | solution.py:30
  162.9 14.1 %collective-permute-start.33 = (bf16[128,1024]{1,0:T(8,128)(2,1)S(1)}, bf16[128,1024]{1,0:T(8,128)(2,1)S(1)}, u32[]{:S(2)}, u32[]{:S(2)}) collective-permute-start(bf16[128,1024]{1,0:T(8,128)(2,1)S(1)} %copy-done.17), channel_id=1, source_target_pairs={{0,12},{1,13},{2,14},{3,15},{4,0},{5,1},{6,2},{7,3},{8,4},{9,5},{1... | collective-permute-start | bytes 786440 | tf_op jit(solution)/shard_map/ppermute | solution.py:30
  166.0 14.7 %collective-permute-start.37 = (bf16[128,1024]{1,0:T(8,128)(2,1)S(1)}, bf16[128,1024]{1,0:T(8,128)(2,1)S(1)}, u32[]{:S(2)}, u32[]{:S(2)}) collective-permute-start(bf16[128,1024]{1,0:T(8,128)(2,1)S(1)} %copy-done.16), channel_id=1, source_target_pairs={{0,16},{1,17},{2,18},{3,19},{4,20},{5,21},{6,22},{7,23},{8,24},{9,... | collective-permute-start | bytes 786440 | tf_op jit(solution)/shard_map/ppermute | solution.py:30
  166.5 14.2 %collective-permute-start.38 = (bf16[128,1024]{1,0:T(8,128)(2,1)S(1)}, bf16[128,1024]{1,0:T(8,128)(2,1)S(1)}, u32[]{:S(2)}, u32[]{:S(2)}) collective-permute-start(bf16[128,1024]{1,0:T(8,128)(2,1)S(1)} %copy-done.15), channel_id=1, source_target_pairs={{0,32},{1,33},{2,34},{3,35},{4,36},{5,37},{6,38},{7,39},{8,40},{9,... | collective-permute-start | bytes 786440 | tf_op jit(solution)/shard_map/ppermute | solution.py:30
  168.6 13.9 %collective-permute-start.39 = (bf16[128,1024]{1,0:T(8,128)(2,1)S(1)}, bf16[128,1024]{1,0:T(8,128)(2,1)S(1)}, u32[]{:S(2)}, u32[]{:S(2)}) collective-permute-start(bf16[128,1024]{1,0:T(8,128)(2,1)S(1)} %copy-done.14), channel_id=1, source_target_pairs={{0,48},{1,49},{2,50},{3,51},{4,52},{5,53},{6,54},{7,55},{8,56},{9,... | collective-permute-start | bytes 786440 | tf_op jit(solution)/shard_map/ppermute | solution.py:30
  173.9 54.4 %collective-permute-start.15 = (f32[512,256]{1,0:T(8,128)}, f32[512,256]{1,0:T(8,128)}, u32[]{:S(2)}, u32[]{:S(2)}) collective-permute-start(f32[512,256]{1,0:T(8,128)} %fusion.2), channel_id=1, source_target_pairs={{0,2},{1,3},{2,0},{3,1},{4,6},{5,7},{6,4},{7,5},{8,10},{9,11},{10,... | collective-permute-start | bytes 1572872 | tf_op jit(solution)/shard_map/ppermute | solution.py:30
  177.0 6.6 %collective-permute-start.21 = (bf16[32,1024]{1,0:T(8,128)(2,1)S(1)}, bf16[32,1024]{1,0:T(8,128)(2,1)S(1)}, u32[]{:S(2)}, u32[]{:S(2)}) collective-permute-start(bf16[32,1024]{1,0:T(8,128)(2,1)S(1)} %get-tuple-element.56), channel_id=1, source_target_pairs={{0,16},{1,17},{2,18},{3,19},{4,20},{5,21},{6,22},{7,23},{8,24},{9,... | collective-permute-start | bytes 196616 | tf_op jit(solution)/shard_map/ppermute | solution.py:30
  180.7 5.2 %collective-permute-start.23 = (bf16[32,1024]{1,0:T(8,128)(2,1)S(1)}, bf16[32,1024]{1,0:T(8,128)(2,1)S(1)}, u32[]{:S(2)}, u32[]{:S(2)}) collective-permute-start(bf16[32,1024]{1,0:T(8,128)(2,1)S(1)} %get-tuple-element.57), channel_id=1, source_target_pairs={{0,48},{1,49},{2,50},{3,51},{4,52},{5,53},{6,54},{7,55},{8,56},{9,... | collective-permute-start | bytes 196616 | tf_op jit(solution)/shard_map/ppermute | solution.py:30
  180.7 7.2 %collective-permute-start.22 = (bf16[32,1024]{1,0:T(8,128)(2,1)S(1)}, bf16[32,1024]{1,0:T(8,128)(2,1)S(1)}, u32[]{:S(2)}, u32[]{:S(2)}) collective-permute-start(bf16[32,1024]{1,0:T(8,128)(2,1)S(1)} %get-tuple-element.58), channel_id=1, source_target_pairs={{0,32},{1,33},{2,34},{3,35},{4,36},{5,37},{6,38},{7,39},{8,40},{9,... | collective-permute-start | bytes 196616 | tf_op jit(solution)/shard_map/ppermute | solution.py:30
  182.4 7.0 %collective-permute-start.27 = (bf16[32,1024]{1,0:T(8,128)(2,1)S(1)}, bf16[32,1024]{1,0:T(8,128)(2,1)S(1)}, u32[]{:S(2)}, u32[]{:S(2)}) collective-permute-start(bf16[32,1024]{1,0:T(8,128)(2,1)S(1)} %get-tuple-element.59), channel_id=1, source_target_pairs={{0,4},{1,5},{2,6},{3,7},{4,8},{5,9},{6,10},{7,11},{8,12},{9,13},{1... | collective-permute-start | bytes 196616 | tf_op jit(solution)/shard_map/ppermute | solution.py:30
  183.7 8.5 %collective-permute-start.29 = (bf16[32,1024]{1,0:T(8,128)(2,1)S(1)}, bf16[32,1024]{1,0:T(8,128)(2,1)S(1)}, u32[]{:S(2)}, u32[]{:S(2)}) collective-permute-start(bf16[32,1024]{1,0:T(8,128)(2,1)S(1)} %get-tuple-element.60), channel_id=1, source_target_pairs={{0,12},{1,13},{2,14},{3,15},{4,0},{5,1},{6,2},{7,3},{8,4},{9,5},{1... | collective-permute-start | bytes 196616 | tf_op jit(solution)/shard_map/ppermute | solution.py:30
  185.9 7.3 %collective-permute-start.28 = (bf16[32,1024]{1,0:T(8,128)(2,1)S(1)}, bf16[32,1024]{1,0:T(8,128)(2,1)S(1)}, u32[]{:S(2)}, u32[]{:S(2)}) collective-permute-start(bf16[32,1024]{1,0:T(8,128)(2,1)S(1)} %get-tuple-element.61), channel_id=1, source_target_pairs={{0,8},{1,9},{2,10},{3,11},{4,12},{5,13},{6,14},{7,15},{8,0},{9,1},... | collective-permute-start | bytes 196616 | tf_op jit(solution)/shard_map/ppermute | solution.py:30
  187.9 7.4 %collective-permute-start.34 = (bf16[32,1024]{1,0:T(8,128)(2,1)S(1)}, bf16[32,1024]{1,0:T(8,128)(2,1)S(1)}, u32[]{:S(2)}, u32[]{:S(2)}) collective-permute-start(bf16[32,1024]{1,0:T(8,128)(2,1)S(1)} %get-tuple-element.62), channel_id=1, source_target_pairs={{0,16},{1,17},{2,18},{3,19},{4,20},{5,21},{6,22},{7,23},{8,24},{9,... | collective-permute-start | bytes 196616 | tf_op jit(solution)/shard_map/ppermute | solution.py:30
  189.5 8.6 %collective-permute-start.36 = (bf16[32,1024]{1,0:T(8,128)(2,1)S(1)}, bf16[32,1024]{1,0:T(8,128)(2,1)S(1)}, u32[]{:S(2)}, u32[]{:S(2)}) collective-permute-start(bf16[32,1024]{1,0:T(8,128)(2,1)S(1)} %get-tuple-element.63), channel_id=1, source_target_pairs={{0,48},{1,49},{2,50},{3,51},{4,52},{5,53},{6,54},{7,55},{8,56},{9,... | collective-permute-start | bytes 196616 | tf_op jit(solution)/shard_map/ppermute | solution.py:30
  192.2 6.5 %collective-permute-start.35 = (bf16[32,1024]{1,0:T(8,128)(2,1)S(1)}, bf16[32,1024]{1,0:T(8,128)(2,1)S(1)}, u32[]{:S(2)}, u32[]{:S(2)}) collective-permute-start(bf16[32,1024]{1,0:T(8,128)(2,1)S(1)} %get-tuple-element.64), channel_id=1, source_target_pairs={{0,32},{1,33},{2,34},{3,35},{4,36},{5,37},{6,38},{7,39},{8,40},{9,... | collective-permute-start | bytes 196616 | tf_op jit(solution)/shard_map/ppermute | solution.py:30
  193.2 7.7 %collective-permute-start.40 = (bf16[32,1024]{1,0:T(8,128)(2,1)S(1)}, bf16[32,1024]{1,0:T(8,128)(2,1)S(1)}, u32[]{:S(2)}, u32[]{:S(2)}) collective-permute-start(bf16[32,1024]{1,0:T(8,128)(2,1)S(1)} %get-tuple-element.65), channel_id=1, source_target_pairs={{0,4},{1,5},{2,6},{3,7},{4,8},{5,9},{6,10},{7,11},{8,12},{9,13},{1... | collective-permute-start | bytes 196616 | tf_op jit(solution)/shard_map/ppermute | solution.py:30
  195.3 5.6 %collective-permute-start.42 = (bf16[32,1024]{1,0:T(8,128)(2,1)S(1)}, bf16[32,1024]{1,0:T(8,128)(2,1)S(1)}, u32[]{:S(2)}, u32[]{:S(2)}) collective-permute-start(bf16[32,1024]{1,0:T(8,128)(2,1)S(1)} %get-tuple-element.66), channel_id=1, source_target_pairs={{0,12},{1,13},{2,14},{3,15},{4,0},{5,1},{6,2},{7,3},{8,4},{9,5},{1... | collective-permute-start | bytes 196616 | tf_op jit(solution)/shard_map/ppermute | solution.py:30
  198.1 5.8 %collective-permute-start.41 = (bf16[32,1024]{1,0:T(8,128)(2,1)S(1)}, bf16[32,1024]{1,0:T(8,128)(2,1)S(1)}, u32[]{:S(2)}, u32[]{:S(2)}) collective-permute-start(bf16[32,1024]{1,0:T(8,128)(2,1)S(1)} %get-tuple-element.67), channel_id=1, source_target_pairs={{0,8},{1,9},{2,10},{3,11},{4,12},{5,13},{6,14},{7,15},{8,0},{9,1},... | collective-permute-start | bytes 196616 | tf_op jit(solution)/shard_map/ppermute | solution.py:30
  198.7 10.2 %collective-permute-start.30 = (bf16[32,2048]{1,0:T(8,128)(2,1)}, bf16[32,2048]{1,0:T(8,128)(2,1)}, u32[]{:S(2)}, u32[]{:S(2)}) collective-permute-start(bf16[32,2048]{1,0:T(8,128)(2,1)} %fusion.14), channel_id=1, source_target_pairs={{0,64},{2,66},{4,68},{6,70},{8,72},{10,74},{12,76},{14,78},{16,80}... | collective-permute-start | bytes 393224 | tf_op jit(solution)/shard_map/ppermute | solution.py:30
  204.6 14.8 %collective-permute-start.43 = (bf16[32,2048]{1,0:T(8,128)(2,1)}, bf16[32,2048]{1,0:T(8,128)(2,1)}, u32[]{:S(2)}, u32[]{:S(2)}) collective-permute-start(bf16[32,2048]{1,0:T(8,128)(2,1)} %fusion.13), channel_id=1, source_target_pairs={{0,64},{2,66},{4,68},{6,70},{8,72},{10,74},{12,76},{14,78},{16,80}... | collective-permute-start | bytes 393224 | tf_op jit(solution)/shard_map/ppermute | solution.py:30
  207.3 7.0 %collective-permute-start.16 = (bf16[64,1152]{1,0:T(8,128)(2,1)S(1)}, bf16[64,1152]{1,0:T(8,128)(2,1)S(1)}, u32[]{:S(2)}, u32[]{:S(2)}) collective-permute-start(bf16[64,1152]{1,0:T(8,128)(2,1)S(1)} %convert_element_type.299), channel_id=1, source_target_pairs={{1,65},{3,67},{5,69},{7,71},{9,73},{11,75},{13,77},{15,79},{17,81}... | collective-permute-start | bytes 442376 | tf_op jit(solution)/shard_map/ppermute | solution.py:30
  215.4 12.6 %all-to-all-start.2 = ((bf16[16,64,128]{2,1,0:T(8,128)(2,1)}), bf16[16,64,128]{2,1,0:T(8,128)(2,1)S(1)}, u32[]{:S(2)}, u32[]{:S(2)}) async-start(bf16[16,64,128]{2,1,0:T(8,128)(2,1)} %copy.33), calls=%async_computation.2 | async-start | bytes 524288 | tf_op jit(solution)/shard_map/all_to_all | solution.py:183
  228.2 2.5 %collective-permute-start.17 = (bf16[64,1024]{0,1:T(8,128)(2,1)S(1)}, bf16[64,1024]{0,1:T(8,128)(2,1)S(1)}, u32[]{:S(2)}, u32[]{:S(2)}) collective-permute-start(bf16[64,1024]{0,1:T(8,128)(2,1)S(1)} %dynamic-slice_bitcast_fusion.3), channel_id=1, source_target_pairs={{0,2},{1,3},{2,0},{3,1},{4,6},{5,7},{6,4},{7,5},{8,10},{9,11},{10,... | collective-permute-start | bytes 393224 | tf_op jit(solution)/shard_map/ppermute | solution.py:30
  (18 other events, 276.5 us)

commit v3 on v0

v3 whole, which is shorter than its diff:
```python
import functools

import jax
import jax.numpy as jnp
import numpy as np
from jax import lax
from jax.experimental import pallas as pl
from jax.experimental.pallas import tpu as pltpu
from jax.sharding import Mesh
from jax.sharding import PartitionSpec as P

AXES = ("yl", "z", "x", "c", "yh")
SIZES = (2, 4, 4, 2, 2)
DP = ("yl", "z", "x", "c")
CHUNKS = ((0, 32, "z", "x"), (32, 64, "x", "z"))
NT = (((1,), (1,)), ((), ()))
TN = (((0,), (0,)), ((), ()))
bf16, f32 = jnp.bfloat16, jnp.float32
VMEM = pl.BlockSpec(memory_space=pltpu.VMEM)
ANY = pl.BlockSpec(memory_space=pl.ANY)
SMEM = pl.BlockSpec(memory_space=pltpu.SMEM)


def send(value, move, only=None):
    pairs = []
    for i in range(int(np.prod(SIZES))):
        at = dict(zip(AXES, (int(v) for v in np.unravel_index(i, SIZES))))
        if only is None or only(at):
            to = {**at, **move(at)}
            pairs.append((i, int(np.ravel_multi_index([to[a] for a in AXES], SIZES))))
    return lax.ppermute(value, AXES, pairs)


def along(axis, k):
    return lambda at: {axis: (at[axis] + k) % 4}


def flip(*axes):
    return lambda at: {a: 1 - at[a] for a in axes}


def kernel_call(body, outs, specs, *args, flops=0):
    nbytes = sum(a.size * a.dtype.itemsize for a in args) + sum(o.size * o.dtype.itemsize for o in outs)
    return pl.pallas_call(
        body,
        out_shape=outs,
        in_specs=specs,
        out_specs=[VMEM] * len(outs),
        cost_estimate=pl.CostEstimate(flops=flops, bytes_accessed=nbytes, transcendentals=0),
    )(*args)


def slots_kernel(f_ref, t_ref, out_ref):
    wide = f_ref.shape[1] // 32
    for s in range(16):
        out_ref[s, :, :wide] = f_ref[:, s * wide : (s + 1) * wide]
        out_ref[s, :, wide : 2 * wide] = f_ref[:, (16 + s) * wide : (17 + s) * wide]
        out_ref[s, :, 2 * wide :] = t_ref[...]


def factor_kernel(wide, slots_ref, after_ref, also_ref, out_ref):
    out_ref[...] = lax.dot_general(
        slots_ref[:, :wide], slots_ref[:, wide:], TN, preferred_element_type=f32
    )


def pick_kernel(at_ref, gt_ref, sib_ref, *outs):
    for (lo, hi, _, _), out_ref in zip(CHUNKS, outs):
        n = hi - lo
        for b in range(16):
            start = pl.ds(pl.multiple_of(b * 128 + at_ref[2] + lo, 16), n)
            out_ref[b * n : (b + 1) * n, :] = gt_ref[start, :]
            out_ref[(16 + b) * n : (17 + b) * n, :] = sib_ref[start, :]


def gram_kernel(rows, stride, z_first, at_ref, a1_ref, a2_ref, b1_ref, b2_ref, after_ref, *outs):
    z, x, base = at_ref[0], at_ref[1], at_ref[2]
    starts = []
    for k in range(4):
        for j in range(4):
            dz, dx = (k, j) if z_first else (j, k)
            block = lax.rem(z + dz, 4) * 4 + lax.rem(x + dx, 4)
            starts.append(pl.ds(pl.multiple_of(block * stride + base, rows), rows))
    left1 = jnp.concatenate([a1_ref[s, :] for s in starts])
    left2 = jnp.concatenate([a2_ref[s, :] for s in starts])
    tile = 256
    for n in range(b1_ref.shape[0] // tile):
        cols = pl.ds(n * tile, tile)
        acc = lax.dot_general(left1, b1_ref[cols, :], NT, preferred_element_type=f32)
        acc += lax.dot_general(left2, b2_ref[cols, :], NT, preferred_element_type=f32)
        for k in range(4):
            outs[k][:, cols] = acc[4 * k * rows : 4 * (k + 1) * rows].astype(bf16)


def gram(at, a1, a2, b1, b2, after, rows, stride, first):
    n = b1.shape[0]
    return kernel_call(
        functools.partial(gram_kernel, rows, stride, first == "z"),
        [jax.ShapeDtypeStruct((4 * rows, n), bf16)] * 4,
        [SMEM] + [VMEM] * 4 + [ANY],
        at, a1, a2, b1, b2, after,
        flops=4 * 16 * rows * n * b1.shape[1],
    )


def scores_kernel(at_ref, pt_ref, *refs):
    h = at_ref[3]
    n = len(CHUNKS)
    own, cross, (keep_ref, give_ref) = refs[:n], refs[n : 2 * n], refs[2 * n :]
    for side, out_ref in enumerate((keep_ref, give_ref)):
        acc = None
        for which, group in ((h, own), (1 - h, cross)):
            for (lo, hi, _, _), ref in zip(CHUNKS, group):
                m = 16 * (hi - lo)
                p = pt_ref[:, pl.ds(which, 1), lo:hi, :].reshape(m, pt_ref.shape[-1])
                d = lax.dot_general(ref[side * m : (side + 1) * m, :], p, TN, preferred_element_type=f32)
                acc = d if acc is None else acc + d
        out_ref[...] = acc


def first_stage(parts, rows, axis):
    got = [send(parts[k], along(axis, k)) for k in (1, 2, 3)]
    mids = []
    for j in range(4):
        cut = lambda v: lax.slice_in_dim(v, j * rows, (j + 1) * rows).astype(f32)
        mids.append(cut(parts[0]) + cut(got[0]) + cut(got[1]) + cut(got[2]))
    return mids


def second_stage(mids, axis):
    got = [send(mids[k].astype(bf16), along(axis, k)) for k in (1, 2, 3)]
    return mids[0] + got[0].astype(f32) + got[1].astype(f32) + got[2].astype(f32)


def on_device(grads, covariance, test_grads, inverse_factor):
    tokens, feats = grads.shape
    z, x, c = lax.axis_index("z"), lax.axis_index("x"), lax.axis_index("c")
    yl, h = lax.axis_index("yl"), lax.axis_index("yh")
    rows = feats // 32
    tests = test_grads.shape[0]
    at = jnp.stack([z, x, c * rows, h]).astype(jnp.int32)
    at_cross = jnp.stack([z, x, 0 * c, h]).astype(jnp.int32)
    shape = jax.ShapeDtypeStruct
    gt = grads.T
    sib = send(gt, flip("c"))

    picked = kernel_call(
        pick_kernel,
        [shape((32 * (hi - lo), tokens), bf16) for lo, hi, _, _ in CHUNKS],
        [SMEM, VMEM, VMEM],
        at, gt, sib,
    )
    arrived = [send(a, flip("yh")) for a in picked]
    own = gram(at, gt, sib, gt, sib, picked[0], rows, 2 * rows, "x")

    (slots,) = kernel_call(
        slots_kernel,
        [shape((16, rows, 4 * rows + tests), bf16)],
        [VMEM, VMEM],
        inverse_factor, test_grads.T,
    )
    slots = lax.all_to_all(slots, ("z", "x"), split_axis=0, concat_axis=0, tiled=True)
    (pt,) = kernel_call(
        functools.partial(factor_kernel, 4 * rows),
        [shape((4 * rows, tests), f32)],
        [VMEM, ANY, ANY],
        slots.reshape(16 * rows, -1), own[0], arrived[0],
        flops=2 * 16 * rows * 4 * rows * tests,
    )
    pt = pt.reshape(2, 2, rows, tests)
    half = lambda i: lax.dynamic_index_in_dim(pt, i, 1, keepdims=False)
    pt = half(c) + send(half(1 - c), flip("c"))
    pt = (pt + send(pt, flip("yl"))).astype(bf16)
    pt = jnp.broadcast_to(pt[None], (16,) + pt.shape)
    pt = lax.all_to_all(pt, ("z", "x"), split_axis=0, concat_axis=0, tiled=True)

    after = own[0]
    own = second_stage(first_stage(own, rows, "x"), "z")
    own = own + send(own.astype(bf16), flip("yl"), lambda at: at["yl"] != at["yh"]).astype(f32)

    cross = []
    for (lo, hi, first, second), a in zip(CHUNKS, arrived):
        n, m = hi - lo, a.shape[0] // 2
        parts = gram(at_cross, a[:m], a[m:], gt, sib, after, n, n, first)
        after = parts[0]
        part = second_stage(first_stage(parts, n, first), second)
        far = send(part.astype(bf16), flip("yl"), lambda at: at["yl"] == at["yh"])
        cross.append(part + far.astype(f32))
    cross = jnp.concatenate(cross, axis=0)
    examples = tokens * 64
    covariance_out = 0.9 * covariance + jnp.where(yl == h, own, cross) / examples

    keep, give = kernel_call(
        scores_kernel,
        [shape((tokens, tests), f32)] * 2,
        [SMEM] + [VMEM] * (1 + 2 * len(CHUNKS)),
        at, pt, *picked, *arrived,
        flops=8 * 16 * rows * tokens * tests,
    )
    return keep + send(give, flip("c")), covariance_out


def solution(mesh):
    grid = Mesh(mesh.devices.reshape(SIZES), AXES)
    return jax.shard_map(
        on_device,
        mesh=grid,
        in_specs=(P(DP, "yh"), P(DP, "yh"), P("yh", DP), P(DP, None)),
        out_specs=(P(DP, "yh"), P(DP, "yh")),
        check_vma=False,
    )
```

time: 445 us -> 180 us (0.40)
  blocking collectives: 336 us -> 0 us
  starting transfers between devices: 0.08 us -> 64.5 us
  Pallas kernels: 0 us -> 35.1 us
  matrix products: 24.8 us -> 0 us
  between operations: 14.1 us -> 0.92 us
  other arithmetic: 1.91 us -> 11.7 us
  waiting for transfers between devices: 65.7 us -> 56.7 us
  local copies, waits for them, and re-layouts: 2.78 us -> 9.39 us
    psum x1 -> x0, blocking collectives: 336 us -> none  [on_device(): summed = lax.psum(partial_value, 'dp')]
    all_gather x1 -> x0, waiting for transfers between devices: 65 us -> none  [on_device(): all_features = lax.all_gather(grads, 'feat', axis=1, tiled=True)]
    ppermute x0 -> x27, waiting for transfers between devices: none -> 56.7 us  [send(): return lax.ppermute(value, AXES, pairs)]
    ppermute x0 -> x27, starting transfers between devices: none -> 50.7 us  [send(): return lax.ppermute(value, AXES, pairs)]
    pallas_call x0 -> x7, Pallas kernels: none -> 35.1 us  [kernel_call(): pl.pallas_call(body, out_shape=outs, in_specs=specs, out_specs=[VMEM] * l...]
    dot_general x3 -> x0, matrix products: 24.8 us -> none  [the longest x1 17.8 us: on_device(): lax.dot_general(all_features, grads, (((0,), (0,)), ((), ())), preferred_...]
    all_to_all x0 -> x2, starting transfers between devices: none -> 13.8 us  [the longest x1 8.33 us: on_device(): pt = lax.all_to_all(pt, ('z', 'x'), split_axis=0, concat_axis=0, tiled=True)]
    convert_element_type x0 -> x7, other arithmetic: none -> 7.49 us  [the longest x3 4.6 us: second_stage(): got = [send(mids[k].astype(bf16), along(axis, k)) for k in (1, 2, 3)]]
  transfers between devices with their start and end apart: 2 -> 29, of which waited for: 1 -> 9; matrix products, arithmetic and copies ran while one was open for 2% -> 9% of each run, Pallas kernels for 0% -> 12%
where the time goes in v3:
time: 180 us; the launch traced here: 178 us
  starting transfers between devices  64.5 us (36%)
  waiting for transfers between devices  56.7 us (32%)
  Pallas kernels  35.1 us (20%)
  other arithmetic  11.7 us (6%)
  local copies, waits for them, and re-layouts  9.39 us (5%)
    ppermute x27, waiting for transfers between devices, send(): return lax.ppermute(value, AXES, pairs)  56.7 us
    ppermute x27, starting transfers between devices, send(): return lax.ppermute(value, AXES, pairs)  50.7 us
    pallas_call x7, Pallas kernels, kernel_call(): pl.pallas_call(body, out_shape=outs, in_specs=specs, out_specs=[VMEM] * l...  35.1 us
    all_to_all x1, starting transfers between devices, on_device(): pt = lax.all_to_all(pt, ('z', 'x'), split_axis=0, concat_axis=0, tiled=True)  8.33 us
    all_to_all x1, starting transfers between devices, on_device(): lax.all_to_all(slots, ('z', 'x'), split_axis=0, concat_axis=0, tiled=True)  5.45 us
    unnamed x23, local copies, waits for them, and re-layouts  4.94 us
    convert_element_type x3, other arithmetic, second_stage(): got = [send(mids[k].astype(bf16), along(axis, k)) for k in (1, 2, 3)]  4.6 us
  transfers between devices with their start and end apart: 29, of which 9 were waited for; matrix products, arithmetic and copies ran while one was open for 9% of the time, Pallas kernels for 12%

profile of v3, /device:TPU:0, one launch (start us, length us, event | category | flops | bytes accessed | tf_op | source)
XLA Modules:
  0.0 178.2 jit_solution(5004089174103928415)
XLA Ops:
  0.6 2.9 %copy.6 = bf16[512,2048]{0,1:T(8,128)(2,1)S(1)} copy(bf16[512,2048]{1,0:T(8,128)(2,1)} %param.4) | data formatting | bytes 4194304 | tf_op args[0]
  4.4 3.5 %collective-permute-done.sib_ref.a2_ref.b2_ref = bf16[2048,512]{1,0:T(8,128)(2,1)} collective-permute-done((bf16[2048,512]{1,0:T(8,128)(2,1)S(1)}, bf16[2048,512]{1,0:T(8,128)(2,1)}, u32[]{:S(2)}, u32[]{:S(2)}) %collective-permute-start) | collective-permute-done | bytes 2097184 | tf_op jit(solution)/shard_map/ppermute | solution.py:31
  7.9 3.7 %shard_map.60 = (bf16[1024,512]{1,0:T(8,128)(2,1)}, bf16[1024,512]{1,0:T(8,128)(2,1)}) custom-call(s32[4]{0:T(128)} %add_add_fusion.at_ref, bf16[2048,512]{1,0:T(8,128)(2,1)} %bitcast.13, bf16[2048,512]{1,0:T(8,128)(2,1)} %collective-permute-done.sib_ref.a2_ref.b2_ref), custom_call_target="tpu_custom_call" | custom-call | bytes 6291472 | tf_op jit(solution)/shard_map/pallas_call | solution.py:44
  11.6 9.8 %shard_map.61 = (bf16[256,2048]{1,0:T(8,128)(2,1)}, bf16[256,2048]{1,0:T(8,128)(2,1)}, bf16[256,2048]{1,0:T(8,128)(2,1)}, bf16[256,2048]{1,0:T(8,128)(2,1)}) custom-call(s32[4]{0:T(128)} %add_add_fusion.at_ref, bf16[2048,512]{1,0:T(8,128)(2,1)} %bitcast.14, bf16[2048,512]{1,0:T(8,128)(2,1)} %collective-permute-done.sib_ref.a2_ref.b2_ref, ...), custom_call_target="tpu_custom_call" | custom-call | flops 4294967296 | bytes 13631504 | tf_op jit(solution)/shard_map/pallas_call | solution.py:44
  21.4 1.6 collective-permute-start.6
  23.0 2.7 %collective-permute-start.7 = (bf16[256,2048]{1,0:T(8,128)(2,1)}, bf16[256,2048]{1,0:T(8,128)(2,1)}, u32[]{:S(2)}, u32[]{:S(2)}) collective-permute-start(bf16[256,2048]{1,0:T(8,128)(2,1)} %get-tuple-element.24), channel_id=1, source_target_pairs={{0,8},{1,9},{2,10},{3,11},{4,12},{5,13},{6,14},{7,15},{8,0},{9,1},... | collective-permute-start | bytes 3145736 | tf_op jit(solution)/shard_map/ppermute | solution.py:31
  25.7 1.4 collective-permute-start.8
  27.1 3.2 %collective-permute-start.1 = (bf16[1024,512]{1,0:T(8,128)(2,1)}, bf16[1024,512]{1,0:T(8,128)(2,1)S(1)}, u32[]{:S(2)}, u32[]{:S(2)}) collective-permute-start(bf16[1024,512]{1,0:T(8,128)(2,1)} %get-tuple-element.18.after_ref.refs_0_), channel_id=1, source_target_pairs={{0,1},{1,0},{2,3},{3,2},{4,5},{5,4},{6,7},{7,6},{8,9},{9,8},{10,11... | collective-permute-start | bytes 3145736 | tf_op jit(solution)/shard_map/ppermute | solution.py:31
  30.3 2.2 %shard_map.59 = bf16[16,64,512]{2,1,0:T(8,128)(2,1)} custom-call(bf16[64,4096]{1,0:T(8,128)(2,1)} %f_ref.1, bf16[64,256]{1,0:T(8,128)(2,1)} %bitcast.21), custom_call_target="tpu_custom_call" | custom-call | bytes 1605632 | tf_op jit(solution)/shard_map/pallas_call | solution.py:44
  32.6 5.4 %all-to-all-start = ((bf16[16,64,512]{2,1,0:T(8,128)(2,1)}), bf16[16,64,512]{2,1,0:T(8,128)(2,1)S(1)}, u32[]{:S(2)}, u32[]{:S(2)}) async-start(bf16[16,64,512]{2,1,0:T(8,128)(2,1)} %shard_map.59), calls=%async_computation | async-start | bytes 2097152 | tf_op jit(solution)/shard_map/all_to_all | solution.py:162
  38.9 10.6 %collective-permute-done.6 = bf16[256,2048]{1,0:T(8,128)(2,1)} collective-permute-done((bf16[256,2048]{1,0:T(8,128)(2,1)}, bf16[256,2048]{1,0:T(8,128)(2,1)}, u32[]{:S(2)}, u32[]{:S(2)}) %collective-permute-start.6) | collective-permute-done | bytes 1048608 | tf_op jit(solution)/shard_map/ppermute | solution.py:31
  49.5 23.1 %collective-permute-done.7 = bf16[256,2048]{1,0:T(8,128)(2,1)} collective-permute-done((bf16[256,2048]{1,0:T(8,128)(2,1)}, bf16[256,2048]{1,0:T(8,128)(2,1)}, u32[]{:S(2)}, u32[]{:S(2)}) %collective-permute-start.7) | collective-permute-done | bytes 1048608 | tf_op jit(solution)/shard_map/ppermute | solution.py:31
  72.6 3.1 %add_convert_fusion.2 = (bf16[64,2048]{1,0:T(8,128)(2,1)}, bf16[64,2048]{1,0:T(8,128)(2,1)}, bf16[64,2048]{1,0:T(8,128)(2,1)}) fusion(bf16[256,2048]{1,0:T(8,128)(2,1)} %collective-permute-done.8, bf16[256,2048]{1,0:T(8,128)(2,1)} %collective-permute-done.7, bf16[256,2048]{1,0:T(8,128)(2,1)} %collective-permute-done.6, ...), kind=kLoop, calls=%fused_computation.6 | loop fusion | flops 3145728 | bytes 3932160 | tf_op jit(solution)/shard_map/convert_element_type | solution.py:131
  75.7 3.9 %collective-permute-start.10 = (bf16[64,2048]{1,0:T(8,128)(2,1)}, bf16[64,2048]{1,0:T(8,128)(2,1)S(1)}, u32[]{:S(2)}, u32[]{:S(2)}) collective-permute-start(bf16[64,2048]{1,0:T(8,128)(2,1)} %get-tuple-element.42), channel_id=1, source_target_pairs={{0,32},{1,33},{2,34},{3,35},{4,36},{5,37},{6,38},{7,39},{8,40},{9,... | collective-permute-start | bytes 786440 | tf_op jit(solution)/shard_map/ppermute | solution.py:31
  80.3 1.3 collective-permute-start.9
  81.6 1.1 fusion.5
  82.7 6.1 %shard_map.64 = (bf16[128,2048]{1,0:T(8,128)(2,1)}, bf16[128,2048]{1,0:T(8,128)(2,1)}, bf16[128,2048]{1,0:T(8,128)(2,1)}, bf16[128,2048]{1,0:T(8,128)(2,1)}) custom-call(s32[4]{0:T(128)} %add_add_fusion.1.at_ref, bf16[512,512]{1,0:T(8,128)(2,1)} %get-tuple-element.50.a1_ref, bf16[512,512]{1,0:T(8,128)(2,1)} %get-tuple-element.49.a2_ref, ...), custom_call_target="tpu_custom_call" | custom-call | flops 2147483648 | bytes 8388624 | tf_op jit(solution)/shard_map/pallas_call | solution.py:44
  88.8 1.0 collective-permute-start.13
  89.9 1.0 copy-done.2
  90.9 2.3 %shard_map.62 = f32[256,256]{1,0:T(8,128)} custom-call(bf16[1024,512]{1,0:T(8,128)(2,1)} %bitcast.18, bf16[256,2048]{1,0:T(8,128)(2,1)} %get-tuple-element.19.after_ref, bf16[1024,512]{1,0:T(8,128)(2,1)} %copy-done), custom_call_target="tpu_custom_call" | custom-call | flops 134217728 | bytes 3407872 | tf_op jit(solution)/shard_map/pallas_call | solution.py:44
  93.2 1.0 dynamic-slice_bitcast_fusion
  94.3 1.2 fusion.6
  95.7 1.6 collective-permute-start.3
  97.3 6.2 %shard_map.65 = (bf16[128,2048]{1,0:T(8,128)(2,1)}, bf16[128,2048]{1,0:T(8,128)(2,1)}, bf16[128,2048]{1,0:T(8,128)(2,1)}, bf16[128,2048]{1,0:T(8,128)(2,1)}) custom-call(s32[4]{0:T(128)} %add_add_fusion.1.at_ref, bf16[512,512]{1,0:T(8,128)(2,1)} %get-tuple-element.52.a1_ref, bf16[512,512]{1,0:T(8,128)(2,1)} %get-tuple-element.51.a2_ref, ...), custom_call_target="tpu_custom_call" | custom-call | flops 2147483648 | bytes 7864336 | tf_op jit(solution)/shard_map/pallas_call | solution.py:44
  103.5 2.6 %collective-permute-start.14 = (bf16[128,2048]{1,0:T(8,128)(2,1)}, bf16[128,2048]{1,0:T(8,128)(2,1)S(1)}, u32[]{:S(2)}, u32[]{:S(2)}) collective-permute-start(bf16[128,2048]{1,0:T(8,128)(2,1)} %get-tuple-element.28), channel_id=1, source_target_pairs={{0,32},{1,33},{2,34},{3,35},{4,36},{5,37},{6,38},{7,39},{8,40},{9,... | collective-permute-start | bytes 1572872 | tf_op jit(solution)/shard_map/ppermute | solution.py:31
  106.5 1.1 broadcast_in_dim.2
  107.6 8.3 %all-to-all-start.1 = ((bf16[16,2,64,256]{3,2,1,0:T(8,128)(2,1)}), bf16[16,2,64,256]{3,2,1,0:T(8,128)(2,1)S(1)}, u32[]{:S(2)}, u32[]{:S(2)}) async-start(bf16[16,2,64,256]{3,2,1,0:T(8,128)(2,1)} %broadcast_in_dim.2), calls=%async_computation.1 | async-start | bytes 2097152 | tf_op jit(solution)/shard_map/all_to_all | solution.py:175
  115.9 2.0 %collective-permute-start.20 = (bf16[128,2048]{1,0:T(8,128)(2,1)}, bf16[128,2048]{1,0:T(8,128)(2,1)S(1)}, u32[]{:S(2)}, u32[]{:S(2)}) collective-permute-start(bf16[128,2048]{1,0:T(8,128)(2,1)} %get-tuple-element.31), channel_id=1, source_target_pairs={{0,4},{1,5},{2,6},{3,7},{4,8},{5,9},{6,10},{7,11},{8,12},{9,13},{1... | collective-permute-start | bytes 1572872 | tf_op jit(solution)/shard_map/ppermute | solution.py:31
  117.9 2.7 %collective-permute-start.21 = (bf16[128,2048]{1,0:T(8,128)(2,1)}, bf16[128,2048]{1,0:T(8,128)(2,1)S(1)}, u32[]{:S(2)}, u32[]{:S(2)}) collective-permute-start(bf16[128,2048]{1,0:T(8,128)(2,1)} %get-tuple-element.32), channel_id=1, source_target_pairs={{0,8},{1,9},{2,10},{3,11},{4,12},{5,13},{6,14},{7,15},{8,0},{9,1},... | collective-permute-start | bytes 1572872 | tf_op jit(solution)/shard_map/ppermute | solution.py:31
  120.6 1.5 collective-permute-start.22
  122.1 1.7 fusion.2
  123.8 1.3 collective-permute-start.12
  125.1 14.3 %collective-permute-done.15 = bf16[128,2048]{1,0:T(8,128)(2,1)S(1)} collective-permute-done((bf16[128,2048]{1,0:T(8,128)(2,1)}, bf16[128,2048]{1,0:T(8,128)(2,1)S(1)}, u32[]{:S(2)}, u32[]{:S(2)}) %collective-permute-start.15) | collective-permute-done | bytes 524320 | tf_op jit(solution)/shard_map/ppermute | solution.py:31
  139.5 1.3 add_convert_fusion.8
  140.7 4.5 %collective-permute-start.16 = (bf16[32,2048]{1,0:T(8,128)(2,1)S(1)}, bf16[32,2048]{1,0:T(8,128)(2,1)S(1)}, u32[]{:S(2)}, u32[]{:S(2)}) collective-permute-start(bf16[32,2048]{1,0:T(8,128)(2,1)S(1)} %get-tuple-element.43), channel_id=1, source_target_pairs={{0,4},{1,5},{2,6},{3,7},{4,8},{5,9},{6,10},{7,11},{8,12},{9,13},{1... | collective-permute-start | bytes 393224 | tf_op jit(solution)/shard_map/ppermute | solution.py:31
  145.3 7.0 %collective-permute-start.17 = (bf16[32,2048]{1,0:T(8,128)(2,1)S(1)}, bf16[32,2048]{1,0:T(8,128)(2,1)S(1)}, u32[]{:S(2)}, u32[]{:S(2)}) collective-permute-start(bf16[32,2048]{1,0:T(8,128)(2,1)S(1)} %get-tuple-element.45), channel_id=1, source_target_pairs={{0,8},{1,9},{2,10},{3,11},{4,12},{5,13},{6,14},{7,15},{8,0},{9,1},... | collective-permute-start | bytes 393224 | tf_op jit(solution)/shard_map/ppermute | solution.py:31
  152.3 2.7 %collective-permute-done.21 = bf16[128,2048]{1,0:T(8,128)(2,1)S(1)} collective-permute-done((bf16[128,2048]{1,0:T(8,128)(2,1)}, bf16[128,2048]{1,0:T(8,128)(2,1)S(1)}, u32[]{:S(2)}, u32[]{:S(2)}) %collective-permute-start.21) | collective-permute-done | bytes 524320 | tf_op jit(solution)/shard_map/ppermute | solution.py:31
  155.2 1.5 collective-permute-start.23
  156.8 3.0 %collective-permute-start.24 = (bf16[32,2048]{1,0:T(8,128)(2,1)S(1)}, bf16[32,2048]{1,0:T(8,128)(2,1)S(1)}, u32[]{:S(2)}, u32[]{:S(2)}) collective-permute-start(bf16[32,2048]{1,0:T(8,128)(2,1)S(1)} %get-tuple-element.48), channel_id=1, source_target_pairs={{0,32},{1,33},{2,34},{3,35},{4,36},{5,37},{6,38},{7,39},{8,40},{9,... | collective-permute-start | bytes 393224 | tf_op jit(solution)/shard_map/ppermute | solution.py:31
  159.8 1.5 collective-permute-start.25
  161.3 1.0 fusion.3
  162.3 2.4 %collective-permute-start.19 = (bf16[32,2048]{1,0:T(8,128)(2,1)S(1)}, bf16[32,2048]{1,0:T(8,128)(2,1)S(1)}, u32[]{:S(2)}, u32[]{:S(2)}) collective-permute-start(bf16[32,2048]{1,0:T(8,128)(2,1)S(1)} %get-tuple-element.36), channel_id=1, source_target_pairs={{0,64},{2,66},{4,68},{6,70},{8,72},{10,74},{12,76},{14,78},{16,80}... | collective-permute-start | bytes 393224 | tf_op jit(solution)/shard_map/ppermute | solution.py:31
  164.7 2.2 %collective-permute-done.25 = bf16[32,2048]{1,0:T(8,128)(2,1)S(1)} collective-permute-done((bf16[32,2048]{1,0:T(8,128)(2,1)S(1)}, bf16[32,2048]{1,0:T(8,128)(2,1)S(1)}, u32[]{:S(2)}, u32[]{:S(2)}) %collective-permute-start.25) | collective-permute-done | bytes 131104 | tf_op jit(solution)/shard_map/ppermute | solution.py:31
  167.0 2.4 %collective-permute-start.26 = (bf16[32,2048]{1,0:T(8,128)(2,1)S(1)}, bf16[32,2048]{1,0:T(8,128)(2,1)S(1)}, u32[]{:S(2)}, u32[]{:S(2)}) collective-permute-start(bf16[32,2048]{1,0:T(8,128)(2,1)S(1)} %get-tuple-element.38), channel_id=1, source_target_pairs={{0,64},{2,66},{4,68},{6,70},{8,72},{10,74},{12,76},{14,78},{16,80}... | collective-permute-start | bytes 393224 | tf_op jit(solution)/shard_map/ppermute | solution.py:31
  169.5 1.0 copy-done.4
  170.5 4.8 %shard_map.63 = (f32[512,256]{1,0:T(8,128)}, f32[512,256]{1,0:T(8,128)}) custom-call(s32[4]{0:T(128)} %add_add_fusion.at_ref, bf16[16,2,64,256]{3,2,1,0:T(8,128)(2,1)} %copy-done.4, bf16[1024,512]{1,0:T(8,128)(2,1)} %get-tuple-element.18.after_ref.refs_0_, bf16[1024,512]{1,0:T(8,128)(2,1)} %get-tuple-element.20.refs_1_, bf16[1024,512]{1,0:T(8,128)(2,1)} %copy-done, ...), custom_call_target="tpu_custom_call" | custom-call | flops 1073741824 | bytes 6291472 | tf_op jit(solution)/shard_map/pallas_call | solution.py:44
  175.3 1.9 %fusion.1 = f32[64,2048]{1,0:T(8,128)} fusion(f32[32,2048]{1,0:T(8,128)S(1)} %convert_add_fusion.1, f32[32,2048]{1,0:T(8,128)S(1)} %convert_add_fusion.3, f32[64,2048]{1,0:T(8,128)S(1)} %get-tuple-element.35, bf16[64,2048]{1,0:T(8,128)(2,1)} %collective-permute-done.12, f32[64,2048]{1,0:T(8,128)S(1)} %copy-done.6, pred[]{:T(512)S(6)} %eq.3), kind=kLoop, calls=%fused_computation.2 | loop fusion | flops 917504 | bytes 2359297 | tf_op jit(solution)/shard_map/add | solution.py:191
  177.3 0.9 add.168
  (58 shorter events, 3.8 us)
Async XLA Ops:
  3.5 4.4 %copy-start.1 = (bf16[512,2048]{0,1:T(8,128)(2,1)}, bf16[512,2048]{0,1:T(8,128)(2,1)S(1)}, u32[]{:S(2)}) copy-start(bf16[512,2048]{0,1:T(8,128)(2,1)S(1)} %copy.6) | copy-start | bytes 6291460
  3.5 4.4 %collective-permute-start = (bf16[2048,512]{1,0:T(8,128)(2,1)S(1)}, bf16[2048,512]{1,0:T(8,128)(2,1)}, u32[]{:S(2)}, u32[]{:S(2)}) collective-permute-start(bf16[2048,512]{1,0:T(8,128)(2,1)S(1)} %bitcast.12), channel_id=1, source_target_pairs={{0,2},{1,3},{2,0},{3,1},{4,6},{5,7},{6,4},{7,5},{8,10},{9,11},{10,... | collective-permute-start | bytes 6291464 | tf_op jit(solution)/shard_map/ppermute | solution.py:31
  21.4 28.1 %collective-permute-start.6 = (bf16[256,2048]{1,0:T(8,128)(2,1)}, bf16[256,2048]{1,0:T(8,128)(2,1)}, u32[]{:S(2)}, u32[]{:S(2)}) collective-permute-start(bf16[256,2048]{1,0:T(8,128)(2,1)} %get-tuple-element.23), channel_id=1, source_target_pairs={{0,4},{1,5},{2,6},{3,7},{4,8},{5,9},{6,10},{7,11},{8,12},{9,13},{1... | collective-permute-start | bytes 3145736 | tf_op jit(solution)/shard_map/ppermute | solution.py:31
  23.0 49.6 %collective-permute-start.7 = (bf16[256,2048]{1,0:T(8,128)(2,1)}, bf16[256,2048]{1,0:T(8,128)(2,1)}, u32[]{:S(2)}, u32[]{:S(2)}) collective-permute-start(bf16[256,2048]{1,0:T(8,128)(2,1)} %get-tuple-element.24), channel_id=1, source_target_pairs={{0,8},{1,9},{2,10},{3,11},{4,12},{5,13},{6,14},{7,15},{8,0},{9,1},... | collective-permute-start | bytes 3145736 | tf_op jit(solution)/shard_map/ppermute | solution.py:31
  25.7 46.9 %collective-permute-start.8 = (bf16[256,2048]{1,0:T(8,128)(2,1)}, bf16[256,2048]{1,0:T(8,128)(2,1)}, u32[]{:S(2)}, u32[]{:S(2)}) collective-permute-start(bf16[256,2048]{1,0:T(8,128)(2,1)} %get-tuple-element.25), channel_id=1, source_target_pairs={{0,12},{1,13},{2,14},{3,15},{4,0},{5,1},{6,2},{7,3},{8,4},{9,5},{1... | collective-permute-start | bytes 3145736 | tf_op jit(solution)/shard_map/ppermute | solution.py:31
  27.1 54.4 %collective-permute-start.1 = (bf16[1024,512]{1,0:T(8,128)(2,1)}, bf16[1024,512]{1,0:T(8,128)(2,1)S(1)}, u32[]{:S(2)}, u32[]{:S(2)}) collective-permute-start(bf16[1024,512]{1,0:T(8,128)(2,1)} %get-tuple-element.18.after_ref.refs_0_), channel_id=1, source_target_pairs={{0,1},{1,0},{2,3},{3,2},{4,5},{5,4},{6,7},{7,6},{8,9},{9,8},{10,11... | collective-permute-start | bytes 3145736 | tf_op jit(solution)/shard_map/ppermute | solution.py:31
  32.6 57.3 %all-to-all-start = ((bf16[16,64,512]{2,1,0:T(8,128)(2,1)}), bf16[16,64,512]{2,1,0:T(8,128)(2,1)S(1)}, u32[]{:S(2)}, u32[]{:S(2)}) async-start(bf16[16,64,512]{2,1,0:T(8,128)(2,1)} %shard_map.59), calls=%async_computation | async-start | bytes 2097152 | tf_op jit(solution)/shard_map/all_to_all | solution.py:162
  38.6 55.6 %collective-permute-start.4 = (bf16[1024,512]{1,0:T(8,128)(2,1)}, bf16[1024,512]{1,0:T(8,128)(2,1)S(1)}, u32[]{:S(2)}, u32[]{:S(2)}) collective-permute-start(bf16[1024,512]{1,0:T(8,128)(2,1)} %get-tuple-element.20.refs_1_), channel_id=1, source_target_pairs={{0,1},{1,0},{2,3},{3,2},{4,5},{5,4},{6,7},{7,6},{8,9},{9,8},{10,11... | collective-permute-start | bytes 3145736 | tf_op jit(solution)/shard_map/ppermute | solution.py:31
  75.7 27.8 %collective-permute-start.10 = (bf16[64,2048]{1,0:T(8,128)(2,1)}, bf16[64,2048]{1,0:T(8,128)(2,1)S(1)}, u32[]{:S(2)}, u32[]{:S(2)}) collective-permute-start(bf16[64,2048]{1,0:T(8,128)(2,1)} %get-tuple-element.42), channel_id=1, source_target_pairs={{0,32},{1,33},{2,34},{3,35},{4,36},{5,37},{6,38},{7,39},{8,40},{9,... | collective-permute-start | bytes 786440 | tf_op jit(solution)/shard_map/ppermute | solution.py:31
  79.5 36.4 %collective-permute-start.11 = (bf16[64,2048]{1,0:T(8,128)(2,1)}, bf16[64,2048]{1,0:T(8,128)(2,1)}, u32[]{:S(2)}, u32[]{:S(2)}) collective-permute-start(bf16[64,2048]{1,0:T(8,128)(2,1)} %get-tuple-element.41), channel_id=1, source_target_pairs={{0,48},{1,49},{2,50},{3,51},{4,52},{5,53},{6,54},{7,55},{8,56},{9,... | collective-permute-start | bytes 786440 | tf_op jit(solution)/shard_map/ppermute | solution.py:31
  80.3 37.6 %collective-permute-start.9 = (bf16[64,2048]{1,0:T(8,128)(2,1)}, bf16[64,2048]{1,0:T(8,128)(2,1)}, u32[]{:S(2)}, u32[]{:S(2)}) collective-permute-start(bf16[64,2048]{1,0:T(8,128)(2,1)} %get-tuple-element.40), channel_id=1, source_target_pairs={{0,16},{1,17},{2,18},{3,19},{4,20},{5,21},{6,22},{7,23},{8,24},{9,... | collective-permute-start | bytes 786440 | tf_op jit(solution)/shard_map/ppermute | solution.py:31
  81.6 7.3 %copy-start = (bf16[1024,512]{1,0:T(8,128)(2,1)}, bf16[1024,512]{1,0:T(8,128)(2,1)S(1)}, u32[]{:S(2)}) copy-start(bf16[1024,512]{1,0:T(8,128)(2,1)S(1)} %collective-permute-done.1.also_ref.refs_2_) | copy-start | bytes 3145732
  88.8 31.7 %collective-permute-start.13 = (bf16[128,2048]{1,0:T(8,128)(2,1)}, bf16[128,2048]{1,0:T(8,128)(2,1)}, u32[]{:S(2)}, u32[]{:S(2)}) collective-permute-start(bf16[128,2048]{1,0:T(8,128)(2,1)} %get-tuple-element.27), channel_id=1, source_target_pairs={{0,16},{1,17},{2,18},{3,19},{4,20},{5,21},{6,22},{7,23},{8,24},{9,... | collective-permute-start | bytes 1572872 | tf_op jit(solution)/shard_map/ppermute | solution.py:31
  89.9 1.1 copy-start.2
  93.2 2.4 %copy-start.5 = (f32[256,256]{1,0:T(8,128)S(1)}, f32[256,256]{1,0:T(8,128)}, u32[]{:S(2)}) copy-start(f32[256,256]{1,0:T(8,128)} %shard_map.62) | copy-start | bytes 786436
  94.2 9.3 %copy-start.3 = (bf16[1024,512]{1,0:T(8,128)(2,1)}, bf16[1024,512]{1,0:T(8,128)(2,1)S(1)}, u32[]{:S(2)}) copy-start(bf16[1024,512]{1,0:T(8,128)(2,1)S(1)} %collective-permute-done.4.refs_3_) | copy-start | bytes 3145732
  94.2 1.4 collective-permute-start.2
  95.7 10.5 %collective-permute-start.3 = (f32[2,64,256]{2,1,0:T(8,128)S(1)}, f32[2,64,256]{2,1,0:T(8,128)S(1)}, u32[]{:S(2)}, u32[]{:S(2)}) collective-permute-start(f32[2,64,256]{2,1,0:T(8,128)S(1)} %bitcast_add_fusion), channel_id=1, source_target_pairs={{0,64},{1,65},{2,66},{3,67},{4,68},{5,69},{6,70},{7,71},{8,72},{9,... | collective-permute-start | bytes 393224 | tf_op jit(solution)/shard_map/ppermute | solution.py:31
  103.5 17.1 %copy-start.10 = (bf16[64,2048]{1,0:T(8,128)(2,1)}, bf16[64,2048]{1,0:T(8,128)(2,1)S(1)}, u32[]{:S(2)}) copy-start(bf16[64,2048]{1,0:T(8,128)(2,1)S(1)} %collective-permute-done.10) | copy-start | bytes 786436
  103.5 20.4 %collective-permute-start.14 = (bf16[128,2048]{1,0:T(8,128)(2,1)}, bf16[128,2048]{1,0:T(8,128)(2,1)S(1)}, u32[]{:S(2)}, u32[]{:S(2)}) collective-permute-start(bf16[128,2048]{1,0:T(8,128)(2,1)} %get-tuple-element.28), channel_id=1, source_target_pairs={{0,32},{1,33},{2,34},{3,35},{4,36},{5,37},{6,38},{7,39},{8,40},{9,... | collective-permute-start | bytes 1572872 | tf_op jit(solution)/shard_map/ppermute | solution.py:31
  106.1 33.3 %collective-permute-start.15 = (bf16[128,2048]{1,0:T(8,128)(2,1)}, bf16[128,2048]{1,0:T(8,128)(2,1)S(1)}, u32[]{:S(2)}, u32[]{:S(2)}) collective-permute-start(bf16[128,2048]{1,0:T(8,128)(2,1)} %get-tuple-element.29), channel_id=1, source_target_pairs={{0,48},{1,49},{2,50},{3,51},{4,52},{5,53},{6,54},{7,55},{8,56},{9,... | collective-permute-start | bytes 1572872 | tf_op jit(solution)/shard_map/ppermute | solution.py:31
  107.6 31.9 %copy-start.8 = (bf16[128,2048]{1,0:T(8,128)(2,1)S(1)}, bf16[128,2048]{1,0:T(8,128)(2,1)}, u32[]{:S(2)}) copy-start(bf16[128,2048]{1,0:T(8,128)(2,1)} %get-tuple-element.26.after_ref) | copy-start | bytes 1572868
  107.6 61.9 %all-to-all-start.1 = ((bf16[16,2,64,256]{3,2,1,0:T(8,128)(2,1)}), bf16[16,2,64,256]{3,2,1,0:T(8,128)(2,1)S(1)}, u32[]{:S(2)}, u32[]{:S(2)}) async-start(bf16[16,2,64,256]{3,2,1,0:T(8,128)(2,1)} %broadcast_in_dim.2), calls=%async_computation.1 | async-start | bytes 2097152 | tf_op jit(solution)/shard_map/all_to_all | solution.py:175
  115.9 29.4 %collective-permute-start.20 = (bf16[128,2048]{1,0:T(8,128)(2,1)}, bf16[128,2048]{1,0:T(8,128)(2,1)S(1)}, u32[]{:S(2)}, u32[]{:S(2)}) collective-permute-start(bf16[128,2048]{1,0:T(8,128)(2,1)} %get-tuple-element.31), channel_id=1, source_target_pairs={{0,4},{1,5},{2,6},{3,7},{4,8},{5,9},{6,10},{7,11},{8,12},{9,13},{1... | collective-permute-start | bytes 1572872 | tf_op jit(solution)/shard_map/ppermute | solution.py:31
  117.9 37.0 %collective-permute-start.21 = (bf16[128,2048]{1,0:T(8,128)(2,1)}, bf16[128,2048]{1,0:T(8,128)(2,1)S(1)}, u32[]{:S(2)}, u32[]{:S(2)}) collective-permute-start(bf16[128,2048]{1,0:T(8,128)(2,1)} %get-tuple-element.32), channel_id=1, source_target_pairs={{0,8},{1,9},{2,10},{3,11},{4,12},{5,13},{6,14},{7,15},{8,0},{9,1},... | collective-permute-start | bytes 1572872 | tf_op jit(solution)/shard_map/ppermute | solution.py:31
  120.6 34.4 %copy-start.9 = (bf16[128,2048]{1,0:T(8,128)(2,1)S(1)}, bf16[128,2048]{1,0:T(8,128)(2,1)}, u32[]{:S(2)}) copy-start(bf16[128,2048]{1,0:T(8,128)(2,1)} %get-tuple-element.30) | copy-start | bytes 1572868
  120.6 34.4 %collective-permute-start.22 = (bf16[128,2048]{1,0:T(8,128)(2,1)}, bf16[128,2048]{1,0:T(8,128)(2,1)S(1)}, u32[]{:S(2)}, u32[]{:S(2)}) collective-permute-start(bf16[128,2048]{1,0:T(8,128)(2,1)} %get-tuple-element.33), channel_id=1, source_target_pairs={{0,12},{1,13},{2,14},{3,15},{4,0},{5,1},{6,2},{7,3},{8,4},{9,5},{1... | collective-permute-start | bytes 1572872 | tf_op jit(solution)/shard_map/ppermute | solution.py:31
  123.8 51.4 %collective-permute-start.12 = (bf16[64,2048]{1,0:T(8,128)(2,1)S(1)}, bf16[64,2048]{1,0:T(8,128)(2,1)}, u32[]{:S(2)}, u32[]{:S(2)}) collective-permute-start(bf16[64,2048]{1,0:T(8,128)(2,1)S(1)} %get-tuple-element.34), channel_id=1, source_target_pairs={{1,65},{3,67},{5,69},{7,71},{9,73},{11,75},{13,77},{15,79},{17,81}... | collective-permute-start | bytes 786440 | tf_op jit(solution)/shard_map/ppermute | solution.py:31
  140.7 16.1 %collective-permute-start.16 = (bf16[32,2048]{1,0:T(8,128)(2,1)S(1)}, bf16[32,2048]{1,0:T(8,128)(2,1)S(1)}, u32[]{:S(2)}, u32[]{:S(2)}) collective-permute-start(bf16[32,2048]{1,0:T(8,128)(2,1)S(1)} %get-tuple-element.43), channel_id=1, source_target_pairs={{0,4},{1,5},{2,6},{3,7},{4,8},{5,9},{6,10},{7,11},{8,12},{9,13},{1... | collective-permute-start | bytes 393224 | tf_op jit(solution)/shard_map/ppermute | solution.py:31
  145.3 14.5 %collective-permute-start.17 = (bf16[32,2048]{1,0:T(8,128)(2,1)S(1)}, bf16[32,2048]{1,0:T(8,128)(2,1)S(1)}, u32[]{:S(2)}, u32[]{:S(2)}) collective-permute-start(bf16[32,2048]{1,0:T(8,128)(2,1)S(1)} %get-tuple-element.45), channel_id=1, source_target_pairs={{0,8},{1,9},{2,10},{3,11},{4,12},{5,13},{6,14},{7,15},{8,0},{9,1},... | collective-permute-start | bytes 393224 | tf_op jit(solution)/shard_map/ppermute | solution.py:31
  154.9 6.3 %collective-permute-start.18 = (bf16[32,2048]{1,0:T(8,128)(2,1)S(1)}, bf16[32,2048]{1,0:T(8,128)(2,1)S(1)}, u32[]{:S(2)}, u32[]{:S(2)}) collective-permute-start(bf16[32,2048]{1,0:T(8,128)(2,1)S(1)} %get-tuple-element.44), channel_id=1, source_target_pairs={{0,12},{1,13},{2,14},{3,15},{4,0},{5,1},{6,2},{7,3},{8,4},{9,5},{1... | collective-permute-start | bytes 393224 | tf_op jit(solution)/shard_map/ppermute | solution.py:31
  155.2 9.5 %collective-permute-start.23 = (bf16[32,2048]{1,0:T(8,128)(2,1)S(1)}, bf16[32,2048]{1,0:T(8,128)(2,1)S(1)}, u32[]{:S(2)}, u32[]{:S(2)}) collective-permute-start(bf16[32,2048]{1,0:T(8,128)(2,1)S(1)} %get-tuple-element.46), channel_id=1, source_target_pairs={{0,16},{1,17},{2,18},{3,19},{4,20},{5,21},{6,22},{7,23},{8,24},{9,... | collective-permute-start | bytes 393224 | tf_op jit(solution)/shard_map/ppermute | solution.py:31
  156.8 7.9 %collective-permute-start.24 = (bf16[32,2048]{1,0:T(8,128)(2,1)S(1)}, bf16[32,2048]{1,0:T(8,128)(2,1)S(1)}, u32[]{:S(2)}, u32[]{:S(2)}) collective-permute-start(bf16[32,2048]{1,0:T(8,128)(2,1)S(1)} %get-tuple-element.48), channel_id=1, source_target_pairs={{0,32},{1,33},{2,34},{3,35},{4,36},{5,37},{6,38},{7,39},{8,40},{9,... | collective-permute-start | bytes 393224 | tf_op jit(solution)/shard_map/ppermute | solution.py:31
  159.8 7.1 %collective-permute-start.25 = (bf16[32,2048]{1,0:T(8,128)(2,1)S(1)}, bf16[32,2048]{1,0:T(8,128)(2,1)S(1)}, u32[]{:S(2)}, u32[]{:S(2)}) collective-permute-start(bf16[32,2048]{1,0:T(8,128)(2,1)S(1)} %get-tuple-element.47), channel_id=1, source_target_pairs={{0,48},{1,49},{2,50},{3,51},{4,52},{5,53},{6,54},{7,55},{8,56},{9,... | collective-permute-start | bytes 393224 | tf_op jit(solution)/shard_map/ppermute | solution.py:31
  162.3 7.1 %collective-permute-start.19 = (bf16[32,2048]{1,0:T(8,128)(2,1)S(1)}, bf16[32,2048]{1,0:T(8,128)(2,1)S(1)}, u32[]{:S(2)}, u32[]{:S(2)}) collective-permute-start(bf16[32,2048]{1,0:T(8,128)(2,1)S(1)} %get-tuple-element.36), channel_id=1, source_target_pairs={{0,64},{2,66},{4,68},{6,70},{8,72},{10,74},{12,76},{14,78},{16,80}... | collective-permute-start | bytes 393224 | tf_op jit(solution)/shard_map/ppermute | solution.py:31
  167.0 8.2 %collective-permute-start.26 = (bf16[32,2048]{1,0:T(8,128)(2,1)S(1)}, bf16[32,2048]{1,0:T(8,128)(2,1)S(1)}, u32[]{:S(2)}, u32[]{:S(2)}) collective-permute-start(bf16[32,2048]{1,0:T(8,128)(2,1)S(1)} %get-tuple-element.38), channel_id=1, source_target_pairs={{0,64},{2,66},{4,68},{6,70},{8,72},{10,74},{12,76},{14,78},{16,80}... | collective-permute-start | bytes 393224 | tf_op jit(solution)/shard_map/ppermute | solution.py:31
  169.4 5.8 %copy-start.6 = (f32[64,2048]{1,0:T(8,128)S(1)}, f32[64,2048]{1,0:T(8,128)}, u32[]{:S(2)}) copy-start(f32[64,2048]{1,0:T(8,128)} %param.5) | copy-start | bytes 1572868
  169.5 1.0 copy-start.4
  175.2 2.1 %copy-start.7 = (f32[512,256]{1,0:T(8,128)S(1)}, f32[512,256]{1,0:T(8,128)}, u32[]{:S(2)}) copy-start(f32[512,256]{1,0:T(8,128)} %get-tuple-element.21) | copy-start | bytes 1572868
  175.2 2.1 %collective-permute-start.5 = (f32[512,256]{1,0:T(8,128)}, f32[512,256]{1,0:T(8,128)S(1)}, u32[]{:S(2)}, u32[]{:S(2)}) collective-permute-start(f32[512,256]{1,0:T(8,128)} %get-tuple-element.22), channel_id=1, source_target_pairs={{0,2},{1,3},{2,0},{3,1},{4,6},{5,7},{6,4},{7,5},{8,10},{9,11},{10,... | collective-permute-start | bytes 1572872 | tf_op jit(solution)/shard_map/ppermute | solution.py:31

commit v4 on v3

v4 whole, which is shorter than its diff:
```python
import functools

import jax
import jax.numpy as jnp
import numpy as np
from jax import lax
from jax.experimental import pallas as pl
from jax.experimental.pallas import tpu as pltpu
from jax.sharding import Mesh
from jax.sharding import PartitionSpec as P

AXES = ("yl", "z", "x", "c", "yh")
SIZES = (2, 4, 4, 2, 2)
DP = ("yl", "z", "x", "c")
CHUNKS = ((0, 32), (32, 64))
OWN_AXES = (("x", "z"), ("z", "x"))
CROSS_AXES = (("z", "x"), ("x", "z"))
NT = (((1,), (1,)), ((), ()))
TN = (((0,), (0,)), ((), ()))
bf16, f32 = jnp.bfloat16, jnp.float32
VMEM = pl.BlockSpec(memory_space=pltpu.VMEM)
ANY = pl.BlockSpec(memory_space=pl.ANY)
SMEM = pl.BlockSpec(memory_space=pltpu.SMEM)


def send(value, move, only=None):
    pairs = []
    for i in range(int(np.prod(SIZES))):
        at = dict(zip(AXES, (int(v) for v in np.unravel_index(i, SIZES))))
        if only is None or only(at):
            to = {**at, **move(at)}
            pairs.append((i, int(np.ravel_multi_index([to[a] for a in AXES], SIZES))))
    return lax.ppermute(value, AXES, pairs)


def along(axis, k):
    return lambda at: {axis: (at[axis] + k) % 4}


def flip(*axes):
    return lambda at: {a: 1 - at[a] for a in axes}


def kernel_call(body, outs, specs, *args, flops=0):
    nbytes = sum(a.size * a.dtype.itemsize for a in args) + sum(o.size * o.dtype.itemsize for o in outs)
    return pl.pallas_call(
        body,
        out_shape=outs,
        in_specs=specs,
        out_specs=[VMEM] * len(outs),
        cost_estimate=pl.CostEstimate(flops=flops, bytes_accessed=nbytes, transcendentals=0),
    )(*args)


def slots_kernel(f_ref, t_ref, out_ref):
    wide = f_ref.shape[1] // 32
    for s in range(16):
        out_ref[s, :, :wide] = f_ref[:, s * wide : (s + 1) * wide]
        out_ref[s, :, wide : 2 * wide] = f_ref[:, (16 + s) * wide : (17 + s) * wide]
        out_ref[s, :, 2 * wide :] = t_ref[...]


def factor_kernel(wide, slots_ref, after_ref, also_ref, out_ref):
    out_ref[...] = lax.dot_general(
        slots_ref[:, :wide], slots_ref[:, wide:], TN, preferred_element_type=f32
    )


def copy_rows(src_ref, base, lo, hi, out_ref, first):
    n = hi - lo
    for b in range(16):
        start = pl.ds(pl.multiple_of(b * 128 + base + lo, 16), n)
        out_ref[first + b * n : first + (b + 1) * n, :] = src_ref[start, :]


def pick_mine_kernel(at_ref, gt_ref, one_ref, two_ref):
    for chunk, out_ref in zip(CHUNKS, (one_ref, two_ref)):
        copy_rows(gt_ref, at_ref[2], *chunk, out_ref, 0)


def pick_both_kernel(at_ref, two_ref, sib_ref, one_out, two_out):
    copy_rows(sib_ref, at_ref[2], *CHUNKS[0], one_out, 0)
    m = two_ref.shape[0]
    two_out[:m, :] = two_ref[...]
    copy_rows(sib_ref, at_ref[2], *CHUNKS[1], two_out, m)


def gram_kernel(rows, stride, lo, z_first, at_ref, a1_ref, a2_ref, b1_ref, b2_ref, after_ref, *outs):
    z, x, base1, base2 = at_ref[0], at_ref[1], at_ref[2], at_ref[3]
    left1, left2 = [], []
    for k in range(4):
        for j in range(4):
            dz, dx = (k, j) if z_first else (j, k)
            block = (lax.rem(z + dz, 4) * 4 + lax.rem(x + dx, 4)) * stride + lo
            left1.append(a1_ref[pl.ds(pl.multiple_of(block + base1, rows), rows), :])
            left2.append(a2_ref[pl.ds(pl.multiple_of(block + base2, rows), rows), :])
    left1, left2 = jnp.concatenate(left1), jnp.concatenate(left2)
    tile = 256
    for n in range(b1_ref.shape[0] // tile):
        cols = pl.ds(n * tile, tile)
        acc = lax.dot_general(left1, b1_ref[cols, :], NT, preferred_element_type=f32)
        acc += lax.dot_general(left2, b2_ref[cols, :], NT, preferred_element_type=f32)
        for k in range(4):
            outs[k][:, cols] = acc[4 * k * rows : 4 * (k + 1) * rows].astype(bf16)


def gram(at, a1, a2, b1, b2, after, rows, stride, lo, first):
    n = b1.shape[0]
    return kernel_call(
        functools.partial(gram_kernel, rows, stride, lo, first == "z"),
        [jax.ShapeDtypeStruct((4 * rows, n), bf16)] * 4,
        [SMEM] + [VMEM] * 4 + [ANY],
        at, a1, a2, b1, b2, after,
        flops=4 * 16 * rows * n * b1.shape[1],
    )


def scores_kernel(at_ref, pt_ref, *refs):
    h = at_ref[4]
    keep_ref, give_ref = refs[6:]
    for side, out_ref in enumerate((keep_ref, give_ref)):
        acc = None
        for which, group in ((h, refs[:3]), (1 - h, refs[3:6])):
            m = group[0].shape[0]
            lefts = (group[side][...], group[2][side * m : (side + 1) * m, :])
            for (lo, hi), left in zip(CHUNKS, lefts):
                p = pt_ref[:, pl.ds(which, 1), lo:hi, :].reshape(m, pt_ref.shape[-1])
                d = lax.dot_general(left, p, TN, preferred_element_type=f32)
                acc = d if acc is None else acc + d
        out_ref[...] = acc


def sum_kernel(mine_ref, g1_ref, g2_ref, g3_ref, after_ref, out_ref):
    out_ref[...] = mine_ref[...] + g1_ref[...].astype(f32) + g2_ref[...].astype(f32) + g3_ref[...].astype(f32)


def first_stage(parts, rows, axis):
    got = [send(parts[k], along(axis, k)) for k in (1, 2, 3)]
    mids = []
    for j in range(4):
        cut = lambda v: lax.slice_in_dim(v, j * rows, (j + 1) * rows).astype(f32)
        mids.append(cut(parts[0]) + cut(got[0]) + cut(got[1]) + cut(got[2]))
    return mids


def second_stage(mids, axis, after=None):
    got = [send(mids[k].astype(bf16), along(axis, k)) for k in (1, 2, 3)]
    if after is not None:
        out = jax.ShapeDtypeStruct(mids[0].shape, f32)
        return kernel_call(sum_kernel, [out], [VMEM] * 4 + [ANY], mids[0], *got, after)[0]
    return mids[0] + got[0].astype(f32) + got[1].astype(f32) + got[2].astype(f32)


def on_device(grads, covariance, test_grads, inverse_factor):
    tokens, feats = grads.shape
    z, x, c = lax.axis_index("z"), lax.axis_index("x"), lax.axis_index("c")
    yl, h = lax.axis_index("yl"), lax.axis_index("yh")
    rows = feats // 32
    tests = test_grads.shape[0]
    zero = 0 * c
    at = jnp.stack([z, x, c * rows, c * rows, h]).astype(jnp.int32)
    at_cross = jnp.stack([z, x, zero, zero, h]).astype(jnp.int32)
    at_cross2 = jnp.stack([z, x, zero, zero + feats // 4, h]).astype(jnp.int32)
    shape = jax.ShapeDtypeStruct
    gt = grads.T
    sib = send(gt, flip("c"))

    part = shape((feats // 4, tokens), bf16)
    picked1, picked2 = kernel_call(pick_mine_kernel, [part] * 2, [SMEM, VMEM], at, gt)
    arrived1 = send(picked1, flip("yh"))
    picked3, picked4 = kernel_call(
        pick_both_kernel, [part, shape((feats // 2, tokens), bf16)], [SMEM, VMEM, VMEM], at, picked2, sib
    )
    arrived3, arrived4 = send(picked3, flip("yh")), send(picked4, flip("yh"))

    own, after = [], picked3
    for (lo, hi), (first, _) in zip(CHUNKS, OWN_AXES):
        own.append(gram(at, gt, sib, gt, sib, after, hi - lo, 2 * rows, lo, first))
        after = own[-1][0]
    n = rows // 2
    cross = [gram(at_cross, arrived1, arrived3, gt, sib, after, n, n, 0, CROSS_AXES[0][0])]
    cross.append(gram(at_cross2, arrived4, arrived4, gt, sib, cross[0][0], n, n, 0, CROSS_AXES[1][0]))

    (slots,) = kernel_call(
        slots_kernel,
        [shape((16, rows, 4 * rows + tests), bf16)],
        [VMEM, VMEM],
        inverse_factor, test_grads.T,
    )
    slots = lax.all_to_all(slots, ("z", "x"), split_axis=0, concat_axis=0, tiled=True)
    (pt,) = kernel_call(
        functools.partial(factor_kernel, 4 * rows),
        [shape((4 * rows, tests), f32)],
        [VMEM, ANY, ANY],
        slots.reshape(16 * rows, -1), own[1][0], arrived3,
        flops=2 * 16 * rows * 4 * rows * tests,
    )
    pt = pt.reshape(2, 2, rows, tests)
    half = lambda i: lax.dynamic_index_in_dim(pt, i, 1, keepdims=False)
    pt = half(c) + send(half(1 - c), flip("c"))
    pt = (pt + send(pt, flip("yl"))).astype(bf16)
    pt = jnp.broadcast_to(pt[None], (16,) + pt.shape)
    pt = lax.all_to_all(pt, ("z", "x"), split_axis=0, concat_axis=0, tiled=True)

    keep, give = kernel_call(
        scores_kernel,
        [shape((tokens, tests), f32)] * 2,
        [SMEM] + [VMEM] * 7,
        at, pt, picked1, picked3, picked4, arrived1, arrived3, arrived4,
        flops=8 * 16 * rows * tokens * tests,
    )
    scores = keep + send(give, flip("c"))

    sums = []
    for parts, axes, owner in ((own, OWN_AXES, True), (cross, CROSS_AXES, False)):
        done = []
        for i, (first, second) in enumerate(axes):
            last = not owner and i == 1
            total = second_stage(first_stage(parts[i], n, first), second, keep if last else None)
            far = send(total.astype(bf16), flip("yl"), lambda at: (at["yl"] != at["yh"]) == owner)
            done.append(total + far.astype(f32))
        sums.append(jnp.concatenate(done, axis=0))
    examples = tokens * 64
    covariance_out = 0.9 * covariance + jnp.where(yl == h, *sums) / examples
    return scores, covariance_out


def solution(mesh):
    grid = Mesh(mesh.devices.reshape(SIZES), AXES)
    return jax.shard_map(
        on_device,
        mesh=grid,
        in_specs=(P(DP, "yh"), P(DP, "yh"), P("yh", DP), P(DP, None)),
        out_specs=(P(DP, "yh"), P(DP, "yh")),
        check_vma=False,
    )
```

time: 180 us -> 209 us (1.16)
  Pallas kernels: 35.1 us -> 44.1 us
  waiting for transfers between devices: 56.7 us -> 64.1 us
  starting transfers between devices: 64.5 us -> 71 us
  other arithmetic: 11.7 us -> 17 us
    pallas_call x7 -> x10, Pallas kernels: 35.1 us -> 44.1 us  [kernel_call(): pl.pallas_call(body, out_shape=outs, in_specs=specs, out_specs=[VMEM] * l...]
    ppermute x27 -> x35, waiting for transfers between devices: 56.7 us -> 64.1 us  [send(): return lax.ppermute(value, AXES, pairs)]
    ppermute x27 -> x35, starting transfers between devices: 50.7 us -> 56.6 us  [send(): return lax.ppermute(value, AXES, pairs)]
    convert_element_type x3 -> x4, other arithmetic: 2.87 us -> 5.73 us  [on_device(): total.astype(bf16)]
    all_to_all x1, starting transfers between devices: 5.45 us -> 7.96 us  [on_device(): lax.all_to_all(slots, ('z', 'x'), split_axis=0, concat_axis=0, tiled=True)]
    slice x2 -> x0, local copies, waits for them, and re-layouts: 2.36 us -> none  [on_device(): parts = gram(at_cross, a[:m], a[m:], gt, sib, after, n, n, first)]
    convert_element_type x3 -> x4, other arithmetic: 4.6 us -> 6.05 us  [second_stage(): got = [send(mids[k].astype(bf16), along(axis, k)) for k in (1, 2, 3)]]
    unnamed x23 -> x39, local copies, waits for them, and re-layouts: 4.94 us -> 6.25 us
  transfers between devices with their start and end apart: 29 -> 37, of which waited for: 9 -> 12; matrix products, arithmetic and copies ran while one was open for 9% -> 9% of each run, Pallas kernels for 12% -> 21%
where the time goes in v4:
time: 209 us; the launch traced here: 207 us
  starting transfers between devices  71 us (34%)
  waiting for transfers between devices  64.1 us (31%)
  Pallas kernels  44.1 us (21%)
  other arithmetic  17 us (8%)
  local copies, waits for them, and re-layouts  9.62 us (5%)
    ppermute x35, waiting for transfers between devices, send(): return lax.ppermute(value, AXES, pairs)  64.1 us
    ppermute x35, starting transfers between devices, send(): return lax.ppermute(value, AXES, pairs)  56.6 us
    pallas_call x10, Pallas kernels, kernel_call(): pl.pallas_call(body, out_shape=outs, in_specs=specs, out_specs=[VMEM] * l...  44.1 us
    all_to_all x1, starting transfers between devices, on_device(): lax.all_to_all(slots, ('z', 'x'), split_axis=0, concat_axis=0, tiled=True)  7.96 us
    all_to_all x1, starting transfers between devices, on_device(): pt = lax.all_to_all(pt, ('z', 'x'), split_axis=0, concat_axis=0, tiled=True)  6.41 us
    unnamed x39, local copies, waits for them, and re-layouts  6.25 us
    convert_element_type x4, other arithmetic, second_stage(): got = [send(mids[k].astype(bf16), along(axis, k)) for k in (1, 2, 3)]  6.05 us
    convert_element_type x4, other arithmetic, on_device(): total.astype(bf16)  5.73 us
  transfers between devices with their start and end apart: 37, of which 12 were waited for; matrix products, arithmetic and copies ran while one was open for 9% of the time, Pallas kernels for 21%

profile of v4, /device:TPU:0, one launch (start us, length us, event | category | flops | bytes accessed | tf_op | source)
XLA Modules:
  0.0 206.8 jit_solution(7641444526393455233)
XLA Ops:
  0.6 2.9 %copy.6 = bf16[512,2048]{0,1:T(8,128)(2,1)S(1)} copy(bf16[512,2048]{1,0:T(8,128)(2,1)} %param.4) | data formatting | bytes 4194304 | tf_op args[0]
  3.6 2.6 %shard_map.59 = bf16[16,64,512]{2,1,0:T(8,128)(2,1)} custom-call(bf16[64,4096]{1,0:T(8,128)(2,1)} %f_ref.1, bf16[64,256]{1,0:T(8,128)(2,1)} %bitcast.23), custom_call_target="tpu_custom_call" | custom-call | bytes 1605632 | tf_op jit(solution)/shard_map/pallas_call | solution.py:46
  6.2 8.0 %all-to-all-start = ((bf16[16,64,512]{2,1,0:T(8,128)(2,1)}), bf16[16,64,512]{2,1,0:T(8,128)(2,1)S(1)}, u32[]{:S(2)}, u32[]{:S(2)}) async-start(bf16[16,64,512]{2,1,0:T(8,128)(2,1)} %shard_map.59), calls=%async_computation | async-start | bytes 2097152 | tf_op jit(solution)/shard_map/all_to_all | solution.py:190
  14.8 2.6 %shard_map.60 = (bf16[512,512]{1,0:T(8,128)(2,1)}, bf16[512,512]{1,0:T(8,128)(2,1)}) custom-call(s32[5]{0:T(128)} %stack.32.at_ref, bf16[2048,512]{1,0:T(8,128)(2,1)} %bitcast.13), custom_call_target="tpu_custom_call" | custom-call | bytes 3145748 | tf_op jit(solution)/shard_map/pallas_call | solution.py:46
  17.4 3.0 %shard_map.61 = (bf16[512,512]{1,0:T(8,128)(2,1)}, bf16[1024,512]{1,0:T(8,128)(2,1)}) custom-call(s32[5]{0:T(128)} %stack.32.at_ref, bf16[512,512]{1,0:T(8,128)(2,1)} %get-tuple-element.24.two_ref, bf16[2048,512]{1,0:T(8,128)(2,1)} %collective-permute-done.sib_ref.a2_ref.b2_ref), custom_call_target="tpu_custom_call" | custom-call | bytes 4194324 | tf_op jit(solution)/shard_map/pallas_call | solution.py:46
  20.5 3.2 %collective-permute-start.1 = (bf16[512,512]{1,0:T(8,128)(2,1)}, bf16[512,512]{1,0:T(8,128)(2,1)S(1)}, u32[]{:S(2)}, u32[]{:S(2)}) collective-permute-start(bf16[512,512]{1,0:T(8,128)(2,1)} %get-tuple-element.25.after_ref.refs_1_), channel_id=1, source_target_pairs={{0,1},{1,0},{2,3},{3,2},{4,5},{5,4},{6,7},{7,6},{8,9},{9,8},{10,11... | collective-permute-start | bytes 1572872 | tf_op jit(solution)/shard_map/ppermute | solution.py:33
  23.7 7.1 %shard_map.62 = (bf16[128,2048]{1,0:T(8,128)(2,1)}, bf16[128,2048]{1,0:T(8,128)(2,1)}, bf16[128,2048]{1,0:T(8,128)(2,1)}, bf16[128,2048]{1,0:T(8,128)(2,1)}) custom-call(s32[5]{0:T(128)} %stack.32.at_ref, bf16[2048,512]{1,0:T(8,128)(2,1)} %bitcast.14, bf16[2048,512]{1,0:T(8,128)(2,1)} %collective-permute-done.sib_ref.a2_ref.b2_ref, ...), custom_call_target="tpu_custom_call" | custom-call | flops 2147483648 | bytes 11010068 | tf_op jit(solution)/shard_map/pallas_call | solution.py:46
  30.8 1.9 collective-permute-start.7
  32.7 2.7 %collective-permute-start.8 = (bf16[128,2048]{1,0:T(8,128)(2,1)}, bf16[128,2048]{1,0:T(8,128)(2,1)}, u32[]{:S(2)}, u32[]{:S(2)}) collective-permute-start(bf16[128,2048]{1,0:T(8,128)(2,1)} %get-tuple-element.33), channel_id=1, source_target_pairs={{0,8},{1,9},{2,10},{3,11},{4,12},{5,13},{6,14},{7,15},{8,0},{9,1},... | collective-permute-start | bytes 1572872 | tf_op jit(solution)/shard_map/ppermute | solution.py:33
  35.4 1.5 collective-permute-start.9
  38.5 7.1 %shard_map.63 = (bf16[128,2048]{1,0:T(8,128)(2,1)}, bf16[128,2048]{1,0:T(8,128)(2,1)}, bf16[128,2048]{1,0:T(8,128)(2,1)}, bf16[128,2048]{1,0:T(8,128)(2,1)}) custom-call(s32[5]{0:T(128)} %stack.32.at_ref, bf16[2048,512]{1,0:T(8,128)(2,1)} %bitcast.16, bf16[2048,512]{1,0:T(8,128)(2,1)} %collective-permute-done.sib_ref.a2_ref.b2_ref, ...), custom_call_target="tpu_custom_call" | custom-call | flops 2147483648 | bytes 11010068 | tf_op jit(solution)/shard_map/pallas_call | solution.py:46
  45.6 3.3 %collective-permute-start.5 = (bf16[1024,512]{1,0:T(8,128)(2,1)}, bf16[1024,512]{1,0:T(8,128)(2,1)}, u32[]{:S(2)}, u32[]{:S(2)}) collective-permute-start(bf16[1024,512]{1,0:T(8,128)(2,1)} %get-tuple-element.29.refs_2_), channel_id=1, source_target_pairs={{0,1},{1,0},{2,3},{3,2},{4,5},{5,4},{6,7},{7,6},{8,9},{9,8},{10,11... | collective-permute-start | bytes 3145736 | tf_op jit(solution)/shard_map/ppermute | solution.py:33
  49.9 2.4 %shard_map.64 = f32[256,256]{1,0:T(8,128)} custom-call(bf16[1024,512]{1,0:T(8,128)(2,1)} %bitcast.20, bf16[128,2048]{1,0:T(8,128)(2,1)} %get-tuple-element.27.after_ref, bf16[512,512]{1,0:T(8,128)(2,1)} %copy-done.6), custom_call_target="tpu_custom_call" | custom-call | flops 134217728 | bytes 2359296 | tf_op jit(solution)/shard_map/pallas_call | solution.py:46
  52.2 1.5 collective-permute-start.14
  53.7 4.3 %collective-permute-done.8 = bf16[128,2048]{1,0:T(8,128)(2,1)} collective-permute-done((bf16[128,2048]{1,0:T(8,128)(2,1)}, bf16[128,2048]{1,0:T(8,128)(2,1)}, u32[]{:S(2)}, u32[]{:S(2)}) %collective-permute-start.8) | collective-permute-done | bytes 524320 | tf_op jit(solution)/shard_map/ppermute | solution.py:33
  58.0 3.0 %collective-permute-start.15 = (bf16[128,2048]{1,0:T(8,128)(2,1)}, bf16[128,2048]{1,0:T(8,128)(2,1)S(1)}, u32[]{:S(2)}, u32[]{:S(2)}) collective-permute-start(bf16[128,2048]{1,0:T(8,128)(2,1)} %get-tuple-element.36), channel_id=1, source_target_pairs={{0,32},{1,33},{2,34},{3,35},{4,36},{5,37},{6,38},{7,39},{8,40},{9,... | collective-permute-start | bytes 1572872 | tf_op jit(solution)/shard_map/ppermute | solution.py:33
  61.0 1.2 collective-permute-start.16
  62.1 2.2 %add_convert_fusion.11 = (bf16[32,2048]{1,0:T(8,128)(2,1)}, bf16[32,2048]{1,0:T(8,128)(2,1)}, bf16[32,2048]{1,0:T(8,128)(2,1)S(1)}) fusion(bf16[128,2048]{1,0:T(8,128)(2,1)} %collective-permute-done.9, bf16[128,2048]{1,0:T(8,128)(2,1)} %collective-permute-done.8, bf16[128,2048]{1,0:T(8,128)(2,1)S(1)} %collective-permute-done.7, ...), kind=kLoop, calls=%fused_computation.22 | loop fusion | flops 1572864 | bytes 1966080 | tf_op jit(solution)/shard_map/convert_element_type | solution.py:147
  65.2 2.7 %collective-permute-done.14 = bf16[128,2048]{1,0:T(8,128)(2,1)S(1)} collective-permute-done((bf16[128,2048]{1,0:T(8,128)(2,1)}, bf16[128,2048]{1,0:T(8,128)(2,1)S(1)}, u32[]{:S(2)}, u32[]{:S(2)}) %collective-permute-start.14) | collective-permute-done | bytes 524320 | tf_op jit(solution)/shard_map/ppermute | solution.py:33
  67.9 7.1 %collective-permute-start.10 = (bf16[32,2048]{1,0:T(8,128)(2,1)}, bf16[32,2048]{1,0:T(8,128)(2,1)S(1)}, u32[]{:S(2)}, u32[]{:S(2)}) collective-permute-start(bf16[32,2048]{1,0:T(8,128)(2,1)} %get-tuple-element.59), channel_id=1, source_target_pairs={{0,16},{1,17},{2,18},{3,19},{4,20},{5,21},{6,22},{7,23},{8,24},{9,... | collective-permute-start | bytes 393224 | tf_op jit(solution)/shard_map/ppermute | solution.py:33
  75.0 4.0 %collective-permute-done.15 = bf16[128,2048]{1,0:T(8,128)(2,1)S(1)} collective-permute-done((bf16[128,2048]{1,0:T(8,128)(2,1)}, bf16[128,2048]{1,0:T(8,128)(2,1)S(1)}, u32[]{:S(2)}, u32[]{:S(2)}) %collective-permute-start.15) | collective-permute-done | bytes 524320 | tf_op jit(solution)/shard_map/ppermute | solution.py:33
  79.0 5.6 %collective-permute-done.16 = bf16[128,2048]{1,0:T(8,128)(2,1)S(1)} collective-permute-done((bf16[128,2048]{1,0:T(8,128)(2,1)}, bf16[128,2048]{1,0:T(8,128)(2,1)S(1)}, u32[]{:S(2)}, u32[]{:S(2)}) %collective-permute-start.16) | collective-permute-done | bytes 524320 | tf_op jit(solution)/shard_map/ppermute | solution.py:33
  84.6 2.1 collective-permute-start.11
  87.7 6.2 %shard_map.66 = (bf16[128,2048]{1,0:T(8,128)(2,1)}, bf16[128,2048]{1,0:T(8,128)(2,1)}, bf16[128,2048]{1,0:T(8,128)(2,1)}, bf16[128,2048]{1,0:T(8,128)(2,1)}) custom-call(s32[5]{0:T(128)} %pad_add_fusion.at_ref, bf16[512,512]{1,0:T(8,128)(2,1)} %collective-permute-done.4.refs_3_.a1_ref, bf16[512,512]{1,0:T(8,128)(2,1)} %copy-done.6, ...), custom_call_target="tpu_custom_call" | custom-call | flops 2147483648 | bytes 7864340 | tf_op jit(solution)/shard_map/pallas_call | solution.py:46
  94.0 3.2 %collective-permute-start.19 = (bf16[32,2048]{1,0:T(8,128)(2,1)}, bf16[32,2048]{1,0:T(8,128)(2,1)S(1)}, u32[]{:S(2)}, u32[]{:S(2)}) collective-permute-start(bf16[32,2048]{1,0:T(8,128)(2,1)} %get-tuple-element.63), channel_id=1, source_target_pairs={{0,12},{1,13},{2,14},{3,15},{4,0},{5,1},{6,2},{7,3},{8,4},{9,5},{1... | collective-permute-start | bytes 393224 | tf_op jit(solution)/shard_map/ppermute | solution.py:33
  97.2 1.7 fusion.3
  101.3 1.5 collective-permute-start.22
  103.5 1.3 collective-permute-start.23
  106.6 3.1 %collective-permute-done.3 = f32[2,64,256]{2,1,0:T(8,128)S(1)} collective-permute-done((f32[2,64,256]{2,1,0:T(8,128)S(1)}, f32[2,64,256]{2,1,0:T(8,128)S(1)}, u32[]{:S(2)}, u32[]{:S(2)}) %collective-permute-start.3) | collective-permute-done | bytes 131104 | tf_op jit(solution)/shard_map/ppermute | solution.py:33
  109.7 1.3 collective-permute-start.13
  112.1 6.4 %all-to-all-start.1 = ((bf16[16,2,64,256]{3,2,1,0:T(8,128)(2,1)}), bf16[16,2,64,256]{3,2,1,0:T(8,128)(2,1)S(1)}, u32[]{:S(2)}, u32[]{:S(2)}) async-start(bf16[16,2,64,256]{3,2,1,0:T(8,128)(2,1)} %broadcast_in_dim.2), calls=%async_computation.1 | async-start | bytes 2097152 | tf_op jit(solution)/shard_map/all_to_all | solution.py:203
  118.5 18.0 %collective-permute-done.21 = bf16[128,2048]{1,0:T(8,128)(2,1)S(1)} collective-permute-done((bf16[128,2048]{1,0:T(8,128)(2,1)}, bf16[128,2048]{1,0:T(8,128)(2,1)S(1)}, u32[]{:S(2)}, u32[]{:S(2)}) %collective-permute-start.21) | collective-permute-done | bytes 524320 | tf_op jit(solution)/shard_map/ppermute | solution.py:33
  137.6 1.9 add_convert_fusion.5
  140.6 6.5 %shard_map.67 = (bf16[128,2048]{1,0:T(8,128)(2,1)}, bf16[128,2048]{1,0:T(8,128)(2,1)}, bf16[128,2048]{1,0:T(8,128)(2,1)}, bf16[128,2048]{1,0:T(8,128)(2,1)}) custom-call(s32[5]{0:T(128)} %stack.34.at_ref, bf16[1024,512]{1,0:T(8,128)(2,1)} %collective-permute-done.5.refs_5_.a1_ref.a2_ref, bf16[1024,512]{1,0:T(8,128)(2,1)} %collective-permute-done.5.refs_5_.a1_ref.a2_ref, ...), custom_call_target="tpu_custom_call" | custom-call | flops 2147483648 | bytes 8912916 | tf_op jit(solution)/shard_map/pallas_call | solution.py:46
  147.1 2.1 %collective-permute-start.28 = (bf16[128,2048]{1,0:T(8,128)(2,1)}, bf16[128,2048]{1,0:T(8,128)(2,1)S(1)}, u32[]{:S(2)}, u32[]{:S(2)}) collective-permute-start(bf16[128,2048]{1,0:T(8,128)(2,1)} %get-tuple-element.43), channel_id=1, source_target_pairs={{0,4},{1,5},{2,6},{3,7},{4,8},{5,9},{6,10},{7,11},{8,12},{9,13},{1... | collective-permute-start | bytes 1572872 | tf_op jit(solution)/shard_map/ppermute | solution.py:33
  149.2 1.4 collective-permute-start.29
  150.7 1.3 collective-permute-start.30
  152.0 1.3 collective-permute-start.26
  153.3 1.4 collective-permute-start.25
  155.7 20.6 %collective-permute-done.26 = bf16[32,2048]{1,0:T(8,128)(2,1)S(1)} collective-permute-done((bf16[32,2048]{1,0:T(8,128)(2,1)}, bf16[32,2048]{1,0:T(8,128)(2,1)S(1)}, u32[]{:S(2)}, u32[]{:S(2)}) %collective-permute-start.26) | collective-permute-done | bytes 131104 | tf_op jit(solution)/shard_map/ppermute | solution.py:33
  176.3 1.3 collective-permute-start.20
  177.6 1.8 fusion.2
  179.4 4.5 %collective-permute-start.27 = (bf16[32,2048]{1,0:T(8,128)(2,1)}, bf16[32,2048]{1,0:T(8,128)(2,1)S(1)}, u32[]{:S(2)}, u32[]{:S(2)}) collective-permute-start(bf16[32,2048]{1,0:T(8,128)(2,1)} %get-tuple-element.46), channel_id=1, source_target_pairs={{0,64},{2,66},{4,68},{6,70},{8,72},{10,74},{12,76},{14,78},{16,80}... | collective-permute-start | bytes 393224 | tf_op jit(solution)/shard_map/ppermute | solution.py:33
  185.0 3.8 %collective-permute-start.33 = (bf16[32,2048]{1,0:T(8,128)(2,1)S(1)}, bf16[32,2048]{1,0:T(8,128)(2,1)S(1)}, u32[]{:S(2)}, u32[]{:S(2)}) collective-permute-start(bf16[32,2048]{1,0:T(8,128)(2,1)S(1)} %get-tuple-element.55), channel_id=1, source_target_pairs={{0,48},{1,49},{2,50},{3,51},{4,52},{5,53},{6,54},{7,55},{8,56},{9,... | collective-permute-start | bytes 393224 | tf_op jit(solution)/shard_map/ppermute | solution.py:33
  190.8 4.8 %shard_map.65 = (f32[512,256]{1,0:T(8,128)}, f32[512,256]{1,0:T(8,128)}) custom-call(s32[5]{0:T(128)} %stack.32.at_ref, bf16[16,2,64,256]{3,2,1,0:T(8,128)(2,1)} %copy-done.2, bf16[512,512]{1,0:T(8,128)(2,1)} %get-tuple-element.28.refs_0_, bf16[512,512]{1,0:T(8,128)(2,1)} %get-tuple-element.25.after_ref.refs_1_, ...), custom_call_target="tpu_custom_call" | custom-call | flops 1073741824 | bytes 6291476 | tf_op jit(solution)/shard_map/pallas_call | solution.py:46
  197.4 1.9 shard_map.68
  200.3 1.3 collective-permute-start.34
  201.7 2.3 %collective-permute-done.34 = bf16[32,2048]{1,0:T(8,128)(2,1)S(1)} collective-permute-done((bf16[32,2048]{1,0:T(8,128)(2,1)S(1)}, bf16[32,2048]{1,0:T(8,128)(2,1)S(1)}, u32[]{:S(2)}, u32[]{:S(2)}) %collective-permute-start.34) | collective-permute-done | bytes 131104 | tf_op jit(solution)/shard_map/ppermute | solution.py:33
  (97 shorter events, 23.0 us)
Async XLA Ops:
  3.5 11.3 %copy-start = (bf16[512,2048]{0,1:T(8,128)(2,1)}, bf16[512,2048]{0,1:T(8,128)(2,1)S(1)}, u32[]{:S(2)}) copy-start(bf16[512,2048]{0,1:T(8,128)(2,1)S(1)} %copy.6) | copy-start | bytes 6291460
  3.5 13.9 %collective-permute-start = (bf16[2048,512]{1,0:T(8,128)(2,1)S(1)}, bf16[2048,512]{1,0:T(8,128)(2,1)}, u32[]{:S(2)}, u32[]{:S(2)}) collective-permute-start(bf16[2048,512]{1,0:T(8,128)(2,1)S(1)} %bitcast.12), channel_id=1, source_target_pairs={{0,2},{1,3},{2,0},{3,1},{4,6},{5,7},{6,4},{7,5},{8,10},{9,11},{10,... | collective-permute-start | bytes 6291464 | tf_op jit(solution)/shard_map/ppermute | solution.py:33
  6.2 42.7 %all-to-all-start = ((bf16[16,64,512]{2,1,0:T(8,128)(2,1)}), bf16[16,64,512]{2,1,0:T(8,128)(2,1)S(1)}, u32[]{:S(2)}, u32[]{:S(2)}) async-start(bf16[16,64,512]{2,1,0:T(8,128)(2,1)} %shard_map.59), calls=%async_computation | async-start | bytes 2097152 | tf_op jit(solution)/shard_map/all_to_all | solution.py:190
  20.5 25.1 %collective-permute-start.1 = (bf16[512,512]{1,0:T(8,128)(2,1)}, bf16[512,512]{1,0:T(8,128)(2,1)S(1)}, u32[]{:S(2)}, u32[]{:S(2)}) collective-permute-start(bf16[512,512]{1,0:T(8,128)(2,1)} %get-tuple-element.25.after_ref.refs_1_), channel_id=1, source_target_pairs={{0,1},{1,0},{2,3},{3,2},{4,5},{5,4},{6,7},{7,6},{8,9},{9,8},{10,11... | collective-permute-start | bytes 1572872 | tf_op jit(solution)/shard_map/ppermute | solution.py:33
  30.8 21.4 %collective-permute-start.7 = (bf16[128,2048]{1,0:T(8,128)(2,1)}, bf16[128,2048]{1,0:T(8,128)(2,1)S(1)}, u32[]{:S(2)}, u32[]{:S(2)}) collective-permute-start(bf16[128,2048]{1,0:T(8,128)(2,1)} %get-tuple-element.32), channel_id=1, source_target_pairs={{0,4},{1,5},{2,6},{3,7},{4,8},{5,9},{6,10},{7,11},{8,12},{9,13},{1... | collective-permute-start | bytes 1572872 | tf_op jit(solution)/shard_map/ppermute | solution.py:33
  32.7 25.3 %collective-permute-start.8 = (bf16[128,2048]{1,0:T(8,128)(2,1)}, bf16[128,2048]{1,0:T(8,128)(2,1)}, u32[]{:S(2)}, u32[]{:S(2)}) collective-permute-start(bf16[128,2048]{1,0:T(8,128)(2,1)} %get-tuple-element.33), channel_id=1, source_target_pairs={{0,8},{1,9},{2,10},{3,11},{4,12},{5,13},{6,14},{7,15},{8,0},{9,1},... | collective-permute-start | bytes 1572872 | tf_op jit(solution)/shard_map/ppermute | solution.py:33
  35.4 25.6 %collective-permute-start.9 = (bf16[128,2048]{1,0:T(8,128)(2,1)}, bf16[128,2048]{1,0:T(8,128)(2,1)}, u32[]{:S(2)}, u32[]{:S(2)}) collective-permute-start(bf16[128,2048]{1,0:T(8,128)(2,1)} %get-tuple-element.34), channel_id=1, source_target_pairs={{0,12},{1,13},{2,14},{3,15},{4,0},{5,1},{6,2},{7,3},{8,4},{9,5},{1... | collective-permute-start | bytes 1572872 | tf_op jit(solution)/shard_map/ppermute | solution.py:33
  36.8 50.7 %collective-permute-start.4 = (bf16[512,512]{1,0:T(8,128)(2,1)}, bf16[512,512]{1,0:T(8,128)(2,1)}, u32[]{:S(2)}, u32[]{:S(2)}) collective-permute-start(bf16[512,512]{1,0:T(8,128)(2,1)} %get-tuple-element.28.refs_0_), channel_id=1, source_target_pairs={{0,1},{1,0},{2,3},{3,2},{4,5},{5,4},{6,7},{7,6},{8,9},{9,8},{10,11... | collective-permute-start | bytes 1572872 | tf_op jit(solution)/shard_map/ppermute | solution.py:33
  45.6 16.6 %copy-start.3 = (bf16[128,2048]{1,0:T(8,128)(2,1)S(1)}, bf16[128,2048]{1,0:T(8,128)(2,1)}, u32[]{:S(2)}) copy-start(bf16[128,2048]{1,0:T(8,128)(2,1)} %get-tuple-element.26.after_ref) | copy-start | bytes 1572868
  45.6 3.3 %copy-start.6 = (bf16[512,512]{1,0:T(8,128)(2,1)}, bf16[512,512]{1,0:T(8,128)(2,1)S(1)}, u32[]{:S(2)}) copy-start(bf16[512,512]{1,0:T(8,128)(2,1)S(1)} %collective-permute-done.1.also_ref.refs_4_.a2_ref) | copy-start | bytes 1572868
  45.6 95.0 %collective-permute-start.5 = (bf16[1024,512]{1,0:T(8,128)(2,1)}, bf16[1024,512]{1,0:T(8,128)(2,1)}, u32[]{:S(2)}, u32[]{:S(2)}) collective-permute-start(bf16[1024,512]{1,0:T(8,128)(2,1)} %get-tuple-element.29.refs_2_), channel_id=1, source_target_pairs={{0,1},{1,0},{2,3},{3,2},{4,5},{5,4},{6,7},{7,6},{8,9},{9,8},{10,11... | collective-permute-start | bytes 3145736 | tf_op jit(solution)/shard_map/ppermute | solution.py:33
  49.9 36.8 %copy-start.5 = (bf16[128,2048]{1,0:T(8,128)(2,1)S(1)}, bf16[128,2048]{1,0:T(8,128)(2,1)}, u32[]{:S(2)}) copy-start(bf16[128,2048]{1,0:T(8,128)(2,1)} %get-tuple-element.27.after_ref) | copy-start | bytes 1572868
  52.2 15.7 %collective-permute-start.14 = (bf16[128,2048]{1,0:T(8,128)(2,1)}, bf16[128,2048]{1,0:T(8,128)(2,1)S(1)}, u32[]{:S(2)}, u32[]{:S(2)}) collective-permute-start(bf16[128,2048]{1,0:T(8,128)(2,1)} %get-tuple-element.35), channel_id=1, source_target_pairs={{0,16},{1,17},{2,18},{3,19},{4,20},{5,21},{6,22},{7,23},{8,24},{9,... | collective-permute-start | bytes 1572872 | tf_op jit(solution)/shard_map/ppermute | solution.py:33
  58.0 21.0 %collective-permute-start.15 = (bf16[128,2048]{1,0:T(8,128)(2,1)}, bf16[128,2048]{1,0:T(8,128)(2,1)S(1)}, u32[]{:S(2)}, u32[]{:S(2)}) collective-permute-start(bf16[128,2048]{1,0:T(8,128)(2,1)} %get-tuple-element.36), channel_id=1, source_target_pairs={{0,32},{1,33},{2,34},{3,35},{4,36},{5,37},{6,38},{7,39},{8,40},{9,... | collective-permute-start | bytes 1572872 | tf_op jit(solution)/shard_map/ppermute | solution.py:33
  61.0 23.6 %collective-permute-start.16 = (bf16[128,2048]{1,0:T(8,128)(2,1)}, bf16[128,2048]{1,0:T(8,128)(2,1)S(1)}, u32[]{:S(2)}, u32[]{:S(2)}) collective-permute-start(bf16[128,2048]{1,0:T(8,128)(2,1)} %get-tuple-element.37), channel_id=1, source_target_pairs={{0,48},{1,49},{2,50},{3,51},{4,52},{5,53},{6,54},{7,55},{8,56},{9,... | collective-permute-start | bytes 1572872 | tf_op jit(solution)/shard_map/ppermute | solution.py:33
  67.9 25.9 %collective-permute-start.10 = (bf16[32,2048]{1,0:T(8,128)(2,1)}, bf16[32,2048]{1,0:T(8,128)(2,1)S(1)}, u32[]{:S(2)}, u32[]{:S(2)}) collective-permute-start(bf16[32,2048]{1,0:T(8,128)(2,1)} %get-tuple-element.59), channel_id=1, source_target_pairs={{0,16},{1,17},{2,18},{3,19},{4,20},{5,21},{6,22},{7,23},{8,24},{9,... | collective-permute-start | bytes 393224 | tf_op jit(solution)/shard_map/ppermute | solution.py:33
  79.0 14.9 %copy-start.10 = (bf16[128,2048]{1,0:T(8,128)(2,1)}, bf16[128,2048]{1,0:T(8,128)(2,1)S(1)}, u32[]{:S(2)}) copy-start(bf16[128,2048]{1,0:T(8,128)(2,1)S(1)} %collective-permute-done.15) | copy-start | bytes 1572868
  79.0 15.0 %collective-permute-start.12 = (bf16[32,2048]{1,0:T(8,128)(2,1)}, bf16[32,2048]{1,0:T(8,128)(2,1)S(1)}, u32[]{:S(2)}, u32[]{:S(2)}) collective-permute-start(bf16[32,2048]{1,0:T(8,128)(2,1)} %get-tuple-element.60), channel_id=1, source_target_pairs={{0,48},{1,49},{2,50},{3,51},{4,52},{5,53},{6,54},{7,55},{8,56},{9,... | collective-permute-start | bytes 393224 | tf_op jit(solution)/shard_map/ppermute | solution.py:33
  84.6 12.6 %collective-permute-start.11 = (bf16[32,2048]{1,0:T(8,128)(2,1)S(1)}, bf16[32,2048]{1,0:T(8,128)(2,1)S(1)}, u32[]{:S(2)}, u32[]{:S(2)}) collective-permute-start(bf16[32,2048]{1,0:T(8,128)(2,1)S(1)} %get-tuple-element.61), channel_id=1, source_target_pairs={{0,32},{1,33},{2,34},{3,35},{4,36},{5,37},{6,38},{7,39},{8,40},{9,... | collective-permute-start | bytes 393224 | tf_op jit(solution)/shard_map/ppermute | solution.py:33
  87.6 12.2 %copy-start.7 = (f32[256,256]{1,0:T(8,128)S(1)}, f32[256,256]{1,0:T(8,128)}, u32[]{:S(2)}) copy-start(f32[256,256]{1,0:T(8,128)} %shard_map.64) | copy-start | bytes 786436
  87.6 11.4 %collective-permute-start.2 = (f32[2,64,256]{2,1,0:T(8,128)S(1)}, f32[2,64,256]{2,1,0:T(8,128)S(1)}, u32[]{:S(2)}, u32[]{:S(2)}) collective-permute-start(f32[2,64,256]{2,1,0:T(8,128)S(1)} %dynamic-slice_bitcast_fusion), channel_id=1, source_target_pairs={{0,2},{1,3},{2,0},{3,1},{4,6},{5,7},{6,4},{7,5},{8,10},{9,11},{10,... | collective-permute-start | bytes 393224 | tf_op jit(solution)/shard_map/ppermute | solution.py:33
  93.9 7.4 %collective-permute-start.17 = (bf16[32,2048]{1,0:T(8,128)(2,1)}, bf16[32,2048]{1,0:T(8,128)(2,1)S(1)}, u32[]{:S(2)}, u32[]{:S(2)}) collective-permute-start(bf16[32,2048]{1,0:T(8,128)(2,1)} %get-tuple-element.62), channel_id=1, source_target_pairs={{0,4},{1,5},{2,6},{3,7},{4,8},{5,9},{6,10},{7,11},{8,12},{9,13},{1... | collective-permute-start | bytes 393224 | tf_op jit(solution)/shard_map/ppermute | solution.py:33
  94.0 9.5 %collective-permute-start.19 = (bf16[32,2048]{1,0:T(8,128)(2,1)}, bf16[32,2048]{1,0:T(8,128)(2,1)S(1)}, u32[]{:S(2)}, u32[]{:S(2)}) collective-permute-start(bf16[32,2048]{1,0:T(8,128)(2,1)} %get-tuple-element.63), channel_id=1, source_target_pairs={{0,12},{1,13},{2,14},{3,15},{4,0},{5,1},{6,2},{7,3},{8,4},{9,5},{1... | collective-permute-start | bytes 393224 | tf_op jit(solution)/shard_map/ppermute | solution.py:33
  97.2 7.5 %collective-permute-start.18 = (bf16[32,2048]{1,0:T(8,128)(2,1)}, bf16[32,2048]{1,0:T(8,128)(2,1)S(1)}, u32[]{:S(2)}, u32[]{:S(2)}) collective-permute-start(bf16[32,2048]{1,0:T(8,128)(2,1)} %get-tuple-element.64), channel_id=1, source_target_pairs={{0,8},{1,9},{2,10},{3,11},{4,12},{5,13},{6,14},{7,15},{8,0},{9,1},... | collective-permute-start | bytes 393224 | tf_op jit(solution)/shard_map/ppermute | solution.py:33
  99.6 36.9 %collective-permute-start.21 = (bf16[128,2048]{1,0:T(8,128)(2,1)}, bf16[128,2048]{1,0:T(8,128)(2,1)S(1)}, u32[]{:S(2)}, u32[]{:S(2)}) collective-permute-start(bf16[128,2048]{1,0:T(8,128)(2,1)} %get-tuple-element.39), channel_id=1, source_target_pairs={{0,16},{1,17},{2,18},{3,19},{4,20},{5,21},{6,22},{7,23},{8,24},{9,... | collective-permute-start | bytes 1572872 | tf_op jit(solution)/shard_map/ppermute | solution.py:33
  101.3 35.3 %collective-permute-start.22 = (bf16[128,2048]{1,0:T(8,128)(2,1)}, bf16[128,2048]{1,0:T(8,128)(2,1)S(1)}, u32[]{:S(2)}, u32[]{:S(2)}) collective-permute-start(bf16[128,2048]{1,0:T(8,128)(2,1)} %get-tuple-element.40), channel_id=1, source_target_pairs={{0,32},{1,33},{2,34},{3,35},{4,36},{5,37},{6,38},{7,39},{8,40},{9,... | collective-permute-start | bytes 1572872 | tf_op jit(solution)/shard_map/ppermute | solution.py:33
  103.5 34.1 %collective-permute-start.23 = (bf16[128,2048]{1,0:T(8,128)(2,1)}, bf16[128,2048]{1,0:T(8,128)(2,1)}, u32[]{:S(2)}, u32[]{:S(2)}) collective-permute-start(bf16[128,2048]{1,0:T(8,128)(2,1)} %get-tuple-element.41), channel_id=1, source_target_pairs={{0,48},{1,49},{2,50},{3,51},{4,52},{5,53},{6,54},{7,55},{8,56},{9,... | collective-permute-start | bytes 1572872 | tf_op jit(solution)/shard_map/ppermute | solution.py:33
  104.7 5.0 %collective-permute-start.3 = (f32[2,64,256]{2,1,0:T(8,128)S(1)}, f32[2,64,256]{2,1,0:T(8,128)S(1)}, u32[]{:S(2)}, u32[]{:S(2)}) collective-permute-start(f32[2,64,256]{2,1,0:T(8,128)S(1)} %bitcast_add_fusion), channel_id=1, source_target_pairs={{0,64},{1,65},{2,66},{3,67},{4,68},{5,69},{6,70},{7,71},{8,72},{9,... | collective-permute-start | bytes 393224 | tf_op jit(solution)/shard_map/ppermute | solution.py:33
  106.6 31.0 %copy-start.9 = (bf16[128,2048]{1,0:T(8,128)(2,1)S(1)}, bf16[128,2048]{1,0:T(8,128)(2,1)}, u32[]{:S(2)}) copy-start(bf16[128,2048]{1,0:T(8,128)(2,1)} %get-tuple-element.38.after_ref) | copy-start | bytes 1572868
  109.7 42.3 %collective-permute-start.13 = (bf16[32,2048]{1,0:T(8,128)(2,1)}, bf16[32,2048]{1,0:T(8,128)(2,1)S(1)}, u32[]{:S(2)}, u32[]{:S(2)}) collective-permute-start(bf16[32,2048]{1,0:T(8,128)(2,1)} %get-tuple-element.48), channel_id=1, source_target_pairs={{1,65},{3,67},{5,69},{7,71},{9,73},{11,75},{13,77},{15,79},{17,81}... | collective-permute-start | bytes 393224 | tf_op jit(solution)/shard_map/ppermute | solution.py:33
  112.1 77.6 %all-to-all-start.1 = ((bf16[16,2,64,256]{3,2,1,0:T(8,128)(2,1)}), bf16[16,2,64,256]{3,2,1,0:T(8,128)(2,1)S(1)}, u32[]{:S(2)}, u32[]{:S(2)}) async-start(bf16[16,2,64,256]{3,2,1,0:T(8,128)(2,1)} %broadcast_in_dim.2), calls=%async_computation.1 | async-start | bytes 2097152 | tf_op jit(solution)/shard_map/all_to_all | solution.py:203
  139.5 13.8 %collective-permute-start.24 = (bf16[32,2048]{1,0:T(8,128)(2,1)}, bf16[32,2048]{1,0:T(8,128)(2,1)}, u32[]{:S(2)}, u32[]{:S(2)}) collective-permute-start(bf16[32,2048]{1,0:T(8,128)(2,1)} %get-tuple-element.52), channel_id=1, source_target_pairs={{0,4},{1,5},{2,6},{3,7},{4,8},{5,9},{6,10},{7,11},{8,12},{9,13},{1... | collective-permute-start | bytes 393224 | tf_op jit(solution)/shard_map/ppermute | solution.py:33
  147.1 36.9 %copy-start.12 = (bf16[128,2048]{1,0:T(8,128)(2,1)S(1)}, bf16[128,2048]{1,0:T(8,128)(2,1)}, u32[]{:S(2)}) copy-start(bf16[128,2048]{1,0:T(8,128)(2,1)} %get-tuple-element.42) | copy-start | bytes 1572868
  147.1 36.9 %collective-permute-start.28 = (bf16[128,2048]{1,0:T(8,128)(2,1)}, bf16[128,2048]{1,0:T(8,128)(2,1)S(1)}, u32[]{:S(2)}, u32[]{:S(2)}) collective-permute-start(bf16[128,2048]{1,0:T(8,128)(2,1)} %get-tuple-element.43), channel_id=1, source_target_pairs={{0,4},{1,5},{2,6},{3,7},{4,8},{5,9},{6,10},{7,11},{8,12},{9,13},{1... | collective-permute-start | bytes 1572872 | tf_op jit(solution)/shard_map/ppermute | solution.py:33
  149.2 34.7 %collective-permute-start.29 = (bf16[128,2048]{1,0:T(8,128)(2,1)}, bf16[128,2048]{1,0:T(8,128)(2,1)S(1)}, u32[]{:S(2)}, u32[]{:S(2)}) collective-permute-start(bf16[128,2048]{1,0:T(8,128)(2,1)} %get-tuple-element.44), channel_id=1, source_target_pairs={{0,8},{1,9},{2,10},{3,11},{4,12},{5,13},{6,14},{7,15},{8,0},{9,1},... | collective-permute-start | bytes 1572872 | tf_op jit(solution)/shard_map/ppermute | solution.py:33
  150.7 33.3 %collective-permute-start.30 = (bf16[128,2048]{1,0:T(8,128)(2,1)}, bf16[128,2048]{1,0:T(8,128)(2,1)S(1)}, u32[]{:S(2)}, u32[]{:S(2)}) collective-permute-start(bf16[128,2048]{1,0:T(8,128)(2,1)} %get-tuple-element.45), channel_id=1, source_target_pairs={{0,12},{1,13},{2,14},{3,15},{4,0},{5,1},{6,2},{7,3},{8,4},{9,5},{1... | collective-permute-start | bytes 1572872 | tf_op jit(solution)/shard_map/ppermute | solution.py:33
  152.0 24.3 %collective-permute-start.26 = (bf16[32,2048]{1,0:T(8,128)(2,1)}, bf16[32,2048]{1,0:T(8,128)(2,1)S(1)}, u32[]{:S(2)}, u32[]{:S(2)}) collective-permute-start(bf16[32,2048]{1,0:T(8,128)(2,1)} %get-tuple-element.53), channel_id=1, source_target_pairs={{0,12},{1,13},{2,14},{3,15},{4,0},{5,1},{6,2},{7,3},{8,4},{9,5},{1... | collective-permute-start | bytes 393224 | tf_op jit(solution)/shard_map/ppermute | solution.py:33
  153.3 24.2 %collective-permute-start.25 = (bf16[32,2048]{1,0:T(8,128)(2,1)}, bf16[32,2048]{1,0:T(8,128)(2,1)S(1)}, u32[]{:S(2)}, u32[]{:S(2)}) collective-permute-start(bf16[32,2048]{1,0:T(8,128)(2,1)} %get-tuple-element.54), channel_id=1, source_target_pairs={{0,8},{1,9},{2,10},{3,11},{4,12},{5,13},{6,14},{7,15},{8,0},{9,1},... | collective-permute-start | bytes 393224 | tf_op jit(solution)/shard_map/ppermute | solution.py:33
  176.3 13.4 %collective-permute-start.20 = (bf16[32,2048]{1,0:T(8,128)(2,1)S(1)}, bf16[32,2048]{1,0:T(8,128)(2,1)S(1)}, u32[]{:S(2)}, u32[]{:S(2)}) collective-permute-start(bf16[32,2048]{1,0:T(8,128)(2,1)S(1)} %get-tuple-element.50), channel_id=1, source_target_pairs={{1,65},{3,67},{5,69},{7,71},{9,73},{11,75},{13,77},{15,79},{17,81}... | collective-permute-start | bytes 393224 | tf_op jit(solution)/shard_map/ppermute | solution.py:33
  179.4 22.2 %collective-permute-start.27 = (bf16[32,2048]{1,0:T(8,128)(2,1)}, bf16[32,2048]{1,0:T(8,128)(2,1)S(1)}, u32[]{:S(2)}, u32[]{:S(2)}) collective-permute-start(bf16[32,2048]{1,0:T(8,128)(2,1)} %get-tuple-element.46), channel_id=1, source_target_pairs={{0,64},{2,66},{4,68},{6,70},{8,72},{10,74},{12,76},{14,78},{16,80}... | collective-permute-start | bytes 393224 | tf_op jit(solution)/shard_map/ppermute | solution.py:33
  185.0 10.5 %collective-permute-start.33 = (bf16[32,2048]{1,0:T(8,128)(2,1)S(1)}, bf16[32,2048]{1,0:T(8,128)(2,1)S(1)}, u32[]{:S(2)}, u32[]{:S(2)}) collective-permute-start(bf16[32,2048]{1,0:T(8,128)(2,1)S(1)} %get-tuple-element.55), channel_id=1, source_target_pairs={{0,48},{1,49},{2,50},{3,51},{4,52},{5,53},{6,54},{7,55},{8,56},{9,... | collective-permute-start | bytes 393224 | tf_op jit(solution)/shard_map/ppermute | solution.py:33
  188.9 6.7 %collective-permute-start.32 = (bf16[32,2048]{1,0:T(8,128)(2,1)S(1)}, bf16[32,2048]{1,0:T(8,128)(2,1)S(1)}, u32[]{:S(2)}, u32[]{:S(2)}) collective-permute-start(bf16[32,2048]{1,0:T(8,128)(2,1)S(1)} %get-tuple-element.56), channel_id=1, source_target_pairs={{0,32},{1,33},{2,34},{3,35},{4,36},{5,37},{6,38},{7,39},{8,40},{9,... | collective-permute-start | bytes 393224 | tf_op jit(solution)/shard_map/ppermute | solution.py:33
  189.1 7.6 %collective-permute-start.31 = (bf16[32,2048]{1,0:T(8,128)(2,1)S(1)}, bf16[32,2048]{1,0:T(8,128)(2,1)S(1)}, u32[]{:S(2)}, u32[]{:S(2)}) collective-permute-start(bf16[32,2048]{1,0:T(8,128)(2,1)S(1)} %get-tuple-element.57), channel_id=1, source_target_pairs={{0,16},{1,17},{2,18},{3,19},{4,20},{5,21},{6,22},{7,23},{8,24},{9,... | collective-permute-start | bytes 393224 | tf_op jit(solution)/shard_map/ppermute | solution.py:33
  195.6 6.0 %copy-start.18 = (f32[512,256]{1,0:T(8,128)S(1)}, f32[512,256]{1,0:T(8,128)}, u32[]{:S(2)}) copy-start(f32[512,256]{1,0:T(8,128)} %get-tuple-element.31) | copy-start | bytes 1572868
  195.6 9.5 %copy-start.8 = (f32[64,2048]{1,0:T(8,128)S(1)}, f32[64,2048]{1,0:T(8,128)}, u32[]{:S(2)}) copy-start(f32[64,2048]{1,0:T(8,128)} %param.5) | copy-start | bytes 1572868
  199.2 6.7 %copy-start.4 = (f32[512,256]{1,0:T(8,128)S(1)}, f32[512,256]{1,0:T(8,128)}, u32[]{:S(2)}) copy-start(f32[512,256]{1,0:T(8,128)} %get-tuple-element.30.after_ref) | copy-start | bytes 1572868
  200.3 3.8 %collective-permute-start.34 = (bf16[32,2048]{1,0:T(8,128)(2,1)S(1)}, bf16[32,2048]{1,0:T(8,128)(2,1)S(1)}, u32[]{:S(2)}, u32[]{:S(2)}) collective-permute-start(bf16[32,2048]{1,0:T(8,128)(2,1)S(1)} %convert_element_type.374), channel_id=1, source_target_pairs={{0,64},{2,66},{4,68},{6,70},{8,72},{10,74},{12,76},{14,78},{16,80}... | collective-permute-start | bytes 393224 | tf_op jit(solution)/shard_map/ppermute | solution.py:33
  201.6 4.3 %collective-permute-start.6 = (f32[512,256]{1,0:T(8,128)S(1)}, f32[512,256]{1,0:T(8,128)S(1)}, u32[]{:S(2)}, u32[]{:S(2)}) collective-permute-start(f32[512,256]{1,0:T(8,128)S(1)} %copy-done.18), channel_id=1, source_target_pairs={{0,2},{1,3},{2,0},{3,1},{4,6},{5,7},{6,4},{7,5},{8,10},{9,11},{10,... | collective-permute-start | bytes 1572872 | tf_op jit(solution)/shard_map/ppermute | solution.py:33
  (8 other events, 11.3 us)

commit v5 on v3

v5 whole, which is shorter than its diff:
```python
import functools

import jax
import jax.numpy as jnp
import numpy as np
from jax import lax
from jax.experimental import pallas as pl
from jax.experimental.pallas import tpu as pltpu
from jax.sharding import Mesh
from jax.sharding import PartitionSpec as P

AXES = ("yl", "z", "x", "c", "yh")
SIZES = (2, 4, 4, 2, 2)
DP = ("yl", "z", "x", "c")
NT = (((1,), (1,)), ((), ()))
TN = (((0,), (0,)), ((), ()))
bf16, f32 = jnp.bfloat16, jnp.float32
VMEM = pl.BlockSpec(memory_space=pltpu.VMEM)
ANY = pl.BlockSpec(memory_space=pl.ANY)
SMEM = pl.BlockSpec(memory_space=pltpu.SMEM)


def send(value, move, only=None):
    pairs = []
    for i in range(int(np.prod(SIZES))):
        at = dict(zip(AXES, (int(v) for v in np.unravel_index(i, SIZES))))
        if only is None or only(at):
            to = {**at, **move(at)}
            pairs.append((i, int(np.ravel_multi_index([to[a] for a in AXES], SIZES))))
    return lax.ppermute(value, AXES, pairs)


def along(axis, k):
    return lambda at: {axis: (at[axis] + k) % 4}


def flip(*axes):
    return lambda at: {a: 1 - at[a] for a in axes}


def kernel_call(body, outs, specs, *args, flops=0):
    nbytes = sum(a.size * a.dtype.itemsize for a in args) + sum(o.size * o.dtype.itemsize for o in outs)
    return pl.pallas_call(
        body,
        out_shape=outs,
        in_specs=specs,
        out_specs=[VMEM] * len(outs),
        cost_estimate=pl.CostEstimate(flops=flops, bytes_accessed=nbytes, transcendentals=0),
    )(*args)


def slots_kernel(f_ref, t_ref, out_ref):
    wide = f_ref.shape[1] // 32
    for s in range(16):
        out_ref[s, :, :wide] = f_ref[:, s * wide : (s + 1) * wide]
        out_ref[s, :, wide : 2 * wide] = f_ref[:, (16 + s) * wide : (17 + s) * wide]
        out_ref[s, :, 2 * wide :] = t_ref[...]


def factor_kernel(wide, slots_ref, after_ref, also_ref, out_ref):
    out_ref[...] = lax.dot_general(
        slots_ref[:, :wide], slots_ref[:, wide:], TN, preferred_element_type=f32
    )


def pick_kernel(at_ref, gt_ref, sib_ref, out_ref):
    for i, ref in enumerate((gt_ref, sib_ref)):
        for b in range(16):
            start = pl.ds(pl.multiple_of(b * 128 + at_ref[2], 64), 64)
            out_ref[(16 * i + b) * 64 : (16 * i + b + 1) * 64, :] = ref[start, :]


def gram_kernel(at_ref, a_ref, b1_ref, b2_ref, after_ref, *outs):
    z, x = at_ref[0], at_ref[1]
    rows, m, n, tile = 64, a_ref.shape[0] // 2, b1_ref.shape[0] // 2, 256
    for half in range(2):
        left1, left2 = [], []
        for k in range(4):
            for j in range(4):
                dx, dz = (k, j) if half == 0 else (j, k)
                block = (lax.rem(z + dz, 4) * 4 + lax.rem(x + dx, 4)) * rows
                left1.append(a_ref[pl.ds(pl.multiple_of(block, rows), rows), :])
                left2.append(a_ref[pl.ds(pl.multiple_of(block + m, rows), rows), :])
        left1, left2 = jnp.concatenate(left1), jnp.concatenate(left2)
        for t in range(n // tile):
            cols = pl.ds(half * n + t * tile, tile)
            acc = lax.dot_general(left1, b1_ref[cols, :], NT, preferred_element_type=f32)
            acc += lax.dot_general(left2, b2_ref[cols, :], NT, preferred_element_type=f32)
            for k in range(4):
                part = acc[4 * k * rows : 4 * (k + 1) * rows].astype(bf16)
                outs[4 * half + k][:, t * tile : (t + 1) * tile] = part


def gram(at, a, b1, b2, after):
    n = b1.shape[0]
    return kernel_call(
        gram_kernel,
        [jax.ShapeDtypeStruct((256, n // 2), bf16)] * 8,
        [SMEM] + [VMEM] * 3 + [ANY],
        at, a, b1, b2, after,
        flops=2 * a.shape[0] * n * b1.shape[1],
    )


def scores_kernel(at_ref, pt_ref, own_ref, cross_ref, keep_ref, give_ref):
    h = at_ref[3]
    m = own_ref.shape[0] // 2
    p_own = pt_ref[:, pl.ds(h, 1), :, :].reshape(m, pt_ref.shape[-1])
    p_cross = pt_ref[:, pl.ds(1 - h, 1), :, :].reshape(m, pt_ref.shape[-1])
    for side, out_ref in enumerate((keep_ref, give_ref)):
        s = slice(side * m, (side + 1) * m)
        acc = lax.dot_general(own_ref[s, :], p_own, TN, preferred_element_type=f32)
        out_ref[...] = acc + lax.dot_general(cross_ref[s, :], p_cross, TN, preferred_element_type=f32)


def sum_kernel(mine_ref, g1_ref, g2_ref, g3_ref, after_ref, out_ref):
    out_ref[...] = mine_ref[...] + g1_ref[...].astype(f32) + g2_ref[...].astype(f32) + g3_ref[...].astype(f32)


def scatter_sum(parts, rows, after=None):
    got, mids, sums = [], [], []
    for half, axis in ((0, "x"), (1, "z")):
        got.append([send(parts[4 * half + k], along(axis, k)) for k in (1, 2, 3)])
    for half in range(2):
        mids.append([])
        for j in range(4):
            cut = lambda v: lax.slice_in_dim(v, j * rows, (j + 1) * rows).astype(f32)
            total = cut(parts[4 * half])
            for r in got[half]:
                total = total + cut(r)
            mids[half].append(total)
    for half, axis in ((0, "z"), (1, "x")):
        rs = [send(mids[half][k].astype(bf16), along(axis, k)) for k in (1, 2, 3)]
        if after is not None:
            out = jax.ShapeDtypeStruct(mids[half][0].shape, f32)
            sums.append(kernel_call(sum_kernel, [out], [VMEM] * 4 + [ANY], mids[half][0], *rs, after)[0])
        else:
            sums.append(mids[half][0] + rs[0].astype(f32) + rs[1].astype(f32) + rs[2].astype(f32))
    return jnp.concatenate(sums, axis=1)


def on_device(grads, covariance, test_grads, inverse_factor):
    tokens, feats = grads.shape
    z, x, c = lax.axis_index("z"), lax.axis_index("x"), lax.axis_index("c")
    yl, h = lax.axis_index("yl"), lax.axis_index("yh")
    rows = feats // 32
    tests = test_grads.shape[0]
    at = jnp.stack([z, x, c * rows, h]).astype(jnp.int32)
    shape = jax.ShapeDtypeStruct
    gt = grads.T
    sib = send(gt, flip("c"))

    (picked,) = kernel_call(pick_kernel, [shape((feats, tokens), bf16)], [SMEM, VMEM, VMEM], at, gt, sib)
    arrived = send(picked, flip("yh"))
    own = gram(at, picked, gt, sib, picked)
    cross = gram(at, arrived, gt, sib, own[0])

    (slots,) = kernel_call(
        slots_kernel,
        [shape((16, rows, 4 * rows + tests), bf16)],
        [VMEM, VMEM],
        inverse_factor, test_grads.T,
    )
    slots = lax.all_to_all(slots, ("z", "x"), split_axis=0, concat_axis=0, tiled=True)
    (pt,) = kernel_call(
        functools.partial(factor_kernel, 4 * rows),
        [shape((4 * rows, tests), f32)],
        [VMEM, ANY, ANY],
        slots.reshape(16 * rows, -1), own[0], arrived,
        flops=2 * 16 * rows * 4 * rows * tests,
    )
    pt = pt.reshape(2, 2, rows, tests)
    half = lambda i: lax.dynamic_index_in_dim(pt, i, 1, keepdims=False)
    pt = half(c) + send(half(1 - c), flip("c"))
    pt = (pt + send(pt, flip("yl"))).astype(bf16)
    pt = jnp.broadcast_to(pt[None], (16,) + pt.shape)
    pt = lax.all_to_all(pt, ("z", "x"), split_axis=0, concat_axis=0, tiled=True)

    keep, give = kernel_call(
        scores_kernel,
        [shape((tokens, tests), f32)] * 2,
        [SMEM] + [VMEM] * 3,
        at, pt, picked, arrived,
        flops=8 * 16 * rows * tokens * tests,
    )
    scores = keep + send(give, flip("c"))

    own = scatter_sum(own, rows)
    own = own + send(own.astype(bf16), flip("yl"), lambda at: at["yl"] != at["yh"]).astype(f32)
    cross = scatter_sum(cross, rows, keep)
    cross = cross + send(cross.astype(bf16), flip("yl"), lambda at: at["yl"] == at["yh"]).astype(f32)
    examples = tokens * 64
    covariance_out = 0.9 * covariance + jnp.where(yl == h, own, cross) / examples
    return scores, covariance_out


def solution(mesh):
    grid = Mesh(mesh.devices.reshape(SIZES), AXES)
    return jax.shard_map(
        on_device,
        mesh=grid,
        in_specs=(P(DP, "yh"), P(DP, "yh"), P("yh", DP), P(DP, None)),
        out_specs=(P(DP, "yh"), P(DP, "yh")),
        check_vma=False,
    )
```

time: 180 us -> 178 us (0.989)
  waiting for transfers between devices: 56.7 us -> 44.6 us
  starting transfers between devices: 64.5 us -> 70.5 us
  other arithmetic: 11.7 us -> 16.1 us
    ppermute x27 -> x31, waiting for transfers between devices: 56.7 us -> 44.6 us  [send(): return lax.ppermute(value, AXES, pairs)]
    all_to_all x1, starting transfers between devices: 8.33 us -> 14.2 us  [on_device(): pt = lax.all_to_all(pt, ('z', 'x'), split_axis=0, concat_axis=0, tiled=True)]
    convert_element_type x5, other arithmetic: 5.76 us -> 10 us  [the longest x4 8.94 us: scatter_sum(): rs = [send(mids[half][k].astype(bf16), along(axis, k)) for k in (1, 2, 3)]]
    all_to_all x1, starting transfers between devices: 5.45 us -> 7.88 us  [on_device(): lax.all_to_all(slots, ('z', 'x'), split_axis=0, concat_axis=0, tiled=True)]
    add x3, other arithmetic: 0.92 us -> 3.32 us  [the longest x2 2.46 us: scatter_sum(): mids[half][0] + rs[0].astype(f32) + rs[1].astype(f32) + rs[2].astype(f32)]
    slice x2 -> x0, local copies, waits for them, and re-layouts: 2.36 us -> none  [on_device(): parts = gram(at_cross, a[:m], a[m:], gt, sib, after, n, n, first)]
    ppermute x27 -> x31, starting transfers between devices: 50.7 us -> 48.4 us  [send(): return lax.ppermute(value, AXES, pairs)]
    unnamed x23 -> x43, local copies, waits for them, and re-layouts: 4.94 us -> 6.25 us
  transfers between devices with their start and end apart: 29 -> 33, of which waited for: 9 -> 9; matrix products, arithmetic and copies ran while one was open for 9% -> 10% of each run, Pallas kernels for 12% -> 18%
where the time goes in v5:
time: 178 us; the launch traced here: 175 us
  starting transfers between devices  70.5 us (40%)
  waiting for transfers between devices  44.6 us (25%)
  Pallas kernels  35 us (20%)
  other arithmetic  16.1 us (9%)
  local copies, waits for them, and re-layouts  8.29 us (5%)
    ppermute x31, starting transfers between devices, send(): return lax.ppermute(value, AXES, pairs)  48.4 us
    ppermute x31, waiting for transfers between devices, send(): return lax.ppermute(value, AXES, pairs)  44.6 us
    pallas_call x8, Pallas kernels, kernel_call(): pl.pallas_call(body, out_shape=outs, in_specs=specs, out_specs=[VMEM] * l...  35 us
    all_to_all x1, starting transfers between devices, on_device(): pt = lax.all_to_all(pt, ('z', 'x'), split_axis=0, concat_axis=0, tiled=True)  14.2 us
    convert_element_type x4, other arithmetic, scatter_sum(): rs = [send(mids[half][k].astype(bf16), along(axis, k)) for k in (1, 2, 3)]  8.94 us
    all_to_all x1, starting transfers between devices, on_device(): lax.all_to_all(slots, ('z', 'x'), split_axis=0, concat_axis=0, tiled=True)  7.88 us
    unnamed x43, local copies, waits for them, and re-layouts  6.25 us
  transfers between devices with their start and end apart: 33, of which 9 were waited for; matrix products, arithmetic and copies ran while one was open for 10% of the time, Pallas kernels for 18%

profile of v5, /device:TPU:0, one launch (start us, length us, event | category | flops | bytes accessed | tf_op | source)
XLA Modules:
  0.0 175.5 jit_solution(4276370237258101513)
XLA Ops:
  0.6 2.9 %copy.6 = bf16[512,2048]{0,1:T(8,128)(2,1)S(1)} copy(bf16[512,2048]{1,0:T(8,128)(2,1)} %param.4) | data formatting | bytes 4194304 | tf_op args[0]
  4.5 3.4 %collective-permute-done.sib_ref.b2_ref = bf16[2048,512]{1,0:T(8,128)(2,1)} collective-permute-done((bf16[2048,512]{1,0:T(8,128)(2,1)S(1)}, bf16[2048,512]{1,0:T(8,128)(2,1)}, u32[]{:S(2)}, u32[]{:S(2)}) %collective-permute-start) | collective-permute-done | bytes 2097184 | tf_op jit(solution)/shard_map/ppermute | solution.py:30
  7.9 3.7 %shard_map.60.a_ref.after_ref.own_ref = bf16[2048,512]{1,0:T(8,128)(2,1)} custom-call(s32[4]{0:T(128)} %pad_add_fusion.at_ref, bf16[2048,512]{1,0:T(8,128)(2,1)} %bitcast.13, bf16[2048,512]{1,0:T(8,128)(2,1)} %collective-permute-done.sib_ref.b2_ref), custom_call_target="tpu_custom_call" | custom-call | bytes 6291472 | tf_op jit(solution)/shard_map/pallas_call | solution.py:43
  11.6 3.3 %collective-permute-start.1 = (bf16[2048,512]{1,0:T(8,128)(2,1)}, bf16[2048,512]{1,0:T(8,128)(2,1)S(1)}, u32[]{:S(2)}, u32[]{:S(2)}) collective-permute-start(bf16[2048,512]{1,0:T(8,128)(2,1)} %shard_map.60.a_ref.after_ref.own_ref), channel_id=1, source_target_pairs={{0,1},{1,0},{2,3},{3,2},{4,5},{5,4},{6,7},{7,6},{8,9},{9,8},{10,11... | collective-permute-start | bytes 6291464 | tf_op jit(solution)/shard_map/ppermute | solution.py:30
  14.9 2.1 %shard_map.59 = bf16[16,64,512]{2,1,0:T(8,128)(2,1)} custom-call(bf16[64,4096]{1,0:T(8,128)(2,1)} %f_ref.1, bf16[64,256]{1,0:T(8,128)(2,1)} %bitcast.19), custom_call_target="tpu_custom_call" | custom-call | bytes 1605632 | tf_op jit(solution)/shard_map/pallas_call | solution.py:43
  17.0 7.9 %all-to-all-start = ((bf16[16,64,512]{2,1,0:T(8,128)(2,1)}), bf16[16,64,512]{2,1,0:T(8,128)(2,1)S(1)}, u32[]{:S(2)}, u32[]{:S(2)}) async-start(bf16[16,64,512]{2,1,0:T(8,128)(2,1)} %shard_map.59), calls=%async_computation | async-start | bytes 2097152 | tf_op jit(solution)/shard_map/all_to_all | solution.py:164
  24.9 9.1 %shard_map.61 = (bf16[256,1024]{1,0:T(8,128)(2,1)}, bf16[256,1024]{1,0:T(8,128)(2,1)}, bf16[256,1024]{1,0:T(8,128)(2,1)}, bf16[256,1024]{1,0:T(8,128)(2,1)}, bf1...) custom-call(s32[4]{0:T(128)} %pad_add_fusion.at_ref, ...), custom_call_target="tpu_custom_call" | custom-call | flops 4294967296 | bytes 12582928 | tf_op jit(solution)/shard_map/pallas_call | solution.py:43
  34.0 1.9 %collective-permute-start.5 = (bf16[256,1024]{1,0:T(8,128)(2,1)}, bf16[256,1024]{1,0:T(8,128)(2,1)}, u32[]{:S(2)}, u32[]{:S(2)}) collective-permute-start(bf16[256,1024]{1,0:T(8,128)(2,1)} %get-tuple-element.23), channel_id=1, source_target_pairs={{0,4},{1,5},{2,6},{3,7},{4,8},{5,9},{6,10},{7,11},{8,12},{9,13},{1... | collective-permute-start | bytes 1572872 | tf_op jit(solution)/shard_map/ppermute | solution.py:30
  35.9 2.7 %collective-permute-start.6 = (bf16[256,1024]{1,0:T(8,128)(2,1)}, bf16[256,1024]{1,0:T(8,128)(2,1)}, u32[]{:S(2)}, u32[]{:S(2)}) collective-permute-start(bf16[256,1024]{1,0:T(8,128)(2,1)} %get-tuple-element.24), channel_id=1, source_target_pairs={{0,8},{1,9},{2,10},{3,11},{4,12},{5,13},{6,14},{7,15},{8,0},{9,1},... | collective-permute-start | bytes 1572872 | tf_op jit(solution)/shard_map/ppermute | solution.py:30
  38.6 1.5 collective-permute-start.7
  40.0 1.5 collective-permute-start.11
  41.5 10.4 %collective-permute-done.5 = bf16[256,1024]{1,0:T(8,128)(2,1)} collective-permute-done((bf16[256,1024]{1,0:T(8,128)(2,1)}, bf16[256,1024]{1,0:T(8,128)(2,1)}, u32[]{:S(2)}, u32[]{:S(2)}) %collective-permute-start.5) | collective-permute-done | bytes 524320 | tf_op jit(solution)/shard_map/ppermute | solution.py:30
  51.9 3.0 %collective-permute-start.12 = (bf16[256,1024]{1,0:T(8,128)(2,1)}, bf16[256,1024]{1,0:T(8,128)(2,1)}, u32[]{:S(2)}, u32[]{:S(2)}) collective-permute-start(bf16[256,1024]{1,0:T(8,128)(2,1)} %get-tuple-element.28), channel_id=1, source_target_pairs={{0,32},{1,33},{2,34},{3,35},{4,36},{5,37},{6,38},{7,39},{8,40},{9,... | collective-permute-start | bytes 1572872 | tf_op jit(solution)/shard_map/ppermute | solution.py:30
  54.9 7.7 %collective-permute-done.6 = bf16[256,1024]{1,0:T(8,128)(2,1)} collective-permute-done((bf16[256,1024]{1,0:T(8,128)(2,1)}, bf16[256,1024]{1,0:T(8,128)(2,1)}, u32[]{:S(2)}, u32[]{:S(2)}) %collective-permute-start.6) | collective-permute-done | bytes 524320 | tf_op jit(solution)/shard_map/ppermute | solution.py:30
  62.6 2.7 %collective-permute-start.13 = (bf16[256,1024]{1,0:T(8,128)(2,1)}, bf16[256,1024]{1,0:T(8,128)(2,1)}, u32[]{:S(2)}, u32[]{:S(2)}) collective-permute-start(bf16[256,1024]{1,0:T(8,128)(2,1)} %get-tuple-element.29), channel_id=1, source_target_pairs={{0,48},{1,49},{2,50},{3,51},{4,52},{5,53},{6,54},{7,55},{8,56},{9,... | collective-permute-start | bytes 1572872 | tf_op jit(solution)/shard_map/ppermute | solution.py:30
  65.2 2.4 %add_convert_fusion.11 = (bf16[64,1024]{1,0:T(8,128)(2,1)}, bf16[64,1024]{1,0:T(8,128)(2,1)S(1)}, bf16[64,1024]{1,0:T(8,128)(2,1)}) fusion(bf16[256,1024]{1,0:T(8,128)(2,1)} %collective-permute-done.7, bf16[256,1024]{1,0:T(8,128)(2,1)} %collective-permute-done.6, bf16[256,1024]{1,0:T(8,128)(2,1)} %collective-permute-done.5, ...), kind=kLoop, calls=%fused_computation.20 | loop fusion | flops 1572864 | bytes 1966080 | tf_op jit(solution)/shard_map/convert_element_type | solution.py:133
  68.5 1.2 collective-permute-start.8
  70.7 2.3 %shard_map.62 = f32[256,256]{1,0:T(8,128)} custom-call(bf16[1024,512]{1,0:T(8,128)(2,1)} %bitcast.16, bf16[256,1024]{1,0:T(8,128)(2,1)} %get-tuple-element.20.after_ref, bf16[2048,512]{1,0:T(8,128)(2,1)} %copy-done.1), custom_call_target="tpu_custom_call" | custom-call | flops 134217728 | bytes 3932160 | tf_op jit(solution)/shard_map/pallas_call | solution.py:43
  73.9 9.1 %shard_map.64 = (bf16[256,1024]{1,0:T(8,128)(2,1)}, bf16[256,1024]{1,0:T(8,128)(2,1)}, bf16[256,1024]{1,0:T(8,128)(2,1)}, bf16[256,1024]{1,0:T(8,128)(2,1)}, bf1...) custom-call(s32[4]{0:T(128)} %pad_add_fusion.at_ref, ...), custom_call_target="tpu_custom_call" | custom-call | flops 4294967296 | bytes 11010064 | tf_op jit(solution)/shard_map/pallas_call | solution.py:43
  83.9 1.2 collective-permute-start.18
  85.1 1.6 add_convert_fusion.8
  86.7 2.7 %collective-permute-start.14 = (bf16[64,1024]{1,0:T(8,128)(2,1)S(1)}, bf16[64,1024]{1,0:T(8,128)(2,1)S(1)}, u32[]{:S(2)}, u32[]{:S(2)}) collective-permute-start(bf16[64,1024]{1,0:T(8,128)(2,1)S(1)} %get-tuple-element.41), channel_id=1, source_target_pairs={{0,4},{1,5},{2,6},{3,7},{4,8},{5,9},{6,10},{7,11},{8,12},{9,13},{1... | collective-permute-start | bytes 393224 | tf_op jit(solution)/shard_map/ppermute | solution.py:30
  90.5 1.8 %collective-permute-start.16 = (bf16[64,1024]{1,0:T(8,128)(2,1)S(1)}, bf16[64,1024]{1,0:T(8,128)(2,1)S(1)}, u32[]{:S(2)}, u32[]{:S(2)}) collective-permute-start(bf16[64,1024]{1,0:T(8,128)(2,1)S(1)} %get-tuple-element.42), channel_id=1, source_target_pairs={{0,12},{1,13},{2,14},{3,15},{4,0},{5,1},{6,2},{7,3},{8,4},{9,5},{1... | collective-permute-start | bytes 393224 | tf_op jit(solution)/shard_map/ppermute | solution.py:30
  93.2 7.3 %collective-permute-done.14 = bf16[64,1024]{1,0:T(8,128)(2,1)S(1)} collective-permute-done((bf16[64,1024]{1,0:T(8,128)(2,1)S(1)}, bf16[64,1024]{1,0:T(8,128)(2,1)S(1)}, u32[]{:S(2)}, u32[]{:S(2)}) %collective-permute-start.14) | collective-permute-done | bytes 131104 | tf_op jit(solution)/shard_map/ppermute | solution.py:30
  100.5 3.5 %collective-permute-start.20 = (bf16[256,1024]{1,0:T(8,128)(2,1)}, bf16[256,1024]{1,0:T(8,128)(2,1)}, u32[]{:S(2)}, u32[]{:S(2)}) collective-permute-start(bf16[256,1024]{1,0:T(8,128)(2,1)} %get-tuple-element.33), channel_id=1, source_target_pairs={{0,12},{1,13},{2,14},{3,15},{4,0},{5,1},{6,2},{7,3},{8,4},{9,5},{1... | collective-permute-start | bytes 1572872 | tf_op jit(solution)/shard_map/ppermute | solution.py:30
  104.0 2.2 %collective-permute-done.15 = bf16[64,1024]{1,0:T(8,128)(2,1)S(1)} collective-permute-done((bf16[64,1024]{1,0:T(8,128)(2,1)S(1)}, bf16[64,1024]{1,0:T(8,128)(2,1)S(1)}, u32[]{:S(2)}, u32[]{:S(2)}) %collective-permute-start.15) | collective-permute-done | bytes 131104 | tf_op jit(solution)/shard_map/ppermute | solution.py:30
  107.0 1.2 convert_add_fusion.3
  108.4 2.9 %collective-permute-done.3 = f32[2,64,256]{2,1,0:T(8,128)S(1)} collective-permute-done((f32[2,64,256]{2,1,0:T(8,128)S(1)}, f32[2,64,256]{2,1,0:T(8,128)S(1)}, u32[]{:S(2)}, u32[]{:S(2)}) %collective-permute-start.3) | collective-permute-done | bytes 131104 | tf_op jit(solution)/shard_map/ppermute | solution.py:30
  111.3 1.4 collective-permute-start.25
  112.6 1.4 collective-permute-start.26
  114.1 1.1 broadcast_in_dim.2
  115.2 14.2 %all-to-all-start.1 = ((bf16[16,2,64,256]{3,2,1,0:T(8,128)(2,1)}), bf16[16,2,64,256]{3,2,1,0:T(8,128)(2,1)S(1)}, u32[]{:S(2)}, u32[]{:S(2)}) async-start(bf16[16,2,64,256]{3,2,1,0:T(8,128)(2,1)} %broadcast_in_dim.2), calls=%async_computation.1 | async-start | bytes 2097152 | tf_op jit(solution)/shard_map/all_to_all | solution.py:177
  129.5 1.2 convert_add_fusion.2
  130.7 2.4 %add_convert_fusion.3 = (bf16[64,1024]{1,0:T(8,128)(2,1)S(1)}, bf16[64,1024]{1,0:T(8,128)(2,1)}, bf16[64,1024]{1,0:T(8,128)(2,1)S(1)}, f32[64,1024]{1,0:T(8,128)}) fusion(bf16[256,1024]{1,0:T(8,128)(2,1)} %collective-permute-done.20, bf16[256,1024]{1,0:T(8,128)(2,1)} %collective-permute-done.19, bf16[256,1024]{1,0:T(8,128)(2,1)S(1)} %collective-permute-done.18, ...), kind=kLoop, calls=%fused_computation.9 | loop fusion | flops 2031616 | bytes 2752512 | tf_op jit(solution)/shard_map/convert_element_type | solution.py:133
  133.1 1.9 %collective-permute-start.21 = (bf16[64,1024]{1,0:T(8,128)(2,1)S(1)}, bf16[64,1024]{1,0:T(8,128)(2,1)S(1)}, u32[]{:S(2)}, u32[]{:S(2)}) collective-permute-start(bf16[64,1024]{1,0:T(8,128)(2,1)S(1)} %get-tuple-element.46), channel_id=1, source_target_pairs={{0,16},{1,17},{2,18},{3,19},{4,20},{5,21},{6,22},{7,23},{8,24},{9,... | collective-permute-start | bytes 393224 | tf_op jit(solution)/shard_map/ppermute | solution.py:30
  135.1 2.7 %collective-permute-start.22 = (bf16[64,1024]{1,0:T(8,128)(2,1)}, bf16[64,1024]{1,0:T(8,128)(2,1)S(1)}, u32[]{:S(2)}, u32[]{:S(2)}) collective-permute-start(bf16[64,1024]{1,0:T(8,128)(2,1)} %get-tuple-element.45), channel_id=1, source_target_pairs={{0,32},{1,33},{2,34},{3,35},{4,36},{5,37},{6,38},{7,39},{8,40},{9,... | collective-permute-start | bytes 393224 | tf_op jit(solution)/shard_map/ppermute | solution.py:30
  137.7 5.9 %collective-permute-done.24 = bf16[256,1024]{1,0:T(8,128)(2,1)} collective-permute-done((bf16[256,1024]{1,0:T(8,128)(2,1)}, bf16[256,1024]{1,0:T(8,128)(2,1)}, u32[]{:S(2)}, u32[]{:S(2)}) %collective-permute-start.24) | collective-permute-done | bytes 524320 | tf_op jit(solution)/shard_map/ppermute | solution.py:30
  143.7 1.0 collective-permute-done.26
  144.7 2.5 %add_convert_fusion = (bf16[64,1024]{1,0:T(8,128)(2,1)}, bf16[64,1024]{1,0:T(8,128)(2,1)}, bf16[64,1024]{1,0:T(8,128)(2,1)}, f32[64,1024]{1,0:T(8,128)}) fusion(bf16[256,1024]{1,0:T(8,128)(2,1)} %collective-permute-done.26, bf16[256,1024]{1,0:T(8,128)(2,1)} %collective-permute-done.25, bf16[256,1024]{1,0:T(8,128)(2,1)} %collective-permute-done.24, ...), kind=kLoop, calls=%fused_computation.5 | loop fusion | flops 2031616 | bytes 2752512 | tf_op jit(solution)/shard_map/convert_element_type | solution.py:133
  147.3 3.4 %collective-permute-start.28 = (bf16[64,1024]{1,0:T(8,128)(2,1)}, bf16[64,1024]{1,0:T(8,128)(2,1)S(1)}, u32[]{:S(2)}, u32[]{:S(2)}) collective-permute-start(bf16[64,1024]{1,0:T(8,128)(2,1)} %get-tuple-element.49), channel_id=1, source_target_pairs={{0,8},{1,9},{2,10},{3,11},{4,12},{5,13},{6,14},{7,15},{8,0},{9,1},... | collective-permute-start | bytes 393224 | tf_op jit(solution)/shard_map/ppermute | solution.py:30
  151.7 4.8 %shard_map.63 = (f32[512,256]{1,0:T(8,128)}, f32[512,256]{1,0:T(8,128)}) custom-call(s32[4]{0:T(128)} %pad_add_fusion.at_ref, bf16[16,2,64,256]{3,2,1,0:T(8,128)(2,1)} %copy-done.3, bf16[2048,512]{1,0:T(8,128)(2,1)} %shard_map.60.a_ref.after_ref.own_ref, bf16[2048,512]{1,0:T(8,128)(2,1)} %copy-done.1), custom_call_target="tpu_custom_call" | custom-call | flops 1073741824 | bytes 6291472 | tf_op jit(solution)/shard_map/pallas_call | solution.py:43
  156.5 1.4 collective-permute-start.17
  158.6 1.9 %shard_map.65 = f32[64,1024]{1,0:T(8,128)} custom-call(f32[64,1024]{1,0:T(8,128)} %get-tuple-element.47.mine_ref, bf16[64,1024]{1,0:T(8,128)(2,1)} %copy-done.15, bf16[64,1024]{1,0:T(8,128)(2,1)} %copy-done.16, bf16[64,1024]{1,0:T(8,128)(2,1)} %copy-done.17, f32[512,256]{1,0:T(8,128)} %get-tuple-element.21.after_ref), custom_call_target="tpu_custom_call" | custom-call | bytes 1441792 | tf_op jit(solution)/shard_map/pallas_call | solution.py:43
  161.2 1.9 %shard_map.66 = f32[64,1024]{1,0:T(8,128)} custom-call(f32[64,1024]{1,0:T(8,128)} %get-tuple-element.51.mine_ref, bf16[64,1024]{1,0:T(8,128)(2,1)} %copy-done.18, bf16[64,1024]{1,0:T(8,128)(2,1)} %copy-done.19, bf16[64,1024]{1,0:T(8,128)(2,1)} %copy-done.20, f32[512,256]{1,0:T(8,128)} %get-tuple-element.21.after_ref), custom_call_target="tpu_custom_call" | custom-call | bytes 1441792 | tf_op jit(solution)/shard_map/pallas_call | solution.py:43
  163.2 1.1 fusion
  164.3 4.6 %collective-permute-start.30 = (bf16[64,2048]{1,0:T(8,128)(2,1)S(1)}, bf16[64,2048]{1,0:T(8,128)(2,1)S(1)}, u32[]{:S(2)}, u32[]{:S(2)}) collective-permute-start(bf16[64,2048]{1,0:T(8,128)(2,1)S(1)} %fusion), channel_id=1, source_target_pairs={{0,64},{2,66},{4,68},{6,70},{8,72},{10,74},{12,76},{14,78},{16,80}... | collective-permute-start | bytes 786440 | tf_op jit(solution)/shard_map/ppermute | solution.py:30
  168.9 3.7 %collective-permute-done.30 = bf16[64,2048]{1,0:T(8,128)(2,1)S(1)} collective-permute-done((bf16[64,2048]{1,0:T(8,128)(2,1)S(1)}, bf16[64,2048]{1,0:T(8,128)(2,1)S(1)}, u32[]{:S(2)}, u32[]{:S(2)}) %collective-permute-start.30) | collective-permute-done | bytes 262176 | tf_op jit(solution)/shard_map/ppermute | solution.py:30
  172.7 1.9 %multiply_add_fusion = f32[64,2048]{1,0:T(8,128)} fusion(bf16[64,2048]{1,0:T(8,128)(2,1)S(1)} %collective-permute-done.30, bf16[64,2048]{1,0:T(8,128)(2,1)S(1)} %collective-permute-done.17, f32[64,2048]{1,0:T(8,128)S(1)} %copy-done.7, f32[64,1024]{1,0:T(8,128)} %shard_map.66, f32[64,1024]{1,0:T(8,128)S(1)} %copy-done.5, f32[64,1024]{1,0:T(8,128)S(1)} %convert_add_fusion.2, ...), kind=kLoop, calls=%fused_computation.2 | loop fusion | flops 1310720 | bytes 2621441 | tf_op jit(solution)/shard_map/add | solution.py:193
  (84 shorter events, 10.8 us)
Async XLA Ops:
  3.5 4.4 %copy-start = (bf16[512,2048]{0,1:T(8,128)(2,1)}, bf16[512,2048]{0,1:T(8,128)(2,1)S(1)}, u32[]{:S(2)}) copy-start(bf16[512,2048]{0,1:T(8,128)(2,1)S(1)} %copy.6) | copy-start | bytes 6291460
  3.5 4.4 %collective-permute-start = (bf16[2048,512]{1,0:T(8,128)(2,1)S(1)}, bf16[2048,512]{1,0:T(8,128)(2,1)}, u32[]{:S(2)}, u32[]{:S(2)}) collective-permute-start(bf16[2048,512]{1,0:T(8,128)(2,1)S(1)} %bitcast.12), channel_id=1, source_target_pairs={{0,2},{1,3},{2,0},{3,1},{4,6},{5,7},{6,4},{7,5},{8,10},{9,11},{10,... | collective-permute-start | bytes 6291464 | tf_op jit(solution)/shard_map/ppermute | solution.py:30
  11.6 56.9 %collective-permute-start.1 = (bf16[2048,512]{1,0:T(8,128)(2,1)}, bf16[2048,512]{1,0:T(8,128)(2,1)S(1)}, u32[]{:S(2)}, u32[]{:S(2)}) collective-permute-start(bf16[2048,512]{1,0:T(8,128)(2,1)} %shard_map.60.a_ref.after_ref.own_ref), channel_id=1, source_target_pairs={{0,1},{1,0},{2,3},{3,2},{4,5},{5,4},{6,7},{7,6},{8,9},{9,8},{10,11... | collective-permute-start | bytes 6291464 | tf_op jit(solution)/shard_map/ppermute | solution.py:30
  17.0 52.7 %all-to-all-start = ((bf16[16,64,512]{2,1,0:T(8,128)(2,1)}), bf16[16,64,512]{2,1,0:T(8,128)(2,1)S(1)}, u32[]{:S(2)}, u32[]{:S(2)}) async-start(bf16[16,64,512]{2,1,0:T(8,128)(2,1)} %shard_map.59), calls=%async_computation | async-start | bytes 2097152 | tf_op jit(solution)/shard_map/all_to_all | solution.py:164
  34.0 17.9 %collective-permute-start.5 = (bf16[256,1024]{1,0:T(8,128)(2,1)}, bf16[256,1024]{1,0:T(8,128)(2,1)}, u32[]{:S(2)}, u32[]{:S(2)}) collective-permute-start(bf16[256,1024]{1,0:T(8,128)(2,1)} %get-tuple-element.23), channel_id=1, source_target_pairs={{0,4},{1,5},{2,6},{3,7},{4,8},{5,9},{6,10},{7,11},{8,12},{9,13},{1... | collective-permute-start | bytes 1572872 | tf_op jit(solution)/shard_map/ppermute | solution.py:30
  35.9 26.7 %collective-permute-start.6 = (bf16[256,1024]{1,0:T(8,128)(2,1)}, bf16[256,1024]{1,0:T(8,128)(2,1)}, u32[]{:S(2)}, u32[]{:S(2)}) collective-permute-start(bf16[256,1024]{1,0:T(8,128)(2,1)} %get-tuple-element.24), channel_id=1, source_target_pairs={{0,8},{1,9},{2,10},{3,11},{4,12},{5,13},{6,14},{7,15},{8,0},{9,1},... | collective-permute-start | bytes 1572872 | tf_op jit(solution)/shard_map/ppermute | solution.py:30
  38.6 26.7 %collective-permute-start.7 = (bf16[256,1024]{1,0:T(8,128)(2,1)}, bf16[256,1024]{1,0:T(8,128)(2,1)}, u32[]{:S(2)}, u32[]{:S(2)}) collective-permute-start(bf16[256,1024]{1,0:T(8,128)(2,1)} %get-tuple-element.25), channel_id=1, source_target_pairs={{0,12},{1,13},{2,14},{3,15},{4,0},{5,1},{6,2},{7,3},{8,4},{9,5},{1... | collective-permute-start | bytes 1572872 | tf_op jit(solution)/shard_map/ppermute | solution.py:30
  40.0 43.0 %collective-permute-start.11 = (bf16[256,1024]{1,0:T(8,128)(2,1)}, bf16[256,1024]{1,0:T(8,128)(2,1)}, u32[]{:S(2)}, u32[]{:S(2)}) collective-permute-start(bf16[256,1024]{1,0:T(8,128)(2,1)} %get-tuple-element.27), channel_id=1, source_target_pairs={{0,16},{1,17},{2,18},{3,19},{4,20},{5,21},{6,22},{7,23},{8,24},{9,... | collective-permute-start | bytes 1572872 | tf_op jit(solution)/shard_map/ppermute | solution.py:30
  51.9 31.9 %collective-permute-start.12 = (bf16[256,1024]{1,0:T(8,128)(2,1)}, bf16[256,1024]{1,0:T(8,128)(2,1)}, u32[]{:S(2)}, u32[]{:S(2)}) collective-permute-start(bf16[256,1024]{1,0:T(8,128)(2,1)} %get-tuple-element.28), channel_id=1, source_target_pairs={{0,32},{1,33},{2,34},{3,35},{4,36},{5,37},{6,38},{7,39},{8,40},{9,... | collective-permute-start | bytes 1572872 | tf_op jit(solution)/shard_map/ppermute | solution.py:30
  62.6 22.5 %collective-permute-start.13 = (bf16[256,1024]{1,0:T(8,128)(2,1)}, bf16[256,1024]{1,0:T(8,128)(2,1)}, u32[]{:S(2)}, u32[]{:S(2)}) collective-permute-start(bf16[256,1024]{1,0:T(8,128)(2,1)} %get-tuple-element.29), channel_id=1, source_target_pairs={{0,48},{1,49},{2,50},{3,51},{4,52},{5,53},{6,54},{7,55},{8,56},{9,... | collective-permute-start | bytes 1572872 | tf_op jit(solution)/shard_map/ppermute | solution.py:30
  67.7 19.0 %collective-permute-start.10 = (bf16[64,1024]{1,0:T(8,128)(2,1)S(1)}, bf16[64,1024]{1,0:T(8,128)(2,1)S(1)}, u32[]{:S(2)}, u32[]{:S(2)}) collective-permute-start(bf16[64,1024]{1,0:T(8,128)(2,1)S(1)} %get-tuple-element.39), channel_id=1, source_target_pairs={{0,48},{1,49},{2,50},{3,51},{4,52},{5,53},{6,54},{7,55},{8,56},{9,... | collective-permute-start | bytes 393224 | tf_op jit(solution)/shard_map/ppermute | solution.py:30
  68.5 1.4 copy-start.1
  68.5 21.9 %collective-permute-start.8 = (bf16[64,1024]{1,0:T(8,128)(2,1)}, bf16[64,1024]{1,0:T(8,128)(2,1)S(1)}, u32[]{:S(2)}, u32[]{:S(2)}) collective-permute-start(bf16[64,1024]{1,0:T(8,128)(2,1)} %get-tuple-element.38), channel_id=1, source_target_pairs={{0,16},{1,17},{2,18},{3,19},{4,20},{5,21},{6,22},{7,23},{8,24},{9,... | collective-permute-start | bytes 393224 | tf_op jit(solution)/shard_map/ppermute | solution.py:30
  73.9 11.2 %copy-start.8 = (bf16[256,1024]{1,0:T(8,128)(2,1)S(1)}, bf16[256,1024]{1,0:T(8,128)(2,1)}, u32[]{:S(2)}) copy-start(bf16[256,1024]{1,0:T(8,128)(2,1)} %get-tuple-element.26) | copy-start | bytes 1572868
  73.9 16.5 %copy-start.6 = (f32[256,256]{1,0:T(8,128)S(1)}, f32[256,256]{1,0:T(8,128)}, u32[]{:S(2)}) copy-start(f32[256,256]{1,0:T(8,128)} %shard_map.62) | copy-start | bytes 786436
  83.0 9.3 %collective-permute-start.9 = (bf16[64,1024]{1,0:T(8,128)(2,1)}, bf16[64,1024]{1,0:T(8,128)(2,1)S(1)}, u32[]{:S(2)}, u32[]{:S(2)}) collective-permute-start(bf16[64,1024]{1,0:T(8,128)(2,1)} %get-tuple-element.40), channel_id=1, source_target_pairs={{0,32},{1,33},{2,34},{3,35},{4,36},{5,37},{6,38},{7,39},{8,40},{9,... | collective-permute-start | bytes 393224 | tf_op jit(solution)/shard_map/ppermute | solution.py:30
  83.9 28.7 %collective-permute-start.18 = (bf16[256,1024]{1,0:T(8,128)(2,1)}, bf16[256,1024]{1,0:T(8,128)(2,1)S(1)}, u32[]{:S(2)}, u32[]{:S(2)}) collective-permute-start(bf16[256,1024]{1,0:T(8,128)(2,1)} %get-tuple-element.31), channel_id=1, source_target_pairs={{0,4},{1,5},{2,6},{3,7},{4,8},{5,9},{6,10},{7,11},{8,12},{9,13},{1... | collective-permute-start | bytes 1572872 | tf_op jit(solution)/shard_map/ppermute | solution.py:30
  85.1 4.3 %collective-permute-start.2 = (f32[2,64,256]{2,1,0:T(8,128)S(1)}, f32[2,64,256]{2,1,0:T(8,128)S(1)}, u32[]{:S(2)}, u32[]{:S(2)}) collective-permute-start(f32[2,64,256]{2,1,0:T(8,128)S(1)} %dynamic-slice_bitcast_fusion), channel_id=1, source_target_pairs={{0,2},{1,3},{2,0},{3,1},{4,6},{5,7},{6,4},{7,5},{8,10},{9,11},{10,... | collective-permute-start | bytes 393224 | tf_op jit(solution)/shard_map/ppermute | solution.py:30
  86.7 13.8 %collective-permute-start.14 = (bf16[64,1024]{1,0:T(8,128)(2,1)S(1)}, bf16[64,1024]{1,0:T(8,128)(2,1)S(1)}, u32[]{:S(2)}, u32[]{:S(2)}) collective-permute-start(bf16[64,1024]{1,0:T(8,128)(2,1)S(1)} %get-tuple-element.41), channel_id=1, source_target_pairs={{0,4},{1,5},{2,6},{3,7},{4,8},{5,9},{6,10},{7,11},{8,12},{9,13},{1... | collective-permute-start | bytes 393224 | tf_op jit(solution)/shard_map/ppermute | solution.py:30
  89.4 16.9 %collective-permute-start.15 = (bf16[64,1024]{1,0:T(8,128)(2,1)S(1)}, bf16[64,1024]{1,0:T(8,128)(2,1)S(1)}, u32[]{:S(2)}, u32[]{:S(2)}) collective-permute-start(bf16[64,1024]{1,0:T(8,128)(2,1)S(1)} %get-tuple-element.43), channel_id=1, source_target_pairs={{0,8},{1,9},{2,10},{3,11},{4,12},{5,13},{6,14},{7,15},{8,0},{9,1},... | collective-permute-start | bytes 393224 | tf_op jit(solution)/shard_map/ppermute | solution.py:30
  90.5 17.7 %collective-permute-start.16 = (bf16[64,1024]{1,0:T(8,128)(2,1)S(1)}, bf16[64,1024]{1,0:T(8,128)(2,1)S(1)}, u32[]{:S(2)}, u32[]{:S(2)}) collective-permute-start(bf16[64,1024]{1,0:T(8,128)(2,1)S(1)} %get-tuple-element.42), channel_id=1, source_target_pairs={{0,12},{1,13},{2,14},{3,15},{4,0},{5,1},{6,2},{7,3},{8,4},{9,5},{1... | collective-permute-start | bytes 393224 | tf_op jit(solution)/shard_map/ppermute | solution.py:30
  92.3 38.4 %collective-permute-start.19 = (bf16[256,1024]{1,0:T(8,128)(2,1)}, bf16[256,1024]{1,0:T(8,128)(2,1)}, u32[]{:S(2)}, u32[]{:S(2)}) collective-permute-start(bf16[256,1024]{1,0:T(8,128)(2,1)} %get-tuple-element.32), channel_id=1, source_target_pairs={{0,8},{1,9},{2,10},{3,11},{4,12},{5,13},{6,14},{7,15},{8,0},{9,1},... | collective-permute-start | bytes 1572872 | tf_op jit(solution)/shard_map/ppermute | solution.py:30
  100.5 30.2 %collective-permute-start.20 = (bf16[256,1024]{1,0:T(8,128)(2,1)}, bf16[256,1024]{1,0:T(8,128)(2,1)}, u32[]{:S(2)}, u32[]{:S(2)}) collective-permute-start(bf16[256,1024]{1,0:T(8,128)(2,1)} %get-tuple-element.33), channel_id=1, source_target_pairs={{0,12},{1,13},{2,14},{3,15},{4,0},{5,1},{6,2},{7,3},{8,4},{9,5},{1... | collective-permute-start | bytes 1572872 | tf_op jit(solution)/shard_map/ppermute | solution.py:30
  106.3 7.8 %copy-start.11 = (bf16[64,1024]{1,0:T(8,128)(2,1)}, bf16[64,1024]{1,0:T(8,128)(2,1)S(1)}, u32[]{:S(2)}) copy-start(bf16[64,1024]{1,0:T(8,128)(2,1)S(1)} %collective-permute-done.15) | copy-start | bytes 393220
  106.3 5.0 %collective-permute-start.3 = (f32[2,64,256]{2,1,0:T(8,128)S(1)}, f32[2,64,256]{2,1,0:T(8,128)S(1)}, u32[]{:S(2)}, u32[]{:S(2)}) collective-permute-start(f32[2,64,256]{2,1,0:T(8,128)S(1)} %bitcast_add_fusion), channel_id=1, source_target_pairs={{0,64},{1,65},{2,66},{3,67},{4,68},{5,69},{6,70},{7,71},{8,72},{9,... | collective-permute-start | bytes 393224 | tf_op jit(solution)/shard_map/ppermute | solution.py:30
  108.2 5.8 %copy-start.13 = (bf16[64,1024]{1,0:T(8,128)(2,1)}, bf16[64,1024]{1,0:T(8,128)(2,1)S(1)}, u32[]{:S(2)}) copy-start(bf16[64,1024]{1,0:T(8,128)(2,1)S(1)} %collective-permute-done.16) | copy-start | bytes 393220
  108.2 35.4 %collective-permute-start.24 = (bf16[256,1024]{1,0:T(8,128)(2,1)}, bf16[256,1024]{1,0:T(8,128)(2,1)}, u32[]{:S(2)}, u32[]{:S(2)}) collective-permute-start(bf16[256,1024]{1,0:T(8,128)(2,1)} %get-tuple-element.35), channel_id=1, source_target_pairs={{0,16},{1,17},{2,18},{3,19},{4,20},{5,21},{6,22},{7,23},{8,24},{9,... | collective-permute-start | bytes 1572872 | tf_op jit(solution)/shard_map/ppermute | solution.py:30
  111.3 32.4 %collective-permute-start.25 = (bf16[256,1024]{1,0:T(8,128)(2,1)}, bf16[256,1024]{1,0:T(8,128)(2,1)}, u32[]{:S(2)}, u32[]{:S(2)}) collective-permute-start(bf16[256,1024]{1,0:T(8,128)(2,1)} %get-tuple-element.36), channel_id=1, source_target_pairs={{0,32},{1,33},{2,34},{3,35},{4,36},{5,37},{6,38},{7,39},{8,40},{9,... | collective-permute-start | bytes 1572872 | tf_op jit(solution)/shard_map/ppermute | solution.py:30
  112.6 32.1 %collective-permute-start.26 = (bf16[256,1024]{1,0:T(8,128)(2,1)}, bf16[256,1024]{1,0:T(8,128)(2,1)}, u32[]{:S(2)}, u32[]{:S(2)}) collective-permute-start(bf16[256,1024]{1,0:T(8,128)(2,1)} %get-tuple-element.37), channel_id=1, source_target_pairs={{0,48},{1,49},{2,50},{3,51},{4,52},{5,53},{6,54},{7,55},{8,56},{9,... | collective-permute-start | bytes 1572872 | tf_op jit(solution)/shard_map/ppermute | solution.py:30
  114.1 15.4 %copy-start.12 = (bf16[64,1024]{1,0:T(8,128)(2,1)S(1)}, bf16[64,1024]{1,0:T(8,128)(2,1)}, u32[]{:S(2)}) copy-start(bf16[64,1024]{1,0:T(8,128)(2,1)} %copy-done.11) | copy-start | bytes 393220
  114.1 15.4 %copy-start.14 = (bf16[64,1024]{1,0:T(8,128)(2,1)S(1)}, bf16[64,1024]{1,0:T(8,128)(2,1)}, u32[]{:S(2)}) copy-start(bf16[64,1024]{1,0:T(8,128)(2,1)} %copy-done.13) | copy-start | bytes 393220
  114.1 16.6 %copy-start.10 = (bf16[256,1024]{1,0:T(8,128)(2,1)S(1)}, bf16[256,1024]{1,0:T(8,128)(2,1)}, u32[]{:S(2)}) copy-start(bf16[256,1024]{1,0:T(8,128)(2,1)} %get-tuple-element.30) | copy-start | bytes 1572868
  115.2 35.4 %all-to-all-start.1 = ((bf16[16,2,64,256]{3,2,1,0:T(8,128)(2,1)}), bf16[16,2,64,256]{3,2,1,0:T(8,128)(2,1)S(1)}, u32[]{:S(2)}, u32[]{:S(2)}) async-start(bf16[16,2,64,256]{3,2,1,0:T(8,128)(2,1)} %broadcast_in_dim.2), calls=%async_computation.1 | async-start | bytes 2097152 | tf_op jit(solution)/shard_map/all_to_all | solution.py:177
  129.5 15.2 %copy-start.9 = (bf16[256,1024]{1,0:T(8,128)(2,1)S(1)}, bf16[256,1024]{1,0:T(8,128)(2,1)}, u32[]{:S(2)}) copy-start(bf16[256,1024]{1,0:T(8,128)(2,1)} %get-tuple-element.34) | copy-start | bytes 1572868
  133.1 17.5 %collective-permute-start.21 = (bf16[64,1024]{1,0:T(8,128)(2,1)S(1)}, bf16[64,1024]{1,0:T(8,128)(2,1)S(1)}, u32[]{:S(2)}, u32[]{:S(2)}) collective-permute-start(bf16[64,1024]{1,0:T(8,128)(2,1)S(1)} %get-tuple-element.46), channel_id=1, source_target_pairs={{0,16},{1,17},{2,18},{3,19},{4,20},{5,21},{6,22},{7,23},{8,24},{9,... | collective-permute-start | bytes 393224 | tf_op jit(solution)/shard_map/ppermute | solution.py:30
  135.1 21.4 %collective-permute-start.22 = (bf16[64,1024]{1,0:T(8,128)(2,1)}, bf16[64,1024]{1,0:T(8,128)(2,1)S(1)}, u32[]{:S(2)}, u32[]{:S(2)}) collective-permute-start(bf16[64,1024]{1,0:T(8,128)(2,1)} %get-tuple-element.45), channel_id=1, source_target_pairs={{0,32},{1,33},{2,34},{3,35},{4,36},{5,37},{6,38},{7,39},{8,40},{9,... | collective-permute-start | bytes 393224 | tf_op jit(solution)/shard_map/ppermute | solution.py:30
  143.7 14.3 %collective-permute-start.23 = (bf16[64,1024]{1,0:T(8,128)(2,1)S(1)}, bf16[64,1024]{1,0:T(8,128)(2,1)S(1)}, u32[]{:S(2)}, u32[]{:S(2)}) collective-permute-start(bf16[64,1024]{1,0:T(8,128)(2,1)S(1)} %get-tuple-element.44), channel_id=1, source_target_pairs={{0,48},{1,49},{2,50},{3,51},{4,52},{5,53},{6,54},{7,55},{8,56},{9,... | collective-permute-start | bytes 393224 | tf_op jit(solution)/shard_map/ppermute | solution.py:30
  147.2 13.3 %collective-permute-start.27 = (bf16[64,1024]{1,0:T(8,128)(2,1)}, bf16[64,1024]{1,0:T(8,128)(2,1)S(1)}, u32[]{:S(2)}, u32[]{:S(2)}) collective-permute-start(bf16[64,1024]{1,0:T(8,128)(2,1)} %get-tuple-element.50), channel_id=1, source_target_pairs={{0,4},{1,5},{2,6},{3,7},{4,8},{5,9},{6,10},{7,11},{8,12},{9,13},{1... | collective-permute-start | bytes 393224 | tf_op jit(solution)/shard_map/ppermute | solution.py:30
  147.3 13.3 %collective-permute-start.28 = (bf16[64,1024]{1,0:T(8,128)(2,1)}, bf16[64,1024]{1,0:T(8,128)(2,1)S(1)}, u32[]{:S(2)}, u32[]{:S(2)}) collective-permute-start(bf16[64,1024]{1,0:T(8,128)(2,1)} %get-tuple-element.49), channel_id=1, source_target_pairs={{0,8},{1,9},{2,10},{3,11},{4,12},{5,13},{6,14},{7,15},{8,0},{9,1},... | collective-permute-start | bytes 393224 | tf_op jit(solution)/shard_map/ppermute | solution.py:30
  150.6 5.9 %copy-start.15 = (bf16[64,1024]{1,0:T(8,128)(2,1)}, bf16[64,1024]{1,0:T(8,128)(2,1)S(1)}, u32[]{:S(2)}) copy-start(bf16[64,1024]{1,0:T(8,128)(2,1)S(1)} %collective-permute-done.21.g1_ref) | copy-start | bytes 393220
  150.6 9.9 %collective-permute-start.29 = (bf16[64,1024]{1,0:T(8,128)(2,1)}, bf16[64,1024]{1,0:T(8,128)(2,1)S(1)}, u32[]{:S(2)}, u32[]{:S(2)}) collective-permute-start(bf16[64,1024]{1,0:T(8,128)(2,1)} %get-tuple-element.48), channel_id=1, source_target_pairs={{0,12},{1,13},{2,14},{3,15},{4,0},{5,1},{6,2},{7,3},{8,4},{9,5},{1... | collective-permute-start | bytes 393224 | tf_op jit(solution)/shard_map/ppermute | solution.py:30
  156.5 16.2 %copy-start.7 = (f32[64,2048]{1,0:T(8,128)S(1)}, f32[64,2048]{1,0:T(8,128)}, u32[]{:S(2)}) copy-start(f32[64,2048]{1,0:T(8,128)} %param.5) | copy-start | bytes 1572868
  156.5 1.5 copy-start.16
  156.5 12.4 %collective-permute-start.17 = (bf16[64,2048]{1,0:T(8,128)(2,1)S(1)}, bf16[64,2048]{1,0:T(8,128)(2,1)S(1)}, u32[]{:S(2)}, u32[]{:S(2)}) collective-permute-start(bf16[64,2048]{1,0:T(8,128)(2,1)S(1)} %fusion.1), channel_id=1, source_target_pairs={{1,65},{3,67},{5,69},{7,71},{9,73},{11,75},{13,77},{15,79},{17,81}... | collective-permute-start | bytes 786440 | tf_op jit(solution)/shard_map/ppermute | solution.py:30
  160.5 12.2 %copy-start.5 = (f32[64,1024]{1,0:T(8,128)S(1)}, f32[64,1024]{1,0:T(8,128)}, u32[]{:S(2)}) copy-start(f32[64,1024]{1,0:T(8,128)} %shard_map.65) | copy-start | bytes 786436
  161.2 13.3 %copy-start.2 = (f32[512,256]{1,0:T(8,128)S(1)}, f32[512,256]{1,0:T(8,128)}, u32[]{:S(2)}) copy-start(f32[512,256]{1,0:T(8,128)} %get-tuple-element.21.after_ref) | copy-start | bytes 1572868
  164.3 8.4 %collective-permute-start.30 = (bf16[64,2048]{1,0:T(8,128)(2,1)S(1)}, bf16[64,2048]{1,0:T(8,128)(2,1)S(1)}, u32[]{:S(2)}, u32[]{:S(2)}) collective-permute-start(bf16[64,2048]{1,0:T(8,128)(2,1)S(1)} %fusion), channel_id=1, source_target_pairs={{0,64},{2,66},{4,68},{6,70},{8,72},{10,74},{12,76},{14,78},{16,80}... | collective-permute-start | bytes 786440 | tf_op jit(solution)/shard_map/ppermute | solution.py:30
  168.8 5.8 %collective-permute-start.4 = (f32[512,256]{1,0:T(8,128)}, f32[512,256]{1,0:T(8,128)S(1)}, u32[]{:S(2)}, u32[]{:S(2)}) collective-permute-start(f32[512,256]{1,0:T(8,128)} %get-tuple-element.22), channel_id=1, source_target_pairs={{0,2},{1,3},{2,0},{3,1},{4,6},{5,7},{6,4},{7,5},{8,10},{9,11},{10,... | collective-permute-start | bytes 1572872 | tf_op jit(solution)/shard_map/ppermute | solution.py:30
  (6 other events, 4.7 us)

commit v6 on v5

--- a/solution.py
+++ b/solution.py
@@ -63,24 +63,36 @@
     )
 
 
-def pick_kernel(at_ref, gt_ref, sib_ref, out_ref):
-    for i, ref in enumerate((gt_ref, sib_ref)):
-        for b in range(16):
-            start = pl.ds(pl.multiple_of(b * 128 + at_ref[2], 64), 64)
-            out_ref[(16 * i + b) * 64 : (16 * i + b + 1) * 64, :] = ref[start, :]
-
-
-def gram_kernel(at_ref, a_ref, b1_ref, b2_ref, after_ref, *outs):
+def own_kernel(a1_ref, a2_ref, b1_ref, b2_ref, after_ref, out_ref):
+    rows = out_ref.shape[1]
+    wide = 2 * rows
+    for g in range(4):
+        left1 = a1_ref[4 * g * rows : 4 * (g + 1) * rows, :]
+        left2 = a2_ref[4 * g * rows : 4 * (g + 1) * rows, :]
+        for q in range(3):
+            cols = pl.ds((g + q) % 4 * 4 * wide, 4 * wide)
+            acc = lax.dot_general(left1, b1_ref[cols, :], NT, preferred_element_type=f32)
+            acc += lax.dot_general(left2, b2_ref[cols, :], NT, preferred_element_type=f32)
+            acc = acc.astype(bf16)
+            for i in range(4):
+                lo, hi = max(4 * q, i), min(4 * q + 4, i + 9)
+                if lo < hi:
+                    piece = acc[i * rows : (i + 1) * rows, (lo - 4 * q) * wide : (hi - 4 * q) * wide]
+                    out_ref[4 * g + i, :, (lo - i) * wide : (hi - i) * wide] = piece
+
+
+def gram_kernel(at_ref, a1_ref, a2_ref, b1_ref, b2_ref, after_ref, also_ref, *outs):
     z, x = at_ref[0], at_ref[1]
-    rows, m, n, tile = 64, a_ref.shape[0] // 2, b1_ref.shape[0] // 2, 256
+    rows, n, tile = 64, b1_ref.shape[0] // 2, 256
     for half in range(2):
         left1, left2 = [], []
         for k in range(4):
             for j in range(4):
                 dx, dz = (k, j) if half == 0 else (j, k)
                 block = (lax.rem(z + dz, 4) * 4 + lax.rem(x + dx, 4)) * rows
-                left1.append(a_ref[pl.ds(pl.multiple_of(block, rows), rows), :])
-                left2.append(a_ref[pl.ds(pl.multiple_of(block + m, rows), rows), :])
+                start = pl.ds(pl.multiple_of(block, rows), rows)
+                left1.append(a1_ref[start, :])
+                left2.append(a2_ref[start, :])
         left1, left2 = jnp.concatenate(left1), jnp.concatenate(left2)
         for t in range(n // tile):
             cols = pl.ds(half * n + t * tile, tile)
@@ -91,36 +103,44 @@
                 outs[4 * half + k][:, t * tile : (t + 1) * tile] = part
 
 
-def gram(at, a, b1, b2, after):
+def gram(at, a1, a2, b1, b2, after, also):
     n = b1.shape[0]
     return kernel_call(
         gram_kernel,
         [jax.ShapeDtypeStruct((256, n // 2), bf16)] * 8,
-        [SMEM] + [VMEM] * 3 + [ANY],
-        at, a, b1, b2, after,
-        flops=2 * a.shape[0] * n * b1.shape[1],
-    )
-
-
-def scores_kernel(at_ref, pt_ref, own_ref, cross_ref, keep_ref, give_ref):
+        [SMEM] + [VMEM] * 4 + [ANY] * 2,
+        at, a1, a2, b1, b2, after, also,
+        flops=4 * a1.shape[0] * n * b1.shape[1],
+    )
+
+
+def scores_kernel(at_ref, pt_ref, own1_ref, own2_ref, cross1_ref, cross2_ref, keep_ref, give_ref):
     h = at_ref[3]
-    m = own_ref.shape[0] // 2
+    m = own1_ref.shape[0]
     p_own = pt_ref[:, pl.ds(h, 1), :, :].reshape(m, pt_ref.shape[-1])
     p_cross = pt_ref[:, pl.ds(1 - h, 1), :, :].reshape(m, pt_ref.shape[-1])
-    for side, out_ref in enumerate((keep_ref, give_ref)):
-        s = slice(side * m, (side + 1) * m)
-        acc = lax.dot_general(own_ref[s, :], p_own, TN, preferred_element_type=f32)
-        out_ref[...] = acc + lax.dot_general(cross_ref[s, :], p_cross, TN, preferred_element_type=f32)
+    for own, cross, out_ref in ((own1_ref, cross1_ref, keep_ref), (own2_ref, cross2_ref, give_ref)):
+        acc = lax.dot_general(own[...], p_own, TN, preferred_element_type=f32)
+        out_ref[...] = acc + lax.dot_general(cross[...], p_cross, TN, preferred_element_type=f32)
+
+
+def spread_kernel(in_ref, *refs):
+    refs[-1][...] = jnp.broadcast_to(in_ref[...][None], refs[-1].shape)
 
 
 def sum_kernel(mine_ref, g1_ref, g2_ref, g3_ref, after_ref, out_ref):
     out_ref[...] = mine_ref[...] + g1_ref[...].astype(f32) + g2_ref[...].astype(f32) + g3_ref[...].astype(f32)
 
 
-def scatter_sum(parts, rows, after=None):
-    got, mids, sums = [], [], []
+def first_stage(parts):
+    got = []
     for half, axis in ((0, "x"), (1, "z")):
         got.append([send(parts[4 * half + k], along(axis, k)) for k in (1, 2, 3)])
+    return got
+
+
+def second_stage(parts, got, rows, after):
+    mids, sums = [], []
     for half in range(2):
         mids.append([])
         for j in range(4):
@@ -131,12 +151,34 @@
             mids[half].append(total)
     for half, axis in ((0, "z"), (1, "x")):
         rs = [send(mids[half][k].astype(bf16), along(axis, k)) for k in (1, 2, 3)]
-        if after is not None:
-            out = jax.ShapeDtypeStruct(mids[half][0].shape, f32)
-            sums.append(kernel_call(sum_kernel, [out], [VMEM] * 4 + [ANY], mids[half][0], *rs, after)[0])
-        else:
-            sums.append(mids[half][0] + rs[0].astype(f32) + rs[1].astype(f32) + rs[2].astype(f32))
+        out = jax.ShapeDtypeStruct(mids[half][0].shape, f32)
+        sums.append(kernel_call(sum_kernel, [out], [VMEM] * 4 + [ANY], mids[half][0], *rs, after[half])[0])
     return jnp.concatenate(sums, axis=1)
+
+
+def own_sum_kernel(at_ref, got_ref, direct_ref, mirror_ref):
+    chip = at_ref[0] * 4 + at_ref[1]
+    wide = mirror_ref.shape[2]
+    direct_ref[...] = jnp.zeros_like(direct_ref)
+    mirror_ref[...] = jnp.zeros_like(mirror_ref)
+    for k in range(9):
+        total = jnp.sum(got_ref[:, :, k * wide : (k + 1) * wide].astype(f32), axis=0)
+        to = lax.rem(chip + k, 16)
+        direct_ref[:, pl.ds(pl.multiple_of(to * wide, wide), wide)] = total
+        mirror_ref[pl.ds(to, 1)] = total.astype(bf16)[None]
+
+
+def join_kernel(at_ref, direct_ref, held_ref, given_ref, out_ref):
+    chip = at_ref[0] * 4 + at_ref[1]
+    low = at_ref[2] == 0
+    rows = held_ref.shape[0]
+    for j in range(16):
+        mine = held_ref[:, j * rows : (j + 1) * rows].astype(f32)
+        other = given_ref[:, j * rows : (j + 1) * rows].astype(f32)
+        both = jnp.concatenate([jnp.where(low, mine, other), jnp.where(low, other, mine)], axis=1)
+        cols = slice(2 * j * rows, 2 * (j + 1) * rows)
+        near = lax.rem(j - chip + 16, 16) <= 8
+        out_ref[:, cols] = jnp.where(near, direct_ref[:, cols], both)
 
 
 def on_device(grads, covariance, test_grads, inverse_factor):
@@ -150,10 +192,18 @@
     gt = grads.T
     sib = send(gt, flip("c"))
 
-    (picked,) = kernel_call(pick_kernel, [shape((feats, tokens), bf16)], [SMEM, VMEM, VMEM], at, gt, sib)
-    arrived = send(picked, flip("yh"))
-    own = gram(at, picked, gt, sib, picked)
-    cross = gram(at, arrived, gt, sib, own[0])
+    pick = lambda v: lax.dynamic_index_in_dim(v.reshape(16, 2, rows, tokens), c, 1, keepdims=False)
+    mine = pick(gt).reshape(feats // 2, tokens)
+    far1 = send(mine, flip("yh"))
+    sib_mine = pick(sib).reshape(feats // 2, tokens)
+    far2 = send(sib_mine, flip("yh"))
+    (own,) = kernel_call(
+        own_kernel,
+        [shape((16, rows, 18 * rows), bf16)],
+        [VMEM] * 4 + [ANY],
+        mine, sib_mine, gt, sib, far1,
+        flops=3 * 16 * rows * feats * tokens,
+    )
 
     (slots,) = kernel_call(
         slots_kernel,
@@ -166,31 +216,48 @@
         functools.partial(factor_kernel, 4 * rows),
         [shape((4 * rows, tests), f32)],
         [VMEM, ANY, ANY],
-        slots.reshape(16 * rows, -1), own[0], arrived,
+        slots.reshape(16 * rows, -1), own, far1,
         flops=2 * 16 * rows * 4 * rows * tests,
     )
     pt = pt.reshape(2, 2, rows, tests)
     half = lambda i: lax.dynamic_index_in_dim(pt, i, 1, keepdims=False)
     pt = half(c) + send(half(1 - c), flip("c"))
     pt = (pt + send(pt, flip("yl"))).astype(bf16)
-    pt = jnp.broadcast_to(pt[None], (16,) + pt.shape)
+    own = lax.all_to_all(own, ("z", "x"), split_axis=0, concat_axis=0, tiled=True)
+    direct, mirror = kernel_call(
+        own_sum_kernel,
+        [shape((rows, feats), f32), shape((16, rows, 2 * rows), bf16)],
+        [SMEM, VMEM],
+        at, own,
+    )
+    mirror = lax.all_to_all(mirror, ("z", "x"), split_axis=0, concat_axis=0, tiled=True)
+    cross = gram(at, far1, far2, gt, sib, pt, direct)
+    crossed = first_stage(cross)
+    (pt,) = kernel_call(
+        spread_kernel, [shape((16,) + pt.shape, bf16)], [VMEM] + [ANY] * 4, pt, *crossed[0][:2], *crossed[1][:2]
+    )
     pt = lax.all_to_all(pt, ("z", "x"), split_axis=0, concat_axis=0, tiled=True)
 
     keep, give = kernel_call(
         scores_kernel,
         [shape((tokens, tests), f32)] * 2,
-        [SMEM] + [VMEM] * 3,
-        at, pt, picked, arrived,
+        [SMEM] + [VMEM] * 5,
+        at, pt, mine, sib_mine, far1, far2,
         flops=8 * 16 * rows * tokens * tests,
     )
     scores = keep + send(give, flip("c"))
 
-    own = scatter_sum(own, rows)
-    own = own + send(own.astype(bf16), flip("yl"), lambda at: at["yl"] != at["yh"]).astype(f32)
-    cross = scatter_sum(cross, rows, keep)
-    cross = cross + send(cross.astype(bf16), flip("yl"), lambda at: at["yl"] == at["yh"]).astype(f32)
-    examples = tokens * 64
-    covariance_out = 0.9 * covariance + jnp.where(yl == h, own, cross) / examples
+    mirror = mirror.reshape(16 * rows, 2 * rows).T
+    held = lax.dynamic_slice_in_dim(mirror, c * rows, rows, 0)
+    given = send(lax.dynamic_slice_in_dim(mirror, (1 - c) * rows, rows, 0), flip("c"))
+    (own,) = kernel_call(
+        join_kernel, [shape((rows, feats), f32)], [SMEM] + [VMEM] * 3, at, direct, held, given
+    )
+
+    cross = second_stage(cross, crossed, rows, (keep, own))
+    ours, theirs = jnp.where(yl == h, own, cross), jnp.where(yl == h, cross, own)
+    term = ours + send(theirs.astype(bf16), flip("yl")).astype(f32)
+    covariance_out = 0.9 * covariance + term / (tokens * 64)
     return scores, covariance_out
 
 

time: 178 us -> 189 us (1.062)
  waiting for transfers between devices: 44.6 us -> 73 us
  starting transfers between devices: 70.5 us -> 51.8 us
  local copies, waits for them, and re-layouts: 8.29 us -> 14.4 us
  other arithmetic: 16.1 us -> 11.4 us
    ppermute x31 -> x20, waiting for transfers between devices: 44.6 us -> 68.8 us  [send(): return lax.ppermute(value, AXES, pairs)]
    ppermute x31 -> x20, starting transfers between devices: 48.4 us -> 26.7 us  [send(): return lax.ppermute(value, AXES, pairs)]
    all_to_all x0 -> x2, starting transfers between devices: none -> 12.7 us  [the longest x1 8.06 us: on_device(): lax.all_to_all(own, ('z', 'x'), split_axis=0, concat_axis=0, tiled=True)]
    all_to_all x1, starting transfers between devices: 14.2 us -> 4.49 us  [on_device(): pt = lax.all_to_all(pt, ('z', 'x'), split_axis=0, concat_axis=0, tiled=True)]
    convert_element_type x6 -> x3, other arithmetic: 10 us -> 5.61 us  [the longest x2 4.55 us: second_stage(): rs = [send(mids[half][k].astype(bf16), along(axis, k)) for k in (1, 2, 3)]]
    all_to_all x0 -> x2, waiting for transfers between devices: none -> 4.25 us  [the longest x1 4.25 us: on_device(): lax.all_to_all(own, ('z', 'x'), split_axis=0, concat_axis=0, tiled=True)]
    unnamed x43 -> x57, local copies, waits for them, and re-layouts: 6.25 us -> 10 us
    add x3 -> x1, other arithmetic: 4.35 us -> 1.86 us  [on_device(): covariance_out = 0.9 * covariance + term / (tokens * 64)]
  transfers between devices with their start and end apart: 33 -> 24, of which waited for: 9 -> 8; matrix products, arithmetic and copies ran while one was open for 10% -> 9% of each run, Pallas kernels for 18% -> 14%
where the time goes in v6:
time: 189 us; the launch traced here: 188 us
  waiting for transfers between devices  73 us (39%)
  starting transfers between devices  51.8 us (27%)
  Pallas kernels  36.5 us (19%)
  local copies, waits for them, and re-layouts  14.4 us (8%)
  other arithmetic  11.4 us (6%)
    ppermute x20, waiting for transfers between devices, send(): return lax.ppermute(value, AXES, pairs)  68.8 us
    pallas_call x10, Pallas kernels, kernel_call(): pl.pallas_call(body, out_shape=outs, in_specs=specs, out_specs=[VMEM] * l...  36.5 us
    ppermute x20, starting transfers between devices, send(): return lax.ppermute(value, AXES, pairs)  26.7 us
    unnamed x57, local copies, waits for them, and re-layouts  10 us
    all_to_all x1, starting transfers between devices, on_device(): lax.all_to_all(own, ('z', 'x'), split_axis=0, concat_axis=0, tiled=True)  8.06 us
    all_to_all x1, starting transfers between devices, on_device(): lax.all_to_all(slots, ('z', 'x'), split_axis=0, concat_axis=0, tiled=True)  7.93 us
    all_to_all x1, starting transfers between devices, on_device(): lax.all_to_all(mirror, ('z', 'x'), split_axis=0, concat_axis=0, tiled=True)  4.63 us
    convert_element_type x2, other arithmetic, second_stage(): rs = [send(mids[half][k].astype(bf16), along(axis, k)) for k in (1, 2, 3)]  4.55 us
  transfers between devices with their start and end apart: 24, of which 8 were waited for; matrix products, arithmetic and copies ran while one was open for 9% of the time, Pallas kernels for 14%

profile of v6, /device:TPU:0, one launch (start us, length us, event | category | flops | bytes accessed | tf_op | source)
XLA Modules:
  0.0 187.9 jit_solution(856054334794787473)
XLA Ops:
  0.6 2.9 %copy.12 = bf16[512,2048]{0,1:T(8,128)(2,1)S(1)} copy(bf16[512,2048]{1,0:T(8,128)(2,1)} %param.4) | data formatting | bytes 4194304 | tf_op args[0]
  3.7 3.4 %collective-permute-start.1 = (bf16[1024,512]{1,0:T(8,128)(2,1)S(1)}, bf16[1024,512]{1,0:T(8,128)(2,1)}, u32[]{:S(2)}, u32[]{:S(2)}) collective-permute-start(bf16[1024,512]{1,0:T(8,128)(2,1)S(1)} %bitcast.32), channel_id=1, source_target_pairs={{0,1},{1,0},{2,3},{3,2},{4,5},{5,4},{6,7},{7,6},{8,9},{9,8},{10,11... | collective-permute-start | bytes 3145736 | tf_op jit(solution)/shard_map/ppermute | solution.py:30
  7.1 2.2 %shard_map.59 = bf16[16,64,512]{2,1,0:T(8,128)(2,1)} custom-call(bf16[64,4096]{1,0:T(8,128)(2,1)} %f_ref.1, bf16[64,256]{1,0:T(8,128)(2,1)} %bitcast.42), custom_call_target="tpu_custom_call" | custom-call | bytes 1605632 | tf_op jit(solution)/shard_map/pallas_call | solution.py:43
  9.2 7.9 %all-to-all-start = ((bf16[16,64,512]{2,1,0:T(8,128)(2,1)}), bf16[16,64,512]{2,1,0:T(8,128)(2,1)}, u32[]{:S(2)}, u32[]{:S(2)}) async-start(bf16[16,64,512]{2,1,0:T(8,128)(2,1)} %shard_map.59), calls=%async_computation | async-start | bytes 2097152 | tf_op jit(solution)/shard_map/all_to_all | solution.py:214
  17.2 2.3 %constant_dynamic-slice_fusion.2 = bf16[16,1,64,512]{3,2,1,0:T(8,128)(2,1)} fusion(bf16[16,2,64,512]{3,2,1,0:T(8,128)(2,1)} %bitcast.9, s32[]{:T(128)S(6)} %select_n.28), kind=kLoop, calls=%fused_computation.16 | loop fusion | bytes 2097156 | tf_op jit(solution)/shard_map/jit(dynamic_index_in_dim)/dynamic_slice | solution.py:195
  19.5 11.5 %collective-permute-done.1.after_ref.also_ref.a1_ref.cross1_ref = bf16[1024,512]{1,0:T(8,128)(2,1)} collective-permute-done((bf16[1024,512]{1,0:T(8,128)(2,1)S(1)}, bf16[1024,512]{1,0:T(8,128)(2,1)}, u32[]{:S(2)}, u32[]{:S(2)}) %collective-permute-start.1) | collective-permute-done | bytes 1048608 | tf_op jit(solution)/shard_map/ppermute | solution.py:30
  31.0 7.7 %shard_map.60.after_ref = bf16[16,64,1152]{2,1,0:T(8,128)(2,1)} custom-call(bf16[1024,512]{1,0:T(8,128)(2,1)} %bitcast.33, bf16[1024,512]{1,0:T(8,128)(2,1)} %bitcast.35, bf16[2048,512]{1,0:T(8,128)(2,1)} %bitcast.30, bf16[2048,512]{1,0:T(8,128)(2,1)} %collective-permute-done.b2_ref, bf16[1024,512]{1,0:T(8,128)(2,1)} %collective-permute-done.1.after_ref.also_ref.a1_ref.cross1_ref), custom_call_target="tpu_custom_call" | custom-call | flops 3221225472 | bytes 9699328 | tf_op jit(solution)/shard_map/pallas_call | solution.py:43
  38.7 8.1 %all-to-all-start.1 = ((bf16[16,64,1152]{2,1,0:T(8,128)(2,1)}), bf16[16,64,1152]{2,1,0:T(8,128)(2,1)S(1)}, u32[]{:S(2)}, u32[]{:S(2)}) async-start(bf16[16,64,1152]{2,1,0:T(8,128)(2,1)} %shard_map.60.after_ref), calls=%async_computation.1 | async-start | bytes 4718592 | tf_op jit(solution)/shard_map/all_to_all | solution.py:226
  46.8 3.3 %collective-permute-start.4 = (bf16[1024,512]{1,0:T(8,128)(2,1)S(1)}, bf16[1024,512]{1,0:T(8,128)(2,1)}, u32[]{:S(2)}, u32[]{:S(2)}) collective-permute-start(bf16[1024,512]{1,0:T(8,128)(2,1)S(1)} %bitcast.37), channel_id=1, source_target_pairs={{0,1},{1,0},{2,3},{3,2},{4,5},{5,4},{6,7},{7,6},{8,9},{9,8},{10,11... | collective-permute-start | bytes 3145736 | tf_op jit(solution)/shard_map/ppermute | solution.py:30
  50.1 2.3 %shard_map.61 = f32[256,256]{1,0:T(8,128)} custom-call(bf16[1024,512]{1,0:T(8,128)(2,1)} %bitcast.5.slots_ref, bf16[16,64,1152]{2,1,0:T(8,128)(2,1)} %shard_map.60.after_ref, bf16[1024,512]{1,0:T(8,128)(2,1)} %collective-permute-done.1.after_ref.also_ref.a1_ref.cross1_ref), custom_call_target="tpu_custom_call" | custom-call | flops 134217728 | bytes 4718592 | tf_op jit(solution)/shard_map/pallas_call | solution.py:43
  52.4 0.9 dynamic-slice_bitcast_fusion
  53.4 1.3 collective-permute-done.2
  54.7 0.9 bitcast_add_fusion
  56.9 19.2 %collective-permute-done.3 = f32[2,64,256]{2,1,0:T(8,128)} collective-permute-done((f32[2,64,256]{2,1,0:T(8,128)S(1)}, f32[2,64,256]{2,1,0:T(8,128)}, u32[]{:S(2)}, u32[]{:S(2)}) %collective-permute-start.3) | collective-permute-done | bytes 131104 | tf_op jit(solution)/shard_map/ppermute | solution.py:30
  76.1 1.6 add_convert_fusion.6.after_ref.in_ref
  77.7 4.3 %all-to-all-done.1.got_ref = bf16[16,64,1152]{2,1,0:T(8,128)(2,1)S(1)} async-done(((bf16[16,64,1152]{2,1,0:T(8,128)(2,1)}), bf16[16,64,1152]{2,1,0:T(8,128)(2,1)S(1)}, u32[]{:S(2)}, u32[]{:S(2)}) %all-to-all-start.1) | async-done | bytes 2359328 | tf_op jit(solution)/shard_map/all_to_all | solution.py:226
  81.9 1.4 copy-done
  83.3 2.9 %shard_map.62 = (f32[64,2048]{1,0:T(8,128)}, bf16[16,64,128]{2,1,0:T(8,128)(2,1)}) custom-call(s32[4]{0:T(128)} %pad_add_fusion.at_ref, bf16[16,64,1152]{2,1,0:T(8,128)(2,1)} %copy-done), custom_call_target="tpu_custom_call" | custom-call | bytes 3145744 | tf_op jit(solution)/shard_map/pallas_call | solution.py:43
  86.3 8.8 %shard_map.63 = (bf16[256,1024]{1,0:T(8,128)(2,1)}, bf16[256,1024]{1,0:T(8,128)(2,1)}, bf16[256,1024]{1,0:T(8,128)(2,1)}, bf16[256,1024]{1,0:T(8,128)(2,1)}, bf1...) custom-call(s32[4]{0:T(128)} %pad_add_fusion.at_ref, ...), custom_call_target="tpu_custom_call" | custom-call | flops 4294967296 | bytes 11075600 | tf_op jit(solution)/shard_map/pallas_call | solution.py:43
  95.1 1.2 collective-permute-start.6
  96.8 2.7 %collective-permute-start.8 = (bf16[256,1024]{1,0:T(8,128)(2,1)}, bf16[256,1024]{1,0:T(8,128)(2,1)S(1)}, u32[]{:S(2)}, u32[]{:S(2)}) collective-permute-start(bf16[256,1024]{1,0:T(8,128)(2,1)} %get-tuple-element.18), channel_id=1, source_target_pairs={{0,32},{1,33},{2,34},{3,35},{4,36},{5,37},{6,38},{7,39},{8,40},{9,... | collective-permute-start | bytes 1572872 | tf_op jit(solution)/shard_map/ppermute | solution.py:30
  99.5 4.6 %all-to-all-start.3 = ((bf16[16,64,128]{2,1,0:T(8,128)(2,1)}), bf16[16,64,128]{2,1,0:T(8,128)(2,1)S(1)}, u32[]{:S(2)}, u32[]{:S(2)}) async-start(bf16[16,64,128]{2,1,0:T(8,128)(2,1)} %get-tuple-element.21), calls=%async_computation.3 | async-start | bytes 524288 | tf_op jit(solution)/shard_map/all_to_all | solution.py:233
  104.1 3.1 %collective-permute-start.15 = (bf16[256,1024]{1,0:T(8,128)(2,1)}, bf16[256,1024]{1,0:T(8,128)(2,1)}, u32[]{:S(2)}, u32[]{:S(2)}) collective-permute-start(bf16[256,1024]{1,0:T(8,128)(2,1)} %get-tuple-element.25), channel_id=1, source_target_pairs={{0,48},{1,49},{2,50},{3,51},{4,52},{5,53},{6,54},{7,55},{8,56},{9,... | collective-permute-start | bytes 1572872 | tf_op jit(solution)/shard_map/ppermute | solution.py:30
  107.3 15.0 %collective-permute-done.5.refs_0_ = bf16[256,1024]{1,0:T(8,128)(2,1)S(1)} collective-permute-done((bf16[256,1024]{1,0:T(8,128)(2,1)}, bf16[256,1024]{1,0:T(8,128)(2,1)S(1)}, u32[]{:S(2)}, u32[]{:S(2)}) %collective-permute-start.5) | collective-permute-done | bytes 524320 | tf_op jit(solution)/shard_map/ppermute | solution.py:30
  122.3 1.7 collective-permute-done.8.refs_3_
  124.8 2.0 %shard_map.64 = bf16[16,2,64,256]{3,2,1,0:T(8,128)(2,1)} custom-call(bf16[2,64,256]{2,1,0:T(8,128)(2,1)} %add_convert_fusion.6.after_ref.in_ref, bf16[256,1024]{1,0:T(8,128)(2,1)} %copy-done.7, bf16[256,1024]{1,0:T(8,128)(2,1)} %copy-done.9, bf16[256,1024]{1,0:T(8,128)(2,1)} %copy-done.11, bf16[256,1024]{1,0:T(8,128)(2,1)} %copy-done.13), custom_call_target="tpu_custom_call" | custom-call | bytes 3211264 | tf_op jit(solution)/shard_map/pallas_call | solution.py:43
  126.7 4.5 %all-to-all-start.2 = ((bf16[16,2,64,256]{3,2,1,0:T(8,128)(2,1)}), bf16[16,2,64,256]{3,2,1,0:T(8,128)(2,1)S(1)}, u32[]{:S(2)}, u32[]{:S(2)}) async-start(bf16[16,2,64,256]{3,2,1,0:T(8,128)(2,1)} %shard_map.64), calls=%async_computation.2 | async-start | bytes 2097152 | tf_op jit(solution)/shard_map/all_to_all | solution.py:239
  131.2 3.1 %collective-permute-start.11 = (bf16[256,1024]{1,0:T(8,128)(2,1)}, bf16[256,1024]{1,0:T(8,128)(2,1)}, u32[]{:S(2)}, u32[]{:S(2)}) collective-permute-start(bf16[256,1024]{1,0:T(8,128)(2,1)} %get-tuple-element.23), channel_id=1, source_target_pairs={{0,12},{1,13},{2,14},{3,15},{4,0},{5,1},{6,2},{7,3},{8,4},{9,5},{1... | collective-permute-start | bytes 1572872 | tf_op jit(solution)/shard_map/ppermute | solution.py:30
  134.4 1.0 constant_dynamic-slice_fusion
  135.4 1.7 copy.24
  137.1 2.4 %add_convert_fusion = (bf16[64,1024]{1,0:T(8,128)(2,1)S(1)}, bf16[64,1024]{1,0:T(8,128)(2,1)}, bf16[64,1024]{1,0:T(8,128)(2,1)}, f32[64,1024]{1,0:T(8,128)}) fusion(bf16[256,1024]{1,0:T(8,128)(2,1)} %collective-permute-done.15, bf16[256,1024]{1,0:T(8,128)(2,1)S(1)} %copy-done.14, bf16[256,1024]{1,0:T(8,128)(2,1)S(1)} %copy-done.12, ...), kind=kLoop, calls=%fused_computation.3 | loop fusion | flops 2031616 | bytes 2752512 | tf_op jit(solution)/shard_map/convert_element_type | solution.py:153
  139.6 0.9 collective-permute-start.18
  140.8 1.2 collective-permute-start.16
  142.0 15.3 %collective-permute-done.11 = bf16[256,1024]{1,0:T(8,128)(2,1)} collective-permute-done((bf16[256,1024]{1,0:T(8,128)(2,1)}, bf16[256,1024]{1,0:T(8,128)(2,1)}, u32[]{:S(2)}, u32[]{:S(2)}) %collective-permute-start.11) | collective-permute-done | bytes 524320 | tf_op jit(solution)/shard_map/ppermute | solution.py:30
  157.3 2.1 %add_convert_fusion.3 = (bf16[64,1024]{1,0:T(8,128)(2,1)S(1)}, bf16[64,1024]{1,0:T(8,128)(2,1)S(1)}, bf16[64,1024]{1,0:T(8,128)(2,1)S(1)}, f32[64,1024]{1,0:T(8,128)}) fusion(bf16[256,1024]{1,0:T(8,128)(2,1)} %collective-permute-done.11, bf16[256,1024]{1,0:T(8,128)(2,1)S(1)} %copy-done.10, bf16[256,1024]{1,0:T(8,128)(2,1)S(1)} %copy-done.8, ...), kind=kLoop, calls=%fused_computation.7 | loop fusion | flops 2031616 | bytes 2752512 | tf_op jit(solution)/shard_map/convert_element_type | solution.py:153
  159.4 2.5 %collective-permute-start.14 = (bf16[64,1024]{1,0:T(8,128)(2,1)S(1)}, bf16[64,1024]{1,0:T(8,128)(2,1)S(1)}, u32[]{:S(2)}, u32[]{:S(2)}) collective-permute-start(bf16[64,1024]{1,0:T(8,128)(2,1)S(1)} %get-tuple-element.26), channel_id=1, source_target_pairs={{0,48},{1,49},{2,50},{3,51},{4,52},{5,53},{6,54},{7,55},{8,56},{9,... | collective-permute-start | bytes 393224 | tf_op jit(solution)/shard_map/ppermute | solution.py:30
  162.0 0.9 collective-permute-start.13
  162.8 1.0 collective-permute-start.12
  164.6 2.1 %shard_map.66.after_ref = f32[64,2048]{1,0:T(8,128)} custom-call(s32[4]{0:T(128)} %pad_add_fusion.at_ref, f32[64,2048]{1,0:T(8,128)} %get-tuple-element.14.also_ref.direct_ref, bf16[64,1024]{1,0:T(8,128)(2,1)} %bitcast.41, bf16[64,1024]{1,0:T(8,128)(2,1)} %copy-done.19), custom_call_target="tpu_custom_call" | custom-call | bytes 1310736 | tf_op jit(solution)/shard_map/pallas_call | solution.py:43
  167.4 1.9 shard_map.68
  169.3 1.0 copy-done.5
  170.3 4.8 %shard_map.65 = (f32[512,256]{1,0:T(8,128)}, f32[512,256]{1,0:T(8,128)}) custom-call(s32[4]{0:T(128)} %pad_add_fusion.at_ref, bf16[16,2,64,256]{3,2,1,0:T(8,128)(2,1)} %copy-done.5, bf16[1024,512]{1,0:T(8,128)(2,1)} %bitcast.34, bf16[1024,512]{1,0:T(8,128)(2,1)} %bitcast.36, bf16[1024,512]{1,0:T(8,128)(2,1)} %collective-permute-done.1.after_ref.also_ref.a1_ref.cross1_ref, ...), custom_call_target="tpu_custom_call" | custom-call | flops 1073741824 | bytes 6291472 | tf_op jit(solution)/shard_map/pallas_call | solution.py:43
  175.8 1.9 %shard_map.67 = f32[64,1024]{1,0:T(8,128)} custom-call(f32[64,1024]{1,0:T(8,128)} %get-tuple-element.29.mine_ref, bf16[64,1024]{1,0:T(8,128)(2,1)} %copy-done.25, bf16[64,1024]{1,0:T(8,128)(2,1)} %copy-done.22, bf16[64,1024]{1,0:T(8,128)(2,1)} %copy-done.20, f32[512,256]{1,0:T(8,128)} %get-tuple-element.19.after_ref), custom_call_target="tpu_custom_call" | custom-call | bytes 1441792 | tf_op jit(solution)/shard_map/pallas_call | solution.py:43
  177.7 1.1 select_convert_fusion
  178.8 1.7 collective-permute-start.19
  180.4 4.8 %collective-permute-done.19 = bf16[64,2048]{1,0:T(8,128)(2,1)S(1)} collective-permute-done((bf16[64,2048]{1,0:T(8,128)(2,1)S(1)}, bf16[64,2048]{1,0:T(8,128)(2,1)S(1)}, u32[]{:S(2)}, u32[]{:S(2)}) %collective-permute-start.19) | collective-permute-done | bytes 262176 | tf_op jit(solution)/shard_map/ppermute | solution.py:30
  185.2 1.9 multiply_add_fusion
  187.1 0.9 add.108
  (79 shorter events, 5.5 us)
Async XLA Ops:
  3.5 5.7 %copy-start.2 = (bf16[512,2048]{0,1:T(8,128)(2,1)}, bf16[512,2048]{0,1:T(8,128)(2,1)S(1)}, u32[]{:S(2)}) copy-start(bf16[512,2048]{0,1:T(8,128)(2,1)S(1)} %copy.12) | copy-start | bytes 6291460
  3.5 13.7 %collective-permute-start = (bf16[2048,512]{1,0:T(8,128)(2,1)S(1)}, bf16[2048,512]{1,0:T(8,128)(2,1)}, u32[]{:S(2)}, u32[]{:S(2)}) collective-permute-start(bf16[2048,512]{1,0:T(8,128)(2,1)S(1)} %bitcast.28), channel_id=1, source_target_pairs={{0,2},{1,3},{2,0},{3,1},{4,6},{5,7},{6,4},{7,5},{8,10},{9,11},{10,... | collective-permute-start | bytes 6291464 | tf_op jit(solution)/shard_map/ppermute | solution.py:30
  3.7 15.8 %copy-start.3 = (bf16[16,1,64,512]{3,2,1,0:T(8,128)(2,1)}, bf16[16,1,64,512]{3,2,1,0:T(8,128)(2,1)S(1)}, u32[]{:S(2)}) copy-start(bf16[16,1,64,512]{3,2,1,0:T(8,128)(2,1)S(1)} %constant_dynamic-slice_fusion.3) | copy-start | bytes 3145732
  3.7 27.3 %collective-permute-start.1 = (bf16[1024,512]{1,0:T(8,128)(2,1)S(1)}, bf16[1024,512]{1,0:T(8,128)(2,1)}, u32[]{:S(2)}, u32[]{:S(2)}) collective-permute-start(bf16[1024,512]{1,0:T(8,128)(2,1)S(1)} %bitcast.32), channel_id=1, source_target_pairs={{0,1},{1,0},{2,3},{3,2},{4,5},{5,4},{6,7},{7,6},{8,9},{9,8},{10,11... | collective-permute-start | bytes 3145736 | tf_op jit(solution)/shard_map/ppermute | solution.py:30
  9.2 29.5 %all-to-all-start = ((bf16[16,64,512]{2,1,0:T(8,128)(2,1)}), bf16[16,64,512]{2,1,0:T(8,128)(2,1)}, u32[]{:S(2)}, u32[]{:S(2)}) async-start(bf16[16,64,512]{2,1,0:T(8,128)(2,1)} %shard_map.59), calls=%async_computation | async-start | bytes 2097152 | tf_op jit(solution)/shard_map/all_to_all | solution.py:214
  38.7 8.1 %copy-start.4 = (bf16[16,1,64,512]{3,2,1,0:T(8,128)(2,1)S(1)}, bf16[16,1,64,512]{3,2,1,0:T(8,128)(2,1)}, u32[]{:S(2)}) copy-start(bf16[16,1,64,512]{3,2,1,0:T(8,128)(2,1)} %constant_dynamic-slice_fusion.2) | copy-start | bytes 3145732
  38.7 43.2 %all-to-all-start.1 = ((bf16[16,64,1152]{2,1,0:T(8,128)(2,1)}), bf16[16,64,1152]{2,1,0:T(8,128)(2,1)S(1)}, u32[]{:S(2)}, u32[]{:S(2)}) async-start(bf16[16,64,1152]{2,1,0:T(8,128)(2,1)} %shard_map.60.after_ref), calls=%async_computation.1 | async-start | bytes 4718592 | tf_op jit(solution)/shard_map/all_to_all | solution.py:226
  46.8 39.5 %collective-permute-start.4 = (bf16[1024,512]{1,0:T(8,128)(2,1)S(1)}, bf16[1024,512]{1,0:T(8,128)(2,1)}, u32[]{:S(2)}, u32[]{:S(2)}) collective-permute-start(bf16[1024,512]{1,0:T(8,128)(2,1)S(1)} %bitcast.37), channel_id=1, source_target_pairs={{0,1},{1,0},{2,3},{3,2},{4,5},{5,4},{6,7},{7,6},{8,9},{9,8},{10,11... | collective-permute-start | bytes 3145736 | tf_op jit(solution)/shard_map/ppermute | solution.py:30
  53.3 1.4 collective-permute-start.2
  55.6 20.5 %collective-permute-start.3 = (f32[2,64,256]{2,1,0:T(8,128)S(1)}, f32[2,64,256]{2,1,0:T(8,128)}, u32[]{:S(2)}, u32[]{:S(2)}) collective-permute-start(f32[2,64,256]{2,1,0:T(8,128)S(1)} %bitcast_add_fusion), channel_id=1, source_target_pairs={{0,64},{1,65},{2,66},{3,67},{4,68},{5,69},{6,70},{7,71},{8,72},{9,... | collective-permute-start | bytes 393224 | tf_op jit(solution)/shard_map/ppermute | solution.py:30
  81.9 1.4 copy-start
  95.1 27.1 %collective-permute-start.5 = (bf16[256,1024]{1,0:T(8,128)(2,1)}, bf16[256,1024]{1,0:T(8,128)(2,1)S(1)}, u32[]{:S(2)}, u32[]{:S(2)}) collective-permute-start(bf16[256,1024]{1,0:T(8,128)(2,1)} %get-tuple-element.15), channel_id=1, source_target_pairs={{0,4},{1,5},{2,6},{3,7},{4,8},{5,9},{6,10},{7,11},{8,12},{9,13},{1... | collective-permute-start | bytes 1572872 | tf_op jit(solution)/shard_map/ppermute | solution.py:30
  95.1 27.1 %collective-permute-start.6 = (bf16[256,1024]{1,0:T(8,128)(2,1)}, bf16[256,1024]{1,0:T(8,128)(2,1)S(1)}, u32[]{:S(2)}, u32[]{:S(2)}) collective-permute-start(bf16[256,1024]{1,0:T(8,128)(2,1)} %get-tuple-element.16), channel_id=1, source_target_pairs={{0,8},{1,9},{2,10},{3,11},{4,12},{5,13},{6,14},{7,15},{8,0},{9,1},... | collective-permute-start | bytes 1572872 | tf_op jit(solution)/shard_map/ppermute | solution.py:30
  96.3 25.9 %collective-permute-start.7 = (bf16[256,1024]{1,0:T(8,128)(2,1)}, bf16[256,1024]{1,0:T(8,128)(2,1)S(1)}, u32[]{:S(2)}, u32[]{:S(2)}) collective-permute-start(bf16[256,1024]{1,0:T(8,128)(2,1)} %get-tuple-element.17), channel_id=1, source_target_pairs={{0,16},{1,17},{2,18},{3,19},{4,20},{5,21},{6,22},{7,23},{8,24},{9,... | collective-permute-start | bytes 1572872 | tf_op jit(solution)/shard_map/ppermute | solution.py:30
  96.8 27.1 %collective-permute-start.8 = (bf16[256,1024]{1,0:T(8,128)(2,1)}, bf16[256,1024]{1,0:T(8,128)(2,1)S(1)}, u32[]{:S(2)}, u32[]{:S(2)}) collective-permute-start(bf16[256,1024]{1,0:T(8,128)(2,1)} %get-tuple-element.18), channel_id=1, source_target_pairs={{0,32},{1,33},{2,34},{3,35},{4,36},{5,37},{6,38},{7,39},{8,40},{9,... | collective-permute-start | bytes 1572872 | tf_op jit(solution)/shard_map/ppermute | solution.py:30
  99.5 27.2 %all-to-all-start.3 = ((bf16[16,64,128]{2,1,0:T(8,128)(2,1)}), bf16[16,64,128]{2,1,0:T(8,128)(2,1)S(1)}, u32[]{:S(2)}, u32[]{:S(2)}) async-start(bf16[16,64,128]{2,1,0:T(8,128)(2,1)} %get-tuple-element.21), calls=%async_computation.3 | async-start | bytes 524288 | tf_op jit(solution)/shard_map/all_to_all | solution.py:233
  104.1 33.0 %collective-permute-start.15 = (bf16[256,1024]{1,0:T(8,128)(2,1)}, bf16[256,1024]{1,0:T(8,128)(2,1)}, u32[]{:S(2)}, u32[]{:S(2)}) collective-permute-start(bf16[256,1024]{1,0:T(8,128)(2,1)} %get-tuple-element.25), channel_id=1, source_target_pairs={{0,48},{1,49},{2,50},{3,51},{4,52},{5,53},{6,54},{7,55},{8,56},{9,... | collective-permute-start | bytes 1572872 | tf_op jit(solution)/shard_map/ppermute | solution.py:30
  122.2 1.7 copy-start.7
  122.2 1.7 copy-start.9
  122.3 1.7 copy-start.11
  123.9 0.8 copy-start.13
  126.7 10.4 %copy-start.12 = (bf16[256,1024]{1,0:T(8,128)(2,1)S(1)}, bf16[256,1024]{1,0:T(8,128)(2,1)}, u32[]{:S(2)}) copy-start(bf16[256,1024]{1,0:T(8,128)(2,1)} %copy-done.11) | copy-start | bytes 1572868
  126.7 10.4 %copy-start.14 = (bf16[256,1024]{1,0:T(8,128)(2,1)S(1)}, bf16[256,1024]{1,0:T(8,128)(2,1)}, u32[]{:S(2)}) copy-start(bf16[256,1024]{1,0:T(8,128)(2,1)} %copy-done.13) | copy-start | bytes 1572868
  126.7 42.5 %all-to-all-start.2 = ((bf16[16,2,64,256]{3,2,1,0:T(8,128)(2,1)}), bf16[16,2,64,256]{3,2,1,0:T(8,128)(2,1)S(1)}, u32[]{:S(2)}, u32[]{:S(2)}) async-start(bf16[16,2,64,256]{3,2,1,0:T(8,128)(2,1)} %shard_map.64), calls=%async_computation.2 | async-start | bytes 2097152 | tf_op jit(solution)/shard_map/all_to_all | solution.py:239
  131.2 26.1 %collective-permute-start.11 = (bf16[256,1024]{1,0:T(8,128)(2,1)}, bf16[256,1024]{1,0:T(8,128)(2,1)}, u32[]{:S(2)}, u32[]{:S(2)}) collective-permute-start(bf16[256,1024]{1,0:T(8,128)(2,1)} %get-tuple-element.23), channel_id=1, source_target_pairs={{0,12},{1,13},{2,14},{3,15},{4,0},{5,1},{6,2},{7,3},{8,4},{9,5},{1... | collective-permute-start | bytes 1572872 | tf_op jit(solution)/shard_map/ppermute | solution.py:30
  134.4 22.9 %copy-start.8 = (bf16[256,1024]{1,0:T(8,128)(2,1)S(1)}, bf16[256,1024]{1,0:T(8,128)(2,1)}, u32[]{:S(2)}) copy-start(bf16[256,1024]{1,0:T(8,128)(2,1)} %copy-done.7) | copy-start | bytes 1572868
  134.4 22.9 %copy-start.10 = (bf16[256,1024]{1,0:T(8,128)(2,1)S(1)}, bf16[256,1024]{1,0:T(8,128)(2,1)}, u32[]{:S(2)}) copy-start(bf16[256,1024]{1,0:T(8,128)(2,1)} %copy-done.9) | copy-start | bytes 1572868
  137.1 20.2 %copy-start.18 = (bf16[256,1024]{1,0:T(8,128)(2,1)S(1)}, bf16[256,1024]{1,0:T(8,128)(2,1)}, u32[]{:S(2)}) copy-start(bf16[256,1024]{1,0:T(8,128)(2,1)} %get-tuple-element.22) | copy-start | bytes 1572868
  137.1 24.9 %collective-permute-start.10 = (bf16[64,1024]{1,0:T(8,128)(2,1)}, bf16[64,1024]{1,0:T(8,128)(2,1)S(1)}, u32[]{:S(2)}, u32[]{:S(2)}) collective-permute-start(bf16[64,1024]{1,0:T(8,128)(2,1)} %bitcast.16), channel_id=1, source_target_pairs={{0,2},{1,3},{2,0},{3,1},{4,6},{5,7},{6,4},{7,5},{8,10},{9,11},{10,... | collective-permute-start | bytes 393224 | tf_op jit(solution)/shard_map/ppermute | solution.py:30
  137.1 26.7 %copy-start.16 = (bf16[1024,64]{1,0:T(8,128)(2,1)S(1)}, bf16[1024,64]{1,0:T(8,128)(2,1)}, u32[]{:S(2)}) copy-start(bf16[1024,64]{1,0:T(8,128)(2,1)} %get-tuple-element.35) | copy-start | bytes 393220
  139.6 23.3 %collective-permute-start.18 = (bf16[64,1024]{1,0:T(8,128)(2,1)S(1)}, bf16[64,1024]{1,0:T(8,128)(2,1)S(1)}, u32[]{:S(2)}, u32[]{:S(2)}) collective-permute-start(bf16[64,1024]{1,0:T(8,128)(2,1)S(1)} %get-tuple-element.30), channel_id=1, source_target_pairs={{0,12},{1,13},{2,14},{3,15},{4,0},{5,1},{6,2},{7,3},{8,4},{9,5},{1... | collective-permute-start | bytes 393224 | tf_op jit(solution)/shard_map/ppermute | solution.py:30
  140.4 26.3 %collective-permute-start.17 = (bf16[64,1024]{1,0:T(8,128)(2,1)}, bf16[64,1024]{1,0:T(8,128)(2,1)S(1)}, u32[]{:S(2)}, u32[]{:S(2)}) collective-permute-start(bf16[64,1024]{1,0:T(8,128)(2,1)} %get-tuple-element.31), channel_id=1, source_target_pairs={{0,8},{1,9},{2,10},{3,11},{4,12},{5,13},{6,14},{7,15},{8,0},{9,1},... | collective-permute-start | bytes 393224 | tf_op jit(solution)/shard_map/ppermute | solution.py:30
  140.8 25.9 %collective-permute-start.16 = (bf16[64,1024]{1,0:T(8,128)(2,1)}, bf16[64,1024]{1,0:T(8,128)(2,1)S(1)}, u32[]{:S(2)}, u32[]{:S(2)}) collective-permute-start(bf16[64,1024]{1,0:T(8,128)(2,1)} %get-tuple-element.32), channel_id=1, source_target_pairs={{0,4},{1,5},{2,6},{3,7},{4,8},{5,9},{6,10},{7,11},{8,12},{9,13},{1... | collective-permute-start | bytes 393224 | tf_op jit(solution)/shard_map/ppermute | solution.py:30
  159.4 15.6 %collective-permute-start.14 = (bf16[64,1024]{1,0:T(8,128)(2,1)S(1)}, bf16[64,1024]{1,0:T(8,128)(2,1)S(1)}, u32[]{:S(2)}, u32[]{:S(2)}) collective-permute-start(bf16[64,1024]{1,0:T(8,128)(2,1)S(1)} %get-tuple-element.26), channel_id=1, source_target_pairs={{0,48},{1,49},{2,50},{3,51},{4,52},{5,53},{6,54},{7,55},{8,56},{9,... | collective-permute-start | bytes 393224 | tf_op jit(solution)/shard_map/ppermute | solution.py:30
  162.0 2.6 %copy-start.19 = (bf16[64,1024]{1,0:T(8,128)(2,1)}, bf16[64,1024]{1,0:T(8,128)(2,1)S(1)}, u32[]{:S(2)}) copy-start(bf16[64,1024]{1,0:T(8,128)(2,1)S(1)} %collective-permute-done.10.given_ref) | copy-start | bytes 393220
  162.0 13.1 %collective-permute-start.13 = (bf16[64,1024]{1,0:T(8,128)(2,1)S(1)}, bf16[64,1024]{1,0:T(8,128)(2,1)S(1)}, u32[]{:S(2)}, u32[]{:S(2)}) collective-permute-start(bf16[64,1024]{1,0:T(8,128)(2,1)S(1)} %get-tuple-element.27), channel_id=1, source_target_pairs={{0,32},{1,33},{2,34},{3,35},{4,36},{5,37},{6,38},{7,39},{8,40},{9,... | collective-permute-start | bytes 393224 | tf_op jit(solution)/shard_map/ppermute | solution.py:30
  162.8 3.9 %copy-start.21 = (bf16[64,1024]{1,0:T(8,128)(2,1)}, bf16[64,1024]{1,0:T(8,128)(2,1)S(1)}, u32[]{:S(2)}) copy-start(bf16[64,1024]{1,0:T(8,128)(2,1)S(1)} %collective-permute-done.18.g3_ref) | copy-start | bytes 393220
  162.8 12.2 %collective-permute-start.12 = (bf16[64,1024]{1,0:T(8,128)(2,1)S(1)}, bf16[64,1024]{1,0:T(8,128)(2,1)S(1)}, u32[]{:S(2)}, u32[]{:S(2)}) collective-permute-start(bf16[64,1024]{1,0:T(8,128)(2,1)S(1)} %get-tuple-element.28), channel_id=1, source_target_pairs={{0,16},{1,17},{2,18},{3,19},{4,20},{5,21},{6,22},{7,23},{8,24},{9,... | collective-permute-start | bytes 393224 | tf_op jit(solution)/shard_map/ppermute | solution.py:30
  169.2 8.4 %copy-start.1 = (f32[64,2048]{1,0:T(8,128)S(1)}, f32[64,2048]{1,0:T(8,128)}, u32[]{:S(2)}) copy-start(f32[64,2048]{1,0:T(8,128)} %shard_map.66.after_ref) | copy-start | bytes 1572868
  169.2 8.4 %copy-start.6 = (f32[64,1024]{1,0:T(8,128)S(1)}, f32[64,1024]{1,0:T(8,128)}, u32[]{:S(2)}) copy-start(f32[64,1024]{1,0:T(8,128)} %shard_map.68) | copy-start | bytes 786436
  169.3 1.0 copy-start.5
  175.0 5.4 %copy-start.26 = (f32[512,256]{1,0:T(8,128)S(1)}, f32[512,256]{1,0:T(8,128)}, u32[]{:S(2)}) copy-start(f32[512,256]{1,0:T(8,128)} %get-tuple-element.20) | copy-start | bytes 1572868
  175.0 10.2 %copy-start.17 = (f32[64,2048]{1,0:T(8,128)S(1)}, f32[64,2048]{1,0:T(8,128)}, u32[]{:S(2)}) copy-start(f32[64,2048]{1,0:T(8,128)} %param.5) | copy-start | bytes 1572868
  175.1 0.7 copy-start.22
  175.1 0.7 copy-start.25
  177.7 9.4 %copy-start.15 = (f32[512,256]{1,0:T(8,128)S(1)}, f32[512,256]{1,0:T(8,128)}, u32[]{:S(2)}) copy-start(f32[512,256]{1,0:T(8,128)} %get-tuple-element.19.after_ref) | copy-start | bytes 1572868
  178.8 6.5 %collective-permute-start.19 = (bf16[64,2048]{1,0:T(8,128)(2,1)S(1)}, bf16[64,2048]{1,0:T(8,128)(2,1)S(1)}, u32[]{:S(2)}, u32[]{:S(2)}) collective-permute-start(bf16[64,2048]{1,0:T(8,128)(2,1)S(1)} %select_convert_fusion), channel_id=1, source_target_pairs={{0,64},{1,65},{2,66},{3,67},{4,68},{5,69},{6,70},{7,71},{8,72},{9,... | collective-permute-start | bytes 786440 | tf_op jit(solution)/shard_map/ppermute | solution.py:30
  180.4 6.6 %collective-permute-start.9 = (f32[512,256]{1,0:T(8,128)S(1)}, f32[512,256]{1,0:T(8,128)S(1)}, u32[]{:S(2)}, u32[]{:S(2)}) collective-permute-start(f32[512,256]{1,0:T(8,128)S(1)} %copy-done.26), channel_id=1, source_target_pairs={{0,2},{1,3},{2,0},{3,1},{4,6},{5,7},{6,4},{7,5},{8,10},{9,11},{10,... | collective-permute-start | bytes 1572872 | tf_op jit(solution)/shard_map/ppermute | solution.py:30
  (3 other events, 2.0 us)

commit v7 on v5

--- a/solution.py
+++ b/solution.py
@@ -49,7 +49,7 @@
     )(*args)
 
 
-def slots_kernel(f_ref, t_ref, out_ref):
+def slots_kernel(f_ref, t_ref, after_ref, out_ref):
     wide = f_ref.shape[1] // 32
     for s in range(16):
         out_ref[s, :, :wide] = f_ref[:, s * wide : (s + 1) * wide]
@@ -70,35 +70,33 @@
             out_ref[(16 * i + b) * 64 : (16 * i + b + 1) * 64, :] = ref[start, :]
 
 
-def gram_kernel(at_ref, a_ref, b1_ref, b2_ref, after_ref, *outs):
+def gram_kernel(half, at_ref, a_ref, b1_ref, b2_ref, after_ref, *outs):
     z, x = at_ref[0], at_ref[1]
     rows, m, n, tile = 64, a_ref.shape[0] // 2, b1_ref.shape[0] // 2, 256
-    for half in range(2):
-        left1, left2 = [], []
+    left1, left2 = [], []
+    for k in range(4):
+        for j in range(4):
+            dx, dz = (k, j) if half == 0 else (j, k)
+            block = (lax.rem(z + dz, 4) * 4 + lax.rem(x + dx, 4)) * rows
+            left1.append(a_ref[pl.ds(pl.multiple_of(block, rows), rows), :])
+            left2.append(a_ref[pl.ds(pl.multiple_of(block + m, rows), rows), :])
+    left1, left2 = jnp.concatenate(left1), jnp.concatenate(left2)
+    for t in range(n // tile):
+        cols = pl.ds(half * n + t * tile, tile)
+        acc = lax.dot_general(left1, b1_ref[cols, :], NT, preferred_element_type=f32)
+        acc += lax.dot_general(left2, b2_ref[cols, :], NT, preferred_element_type=f32)
         for k in range(4):
-            for j in range(4):
-                dx, dz = (k, j) if half == 0 else (j, k)
-                block = (lax.rem(z + dz, 4) * 4 + lax.rem(x + dx, 4)) * rows
-                left1.append(a_ref[pl.ds(pl.multiple_of(block, rows), rows), :])
-                left2.append(a_ref[pl.ds(pl.multiple_of(block + m, rows), rows), :])
-        left1, left2 = jnp.concatenate(left1), jnp.concatenate(left2)
-        for t in range(n // tile):
-            cols = pl.ds(half * n + t * tile, tile)
-            acc = lax.dot_general(left1, b1_ref[cols, :], NT, preferred_element_type=f32)
-            acc += lax.dot_general(left2, b2_ref[cols, :], NT, preferred_element_type=f32)
-            for k in range(4):
-                part = acc[4 * k * rows : 4 * (k + 1) * rows].astype(bf16)
-                outs[4 * half + k][:, t * tile : (t + 1) * tile] = part
-
-
-def gram(at, a, b1, b2, after):
+            outs[k][:, t * tile : (t + 1) * tile] = acc[4 * k * rows : 4 * (k + 1) * rows].astype(bf16)
+
+
+def gram(half, at, a, b1, b2, after):
     n = b1.shape[0]
     return kernel_call(
-        gram_kernel,
-        [jax.ShapeDtypeStruct((256, n // 2), bf16)] * 8,
+        functools.partial(gram_kernel, half),
+        [jax.ShapeDtypeStruct((256, n // 2), bf16)] * 4,
         [SMEM] + [VMEM] * 3 + [ANY],
         at, a, b1, b2, after,
-        flops=2 * a.shape[0] * n * b1.shape[1],
+        flops=a.shape[0] * n * b1.shape[1],
     )
 
 
@@ -117,26 +115,20 @@
     out_ref[...] = mine_ref[...] + g1_ref[...].astype(f32) + g2_ref[...].astype(f32) + g3_ref[...].astype(f32)
 
 
-def scatter_sum(parts, rows, after=None):
-    got, mids, sums = [], [], []
-    for half, axis in ((0, "x"), (1, "z")):
-        got.append([send(parts[4 * half + k], along(axis, k)) for k in (1, 2, 3)])
-    for half in range(2):
-        mids.append([])
-        for j in range(4):
-            cut = lambda v: lax.slice_in_dim(v, j * rows, (j + 1) * rows).astype(f32)
-            total = cut(parts[4 * half])
-            for r in got[half]:
-                total = total + cut(r)
-            mids[half].append(total)
-    for half, axis in ((0, "z"), (1, "x")):
-        rs = [send(mids[half][k].astype(bf16), along(axis, k)) for k in (1, 2, 3)]
-        if after is not None:
-            out = jax.ShapeDtypeStruct(mids[half][0].shape, f32)
-            sums.append(kernel_call(sum_kernel, [out], [VMEM] * 4 + [ANY], mids[half][0], *rs, after)[0])
-        else:
-            sums.append(mids[half][0] + rs[0].astype(f32) + rs[1].astype(f32) + rs[2].astype(f32))
-    return jnp.concatenate(sums, axis=1)
+def first_stage(parts, rows, axis):
+    got = [send(parts[k], along(axis, k)) for k in (1, 2, 3)]
+    mids = []
+    for j in range(4):
+        cut = lambda v: lax.slice_in_dim(v, j * rows, (j + 1) * rows).astype(f32)
+        mids.append(cut(parts[0]) + cut(got[0]) + cut(got[1]) + cut(got[2]))
+    return mids
+
+
+def second_stage(own, cross, axis, after):
+    both = [jnp.concatenate([a, b]) for a, b in zip(own, cross)]
+    got = [send(both[k].astype(bf16), along(axis, k)) for k in (1, 2, 3)]
+    out = jax.ShapeDtypeStruct(both[0].shape, f32)
+    return kernel_call(sum_kernel, [out], [VMEM] * 4 + [ANY], both[0], *got, after)[0]
 
 
 def on_device(grads, covariance, test_grads, inverse_factor):
@@ -152,21 +144,23 @@
 
     (picked,) = kernel_call(pick_kernel, [shape((feats, tokens), bf16)], [SMEM, VMEM, VMEM], at, gt, sib)
     arrived = send(picked, flip("yh"))
-    own = gram(at, picked, gt, sib, picked)
-    cross = gram(at, arrived, gt, sib, own[0])
+    own = [gram(0, at, picked, gt, sib, picked)]
+    own.append(gram(1, at, picked, gt, sib, own[0][0]))
+    cross = [gram(0, at, arrived, gt, sib, own[1][0])]
+    cross.append(gram(1, at, arrived, gt, sib, cross[0][0]))
 
     (slots,) = kernel_call(
         slots_kernel,
         [shape((16, rows, 4 * rows + tests), bf16)],
-        [VMEM, VMEM],
-        inverse_factor, test_grads.T,
+        [VMEM, VMEM, ANY],
+        inverse_factor, test_grads.T, own[1][0],
     )
     slots = lax.all_to_all(slots, ("z", "x"), split_axis=0, concat_axis=0, tiled=True)
     (pt,) = kernel_call(
         functools.partial(factor_kernel, 4 * rows),
         [shape((4 * rows, tests), f32)],
         [VMEM, ANY, ANY],
-        slots.reshape(16 * rows, -1), own[0], arrived,
+        slots.reshape(16 * rows, -1), own[1][0], arrived,
         flops=2 * 16 * rows * 4 * rows * tests,
     )
     pt = pt.reshape(2, 2, rows, tests)
@@ -185,12 +179,15 @@
     )
     scores = keep + send(give, flip("c"))
 
-    own = scatter_sum(own, rows)
-    own = own + send(own.astype(bf16), flip("yl"), lambda at: at["yl"] != at["yh"]).astype(f32)
-    cross = scatter_sum(cross, rows, keep)
-    cross = cross + send(cross.astype(bf16), flip("yl"), lambda at: at["yl"] == at["yh"]).astype(f32)
-    examples = tokens * 64
-    covariance_out = 0.9 * covariance + jnp.where(yl == h, own, cross) / examples
+    sums = []
+    for half, (first, second) in enumerate((("x", "z"), ("z", "x"))):
+        mids = [first_stage(parts[half], rows, first) for parts in (own, cross)]
+        sums.append(second_stage(*mids, second, keep))
+    sums = jnp.concatenate(sums, axis=1)
+    own, cross = sums[:rows], sums[rows:]
+    ours, theirs = jnp.where(yl == h, own, cross), jnp.where(yl == h, cross, own)
+    term = ours + send(theirs.astype(bf16), flip("yl")).astype(f32)
+    covariance_out = 0.9 * covariance + term / (tokens * 64)
     return scores, covariance_out
 
 

time: 178 us -> 178 us (level)
  starting transfers between devices: 70.5 us -> 51.9 us
  waiting for transfers between devices: 44.6 us -> 56.3 us
  Pallas kernels: 35 us -> 43 us
    ppermute x31 -> x24, waiting for transfers between devices: 44.6 us -> 56.3 us  [send(): return lax.ppermute(value, AXES, pairs)]
    all_to_all x1, starting transfers between devices: 14.2 us -> 3.65 us  [on_device(): pt = lax.all_to_all(pt, ('z', 'x'), split_axis=0, concat_axis=0, tiled=True)]
    convert_element_type x6 -> x1, other arithmetic: 10 us -> 1.14 us  [on_device(): term = ours + send(theirs.astype(bf16), flip('yl')).astype(f32)]
    pallas_call x8 -> x10, Pallas kernels: 35 us -> 43 us  [kernel_call(): pl.pallas_call(body, out_shape=outs, in_specs=specs, out_specs=[VMEM] * l...]
    another operation x0 -> x4, other arithmetic: none -> 7.64 us
    ppermute x31 -> x24, starting transfers between devices: 48.4 us -> 42.6 us  [send(): return lax.ppermute(value, AXES, pairs)]
    concatenate x0 -> x8, other arithmetic: none -> 3.87 us  [second_stage(): both = [jnp.concatenate([a, b]) for a, b in zip(own, cross)]]
    add x3 -> x1, other arithmetic: 4.35 us -> 1.94 us  [on_device(): covariance_out = 0.9 * covariance + term / (tokens * 64)]
  transfers between devices with their start and end apart: 33 -> 26, of which waited for: 9 -> 8; matrix products, arithmetic and copies ran while one was open for 10% -> 9% of each run, Pallas kernels for 18% -> 20%
where the time goes in v7:
time: 178 us; the launch traced here: 177 us
  waiting for transfers between devices  56.3 us (32%)
  starting transfers between devices  51.9 us (29%)
  Pallas kernels  43 us (24%)
  other arithmetic  16.3 us (9%)
  local copies, waits for them, and re-layouts  8.74 us (5%)
    ppermute x24, waiting for transfers between devices, send(): return lax.ppermute(value, AXES, pairs)  56.3 us
    pallas_call x10, Pallas kernels, kernel_call(): pl.pallas_call(body, out_shape=outs, in_specs=specs, out_specs=[VMEM] * l...  43 us
    ppermute x24, starting transfers between devices, send(): return lax.ppermute(value, AXES, pairs)  42.6 us
    another operation x4, other arithmetic  7.64 us
    unnamed x39, local copies, waits for them, and re-layouts  6.73 us
    all_to_all x1, starting transfers between devices, on_device(): lax.all_to_all(slots, ('z', 'x'), split_axis=0, concat_axis=0, tiled=True)  5.63 us
    concatenate x8, other arithmetic, second_stage(): both = [jnp.concatenate([a, b]) for a, b in zip(own, cross)]  3.87 us
    all_to_all x1, starting transfers between devices, on_device(): pt = lax.all_to_all(pt, ('z', 'x'), split_axis=0, concat_axis=0, tiled=True)  3.65 us
  transfers between devices with their start and end apart: 26, of which 8 were waited for; matrix products, arithmetic and copies ran while one was open for 9% of the time, Pallas kernels for 20%

profile of v7, /device:TPU:0, one launch (start us, length us, event | category | flops | bytes accessed | tf_op | source)
XLA Modules:
  0.0 177.1 jit_solution(2514400777457820447)
XLA Ops:
  0.6 2.9 %copy.6 = bf16[512,2048]{0,1:T(8,128)(2,1)S(1)} copy(bf16[512,2048]{1,0:T(8,128)(2,1)} %param.4) | data formatting | bytes 4194304 | tf_op args[0]
  4.4 3.5 %collective-permute-done.sib_ref.b2_ref = bf16[2048,512]{1,0:T(8,128)(2,1)} collective-permute-done((bf16[2048,512]{1,0:T(8,128)(2,1)S(1)}, bf16[2048,512]{1,0:T(8,128)(2,1)}, u32[]{:S(2)}, u32[]{:S(2)}) %collective-permute-start) | collective-permute-done | bytes 2097184 | tf_op jit(solution)/shard_map/ppermute | solution.py:30
  7.9 3.7 %shard_map.59.a_ref.after_ref.own_ref = bf16[2048,512]{1,0:T(8,128)(2,1)} custom-call(s32[4]{0:T(128)} %pad_add_fusion.at_ref, bf16[2048,512]{1,0:T(8,128)(2,1)} %bitcast.13, bf16[2048,512]{1,0:T(8,128)(2,1)} %collective-permute-done.sib_ref.b2_ref), custom_call_target="tpu_custom_call" | custom-call | bytes 6291472 | tf_op jit(solution)/shard_map/pallas_call | solution.py:43
  11.6 3.3 %collective-permute-start.1 = (bf16[2048,512]{1,0:T(8,128)(2,1)}, bf16[2048,512]{1,0:T(8,128)(2,1)S(1)}, u32[]{:S(2)}, u32[]{:S(2)}) collective-permute-start(bf16[2048,512]{1,0:T(8,128)(2,1)} %shard_map.59.a_ref.after_ref.own_ref), channel_id=1, source_target_pairs={{0,1},{1,0},{2,3},{3,2},{4,5},{5,4},{6,7},{7,6},{8,9},{9,8},{10,11... | collective-permute-start | bytes 6291464 | tf_op jit(solution)/shard_map/ppermute | solution.py:30
  14.9 6.4 %shard_map.60 = (bf16[256,1024]{1,0:T(8,128)(2,1)}, bf16[256,1024]{1,0:T(8,128)(2,1)}, bf16[256,1024]{1,0:T(8,128)(2,1)}, bf16[256,1024]{1,0:T(8,128)(2,1)}) custom-call(s32[4]{0:T(128)} %pad_add_fusion.at_ref, bf16[2048,512]{1,0:T(8,128)(2,1)} %shard_map.59.a_ref.after_ref.own_ref, bf16[2048,512]{1,0:T(8,128)(2,1)} %bitcast.14, ...), custom_call_target="tpu_custom_call" | custom-call | flops 2147483648 | bytes 10485776 | tf_op jit(solution)/shard_map/pallas_call | solution.py:43
  21.3 1.5 collective-permute-start.5
  22.8 2.7 %collective-permute-start.6 = (bf16[256,1024]{1,0:T(8,128)(2,1)}, bf16[256,1024]{1,0:T(8,128)(2,1)}, u32[]{:S(2)}, u32[]{:S(2)}) collective-permute-start(bf16[256,1024]{1,0:T(8,128)(2,1)} %get-tuple-element.25), channel_id=1, source_target_pairs={{0,8},{1,9},{2,10},{3,11},{4,12},{5,13},{6,14},{7,15},{8,0},{9,1},... | collective-permute-start | bytes 1572872 | tf_op jit(solution)/shard_map/ppermute | solution.py:30
  25.5 1.4 collective-permute-start.7
  27.0 6.5 %shard_map.61 = (bf16[256,1024]{1,0:T(8,128)(2,1)}, bf16[256,1024]{1,0:T(8,128)(2,1)}, bf16[256,1024]{1,0:T(8,128)(2,1)}, bf16[256,1024]{1,0:T(8,128)(2,1)}) custom-call(s32[4]{0:T(128)} %pad_add_fusion.at_ref, bf16[2048,512]{1,0:T(8,128)(2,1)} %shard_map.59.a_ref.after_ref.own_ref, bf16[2048,512]{1,0:T(8,128)(2,1)} %bitcast.15, ...), custom_call_target="tpu_custom_call" | custom-call | flops 2147483648 | bytes 8912912 | tf_op jit(solution)/shard_map/pallas_call | solution.py:43
  33.5 2.2 %shard_map.62 = bf16[16,64,512]{2,1,0:T(8,128)(2,1)} custom-call(bf16[64,4096]{1,0:T(8,128)(2,1)} %f_ref.1, bf16[64,256]{1,0:T(8,128)(2,1)} %bitcast.20, bf16[256,1024]{1,0:T(8,128)(2,1)} %get-tuple-element.21.after_ref), custom_call_target="tpu_custom_call" | custom-call | bytes 2129920 | tf_op jit(solution)/shard_map/pallas_call | solution.py:43
  35.6 5.6 %all-to-all-start = ((bf16[16,64,512]{2,1,0:T(8,128)(2,1)}), bf16[16,64,512]{2,1,0:T(8,128)(2,1)}, u32[]{:S(2)}, u32[]{:S(2)}) async-start(bf16[16,64,512]{2,1,0:T(8,128)(2,1)} %shard_map.62), calls=%async_computation | async-start | bytes 2097152 | tf_op jit(solution)/shard_map/all_to_all | solution.py:158
  41.3 1.9 %collective-permute-start.14 = (bf16[256,1024]{1,0:T(8,128)(2,1)}, bf16[256,1024]{1,0:T(8,128)(2,1)}, u32[]{:S(2)}, u32[]{:S(2)}) collective-permute-start(bf16[256,1024]{1,0:T(8,128)(2,1)} %get-tuple-element.31), channel_id=1, source_target_pairs={{0,16},{1,17},{2,18},{3,19},{4,20},{5,21},{6,22},{7,23},{8,24},{9,... | collective-permute-start | bytes 1572872 | tf_op jit(solution)/shard_map/ppermute | solution.py:30
  43.2 2.7 %collective-permute-start.15 = (bf16[256,1024]{1,0:T(8,128)(2,1)}, bf16[256,1024]{1,0:T(8,128)(2,1)}, u32[]{:S(2)}, u32[]{:S(2)}) collective-permute-start(bf16[256,1024]{1,0:T(8,128)(2,1)} %get-tuple-element.32), channel_id=1, source_target_pairs={{0,32},{1,33},{2,34},{3,35},{4,36},{5,37},{6,38},{7,39},{8,40},{9,... | collective-permute-start | bytes 1572872 | tf_op jit(solution)/shard_map/ppermute | solution.py:30
  45.8 4.1 %collective-permute-done.6 = bf16[256,1024]{1,0:T(8,128)(2,1)} collective-permute-done((bf16[256,1024]{1,0:T(8,128)(2,1)}, bf16[256,1024]{1,0:T(8,128)(2,1)}, u32[]{:S(2)}, u32[]{:S(2)}) %collective-permute-start.6) | collective-permute-done | bytes 524320 | tf_op jit(solution)/shard_map/ppermute | solution.py:30
  50.0 4.0 %collective-permute-start.16 = (bf16[256,1024]{1,0:T(8,128)(2,1)}, bf16[256,1024]{1,0:T(8,128)(2,1)}, u32[]{:S(2)}, u32[]{:S(2)}) collective-permute-start(bf16[256,1024]{1,0:T(8,128)(2,1)} %get-tuple-element.33), channel_id=1, source_target_pairs={{0,48},{1,49},{2,50},{3,51},{4,52},{5,53},{6,54},{7,55},{8,56},{9,... | collective-permute-start | bytes 1572872 | tf_op jit(solution)/shard_map/ppermute | solution.py:30
  54.0 2.5 %add_convert_fusion.7 = (bf16[64,1024]{1,0:T(8,128)(2,1)}, bf16[64,1024]{1,0:T(8,128)(2,1)}, bf16[64,1024]{1,0:T(8,128)(2,1)}, f32[64,1024]{1,0:T(8,128)S(1)}) fusion(bf16[256,1024]{1,0:T(8,128)(2,1)} %collective-permute-done.7, bf16[256,1024]{1,0:T(8,128)(2,1)} %collective-permute-done.6, bf16[256,1024]{1,0:T(8,128)(2,1)} %collective-permute-done.5, ...), kind=kLoop, calls=%fused_computation.23 | loop fusion | flops 2031616 | bytes 2752512 | tf_op jit(solution)/shard_map/convert.6
  56.5 12.1 %collective-permute-done.14 = bf16[256,1024]{1,0:T(8,128)(2,1)} collective-permute-done((bf16[256,1024]{1,0:T(8,128)(2,1)}, bf16[256,1024]{1,0:T(8,128)(2,1)}, u32[]{:S(2)}, u32[]{:S(2)}) %collective-permute-start.14) | collective-permute-done | bytes 524320 | tf_op jit(solution)/shard_map/ppermute | solution.py:30
  68.6 9.4 %collective-permute-done.15 = bf16[256,1024]{1,0:T(8,128)(2,1)} collective-permute-done((bf16[256,1024]{1,0:T(8,128)(2,1)}, bf16[256,1024]{1,0:T(8,128)(2,1)}, u32[]{:S(2)}, u32[]{:S(2)}) %collective-permute-start.15) | collective-permute-done | bytes 524320 | tf_op jit(solution)/shard_map/ppermute | solution.py:30
  78.0 1.8 %add_convert_fusion.1 = (bf16[64,1024]{1,0:T(8,128)(2,1)S(1)}, bf16[64,1024]{1,0:T(8,128)(2,1)S(1)}, bf16[64,1024]{1,0:T(8,128)(2,1)S(1)}, f32[64,1024]{1,0:T(8,128)S(1)}) fusion(bf16[256,1024]{1,0:T(8,128)(2,1)} %collective-permute-done.16, bf16[256,1024]{1,0:T(8,128)(2,1)} %collective-permute-done.15, bf16[256,1024]{1,0:T(8,128)(2,1)} %collective-permute-done.14, ...), kind=kLoop, calls=%fused_computation.15 | loop fusion | flops 2031616 | bytes 2752512 | tf_op jit(solution)/shard_map/convert
  79.8 1.4 copy-done.1
  81.2 2.3 %shard_map.63 = f32[256,256]{1,0:T(8,128)} custom-call(bf16[1024,512]{1,0:T(8,128)(2,1)} %bitcast.6.slots_ref, bf16[256,1024]{1,0:T(8,128)(2,1)} %get-tuple-element.21.after_ref, bf16[2048,512]{1,0:T(8,128)(2,1)} %copy-done.1), custom_call_target="tpu_custom_call" | custom-call | flops 134217728 | bytes 3932160 | tf_op jit(solution)/shard_map/pallas_call | solution.py:43
  84.5 6.4 %shard_map.65 = (bf16[256,1024]{1,0:T(8,128)(2,1)}, bf16[256,1024]{1,0:T(8,128)(2,1)}, bf16[256,1024]{1,0:T(8,128)(2,1)}, bf16[256,1024]{1,0:T(8,128)(2,1)}) custom-call(s32[4]{0:T(128)} %pad_add_fusion.at_ref, bf16[2048,512]{1,0:T(8,128)(2,1)} %copy-done.1, bf16[2048,512]{1,0:T(8,128)(2,1)} %bitcast.16, ...), custom_call_target="tpu_custom_call" | custom-call | flops 2147483648 | bytes 8912912 | tf_op jit(solution)/shard_map/pallas_call | solution.py:43
  90.9 1.5 collective-permute-start.8
  92.3 2.7 %collective-permute-start.9 = (bf16[256,1024]{1,0:T(8,128)(2,1)}, bf16[256,1024]{1,0:T(8,128)(2,1)}, u32[]{:S(2)}, u32[]{:S(2)}) collective-permute-start(bf16[256,1024]{1,0:T(8,128)(2,1)} %get-tuple-element.29), channel_id=1, source_target_pairs={{0,8},{1,9},{2,10},{3,11},{4,12},{5,13},{6,14},{7,15},{8,0},{9,1},... | collective-permute-start | bytes 1572872 | tf_op jit(solution)/shard_map/ppermute | solution.py:30
  95.0 1.5 collective-permute-start.10
  96.5 0.9 collective-permute-start.3
  97.4 6.4 %shard_map.67 = (bf16[256,1024]{1,0:T(8,128)(2,1)}, bf16[256,1024]{1,0:T(8,128)(2,1)}, bf16[256,1024]{1,0:T(8,128)(2,1)}, bf16[256,1024]{1,0:T(8,128)(2,1)}) custom-call(s32[4]{0:T(128)} %pad_add_fusion.at_ref, bf16[2048,512]{1,0:T(8,128)(2,1)} %copy-done.1, bf16[2048,512]{1,0:T(8,128)(2,1)} %bitcast.17, ...), custom_call_target="tpu_custom_call" | custom-call | flops 2147483648 | bytes 8912912 | tf_op jit(solution)/shard_map/pallas_call | solution.py:43
  103.8 1.5 collective-permute-start.17
  105.3 1.8 %collective-permute-start.18 = (bf16[256,1024]{1,0:T(8,128)(2,1)}, bf16[256,1024]{1,0:T(8,128)(2,1)}, u32[]{:S(2)}, u32[]{:S(2)}) collective-permute-start(bf16[256,1024]{1,0:T(8,128)(2,1)} %get-tuple-element.36), channel_id=1, source_target_pairs={{0,32},{1,33},{2,34},{3,35},{4,36},{5,37},{6,38},{7,39},{8,40},{9,... | collective-permute-start | bytes 1572872 | tf_op jit(solution)/shard_map/ppermute | solution.py:30
  107.2 1.1 broadcast_in_dim.2
  108.2 3.7 %all-to-all-start.1 = ((bf16[16,2,64,256]{3,2,1,0:T(8,128)(2,1)}), bf16[16,2,64,256]{3,2,1,0:T(8,128)(2,1)S(1)}, u32[]{:S(2)}, u32[]{:S(2)}) async-start(bf16[16,2,64,256]{3,2,1,0:T(8,128)(2,1)} %broadcast_in_dim.2), calls=%async_computation.1 | async-start | bytes 2097152 | tf_op jit(solution)/shard_map/all_to_all | solution.py:171
  112.0 3.2 %collective-permute-start.19 = (bf16[256,1024]{1,0:T(8,128)(2,1)}, bf16[256,1024]{1,0:T(8,128)(2,1)S(1)}, u32[]{:S(2)}, u32[]{:S(2)}) collective-permute-start(bf16[256,1024]{1,0:T(8,128)(2,1)} %get-tuple-element.37), channel_id=1, source_target_pairs={{0,48},{1,49},{2,50},{3,51},{4,52},{5,53},{6,54},{7,55},{8,56},{9,... | collective-permute-start | bytes 1572872 | tf_op jit(solution)/shard_map/ppermute | solution.py:30
  115.1 4.2 %collective-permute-done.9 = bf16[256,1024]{1,0:T(8,128)(2,1)} collective-permute-done((bf16[256,1024]{1,0:T(8,128)(2,1)}, bf16[256,1024]{1,0:T(8,128)(2,1)}, u32[]{:S(2)}, u32[]{:S(2)}) %collective-permute-start.9) | collective-permute-done | bytes 524320 | tf_op jit(solution)/shard_map/ppermute | solution.py:30
  119.3 2.0 %add_convert_fusion.6 = (bf16[64,1024]{1,0:T(8,128)(2,1)S(1)}, bf16[64,1024]{1,0:T(8,128)(2,1)S(1)}, bf16[64,1024]{1,0:T(8,128)(2,1)S(1)}, f32[64,1024]{1,0:T(8,128)S(1)}) fusion(bf16[256,1024]{1,0:T(8,128)(2,1)} %collective-permute-done.10, bf16[256,1024]{1,0:T(8,128)(2,1)} %collective-permute-done.9, bf16[256,1024]{1,0:T(8,128)(2,1)} %copy-done.10, ...), kind=kLoop, calls=%fused_computation.22 | loop fusion | flops 2031616 | bytes 2752512 | tf_op jit(solution)/shard_map/convert.7
  121.3 1.6 collective-permute-start.11
  123.7 1.9 %collective-permute-start.12 = (bf16[128,1024]{1,0:T(8,128)(2,1)}, bf16[128,1024]{1,0:T(8,128)(2,1)}, u32[]{:S(2)}, u32[]{:S(2)}) collective-permute-start(bf16[128,1024]{1,0:T(8,128)(2,1)} %pad_maximum_fusion.4), channel_id=1, source_target_pairs={{0,32},{1,33},{2,34},{3,35},{4,36},{5,37},{6,38},{7,39},{8,40},{9,... | collective-permute-start | bytes 786440 | tf_op jit(solution)/shard_map/ppermute | solution.py:30
  126.2 13.8 %collective-permute-done.17 = bf16[256,1024]{1,0:T(8,128)(2,1)S(1)} collective-permute-done((bf16[256,1024]{1,0:T(8,128)(2,1)}, bf16[256,1024]{1,0:T(8,128)(2,1)S(1)}, u32[]{:S(2)}, u32[]{:S(2)}) %collective-permute-start.17) | collective-permute-done | bytes 524320 | tf_op jit(solution)/shard_map/ppermute | solution.py:30
  140.1 3.4 %collective-permute-done.19 = bf16[256,1024]{1,0:T(8,128)(2,1)S(1)} collective-permute-done((bf16[256,1024]{1,0:T(8,128)(2,1)}, bf16[256,1024]{1,0:T(8,128)(2,1)S(1)}, u32[]{:S(2)}, u32[]{:S(2)}) %collective-permute-start.19) | collective-permute-done | bytes 524320 | tf_op jit(solution)/shard_map/ppermute | solution.py:30
  143.5 1.4 add_convert_fusion
  146.3 4.4 %collective-permute-start.21 = (bf16[128,1024]{1,0:T(8,128)(2,1)}, bf16[128,1024]{1,0:T(8,128)(2,1)S(1)}, u32[]{:S(2)}, u32[]{:S(2)}) collective-permute-start(bf16[128,1024]{1,0:T(8,128)(2,1)} %pad_maximum_fusion.7), channel_id=1, source_target_pairs={{0,8},{1,9},{2,10},{3,11},{4,12},{5,13},{6,14},{7,15},{8,0},{9,1},... | collective-permute-start | bytes 786440 | tf_op jit(solution)/shard_map/ppermute | solution.py:30
  150.7 2.7 %collective-permute-start.22 = (bf16[128,1024]{1,0:T(8,128)(2,1)S(1)}, bf16[128,1024]{1,0:T(8,128)(2,1)S(1)}, u32[]{:S(2)}, u32[]{:S(2)}) collective-permute-start(bf16[128,1024]{1,0:T(8,128)(2,1)S(1)} %pad_maximum_fusion.8), channel_id=1, source_target_pairs={{0,12},{1,13},{2,14},{3,15},{4,0},{5,1},{6,2},{7,3},{8,4},{9,5},{1... | collective-permute-start | bytes 786440 | tf_op jit(solution)/shard_map/ppermute | solution.py:30
  155.1 1.0 copy-done.5
  156.0 4.8 %shard_map.64 = (f32[512,256]{1,0:T(8,128)}, f32[512,256]{1,0:T(8,128)}) custom-call(s32[4]{0:T(128)} %pad_add_fusion.at_ref, bf16[16,2,64,256]{3,2,1,0:T(8,128)(2,1)} %copy-done.5, bf16[2048,512]{1,0:T(8,128)(2,1)} %shard_map.59.a_ref.after_ref.own_ref, bf16[2048,512]{1,0:T(8,128)(2,1)} %copy-done.1), custom_call_target="tpu_custom_call" | custom-call | flops 1073741824 | bytes 6291472 | tf_op jit(solution)/shard_map/pallas_call | solution.py:43
  160.9 2.2 %shard_map.66 = f32[128,1024]{1,0:T(8,128)} custom-call(f32[128,1024]{1,0:T(8,128)} %pad_maximum_fusion.1.mine_ref, bf16[128,1024]{1,0:T(8,128)(2,1)} %copy-done.14, bf16[128,1024]{1,0:T(8,128)(2,1)} %collective-permute-done.12.g2_ref, bf16[128,1024]{1,0:T(8,128)(2,1)} %collective-permute-done.13.g3_ref, f32[512,256]{1,0:T(8,128)} %get-tuple-element.22.after_ref), custom_call_target="tpu_custom_call" | custom-call | bytes 2359296 | tf_op jit(solution)/shard_map/pallas_call | solution.py:43
  164.5 2.2 %shard_map.68 = f32[128,1024]{1,0:T(8,128)} custom-call(f32[128,1024]{1,0:T(8,128)} %pad_maximum_fusion.2.mine_ref, bf16[128,1024]{1,0:T(8,128)(2,1)} %copy-done.15, bf16[128,1024]{1,0:T(8,128)(2,1)} %copy-done.16, bf16[128,1024]{1,0:T(8,128)(2,1)} %copy-done.17, f32[512,256]{1,0:T(8,128)} %get-tuple-element.22.after_ref), custom_call_target="tpu_custom_call" | custom-call | bytes 2359296 | tf_op jit(solution)/shard_map/pallas_call | solution.py:43
  166.7 1.1 select_convert_fusion
  168.6 5.7 %collective-permute-done.23 = bf16[64,2048]{1,0:T(8,128)(2,1)S(1)} collective-permute-done((bf16[64,2048]{1,0:T(8,128)(2,1)S(1)}, bf16[64,2048]{1,0:T(8,128)(2,1)S(1)}, u32[]{:S(2)}, u32[]{:S(2)}) %collective-permute-start.23) | collective-permute-done | bytes 262176 | tf_op jit(solution)/shard_map/ppermute | solution.py:30
  174.3 1.9 %multiply_add_fusion = f32[64,2048]{1,0:T(8,128)} fusion(bf16[64,2048]{1,0:T(8,128)(2,1)S(1)} %collective-permute-done.23, f32[64,2048]{1,0:T(8,128)S(1)} %copy-done.7, pred[]{:T(512)S(6)} %eq.4, f32[128,1024]{1,0:T(8,128)} %shard_map.68, f32[128,1024]{1,0:T(8,128)S(1)} %copy-done.2), kind=kLoop, calls=%fused_computation.6 | loop fusion | flops 1048576 | bytes 2359297 | tf_op jit(solution)/shard_map/add | solution.py:190
  (73 shorter events, 9.6 us)
Async XLA Ops:
  3.5 4.4 %copy-start = (bf16[512,2048]{0,1:T(8,128)(2,1)}, bf16[512,2048]{0,1:T(8,128)(2,1)S(1)}, u32[]{:S(2)}) copy-start(bf16[512,2048]{0,1:T(8,128)(2,1)S(1)} %copy.6) | copy-start | bytes 6291460
  3.5 4.4 %collective-permute-start = (bf16[2048,512]{1,0:T(8,128)(2,1)S(1)}, bf16[2048,512]{1,0:T(8,128)(2,1)}, u32[]{:S(2)}, u32[]{:S(2)}) collective-permute-start(bf16[2048,512]{1,0:T(8,128)(2,1)S(1)} %bitcast.12), channel_id=1, source_target_pairs={{0,2},{1,3},{2,0},{3,1},{4,6},{5,7},{6,4},{7,5},{8,10},{9,11},{10,... | collective-permute-start | bytes 6291464 | tf_op jit(solution)/shard_map/ppermute | solution.py:30
  11.6 68.2 %collective-permute-start.1 = (bf16[2048,512]{1,0:T(8,128)(2,1)}, bf16[2048,512]{1,0:T(8,128)(2,1)S(1)}, u32[]{:S(2)}, u32[]{:S(2)}) collective-permute-start(bf16[2048,512]{1,0:T(8,128)(2,1)} %shard_map.59.a_ref.after_ref.own_ref), channel_id=1, source_target_pairs={{0,1},{1,0},{2,3},{3,2},{4,5},{5,4},{6,7},{7,6},{8,9},{9,8},{10,11... | collective-permute-start | bytes 6291464 | tf_op jit(solution)/shard_map/ppermute | solution.py:30
  21.3 21.8 %collective-permute-start.5 = (bf16[256,1024]{1,0:T(8,128)(2,1)}, bf16[256,1024]{1,0:T(8,128)(2,1)}, u32[]{:S(2)}, u32[]{:S(2)}) collective-permute-start(bf16[256,1024]{1,0:T(8,128)(2,1)} %get-tuple-element.24), channel_id=1, source_target_pairs={{0,4},{1,5},{2,6},{3,7},{4,8},{5,9},{6,10},{7,11},{8,12},{9,13},{1... | collective-permute-start | bytes 1572872 | tf_op jit(solution)/shard_map/ppermute | solution.py:30
  22.8 27.2 %collective-permute-start.6 = (bf16[256,1024]{1,0:T(8,128)(2,1)}, bf16[256,1024]{1,0:T(8,128)(2,1)}, u32[]{:S(2)}, u32[]{:S(2)}) collective-permute-start(bf16[256,1024]{1,0:T(8,128)(2,1)} %get-tuple-element.25), channel_id=1, source_target_pairs={{0,8},{1,9},{2,10},{3,11},{4,12},{5,13},{6,14},{7,15},{8,0},{9,1},... | collective-permute-start | bytes 1572872 | tf_op jit(solution)/shard_map/ppermute | solution.py:30
  25.5 28.5 %collective-permute-start.7 = (bf16[256,1024]{1,0:T(8,128)(2,1)}, bf16[256,1024]{1,0:T(8,128)(2,1)}, u32[]{:S(2)}, u32[]{:S(2)}) collective-permute-start(bf16[256,1024]{1,0:T(8,128)(2,1)} %get-tuple-element.26), channel_id=1, source_target_pairs={{0,12},{1,13},{2,14},{3,15},{4,0},{5,1},{6,2},{7,3},{8,4},{9,5},{1... | collective-permute-start | bytes 1572872 | tf_op jit(solution)/shard_map/ppermute | solution.py:30
  33.5 20.6 %copy-start.9 = (bf16[256,1024]{1,0:T(8,128)(2,1)S(1)}, bf16[256,1024]{1,0:T(8,128)(2,1)}, u32[]{:S(2)}) copy-start(bf16[256,1024]{1,0:T(8,128)(2,1)} %get-tuple-element.20.after_ref) | copy-start | bytes 1572868
  35.6 42.3 %copy-start.3 = (bf16[256,1024]{1,0:T(8,128)(2,1)S(1)}, bf16[256,1024]{1,0:T(8,128)(2,1)}, u32[]{:S(2)}) copy-start(bf16[256,1024]{1,0:T(8,128)(2,1)} %get-tuple-element.21.after_ref) | copy-start | bytes 1572868
  35.6 44.1 %all-to-all-start = ((bf16[16,64,512]{2,1,0:T(8,128)(2,1)}), bf16[16,64,512]{2,1,0:T(8,128)(2,1)}, u32[]{:S(2)}, u32[]{:S(2)}) async-start(bf16[16,64,512]{2,1,0:T(8,128)(2,1)} %shard_map.62), calls=%async_computation | async-start | bytes 2097152 | tf_op jit(solution)/shard_map/all_to_all | solution.py:158
  41.3 27.3 %collective-permute-start.14 = (bf16[256,1024]{1,0:T(8,128)(2,1)}, bf16[256,1024]{1,0:T(8,128)(2,1)}, u32[]{:S(2)}, u32[]{:S(2)}) collective-permute-start(bf16[256,1024]{1,0:T(8,128)(2,1)} %get-tuple-element.31), channel_id=1, source_target_pairs={{0,16},{1,17},{2,18},{3,19},{4,20},{5,21},{6,22},{7,23},{8,24},{9,... | collective-permute-start | bytes 1572872 | tf_op jit(solution)/shard_map/ppermute | solution.py:30
  43.2 34.8 %collective-permute-start.15 = (bf16[256,1024]{1,0:T(8,128)(2,1)}, bf16[256,1024]{1,0:T(8,128)(2,1)}, u32[]{:S(2)}, u32[]{:S(2)}) collective-permute-start(bf16[256,1024]{1,0:T(8,128)(2,1)} %get-tuple-element.32), channel_id=1, source_target_pairs={{0,32},{1,33},{2,34},{3,35},{4,36},{5,37},{6,38},{7,39},{8,40},{9,... | collective-permute-start | bytes 1572872 | tf_op jit(solution)/shard_map/ppermute | solution.py:30
  50.0 28.0 %collective-permute-start.16 = (bf16[256,1024]{1,0:T(8,128)(2,1)}, bf16[256,1024]{1,0:T(8,128)(2,1)}, u32[]{:S(2)}, u32[]{:S(2)}) collective-permute-start(bf16[256,1024]{1,0:T(8,128)(2,1)} %get-tuple-element.33), channel_id=1, source_target_pairs={{0,48},{1,49},{2,50},{3,51},{4,52},{5,53},{6,54},{7,55},{8,56},{9,... | collective-permute-start | bytes 1572872 | tf_op jit(solution)/shard_map/ppermute | solution.py:30
  79.8 1.4 copy-start.1
  84.4 12.1 %copy-start.6 = (f32[256,256]{1,0:T(8,128)S(1)}, f32[256,256]{1,0:T(8,128)}, u32[]{:S(2)}) copy-start(f32[256,256]{1,0:T(8,128)} %shard_map.63) | copy-start | bytes 786436
  84.4 12.1 %collective-permute-start.2 = (f32[2,64,256]{2,1,0:T(8,128)S(1)}, f32[2,64,256]{2,1,0:T(8,128)S(1)}, u32[]{:S(2)}, u32[]{:S(2)}) collective-permute-start(f32[2,64,256]{2,1,0:T(8,128)S(1)} %dynamic-slice_bitcast_fusion), channel_id=1, source_target_pairs={{0,2},{1,3},{2,0},{3,1},{4,6},{5,7},{6,4},{7,5},{8,10},{9,11},{10,... | collective-permute-start | bytes 393224 | tf_op jit(solution)/shard_map/ppermute | solution.py:30
  90.9 21.1 %collective-permute-start.8 = (bf16[256,1024]{1,0:T(8,128)(2,1)}, bf16[256,1024]{1,0:T(8,128)(2,1)S(1)}, u32[]{:S(2)}, u32[]{:S(2)}) collective-permute-start(bf16[256,1024]{1,0:T(8,128)(2,1)} %get-tuple-element.28), channel_id=1, source_target_pairs={{0,4},{1,5},{2,6},{3,7},{4,8},{5,9},{6,10},{7,11},{8,12},{9,13},{1... | collective-permute-start | bytes 1572872 | tf_op jit(solution)/shard_map/ppermute | solution.py:30
  92.3 27.0 %collective-permute-start.9 = (bf16[256,1024]{1,0:T(8,128)(2,1)}, bf16[256,1024]{1,0:T(8,128)(2,1)}, u32[]{:S(2)}, u32[]{:S(2)}) collective-permute-start(bf16[256,1024]{1,0:T(8,128)(2,1)} %get-tuple-element.29), channel_id=1, source_target_pairs={{0,8},{1,9},{2,10},{3,11},{4,12},{5,13},{6,14},{7,15},{8,0},{9,1},... | collective-permute-start | bytes 1572872 | tf_op jit(solution)/shard_map/ppermute | solution.py:30
  95.0 24.3 %collective-permute-start.10 = (bf16[256,1024]{1,0:T(8,128)(2,1)}, bf16[256,1024]{1,0:T(8,128)(2,1)}, u32[]{:S(2)}, u32[]{:S(2)}) collective-permute-start(bf16[256,1024]{1,0:T(8,128)(2,1)} %get-tuple-element.30), channel_id=1, source_target_pairs={{0,12},{1,13},{2,14},{3,15},{4,0},{5,1},{6,2},{7,3},{8,4},{9,5},{1... | collective-permute-start | bytes 1572872 | tf_op jit(solution)/shard_map/ppermute | solution.py:30
  96.5 8.8 %collective-permute-start.3 = (f32[2,64,256]{2,1,0:T(8,128)S(1)}, f32[2,64,256]{2,1,0:T(8,128)S(1)}, u32[]{:S(2)}, u32[]{:S(2)}) collective-permute-start(f32[2,64,256]{2,1,0:T(8,128)S(1)} %bitcast_add_fusion), channel_id=1, source_target_pairs={{0,64},{1,65},{2,66},{3,67},{4,68},{5,69},{6,70},{7,71},{8,72},{9,... | collective-permute-start | bytes 393224 | tf_op jit(solution)/shard_map/ppermute | solution.py:30
  103.8 36.2 %collective-permute-start.17 = (bf16[256,1024]{1,0:T(8,128)(2,1)}, bf16[256,1024]{1,0:T(8,128)(2,1)S(1)}, u32[]{:S(2)}, u32[]{:S(2)}) collective-permute-start(bf16[256,1024]{1,0:T(8,128)(2,1)} %get-tuple-element.35), channel_id=1, source_target_pairs={{0,16},{1,17},{2,18},{3,19},{4,20},{5,21},{6,22},{7,23},{8,24},{9,... | collective-permute-start | bytes 1572872 | tf_op jit(solution)/shard_map/ppermute | solution.py:30
  105.3 34.7 %collective-permute-start.18 = (bf16[256,1024]{1,0:T(8,128)(2,1)}, bf16[256,1024]{1,0:T(8,128)(2,1)}, u32[]{:S(2)}, u32[]{:S(2)}) collective-permute-start(bf16[256,1024]{1,0:T(8,128)(2,1)} %get-tuple-element.36), channel_id=1, source_target_pairs={{0,32},{1,33},{2,34},{3,35},{4,36},{5,37},{6,38},{7,39},{8,40},{9,... | collective-permute-start | bytes 1572872 | tf_op jit(solution)/shard_map/ppermute | solution.py:30
  108.2 46.8 %all-to-all-start.1 = ((bf16[16,2,64,256]{3,2,1,0:T(8,128)(2,1)}), bf16[16,2,64,256]{3,2,1,0:T(8,128)(2,1)S(1)}, u32[]{:S(2)}, u32[]{:S(2)}) async-start(bf16[16,2,64,256]{3,2,1,0:T(8,128)(2,1)} %broadcast_in_dim.2), calls=%async_computation.1 | async-start | bytes 2097152 | tf_op jit(solution)/shard_map/all_to_all | solution.py:171
  111.9 9.4 %copy-start.13 = (bf16[64,1024]{1,0:T(8,128)(2,1)S(1)}, bf16[64,1024]{1,0:T(8,128)(2,1)}, u32[]{:S(2)}) copy-start(bf16[64,1024]{1,0:T(8,128)(2,1)} %get-tuple-element.40) | copy-start | bytes 393220
  111.9 11.0 %copy-start.12 = (bf16[64,1024]{1,0:T(8,128)(2,1)S(1)}, bf16[64,1024]{1,0:T(8,128)(2,1)}, u32[]{:S(2)}) copy-start(bf16[64,1024]{1,0:T(8,128)(2,1)} %get-tuple-element.39) | copy-start | bytes 393220
  111.9 13.6 %copy-start.11 = (bf16[64,1024]{1,0:T(8,128)(2,1)S(1)}, bf16[64,1024]{1,0:T(8,128)(2,1)}, u32[]{:S(2)}) copy-start(bf16[64,1024]{1,0:T(8,128)(2,1)} %get-tuple-element.38) | copy-start | bytes 393220
  111.9 7.4 %copy-start.10 = (bf16[256,1024]{1,0:T(8,128)(2,1)}, bf16[256,1024]{1,0:T(8,128)(2,1)S(1)}, u32[]{:S(2)}) copy-start(bf16[256,1024]{1,0:T(8,128)(2,1)S(1)} %collective-permute-done.8) | copy-start | bytes 1572868
  112.0 31.5 %copy-start.8 = (bf16[256,1024]{1,0:T(8,128)(2,1)S(1)}, bf16[256,1024]{1,0:T(8,128)(2,1)}, u32[]{:S(2)}) copy-start(bf16[256,1024]{1,0:T(8,128)(2,1)} %get-tuple-element.34) | copy-start | bytes 1572868
  112.0 31.5 %collective-permute-start.19 = (bf16[256,1024]{1,0:T(8,128)(2,1)}, bf16[256,1024]{1,0:T(8,128)(2,1)S(1)}, u32[]{:S(2)}, u32[]{:S(2)}) collective-permute-start(bf16[256,1024]{1,0:T(8,128)(2,1)} %get-tuple-element.37), channel_id=1, source_target_pairs={{0,48},{1,49},{2,50},{3,51},{4,52},{5,53},{6,54},{7,55},{8,56},{9,... | collective-permute-start | bytes 1572872 | tf_op jit(solution)/shard_map/ppermute | solution.py:30
  121.3 29.3 %collective-permute-start.11 = (bf16[128,1024]{1,0:T(8,128)(2,1)S(1)}, bf16[128,1024]{1,0:T(8,128)(2,1)S(1)}, u32[]{:S(2)}, u32[]{:S(2)}) collective-permute-start(bf16[128,1024]{1,0:T(8,128)(2,1)S(1)} %pad_maximum_fusion.3), channel_id=1, source_target_pairs={{0,16},{1,17},{2,18},{3,19},{4,20},{5,21},{6,22},{7,23},{8,24},{9,... | collective-permute-start | bytes 786440 | tf_op jit(solution)/shard_map/ppermute | solution.py:30
  123.7 37.2 %collective-permute-start.12 = (bf16[128,1024]{1,0:T(8,128)(2,1)}, bf16[128,1024]{1,0:T(8,128)(2,1)}, u32[]{:S(2)}, u32[]{:S(2)}) collective-permute-start(bf16[128,1024]{1,0:T(8,128)(2,1)} %pad_maximum_fusion.4), channel_id=1, source_target_pairs={{0,32},{1,33},{2,34},{3,35},{4,36},{5,37},{6,38},{7,39},{8,40},{9,... | collective-permute-start | bytes 786440 | tf_op jit(solution)/shard_map/ppermute | solution.py:30
  140.0 20.8 %collective-permute-start.13 = (bf16[128,1024]{1,0:T(8,128)(2,1)}, bf16[128,1024]{1,0:T(8,128)(2,1)}, u32[]{:S(2)}, u32[]{:S(2)}) collective-permute-start(bf16[128,1024]{1,0:T(8,128)(2,1)} %pad_maximum_fusion.5), channel_id=1, source_target_pairs={{0,48},{1,49},{2,50},{3,51},{4,52},{5,53},{6,54},{7,55},{8,56},{9,... | collective-permute-start | bytes 786440 | tf_op jit(solution)/shard_map/ppermute | solution.py:30
  145.0 18.1 %collective-permute-start.20 = (bf16[128,1024]{1,0:T(8,128)(2,1)S(1)}, bf16[128,1024]{1,0:T(8,128)(2,1)S(1)}, u32[]{:S(2)}, u32[]{:S(2)}) collective-permute-start(bf16[128,1024]{1,0:T(8,128)(2,1)S(1)} %pad_maximum_fusion.6), channel_id=1, source_target_pairs={{0,4},{1,5},{2,6},{3,7},{4,8},{5,9},{6,10},{7,11},{8,12},{9,13},{1... | collective-permute-start | bytes 786440 | tf_op jit(solution)/shard_map/ppermute | solution.py:30
  146.3 16.7 %collective-permute-start.21 = (bf16[128,1024]{1,0:T(8,128)(2,1)}, bf16[128,1024]{1,0:T(8,128)(2,1)S(1)}, u32[]{:S(2)}, u32[]{:S(2)}) collective-permute-start(bf16[128,1024]{1,0:T(8,128)(2,1)} %pad_maximum_fusion.7), channel_id=1, source_target_pairs={{0,8},{1,9},{2,10},{3,11},{4,12},{5,13},{6,14},{7,15},{8,0},{9,1},... | collective-permute-start | bytes 786440 | tf_op jit(solution)/shard_map/ppermute | solution.py:30
  150.7 3.5 %copy-start.14 = (bf16[128,1024]{1,0:T(8,128)(2,1)}, bf16[128,1024]{1,0:T(8,128)(2,1)S(1)}, u32[]{:S(2)}) copy-start(bf16[128,1024]{1,0:T(8,128)(2,1)S(1)} %collective-permute-done.11.g1_ref) | copy-start | bytes 786436
  150.7 12.4 %collective-permute-start.22 = (bf16[128,1024]{1,0:T(8,128)(2,1)S(1)}, bf16[128,1024]{1,0:T(8,128)(2,1)S(1)}, u32[]{:S(2)}, u32[]{:S(2)}) collective-permute-start(bf16[128,1024]{1,0:T(8,128)(2,1)S(1)} %pad_maximum_fusion.8), channel_id=1, source_target_pairs={{0,12},{1,13},{2,14},{3,15},{4,0},{5,1},{6,2},{7,3},{8,4},{9,5},{1... | collective-permute-start | bytes 786440 | tf_op jit(solution)/shard_map/ppermute | solution.py:30
  155.1 1.0 copy-start.5
  163.0 3.7 %copy-start.2 = (f32[128,1024]{1,0:T(8,128)S(1)}, f32[128,1024]{1,0:T(8,128)}, u32[]{:S(2)}) copy-start(f32[128,1024]{1,0:T(8,128)} %shard_map.66) | copy-start | bytes 1572868
  163.0 5.6 %copy-start.18 = (f32[512,256]{1,0:T(8,128)S(1)}, f32[512,256]{1,0:T(8,128)}, u32[]{:S(2)}) copy-start(f32[512,256]{1,0:T(8,128)} %get-tuple-element.23) | copy-start | bytes 1572868
  163.0 11.3 %copy-start.7 = (f32[64,2048]{1,0:T(8,128)S(1)}, f32[64,2048]{1,0:T(8,128)}, u32[]{:S(2)}) copy-start(f32[64,2048]{1,0:T(8,128)} %param.5) | copy-start | bytes 1572868
  163.0 0.7 copy-start.15
  163.1 0.8 copy-start.16
  163.8 0.7 copy-start.17
  166.7 9.5 %copy-start.4 = (f32[512,256]{1,0:T(8,128)S(1)}, f32[512,256]{1,0:T(8,128)}, u32[]{:S(2)}) copy-start(f32[512,256]{1,0:T(8,128)} %get-tuple-element.22.after_ref) | copy-start | bytes 1572868
  167.9 6.5 %collective-permute-start.23 = (bf16[64,2048]{1,0:T(8,128)(2,1)S(1)}, bf16[64,2048]{1,0:T(8,128)(2,1)S(1)}, u32[]{:S(2)}, u32[]{:S(2)}) collective-permute-start(bf16[64,2048]{1,0:T(8,128)(2,1)S(1)} %select_convert_fusion), channel_id=1, source_target_pairs={{0,64},{1,65},{2,66},{3,67},{4,68},{5,69},{6,70},{7,71},{8,72},{9,... | collective-permute-start | bytes 786440 | tf_op jit(solution)/shard_map/ppermute | solution.py:30
  168.6 7.6 %collective-permute-start.4 = (f32[512,256]{1,0:T(8,128)S(1)}, f32[512,256]{1,0:T(8,128)S(1)}, u32[]{:S(2)}, u32[]{:S(2)}) collective-permute-start(f32[512,256]{1,0:T(8,128)S(1)} %copy-done.18), channel_id=1, source_target_pairs={{0,2},{1,3},{2,0},{3,1},{4,6},{5,7},{6,4},{7,5},{8,10},{9,11},{10,... | collective-permute-start | bytes 1572872 | tf_op jit(solution)/shard_map/ppermute | solution.py:30

commit v8 on v5

--- a/solution.py
+++ b/solution.py
@@ -68,6 +68,24 @@
         for b in range(16):
             start = pl.ds(pl.multiple_of(b * 128 + at_ref[2], 64), 64)
             out_ref[(16 * i + b) * 64 : (16 * i + b + 1) * 64, :] = ref[start, :]
+
+
+def own_kernel(a_ref, b1_ref, b2_ref, out_ref):
+    rows = out_ref.shape[1]
+    wide = 2 * rows
+    for g in range(4):
+        left1 = a_ref[4 * g * rows : 4 * (g + 1) * rows, :]
+        left2 = a_ref[(16 + 4 * g) * rows : (20 + 4 * g) * rows, :]
+        for q in range(3):
+            cols = pl.ds((g + q) % 4 * 4 * wide, 4 * wide)
+            acc = lax.dot_general(left1, b1_ref[cols, :], NT, preferred_element_type=f32)
+            acc += lax.dot_general(left2, b2_ref[cols, :], NT, preferred_element_type=f32)
+            acc = acc.astype(bf16)
+            for i in range(4):
+                lo, hi = max(4 * q, i), min(4 * q + 4, i + 9)
+                if lo < hi:
+                    piece = acc[i * rows : (i + 1) * rows, (lo - 4 * q) * wide : (hi - 4 * q) * wide]
+                    out_ref[4 * g + i, :, (lo - i) * wide : (hi - i) * wide] = piece
 
 
 def gram_kernel(at_ref, a_ref, b1_ref, b2_ref, after_ref, *outs):
@@ -113,11 +131,7 @@
         out_ref[...] = acc + lax.dot_general(cross_ref[s, :], p_cross, TN, preferred_element_type=f32)
 
 
-def sum_kernel(mine_ref, g1_ref, g2_ref, g3_ref, after_ref, out_ref):
-    out_ref[...] = mine_ref[...] + g1_ref[...].astype(f32) + g2_ref[...].astype(f32) + g3_ref[...].astype(f32)
-
-
-def scatter_sum(parts, rows, after=None):
+def scatter_sum(parts, rows):
     got, mids, sums = [], [], []
     for half, axis in ((0, "x"), (1, "z")):
         got.append([send(parts[4 * half + k], along(axis, k)) for k in (1, 2, 3)])
@@ -131,12 +145,33 @@
             mids[half].append(total)
     for half, axis in ((0, "z"), (1, "x")):
         rs = [send(mids[half][k].astype(bf16), along(axis, k)) for k in (1, 2, 3)]
-        if after is not None:
-            out = jax.ShapeDtypeStruct(mids[half][0].shape, f32)
-            sums.append(kernel_call(sum_kernel, [out], [VMEM] * 4 + [ANY], mids[half][0], *rs, after)[0])
-        else:
-            sums.append(mids[half][0] + rs[0].astype(f32) + rs[1].astype(f32) + rs[2].astype(f32))
+        sums.append(mids[half][0] + rs[0].astype(f32) + rs[1].astype(f32) + rs[2].astype(f32))
     return jnp.concatenate(sums, axis=1)
+
+
+def own_sum_kernel(at_ref, got_ref, direct_ref, mirror_ref):
+    chip = at_ref[0] * 4 + at_ref[1]
+    wide = mirror_ref.shape[2]
+    direct_ref[...] = jnp.zeros_like(direct_ref)
+    mirror_ref[...] = jnp.zeros_like(mirror_ref)
+    for k in range(9):
+        total = jnp.sum(got_ref[:, :, k * wide : (k + 1) * wide].astype(f32), axis=0)
+        to = lax.rem(chip + k, 16)
+        direct_ref[:, pl.ds(pl.multiple_of(to * wide, wide), wide)] = total
+        mirror_ref[pl.ds(to, 1)] = total.astype(bf16)[None]
+
+
+def join_kernel(at_ref, direct_ref, held_ref, given_ref, out_ref):
+    chip = at_ref[0] * 4 + at_ref[1]
+    low = at_ref[2] == 0
+    rows = held_ref.shape[0]
+    for j in range(16):
+        mine = held_ref[:, j * rows : (j + 1) * rows].astype(f32)
+        other = given_ref[:, j * rows : (j + 1) * rows].astype(f32)
+        both = jnp.concatenate([jnp.where(low, mine, other), jnp.where(low, other, mine)], axis=1)
+        cols = slice(2 * j * rows, 2 * (j + 1) * rows)
+        near = lax.rem(j - chip + 16, 16) <= 8
+        out_ref[:, cols] = jnp.where(near, direct_ref[:, cols], both)
 
 
 def on_device(grads, covariance, test_grads, inverse_factor):
@@ -152,8 +187,14 @@
 
     (picked,) = kernel_call(pick_kernel, [shape((feats, tokens), bf16)], [SMEM, VMEM, VMEM], at, gt, sib)
     arrived = send(picked, flip("yh"))
-    own = gram(at, picked, gt, sib, picked)
-    cross = gram(at, arrived, gt, sib, own[0])
+    (own,) = kernel_call(
+        own_kernel,
+        [shape((16, rows, 18 * rows), bf16)],
+        [VMEM] * 3,
+        picked, gt, sib,
+        flops=3 * 16 * rows * feats * tokens,
+    )
+    cross = gram(at, arrived, gt, sib, own)
 
     (slots,) = kernel_call(
         slots_kernel,
@@ -166,7 +207,7 @@
         functools.partial(factor_kernel, 4 * rows),
         [shape((4 * rows, tests), f32)],
         [VMEM, ANY, ANY],
-        slots.reshape(16 * rows, -1), own[0], arrived,
+        slots.reshape(16 * rows, -1), own, arrived,
         flops=2 * 16 * rows * 4 * rows * tests,
     )
     pt = pt.reshape(2, 2, rows, tests)
@@ -185,12 +226,25 @@
     )
     scores = keep + send(give, flip("c"))
 
-    own = scatter_sum(own, rows)
-    own = own + send(own.astype(bf16), flip("yl"), lambda at: at["yl"] != at["yh"]).astype(f32)
-    cross = scatter_sum(cross, rows, keep)
-    cross = cross + send(cross.astype(bf16), flip("yl"), lambda at: at["yl"] == at["yh"]).astype(f32)
-    examples = tokens * 64
-    covariance_out = 0.9 * covariance + jnp.where(yl == h, own, cross) / examples
+    own = lax.all_to_all(own, ("z", "x"), split_axis=0, concat_axis=0, tiled=True)
+    direct, mirror = kernel_call(
+        own_sum_kernel,
+        [shape((rows, feats), f32), shape((16, rows, 2 * rows), bf16)],
+        [SMEM, VMEM],
+        at, own,
+    )
+    mirror = lax.all_to_all(mirror, ("z", "x"), split_axis=0, concat_axis=0, tiled=True)
+    mirror = mirror.reshape(16 * rows, 2 * rows).T
+    held = lax.dynamic_slice_in_dim(mirror, c * rows, rows, 0)
+    given = send(lax.dynamic_slice_in_dim(mirror, (1 - c) * rows, rows, 0), flip("c"))
+    (own,) = kernel_call(
+        join_kernel, [shape((rows, feats), f32)], [SMEM] + [VMEM] * 3, at, direct, held, given
+    )
+
+    cross = scatter_sum(cross, rows)
+    ours, theirs = jnp.where(yl == h, own, cross), jnp.where(yl == h, cross, own)
+    term = ours + send(theirs.astype(bf16), flip("yl")).astype(f32)
+    covariance_out = 0.9 * covariance + term / (tokens * 64)
     return scores, covariance_out
 
 

time: 178 us -> 173 us (0.972)
  waiting for transfers between devices: 44.6 us -> 65.7 us
  starting transfers between devices: 70.5 us -> 51.7 us
  other arithmetic: 16.1 us -> 7.86 us
    ppermute x31 -> x19, starting transfers between devices: 48.4 us -> 27.7 us  [send(): return lax.ppermute(value, AXES, pairs)]
    all_to_all x0 -> x2, waiting for transfers between devices: none -> 11.4 us  [the longest x1 11.4 us: on_device(): lax.all_to_all(mirror, ('z', 'x'), split_axis=0, concat_axis=0, tiled=True)]
    all_to_all x0 -> x2, starting transfers between devices: none -> 9.35 us  [the longest x1 4.71 us: on_device(): lax.all_to_all(own, ('z', 'x'), split_axis=0, concat_axis=0, tiled=True)]
    all_to_all x1, starting transfers between devices: 14.2 us -> 6.66 us  [on_device(): pt = lax.all_to_all(pt, ('z', 'x'), split_axis=0, concat_axis=0, tiled=True)]
    ppermute x31 -> x19, waiting for transfers between devices: 44.6 us -> 51.7 us  [send(): return lax.ppermute(value, AXES, pairs)]
    convert_element_type x4 -> x2, other arithmetic: 8.94 us -> 3.09 us  [scatter_sum(): rs = [send(mids[half][k].astype(bf16), along(axis, k)) for k in (1, 2, 3)]]
    all_to_all x1, waiting for transfers between devices: 0.01 us -> 2.5 us  [on_device(): lax.all_to_all(slots, ('z', 'x'), split_axis=0, concat_axis=0, tiled=True)]
    unnamed x43 -> x29, local copies, waits for them, and re-layouts: 6.25 us -> 7.25 us
  transfers between devices with their start and end apart: 33 -> 23, of which waited for: 9 -> 9; matrix products, arithmetic and copies ran while one was open for 10% -> 6% of each run, Pallas kernels for 18% -> 21%
where the time goes in v8:
time: 173 us; the launch traced here: 171 us
  waiting for transfers between devices  65.7 us (38%)
  starting transfers between devices  51.7 us (30%)
  Pallas kernels  35.1 us (20%)
  local copies, waits for them, and re-layouts  9.49 us (5%)
  other arithmetic  7.86 us (5%)
    ppermute x19, waiting for transfers between devices, send(): return lax.ppermute(value, AXES, pairs)  51.7 us
    pallas_call x8, Pallas kernels, kernel_call(): pl.pallas_call(body, out_shape=outs, in_specs=specs, out_specs=[VMEM] * l...  35.1 us
    ppermute x19, starting transfers between devices, send(): return lax.ppermute(value, AXES, pairs)  27.7 us
    all_to_all x1, waiting for transfers between devices, on_device(): lax.all_to_all(mirror, ('z', 'x'), split_axis=0, concat_axis=0, tiled=True)  11.4 us
    all_to_all x1, starting transfers between devices, on_device(): lax.all_to_all(slots, ('z', 'x'), split_axis=0, concat_axis=0, tiled=True)  7.96 us
    unnamed x29, local copies, waits for them, and re-layouts  7.25 us
    all_to_all x1, starting transfers between devices, on_device(): pt = lax.all_to_all(pt, ('z', 'x'), split_axis=0, concat_axis=0, tiled=True)  6.66 us
    all_to_all x1, starting transfers between devices, on_device(): lax.all_to_all(own, ('z', 'x'), split_axis=0, concat_axis=0, tiled=True)  4.71 us
  transfers between devices with their start and end apart: 23, of which 9 were waited for; matrix products, arithmetic and copies ran while one was open for 6% of the time, Pallas kernels for 21%

profile of v8, /device:TPU:0, one launch (start us, length us, event | category | flops | bytes accessed | tf_op | source)
XLA Modules:
  0.0 170.7 jit_solution(8834911710527562531)
XLA Ops:
  0.6 2.9 %copy.8 = bf16[512,2048]{0,1:T(8,128)(2,1)S(1)} copy(bf16[512,2048]{1,0:T(8,128)(2,1)} %param.4) | data formatting | bytes 4194304 | tf_op args[0]
  3.6 2.5 %shard_map.59 = bf16[16,64,512]{2,1,0:T(8,128)(2,1)} custom-call(bf16[64,4096]{1,0:T(8,128)(2,1)} %f_ref.1, bf16[64,256]{1,0:T(8,128)(2,1)} %bitcast.25), custom_call_target="tpu_custom_call" | custom-call | bytes 1605632 | tf_op jit(solution)/shard_map/pallas_call | solution.py:43
  6.1 8.0 %all-to-all-start = ((bf16[16,64,512]{2,1,0:T(8,128)(2,1)}), bf16[16,64,512]{2,1,0:T(8,128)(2,1)S(1)}, u32[]{:S(2)}, u32[]{:S(2)}) async-start(bf16[16,64,512]{2,1,0:T(8,128)(2,1)} %shard_map.59), calls=%async_computation | async-start | bytes 2097152 | tf_op jit(solution)/shard_map/all_to_all | solution.py:205
  14.1 0.6 pad_add_fusion.at_ref
  14.7 3.7 %shard_map.60.a_ref.own_ref = bf16[2048,512]{1,0:T(8,128)(2,1)} custom-call(s32[4]{0:T(128)} %pad_add_fusion.at_ref, bf16[2048,512]{1,0:T(8,128)(2,1)} %bitcast.16, bf16[2048,512]{1,0:T(8,128)(2,1)} %collective-permute-done.sib_ref.b2_ref), custom_call_target="tpu_custom_call" | custom-call | bytes 6291472 | tf_op jit(solution)/shard_map/pallas_call | solution.py:43
  18.4 3.2 %collective-permute-start.1 = (bf16[2048,512]{1,0:T(8,128)(2,1)}, bf16[2048,512]{1,0:T(8,128)(2,1)}, u32[]{:S(2)}, u32[]{:S(2)}) collective-permute-start(bf16[2048,512]{1,0:T(8,128)(2,1)} %shard_map.60.a_ref.own_ref), channel_id=1, source_target_pairs={{0,1},{1,0},{2,3},{3,2},{4,5},{5,4},{6,7},{7,6},{8,9},{9,8},{10,11... | collective-permute-start | bytes 6291464 | tf_op jit(solution)/shard_map/ppermute | solution.py:30
  21.6 7.8 %shard_map.61.after_ref = bf16[16,64,1152]{2,1,0:T(8,128)(2,1)} custom-call(bf16[2048,512]{1,0:T(8,128)(2,1)} %shard_map.60.a_ref.own_ref, bf16[2048,512]{1,0:T(8,128)(2,1)} %bitcast.17, bf16[2048,512]{1,0:T(8,128)(2,1)} %collective-permute-done.sib_ref.b2_ref), custom_call_target="tpu_custom_call" | custom-call | flops 3221225472 | bytes 8650752 | tf_op jit(solution)/shard_map/pallas_call | solution.py:43
  29.4 2.5 %all-to-all-done = bf16[16,64,512]{2,1,0:T(8,128)(2,1)S(1)} async-done(((bf16[16,64,512]{2,1,0:T(8,128)(2,1)}), bf16[16,64,512]{2,1,0:T(8,128)(2,1)S(1)}, u32[]{:S(2)}, u32[]{:S(2)}) %all-to-all-start) | async-done | bytes 1048608 | tf_op jit(solution)/shard_map/all_to_all | solution.py:205
  31.9 1.0 copy-done.4
  32.9 4.7 %all-to-all-start.2 = ((bf16[16,64,1152]{2,1,0:T(8,128)(2,1)}), bf16[16,64,1152]{2,1,0:T(8,128)(2,1)S(1)}, u32[]{:S(2)}, u32[]{:S(2)}) async-start(bf16[16,64,1152]{2,1,0:T(8,128)(2,1)} %shard_map.61.after_ref), calls=%async_computation.2 | async-start | bytes 4718592 | tf_op jit(solution)/shard_map/all_to_all | solution.py:229
  37.6 30.0 %collective-permute-done.1.also_ref.cross_ref.a_ref = bf16[2048,512]{1,0:T(8,128)(2,1)} collective-permute-done((bf16[2048,512]{1,0:T(8,128)(2,1)}, bf16[2048,512]{1,0:T(8,128)(2,1)}, u32[]{:S(2)}, u32[]{:S(2)}) %collective-permute-start.1) | collective-permute-done | bytes 2097184 | tf_op jit(solution)/shard_map/ppermute | solution.py:30
  67.6 2.3 %shard_map.62 = f32[256,256]{1,0:T(8,128)} custom-call(bf16[1024,512]{1,0:T(8,128)(2,1)} %bitcast.19, bf16[16,64,1152]{2,1,0:T(8,128)(2,1)} %shard_map.61.after_ref, bf16[2048,512]{1,0:T(8,128)(2,1)} %collective-permute-done.1.also_ref.cross_ref.a_ref), custom_call_target="tpu_custom_call" | custom-call | flops 134217728 | bytes 5767168 | tf_op jit(solution)/shard_map/pallas_call | solution.py:43
  69.9 0.9 dynamic-slice_bitcast_fusion
  70.9 9.0 %shard_map.66 = (bf16[256,1024]{1,0:T(8,128)(2,1)}, bf16[256,1024]{1,0:T(8,128)(2,1)}, bf16[256,1024]{1,0:T(8,128)(2,1)}, bf16[256,1024]{1,0:T(8,128)(2,1)}, bf1...) custom-call(s32[4]{0:T(128)} %pad_add_fusion.at_ref, ...), custom_call_target="tpu_custom_call" | custom-call | flops 4294967296 | bytes 12845072 | tf_op jit(solution)/shard_map/pallas_call | solution.py:43
  79.9 2.9 %collective-permute-start.14 = (bf16[256,1024]{1,0:T(8,128)(2,1)}, bf16[256,1024]{1,0:T(8,128)(2,1)S(1)}, u32[]{:S(2)}, u32[]{:S(2)}) collective-permute-start(bf16[256,1024]{1,0:T(8,128)(2,1)} %get-tuple-element.25), channel_id=1, source_target_pairs={{0,48},{1,49},{2,50},{3,51},{4,52},{5,53},{6,54},{7,55},{8,56},{9,... | collective-permute-start | bytes 1572872 | tf_op jit(solution)/shard_map/ppermute | solution.py:30
  82.8 1.4 copy-done
  84.2 2.9 %shard_map.64 = (f32[64,2048]{1,0:T(8,128)}, bf16[16,64,128]{2,1,0:T(8,128)(2,1)}) custom-call(s32[4]{0:T(128)} %pad_add_fusion.at_ref, bf16[16,64,1152]{2,1,0:T(8,128)(2,1)} %copy-done), custom_call_target="tpu_custom_call" | custom-call | bytes 3145744 | tf_op jit(solution)/shard_map/pallas_call | solution.py:43
  87.1 4.6 %all-to-all-start.3 = ((bf16[16,64,128]{2,1,0:T(8,128)(2,1)}), bf16[16,64,128]{2,1,0:T(8,128)(2,1)S(1)}, u32[]{:S(2)}, u32[]{:S(2)}) async-start(bf16[16,64,128]{2,1,0:T(8,128)(2,1)} %get-tuple-element.17), calls=%async_computation.3 | async-start | bytes 524288 | tf_op jit(solution)/shard_map/all_to_all | solution.py:236
  91.8 3.4 %collective-permute-start.13 = (bf16[256,1024]{1,0:T(8,128)(2,1)}, bf16[256,1024]{1,0:T(8,128)(2,1)}, u32[]{:S(2)}, u32[]{:S(2)}) collective-permute-start(bf16[256,1024]{1,0:T(8,128)(2,1)} %get-tuple-element.24), channel_id=1, source_target_pairs={{0,32},{1,33},{2,34},{3,35},{4,36},{5,37},{6,38},{7,39},{8,40},{9,... | collective-permute-start | bytes 1572872 | tf_op jit(solution)/shard_map/ppermute | solution.py:30
  95.2 0.6 collective-permute-start.12
  95.8 1.7 collective-permute-start.3
  97.5 11.4 %all-to-all-done.3 = bf16[16,64,128]{2,1,0:T(8,128)(2,1)S(1)} async-done(((bf16[16,64,128]{2,1,0:T(8,128)(2,1)}), bf16[16,64,128]{2,1,0:T(8,128)(2,1)S(1)}, u32[]{:S(2)}, u32[]{:S(2)}) %all-to-all-start.3) | async-done | bytes 262176 | tf_op jit(solution)/shard_map/all_to_all | solution.py:236
  109.4 3.4 %collective-permute-start.8 = (bf16[256,1024]{1,0:T(8,128)(2,1)}, bf16[256,1024]{1,0:T(8,128)(2,1)}, u32[]{:S(2)}, u32[]{:S(2)}) collective-permute-start(bf16[256,1024]{1,0:T(8,128)(2,1)} %get-tuple-element.21), channel_id=1, source_target_pairs={{0,12},{1,13},{2,14},{3,15},{4,0},{5,1},{6,2},{7,3},{8,4},{9,5},{1... | collective-permute-start | bytes 1572872 | tf_op jit(solution)/shard_map/ppermute | solution.py:30
  112.7 0.9 collective-permute-start.7
  113.7 1.2 collective-permute-start.6
  114.9 1.1 broadcast_in_dim.2
  116.0 6.7 %all-to-all-start.1 = ((bf16[16,2,64,256]{3,2,1,0:T(8,128)(2,1)}), bf16[16,2,64,256]{3,2,1,0:T(8,128)(2,1)S(1)}, u32[]{:S(2)}, u32[]{:S(2)}) async-start(bf16[16,2,64,256]{3,2,1,0:T(8,128)(2,1)} %broadcast_in_dim.2), calls=%async_computation.1 | async-start | bytes 2097152 | tf_op jit(solution)/shard_map/all_to_all | solution.py:218
  122.7 0.8 copy.11
  123.5 2.1 %shard_map.65 = f32[64,2048]{1,0:T(8,128)} custom-call(s32[4]{0:T(128)} %pad_add_fusion.at_ref, f32[64,2048]{1,0:T(8,128)} %get-tuple-element.16.direct_ref, bf16[64,1024]{1,0:T(8,128)(2,1)} %bitcast.23, bf16[64,1024]{1,0:T(8,128)(2,1)} %copy-done.12), custom_call_target="tpu_custom_call" | custom-call | bytes 1310736 | tf_op jit(solution)/shard_map/pallas_call | solution.py:43
  125.6 1.5 add_convert_fusion.2
  127.0 3.2 %collective-permute-start.17 = (bf16[64,1024]{1,0:T(8,128)(2,1)S(1)}, bf16[64,1024]{1,0:T(8,128)(2,1)S(1)}, u32[]{:S(2)}, u32[]{:S(2)}) collective-permute-start(bf16[64,1024]{1,0:T(8,128)(2,1)S(1)} %get-tuple-element.30), channel_id=1, source_target_pairs={{0,12},{1,13},{2,14},{3,15},{4,0},{5,1},{6,2},{7,3},{8,4},{9,5},{1... | collective-permute-start | bytes 393224 | tf_op jit(solution)/shard_map/ppermute | solution.py:30
  130.2 0.9 collective-permute-start.16
  131.1 9.7 %collective-permute-done.8 = bf16[256,1024]{1,0:T(8,128)(2,1)} collective-permute-done((bf16[256,1024]{1,0:T(8,128)(2,1)}, bf16[256,1024]{1,0:T(8,128)(2,1)}, u32[]{:S(2)}, u32[]{:S(2)}) %collective-permute-start.8) | collective-permute-done | bytes 524320 | tf_op jit(solution)/shard_map/ppermute | solution.py:30
  140.8 1.6 add_convert_fusion.5
  142.4 3.0 %collective-permute-start.11 = (bf16[64,1024]{1,0:T(8,128)(2,1)S(1)}, bf16[64,1024]{1,0:T(8,128)(2,1)S(1)}, u32[]{:S(2)}, u32[]{:S(2)}) collective-permute-start(bf16[64,1024]{1,0:T(8,128)(2,1)S(1)} %get-tuple-element.27), channel_id=1, source_target_pairs={{0,48},{1,49},{2,50},{3,51},{4,52},{5,53},{6,54},{7,55},{8,56},{9,... | collective-permute-start | bytes 393224 | tf_op jit(solution)/shard_map/ppermute | solution.py:30
  145.4 1.6 collective-permute-start.10
  147.0 5.8 %collective-permute-done.17 = bf16[64,1024]{1,0:T(8,128)(2,1)S(1)} collective-permute-done((bf16[64,1024]{1,0:T(8,128)(2,1)S(1)}, bf16[64,1024]{1,0:T(8,128)(2,1)S(1)}, u32[]{:S(2)}, u32[]{:S(2)}) %collective-permute-start.17) | collective-permute-done | bytes 131104 | tf_op jit(solution)/shard_map/ppermute | solution.py:30
  152.8 2.6 %collective-permute-done.16 = bf16[64,1024]{1,0:T(8,128)(2,1)S(1)} collective-permute-done((bf16[64,1024]{1,0:T(8,128)(2,1)S(1)}, bf16[64,1024]{1,0:T(8,128)(2,1)S(1)}, u32[]{:S(2)}, u32[]{:S(2)}) %collective-permute-start.16) | collective-permute-done | bytes 131104 | tf_op jit(solution)/shard_map/ppermute | solution.py:30
  155.5 1.1 collective-permute-done.15
  156.5 1.2 convert_add_fusion
  157.7 1.3 collective-permute-done.9
  159.0 1.2 convert_add_fusion.1
  160.2 1.7 collective-permute-start.18
  161.9 1.0 copy-done.3
  162.9 4.8 %shard_map.63 = (f32[512,256]{1,0:T(8,128)}, f32[512,256]{1,0:T(8,128)}) custom-call(s32[4]{0:T(128)} %pad_add_fusion.at_ref, bf16[16,2,64,256]{3,2,1,0:T(8,128)(2,1)} %copy-done.3, bf16[2048,512]{1,0:T(8,128)(2,1)} %shard_map.60.a_ref.own_ref, bf16[2048,512]{1,0:T(8,128)(2,1)} %collective-permute-done.1.also_ref.cross_ref.a_ref), custom_call_target="tpu_custom_call" | custom-call | flops 1073741824 | bytes 6291472 | tf_op jit(solution)/shard_map/pallas_call | solution.py:43
  167.7 0.9 multiply_add_fusion
  168.7 1.2 collective-permute-done.4
  169.8 0.9 add.123
  (48 shorter events, 0.8 us)
Async XLA Ops:
  3.5 11.2 %copy-start.1 = (bf16[512,2048]{0,1:T(8,128)(2,1)}, bf16[512,2048]{0,1:T(8,128)(2,1)S(1)}, u32[]{:S(2)}) copy-start(bf16[512,2048]{0,1:T(8,128)(2,1)S(1)} %copy.8) | copy-start | bytes 6291460
  3.5 11.2 %collective-permute-start = (bf16[2048,512]{1,0:T(8,128)(2,1)S(1)}, bf16[2048,512]{1,0:T(8,128)(2,1)}, u32[]{:S(2)}, u32[]{:S(2)}) collective-permute-start(bf16[2048,512]{1,0:T(8,128)(2,1)S(1)} %bitcast.15), channel_id=1, source_target_pairs={{0,2},{1,3},{2,0},{3,1},{4,6},{5,7},{6,4},{7,5},{8,10},{9,11},{10,... | collective-permute-start | bytes 6291464 | tf_op jit(solution)/shard_map/ppermute | solution.py:30
  6.1 25.8 %all-to-all-start = ((bf16[16,64,512]{2,1,0:T(8,128)(2,1)}), bf16[16,64,512]{2,1,0:T(8,128)(2,1)S(1)}, u32[]{:S(2)}, u32[]{:S(2)}) async-start(bf16[16,64,512]{2,1,0:T(8,128)(2,1)} %shard_map.59), calls=%async_computation | async-start | bytes 2097152 | tf_op jit(solution)/shard_map/all_to_all | solution.py:205
  18.4 49.2 %collective-permute-start.1 = (bf16[2048,512]{1,0:T(8,128)(2,1)}, bf16[2048,512]{1,0:T(8,128)(2,1)}, u32[]{:S(2)}, u32[]{:S(2)}) collective-permute-start(bf16[2048,512]{1,0:T(8,128)(2,1)} %shard_map.60.a_ref.own_ref), channel_id=1, source_target_pairs={{0,1},{1,0},{2,3},{3,2},{4,5},{5,4},{6,7},{7,6},{8,9},{9,8},{10,11... | collective-permute-start | bytes 6291464 | tf_op jit(solution)/shard_map/ppermute | solution.py:30
  31.9 1.0 copy-start.4
  32.9 49.9 %all-to-all-start.2 = ((bf16[16,64,1152]{2,1,0:T(8,128)(2,1)}), bf16[16,64,1152]{2,1,0:T(8,128)(2,1)S(1)}, u32[]{:S(2)}, u32[]{:S(2)}) async-start(bf16[16,64,1152]{2,1,0:T(8,128)(2,1)} %shard_map.61.after_ref), calls=%async_computation.2 | async-start | bytes 4718592 | tf_op jit(solution)/shard_map/all_to_all | solution.py:229
  70.8 25.0 %collective-permute-start.2 = (f32[2,64,256]{2,1,0:T(8,128)S(1)}, f32[2,64,256]{2,1,0:T(8,128)S(1)}, u32[]{:S(2)}, u32[]{:S(2)}) collective-permute-start(f32[2,64,256]{2,1,0:T(8,128)S(1)} %dynamic-slice_bitcast_fusion), channel_id=1, source_target_pairs={{0,2},{1,3},{2,0},{3,1},{4,6},{5,7},{6,4},{7,5},{8,10},{9,11},{10,... | collective-permute-start | bytes 393224 | tf_op jit(solution)/shard_map/ppermute | solution.py:30
  79.9 15.9 %copy-start.5 = (f32[256,256]{1,0:T(8,128)S(1)}, f32[256,256]{1,0:T(8,128)}, u32[]{:S(2)}) copy-start(f32[256,256]{1,0:T(8,128)} %shard_map.62) | copy-start | bytes 786436
  79.9 33.7 %collective-permute-start.14 = (bf16[256,1024]{1,0:T(8,128)(2,1)}, bf16[256,1024]{1,0:T(8,128)(2,1)S(1)}, u32[]{:S(2)}, u32[]{:S(2)}) collective-permute-start(bf16[256,1024]{1,0:T(8,128)(2,1)} %get-tuple-element.25), channel_id=1, source_target_pairs={{0,48},{1,49},{2,50},{3,51},{4,52},{5,53},{6,54},{7,55},{8,56},{9,... | collective-permute-start | bytes 1572872 | tf_op jit(solution)/shard_map/ppermute | solution.py:30
  82.8 1.4 copy-start
  87.1 21.8 %all-to-all-start.3 = ((bf16[16,64,128]{2,1,0:T(8,128)(2,1)}), bf16[16,64,128]{2,1,0:T(8,128)(2,1)S(1)}, u32[]{:S(2)}, u32[]{:S(2)}) async-start(bf16[16,64,128]{2,1,0:T(8,128)(2,1)} %get-tuple-element.17), calls=%async_computation.3 | async-start | bytes 524288 | tf_op jit(solution)/shard_map/all_to_all | solution.py:236
  91.8 33.7 %collective-permute-start.13 = (bf16[256,1024]{1,0:T(8,128)(2,1)}, bf16[256,1024]{1,0:T(8,128)(2,1)}, u32[]{:S(2)}, u32[]{:S(2)}) collective-permute-start(bf16[256,1024]{1,0:T(8,128)(2,1)} %get-tuple-element.24), channel_id=1, source_target_pairs={{0,32},{1,33},{2,34},{3,35},{4,36},{5,37},{6,38},{7,39},{8,40},{9,... | collective-permute-start | bytes 1572872 | tf_op jit(solution)/shard_map/ppermute | solution.py:30
  95.2 30.3 %collective-permute-start.12 = (bf16[256,1024]{1,0:T(8,128)(2,1)}, bf16[256,1024]{1,0:T(8,128)(2,1)}, u32[]{:S(2)}, u32[]{:S(2)}) collective-permute-start(bf16[256,1024]{1,0:T(8,128)(2,1)} %get-tuple-element.23), channel_id=1, source_target_pairs={{0,16},{1,17},{2,18},{3,19},{4,20},{5,21},{6,22},{7,23},{8,24},{9,... | collective-permute-start | bytes 1572872 | tf_op jit(solution)/shard_map/ppermute | solution.py:30
  95.8 13.5 %collective-permute-start.3 = (f32[2,64,256]{2,1,0:T(8,128)S(1)}, f32[2,64,256]{2,1,0:T(8,128)S(1)}, u32[]{:S(2)}, u32[]{:S(2)}) collective-permute-start(f32[2,64,256]{2,1,0:T(8,128)S(1)} %bitcast_add_fusion), channel_id=1, source_target_pairs={{0,64},{1,65},{2,66},{3,67},{4,68},{5,69},{6,70},{7,71},{8,72},{9,... | collective-permute-start | bytes 393224 | tf_op jit(solution)/shard_map/ppermute | solution.py:30
  109.3 3.5 %collective-permute-start.5 = (bf16[64,1024]{1,0:T(8,128)(2,1)S(1)}, bf16[64,1024]{1,0:T(8,128)(2,1)S(1)}, u32[]{:S(2)}, u32[]{:S(2)}) collective-permute-start(bf16[64,1024]{1,0:T(8,128)(2,1)S(1)} %bitcast.24), channel_id=1, source_target_pairs={{0,2},{1,3},{2,0},{3,1},{4,6},{5,7},{6,4},{7,5},{8,10},{9,11},{10,... | collective-permute-start | bytes 393224 | tf_op jit(solution)/shard_map/ppermute | solution.py:30
  109.4 31.4 %collective-permute-start.8 = (bf16[256,1024]{1,0:T(8,128)(2,1)}, bf16[256,1024]{1,0:T(8,128)(2,1)}, u32[]{:S(2)}, u32[]{:S(2)}) collective-permute-start(bf16[256,1024]{1,0:T(8,128)(2,1)} %get-tuple-element.21), channel_id=1, source_target_pairs={{0,12},{1,13},{2,14},{3,15},{4,0},{5,1},{6,2},{7,3},{8,4},{9,5},{1... | collective-permute-start | bytes 1572872 | tf_op jit(solution)/shard_map/ppermute | solution.py:30
  112.7 10.7 %copy-start.12 = (bf16[64,1024]{1,0:T(8,128)(2,1)}, bf16[64,1024]{1,0:T(8,128)(2,1)S(1)}, u32[]{:S(2)}) copy-start(bf16[64,1024]{1,0:T(8,128)(2,1)S(1)} %collective-permute-done.5.given_ref) | copy-start | bytes 393220
  112.7 28.0 %collective-permute-start.7 = (bf16[256,1024]{1,0:T(8,128)(2,1)}, bf16[256,1024]{1,0:T(8,128)(2,1)}, u32[]{:S(2)}, u32[]{:S(2)}) collective-permute-start(bf16[256,1024]{1,0:T(8,128)(2,1)} %get-tuple-element.20), channel_id=1, source_target_pairs={{0,8},{1,9},{2,10},{3,11},{4,12},{5,13},{6,14},{7,15},{8,0},{9,1},... | collective-permute-start | bytes 1572872 | tf_op jit(solution)/shard_map/ppermute | solution.py:30
  113.7 1.2 copy-start.10
  113.7 27.1 %collective-permute-start.6 = (bf16[256,1024]{1,0:T(8,128)(2,1)}, bf16[256,1024]{1,0:T(8,128)(2,1)}, u32[]{:S(2)}, u32[]{:S(2)}) collective-permute-start(bf16[256,1024]{1,0:T(8,128)(2,1)} %get-tuple-element.19), channel_id=1, source_target_pairs={{0,4},{1,5},{2,6},{3,7},{4,8},{5,9},{6,10},{7,11},{8,12},{9,13},{1... | collective-permute-start | bytes 1572872 | tf_op jit(solution)/shard_map/ppermute | solution.py:30
  116.0 9.6 %copy-start.9 = (bf16[256,1024]{1,0:T(8,128)(2,1)S(1)}, bf16[256,1024]{1,0:T(8,128)(2,1)}, u32[]{:S(2)}) copy-start(bf16[256,1024]{1,0:T(8,128)(2,1)} %get-tuple-element.22) | copy-start | bytes 1572868
  116.0 9.6 %copy-start.11 = (bf16[256,1024]{1,0:T(8,128)(2,1)S(1)}, bf16[256,1024]{1,0:T(8,128)(2,1)}, u32[]{:S(2)}) copy-start(bf16[256,1024]{1,0:T(8,128)(2,1)} %copy-done.10) | copy-start | bytes 1572868
  116.0 45.9 %all-to-all-start.1 = ((bf16[16,2,64,256]{3,2,1,0:T(8,128)(2,1)}), bf16[16,2,64,256]{3,2,1,0:T(8,128)(2,1)S(1)}, u32[]{:S(2)}, u32[]{:S(2)}) async-start(bf16[16,2,64,256]{3,2,1,0:T(8,128)(2,1)} %broadcast_in_dim.2), calls=%async_computation.1 | async-start | bytes 2097152 | tf_op jit(solution)/shard_map/all_to_all | solution.py:218
  122.7 18.1 %copy-start.8 = (bf16[256,1024]{1,0:T(8,128)(2,1)S(1)}, bf16[256,1024]{1,0:T(8,128)(2,1)}, u32[]{:S(2)}) copy-start(bf16[256,1024]{1,0:T(8,128)(2,1)} %get-tuple-element.18) | copy-start | bytes 1572868
  127.0 25.8 %collective-permute-start.17 = (bf16[64,1024]{1,0:T(8,128)(2,1)S(1)}, bf16[64,1024]{1,0:T(8,128)(2,1)S(1)}, u32[]{:S(2)}, u32[]{:S(2)}) collective-permute-start(bf16[64,1024]{1,0:T(8,128)(2,1)S(1)} %get-tuple-element.30), channel_id=1, source_target_pairs={{0,12},{1,13},{2,14},{3,15},{4,0},{5,1},{6,2},{7,3},{8,4},{9,5},{1... | collective-permute-start | bytes 393224 | tf_op jit(solution)/shard_map/ppermute | solution.py:30
  130.2 25.2 %collective-permute-start.16 = (bf16[64,1024]{1,0:T(8,128)(2,1)S(1)}, bf16[64,1024]{1,0:T(8,128)(2,1)S(1)}, u32[]{:S(2)}, u32[]{:S(2)}) collective-permute-start(bf16[64,1024]{1,0:T(8,128)(2,1)S(1)} %get-tuple-element.31), channel_id=1, source_target_pairs={{0,8},{1,9},{2,10},{3,11},{4,12},{5,13},{6,14},{7,15},{8,0},{9,1},... | collective-permute-start | bytes 393224 | tf_op jit(solution)/shard_map/ppermute | solution.py:30
  140.7 15.8 %collective-permute-start.15 = (bf16[64,1024]{1,0:T(8,128)(2,1)S(1)}, bf16[64,1024]{1,0:T(8,128)(2,1)S(1)}, u32[]{:S(2)}, u32[]{:S(2)}) collective-permute-start(bf16[64,1024]{1,0:T(8,128)(2,1)S(1)} %get-tuple-element.29), channel_id=1, source_target_pairs={{0,4},{1,5},{2,6},{3,7},{4,8},{5,9},{6,10},{7,11},{8,12},{9,13},{1... | collective-permute-start | bytes 393224 | tf_op jit(solution)/shard_map/ppermute | solution.py:30
  140.8 19.4 %copy-start.2 = (f32[64,2048]{1,0:T(8,128)S(1)}, f32[64,2048]{1,0:T(8,128)}, u32[]{:S(2)}) copy-start(f32[64,2048]{1,0:T(8,128)} %shard_map.65) | copy-start | bytes 1572868
  142.4 15.3 %collective-permute-start.11 = (bf16[64,1024]{1,0:T(8,128)(2,1)S(1)}, bf16[64,1024]{1,0:T(8,128)(2,1)S(1)}, u32[]{:S(2)}, u32[]{:S(2)}) collective-permute-start(bf16[64,1024]{1,0:T(8,128)(2,1)S(1)} %get-tuple-element.27), channel_id=1, source_target_pairs={{0,48},{1,49},{2,50},{3,51},{4,52},{5,53},{6,54},{7,55},{8,56},{9,... | collective-permute-start | bytes 393224 | tf_op jit(solution)/shard_map/ppermute | solution.py:30
  145.4 12.3 %collective-permute-start.10 = (bf16[64,1024]{1,0:T(8,128)(2,1)S(1)}, bf16[64,1024]{1,0:T(8,128)(2,1)S(1)}, u32[]{:S(2)}, u32[]{:S(2)}) collective-permute-start(bf16[64,1024]{1,0:T(8,128)(2,1)S(1)} %get-tuple-element.28), channel_id=1, source_target_pairs={{0,32},{1,33},{2,34},{3,35},{4,36},{5,37},{6,38},{7,39},{8,40},{9,... | collective-permute-start | bytes 393224 | tf_op jit(solution)/shard_map/ppermute | solution.py:30
  152.8 6.2 %collective-permute-start.9 = (bf16[64,1024]{1,0:T(8,128)(2,1)S(1)}, bf16[64,1024]{1,0:T(8,128)(2,1)S(1)}, u32[]{:S(2)}, u32[]{:S(2)}) collective-permute-start(bf16[64,1024]{1,0:T(8,128)(2,1)S(1)} %get-tuple-element.26), channel_id=1, source_target_pairs={{0,16},{1,17},{2,18},{3,19},{4,20},{5,21},{6,22},{7,23},{8,24},{9,... | collective-permute-start | bytes 393224 | tf_op jit(solution)/shard_map/ppermute | solution.py:30
  160.2 7.5 %copy-start.6 = (f32[64,2048]{1,0:T(8,128)S(1)}, f32[64,2048]{1,0:T(8,128)}, u32[]{:S(2)}) copy-start(f32[64,2048]{1,0:T(8,128)} %param.5) | copy-start | bytes 1572868
  160.2 7.5 %collective-permute-start.18 = (bf16[64,2048]{1,0:T(8,128)(2,1)S(1)}, bf16[64,2048]{1,0:T(8,128)(2,1)S(1)}, u32[]{:S(2)}, u32[]{:S(2)}) collective-permute-start(bf16[64,2048]{1,0:T(8,128)(2,1)S(1)} %select_convert_fusion), channel_id=1, source_target_pairs={{0,64},{1,65},{2,66},{3,67},{4,68},{5,69},{6,70},{7,71},{8,72},{9,... | collective-permute-start | bytes 786440 | tf_op jit(solution)/shard_map/ppermute | solution.py:30
  161.9 1.0 copy-start.3
  167.7 2.1 %copy-start.7 = (f32[512,256]{1,0:T(8,128)S(1)}, f32[512,256]{1,0:T(8,128)}, u32[]{:S(2)}) copy-start(f32[512,256]{1,0:T(8,128)} %get-tuple-element.14) | copy-start | bytes 1572868
  167.7 2.1 %collective-permute-start.4 = (f32[512,256]{1,0:T(8,128)}, f32[512,256]{1,0:T(8,128)S(1)}, u32[]{:S(2)}, u32[]{:S(2)}) collective-permute-start(f32[512,256]{1,0:T(8,128)} %get-tuple-element.15), channel_id=1, source_target_pairs={{0,2},{1,3},{2,0},{3,1},{4,6},{5,7},{6,4},{7,5},{8,10},{9,11},{10,... | collective-permute-start | bytes 1572872 | tf_op jit(solution)/shard_map/ppermute | solution.py:30

commit v9 on v8

--- a/solution.py
+++ b/solution.py
@@ -123,42 +123,49 @@
 def scores_kernel(at_ref, pt_ref, own_ref, cross_ref, keep_ref, give_ref):
     h = at_ref[3]
     m = own_ref.shape[0] // 2
-    p_own = pt_ref[:, pl.ds(h, 1), :, :].reshape(m, pt_ref.shape[-1])
-    p_cross = pt_ref[:, pl.ds(1 - h, 1), :, :].reshape(m, pt_ref.shape[-1])
+    p_own = pt_ref[:, pl.ds(pl.multiple_of(h * 64, 64), 64), :].reshape(m, pt_ref.shape[-1])
+    p_cross = pt_ref[:, pl.ds(pl.multiple_of((1 - h) * 64, 64), 64), :].reshape(m, pt_ref.shape[-1])
     for side, out_ref in enumerate((keep_ref, give_ref)):
         s = slice(side * m, (side + 1) * m)
         acc = lax.dot_general(own_ref[s, :], p_own, TN, preferred_element_type=f32)
         out_ref[...] = acc + lax.dot_general(cross_ref[s, :], p_cross, TN, preferred_element_type=f32)
 
 
-def scatter_sum(parts, rows):
-    got, mids, sums = [], [], []
+def first_stage(parts):
+    got = []
     for half, axis in ((0, "x"), (1, "z")):
         got.append([send(parts[4 * half + k], along(axis, k)) for k in (1, 2, 3)])
-    for half in range(2):
-        mids.append([])
+    return got
+
+
+def second_stage(parts, got, rows):
+    sums = []
+    for half, axis in ((0, "z"), (1, "x")):
+        mids = []
         for j in range(4):
             cut = lambda v: lax.slice_in_dim(v, j * rows, (j + 1) * rows).astype(f32)
             total = cut(parts[4 * half])
             for r in got[half]:
                 total = total + cut(r)
-            mids[half].append(total)
-    for half, axis in ((0, "z"), (1, "x")):
-        rs = [send(mids[half][k].astype(bf16), along(axis, k)) for k in (1, 2, 3)]
-        sums.append(mids[half][0] + rs[0].astype(f32) + rs[1].astype(f32) + rs[2].astype(f32))
+            mids.append(total)
+        rs = [send(mids[k].astype(bf16), along(axis, k)) for k in (1, 2, 3)]
+        sums.append(mids[0] + rs[0].astype(f32) + rs[1].astype(f32) + rs[2].astype(f32))
     return jnp.concatenate(sums, axis=1)
 
 
-def own_sum_kernel(at_ref, got_ref, direct_ref, mirror_ref):
+def own_sum_kernel(at_ref, got_ref, pt_ref, after_ref, also_ref, direct_ref, slots_ref):
     chip = at_ref[0] * 4 + at_ref[1]
-    wide = mirror_ref.shape[2]
+    rows = direct_ref.shape[0]
+    wide, low = 2 * rows, rows // 2
     direct_ref[...] = jnp.zeros_like(direct_ref)
-    mirror_ref[...] = jnp.zeros_like(mirror_ref)
+    slots_ref[:, :wide, :] = jnp.broadcast_to(pt_ref[...][None], (16, wide, pt_ref.shape[1]))
+    slots_ref[:, wide:, :] = jnp.zeros_like(slots_ref[:, wide:, :])
     for k in range(9):
         total = jnp.sum(got_ref[:, :, k * wide : (k + 1) * wide].astype(f32), axis=0)
         to = lax.rem(chip + k, 16)
         direct_ref[:, pl.ds(pl.multiple_of(to * wide, wide), wide)] = total
-        mirror_ref[pl.ds(to, 1)] = total.astype(bf16)[None]
+        both = jnp.concatenate([total[:low], total[low:]], axis=1).astype(bf16)
+        slots_ref[pl.ds(to, 1), wide:, :] = both[None]
 
 
 def join_kernel(at_ref, direct_ref, held_ref, given_ref, out_ref):
@@ -195,6 +202,7 @@
         flops=3 * 16 * rows * feats * tokens,
     )
     cross = gram(at, arrived, gt, sib, own)
+    crossed = first_stage(cross)
 
     (slots,) = kernel_call(
         slots_kernel,
@@ -207,33 +215,34 @@
         functools.partial(factor_kernel, 4 * rows),
         [shape((4 * rows, tests), f32)],
         [VMEM, ANY, ANY],
-        slots.reshape(16 * rows, -1), own, arrived,
+        slots.reshape(16 * rows, -1), own, cross[0],
         flops=2 * 16 * rows * 4 * rows * tests,
     )
     pt = pt.reshape(2, 2, rows, tests)
     half = lambda i: lax.dynamic_index_in_dim(pt, i, 1, keepdims=False)
     pt = half(c) + send(half(1 - c), flip("c"))
     pt = (pt + send(pt, flip("yl"))).astype(bf16)
-    pt = jnp.broadcast_to(pt[None], (16,) + pt.shape)
-    pt = lax.all_to_all(pt, ("z", "x"), split_axis=0, concat_axis=0, tiled=True)
+
+    own = lax.all_to_all(own, ("z", "x"), split_axis=0, concat_axis=0, tiled=True)
+    direct, slots = kernel_call(
+        own_sum_kernel,
+        [shape((rows, feats), f32), shape((16, 2 * rows + rows // 2, tests), bf16)],
+        [SMEM, VMEM, VMEM, ANY, ANY],
+        at, own, pt.reshape(2 * rows, tests), crossed[0][0], crossed[1][0],
+    )
+    slots = lax.all_to_all(slots, ("z", "x"), split_axis=0, concat_axis=0, tiled=True)
+    mirror = slots[:, 2 * rows :]
+    mirror = jnp.concatenate([mirror[..., : 2 * rows], mirror[..., 2 * rows :]], axis=1)
 
     keep, give = kernel_call(
         scores_kernel,
         [shape((tokens, tests), f32)] * 2,
         [SMEM] + [VMEM] * 3,
-        at, pt, picked, arrived,
+        at, slots, picked, arrived,
         flops=8 * 16 * rows * tokens * tests,
     )
     scores = keep + send(give, flip("c"))
 
-    own = lax.all_to_all(own, ("z", "x"), split_axis=0, concat_axis=0, tiled=True)
-    direct, mirror = kernel_call(
-        own_sum_kernel,
-        [shape((rows, feats), f32), shape((16, rows, 2 * rows), bf16)],
-        [SMEM, VMEM],
-        at, own,
-    )
-    mirror = lax.all_to_all(mirror, ("z", "x"), split_axis=0, concat_axis=0, tiled=True)
     mirror = mirror.reshape(16 * rows, 2 * rows).T
     held = lax.dynamic_slice_in_dim(mirror, c * rows, rows, 0)
     given = send(lax.dynamic_slice_in_dim(mirror, (1 - c) * rows, rows, 0), flip("c"))
@@ -241,7 +250,7 @@
         join_kernel, [shape((rows, feats), f32)], [SMEM] + [VMEM] * 3, at, direct, held, given
     )
 
-    cross = scatter_sum(cross, rows)
+    cross = second_stage(cross, crossed, rows)
     ours, theirs = jnp.where(yl == h, own, cross), jnp.where(yl == h, cross, own)
     term = ours + send(theirs.astype(bf16), flip("yl")).astype(f32)
     covariance_out = 0.9 * covariance + term / (tokens * 64)

time: 173 us -> 172 us (level)
  starting transfers between devices: 51.7 us -> 48.8 us
  other arithmetic: 7.86 us -> 10.2 us
    all_to_all x2 -> x0, waiting for transfers between devices: 11.4 us -> none  [the longest x1 11.4 us: on_device(): lax.all_to_all(mirror, ('z', 'x'), split_axis=0, concat_axis=0, tiled=True)]
    all_to_all x2 -> x0, starting transfers between devices: 11.3 us -> none  [the longest x1 6.66 us: on_device(): pt = lax.all_to_all(pt, ('z', 'x'), split_axis=0, concat_axis=0, tiled=True)]
    all_to_all x1 -> x2, waiting for transfers between devices: 2.5 us -> 9.9 us  [on_device(): lax.all_to_all(slots, ('z', 'x'), split_axis=0, concat_axis=0, tiled=True)]
    ppermute x19, waiting for transfers between devices: 51.7 us -> 57.1 us  [send(): return lax.ppermute(value, AXES, pairs)]
    all_to_all x1 -> x2, starting transfers between devices: 7.96 us -> 13.3 us  [on_device(): lax.all_to_all(slots, ('z', 'x'), split_axis=0, concat_axis=0, tiled=True)]
    ppermute x19, starting transfers between devices: 27.7 us -> 31.7 us  [send(): return lax.ppermute(value, AXES, pairs)]
    unnamed x29 -> x31, local copies, waits for them, and re-layouts: 7.25 us -> 6.26 us
  transfers between devices with their start and end apart: 23 -> 22, of which waited for: 9 -> 12; matrix products, arithmetic and copies ran while one was open for 6% -> 7% of each run, Pallas kernels for 21% -> 17%
where the time goes in v9:
time: 172 us; the launch traced here: 170 us
  waiting for transfers between devices  67 us (39%)
  starting transfers between devices  48.8 us (28%)
  Pallas kernels  35.3 us (21%)
  other arithmetic  10.2 us (6%)
  local copies, waits for them, and re-layouts  8.08 us (5%)
    ppermute x19, waiting for transfers between devices, send(): return lax.ppermute(value, AXES, pairs)  57.1 us
    pallas_call x8, Pallas kernels, kernel_call(): pl.pallas_call(body, out_shape=outs, in_specs=specs, out_specs=[VMEM] * l...  35.3 us
    ppermute x19, starting transfers between devices, send(): return lax.ppermute(value, AXES, pairs)  31.7 us
    all_to_all x2, starting transfers between devices, on_device(): lax.all_to_all(slots, ('z', 'x'), split_axis=0, concat_axis=0, tiled=True)  13.3 us
    all_to_all x2, waiting for transfers between devices, on_device(): lax.all_to_all(slots, ('z', 'x'), split_axis=0, concat_axis=0, tiled=True)  9.9 us
    unnamed x31, local copies, waits for them, and re-layouts  6.26 us
    all_to_all x1, starting transfers between devices, on_device(): lax.all_to_all(own, ('z', 'x'), split_axis=0, concat_axis=0, tiled=True)  3.72 us
    convert_element_type x2, other arithmetic, second_stage(): rs = [send(mids[k].astype(bf16), along(axis, k)) for k in (1, 2, 3)]  3.57 us
  transfers between devices with their start and end apart: 22, of which 12 were waited for; matrix products, arithmetic and copies ran while one was open for 7% of the time, Pallas kernels for 17%

profile of v9, /device:TPU:0, one launch (start us, length us, event | category | flops | bytes accessed | tf_op | source)
XLA Modules:
  0.0 170.2 jit_solution(9042691448675568682)
XLA Ops:
  0.6 2.9 %copy.8 = bf16[512,2048]{0,1:T(8,128)(2,1)S(1)} copy(bf16[512,2048]{1,0:T(8,128)(2,1)} %param.4) | data formatting | bytes 4194304 | tf_op args[0]
  3.6 0.8 pad_add_fusion.at_ref
  4.5 3.4 %collective-permute-done.sib_ref.b2_ref = bf16[2048,512]{1,0:T(8,128)(2,1)} collective-permute-done((bf16[2048,512]{1,0:T(8,128)(2,1)S(1)}, bf16[2048,512]{1,0:T(8,128)(2,1)}, u32[]{:S(2)}, u32[]{:S(2)}) %collective-permute-start) | collective-permute-done | bytes 2097184 | tf_op jit(solution)/shard_map/ppermute | solution.py:30
  7.9 3.7 %shard_map.59.a_ref.own_ref = bf16[2048,512]{1,0:T(8,128)(2,1)} custom-call(s32[4]{0:T(128)} %pad_add_fusion.at_ref, bf16[2048,512]{1,0:T(8,128)(2,1)} %bitcast.17, bf16[2048,512]{1,0:T(8,128)(2,1)} %collective-permute-done.sib_ref.b2_ref), custom_call_target="tpu_custom_call" | custom-call | bytes 6291472 | tf_op jit(solution)/shard_map/pallas_call | solution.py:43
  11.6 3.3 %collective-permute-start.1 = (bf16[2048,512]{1,0:T(8,128)(2,1)}, bf16[2048,512]{1,0:T(8,128)(2,1)}, u32[]{:S(2)}, u32[]{:S(2)}) collective-permute-start(bf16[2048,512]{1,0:T(8,128)(2,1)} %shard_map.59.a_ref.own_ref), channel_id=1, source_target_pairs={{0,1},{1,0},{2,3},{3,2},{4,5},{5,4},{6,7},{7,6},{8,9},{9,8},{10,11... | collective-permute-start | bytes 6291464 | tf_op jit(solution)/shard_map/ppermute | solution.py:30
  14.9 2.1 %shard_map.61 = bf16[16,64,512]{2,1,0:T(8,128)(2,1)} custom-call(bf16[64,4096]{1,0:T(8,128)(2,1)} %f_ref.1, bf16[64,256]{1,0:T(8,128)(2,1)} %bitcast.27), custom_call_target="tpu_custom_call" | custom-call | bytes 1605632 | tf_op jit(solution)/shard_map/pallas_call | solution.py:43
  17.0 7.9 %all-to-all-start.1 = ((bf16[16,64,512]{2,1,0:T(8,128)(2,1)}), bf16[16,64,512]{2,1,0:T(8,128)(2,1)S(1)}, u32[]{:S(2)}, u32[]{:S(2)}) async-start(bf16[16,64,512]{2,1,0:T(8,128)(2,1)} %shard_map.61), calls=%async_computation.1 | async-start | bytes 2097152 | tf_op jit(solution)/shard_map/all_to_all | solution.py:213
  24.9 7.8 %shard_map.60.after_ref = bf16[16,64,1152]{2,1,0:T(8,128)(2,1)} custom-call(bf16[2048,512]{1,0:T(8,128)(2,1)} %shard_map.59.a_ref.own_ref, bf16[2048,512]{1,0:T(8,128)(2,1)} %bitcast.18, bf16[2048,512]{1,0:T(8,128)(2,1)} %collective-permute-done.sib_ref.b2_ref), custom_call_target="tpu_custom_call" | custom-call | flops 3221225472 | bytes 8650752 | tf_op jit(solution)/shard_map/pallas_call | solution.py:43
  32.7 9.9 %all-to-all-done.1 = bf16[16,64,512]{2,1,0:T(8,128)(2,1)S(1)} async-done(((bf16[16,64,512]{2,1,0:T(8,128)(2,1)}), bf16[16,64,512]{2,1,0:T(8,128)(2,1)S(1)}, u32[]{:S(2)}, u32[]{:S(2)}) %all-to-all-start.1) | async-done | bytes 1048608 | tf_op jit(solution)/shard_map/all_to_all | solution.py:213
  42.6 1.0 copy-done.4
  43.6 3.7 %all-to-all-start = ((bf16[16,64,1152]{2,1,0:T(8,128)(2,1)}), bf16[16,64,1152]{2,1,0:T(8,128)(2,1)S(1)}, u32[]{:S(2)}, u32[]{:S(2)}) async-start(bf16[16,64,1152]{2,1,0:T(8,128)(2,1)} %shard_map.60.after_ref), calls=%async_computation | async-start | bytes 4718592 | tf_op jit(solution)/shard_map/all_to_all | solution.py:226
  47.3 13.8 %collective-permute-done.1.a_ref.cross_ref = bf16[2048,512]{1,0:T(8,128)(2,1)} collective-permute-done((bf16[2048,512]{1,0:T(8,128)(2,1)}, bf16[2048,512]{1,0:T(8,128)(2,1)}, u32[]{:S(2)}, u32[]{:S(2)}) %collective-permute-start.1) | collective-permute-done | bytes 2097184 | tf_op jit(solution)/shard_map/ppermute | solution.py:30
  61.1 9.0 %shard_map.62 = (bf16[256,1024]{1,0:T(8,128)(2,1)}, bf16[256,1024]{1,0:T(8,128)(2,1)}, bf16[256,1024]{1,0:T(8,128)(2,1)}, bf16[256,1024]{1,0:T(8,128)(2,1)}, bf1...) custom-call(s32[4]{0:T(128)} %pad_add_fusion.at_ref, ...), custom_call_target="tpu_custom_call" | custom-call | flops 4294967296 | bytes 12845072 | tf_op jit(solution)/shard_map/pallas_call | solution.py:43
  70.2 2.3 %shard_map.63 = f32[256,256]{1,0:T(8,128)} custom-call(bf16[1024,512]{1,0:T(8,128)(2,1)} %bitcast.20, bf16[16,64,1152]{2,1,0:T(8,128)(2,1)} %shard_map.60.after_ref, bf16[256,1024]{1,0:T(8,128)(2,1)} %get-tuple-element.14.also_ref), custom_call_target="tpu_custom_call" | custom-call | flops 134217728 | bytes 4194304 | tf_op jit(solution)/shard_map/pallas_call | solution.py:43
  72.4 1.6 dynamic-slice_bitcast_fusion
  74.0 1.5 collective-permute-start.4
  75.6 1.9 %collective-permute-start.5 = (bf16[256,1024]{1,0:T(8,128)(2,1)}, bf16[256,1024]{1,0:T(8,128)(2,1)S(1)}, u32[]{:S(2)}, u32[]{:S(2)}) collective-permute-start(bf16[256,1024]{1,0:T(8,128)(2,1)} %get-tuple-element.16), channel_id=1, source_target_pairs={{0,16},{1,17},{2,18},{3,19},{4,20},{5,21},{6,22},{7,23},{8,24},{9,... | collective-permute-start | bytes 1572872 | tf_op jit(solution)/shard_map/ppermute | solution.py:30
  77.5 0.9 bitcast_add_fusion
  78.4 1.7 collective-permute-start.3
  80.1 2.7 %collective-permute-start.8 = (bf16[256,1024]{1,0:T(8,128)(2,1)}, bf16[256,1024]{1,0:T(8,128)(2,1)}, u32[]{:S(2)}, u32[]{:S(2)}) collective-permute-start(bf16[256,1024]{1,0:T(8,128)(2,1)} %get-tuple-element.21), channel_id=1, source_target_pairs={{0,8},{1,9},{2,10},{3,11},{4,12},{5,13},{6,14},{7,15},{8,0},{9,1},... | collective-permute-start | bytes 1572872 | tf_op jit(solution)/shard_map/ppermute | solution.py:30
  82.8 1.4 collective-permute-start.9
  84.9 5.3 %collective-permute-done.4.after_ref = bf16[256,1024]{1,0:T(8,128)(2,1)S(1)} collective-permute-done((bf16[256,1024]{1,0:T(8,128)(2,1)}, bf16[256,1024]{1,0:T(8,128)(2,1)S(1)}, u32[]{:S(2)}, u32[]{:S(2)}) %collective-permute-start.4) | collective-permute-done | bytes 524320 | tf_op jit(solution)/shard_map/ppermute | solution.py:30
  90.2 1.9 %collective-permute-done.5.also_ref = bf16[256,1024]{1,0:T(8,128)(2,1)S(1)} collective-permute-done((bf16[256,1024]{1,0:T(8,128)(2,1)}, bf16[256,1024]{1,0:T(8,128)(2,1)S(1)}, u32[]{:S(2)}, u32[]{:S(2)}) %collective-permute-start.5) | collective-permute-done | bytes 524320 | tf_op jit(solution)/shard_map/ppermute | solution.py:30
  92.1 0.8 copy-done.5
  92.9 3.4 %shard_map.64 = (f32[64,2048]{1,0:T(8,128)}, bf16[16,160,256]{2,1,0:T(8,128)(2,1)}) custom-call(s32[4]{0:T(128)} %pad_add_fusion.at_ref, bf16[16,64,1152]{2,1,0:T(8,128)(2,1)} %copy-done, bf16[128,256]{1,0:T(8,128)(2,1)} %bitcast.25, bf16[256,1024]{1,0:T(8,128)(2,1)} %copy-done.7, bf16[256,1024]{1,0:T(8,128)(2,1)} %copy-done.5), custom_call_target="tpu_custom_call" | custom-call | bytes 5308432 | tf_op jit(solution)/shard_map/pallas_call | solution.py:43
  96.4 5.4 %all-to-all-start.2 = ((bf16[16,160,256]{2,1,0:T(8,128)(2,1)}), bf16[16,160,256]{2,1,0:T(8,128)(2,1)S(1)}, u32[]{:S(2)}, u32[]{:S(2)}) async-start(bf16[16,160,256]{2,1,0:T(8,128)(2,1)} %get-tuple-element.17), calls=%async_computation.2 | async-start | bytes 2621440 | tf_op jit(solution)/shard_map/all_to_all | solution.py:233
  101.8 3.4 %collective-permute-start.13 = (bf16[256,1024]{1,0:T(8,128)(2,1)}, bf16[256,1024]{1,0:T(8,128)(2,1)}, u32[]{:S(2)}, u32[]{:S(2)}) collective-permute-start(bf16[256,1024]{1,0:T(8,128)(2,1)} %get-tuple-element.24), channel_id=1, source_target_pairs={{0,32},{1,33},{2,34},{3,35},{4,36},{5,37},{6,38},{7,39},{8,40},{9,... | collective-permute-start | bytes 1572872 | tf_op jit(solution)/shard_map/ppermute | solution.py:30
  105.2 1.2 collective-permute-start.14
  106.4 0.7 collective-permute-done.9
  107.1 1.5 add_convert_fusion.5
  108.5 2.0 %collective-permute-start.10 = (bf16[64,1024]{1,0:T(8,128)(2,1)S(1)}, bf16[64,1024]{1,0:T(8,128)(2,1)S(1)}, u32[]{:S(2)}, u32[]{:S(2)}) collective-permute-start(bf16[64,1024]{1,0:T(8,128)(2,1)S(1)} %get-tuple-element.26), channel_id=1, source_target_pairs={{0,16},{1,17},{2,18},{3,19},{4,20},{5,21},{6,22},{7,23},{8,24},{9,... | collective-permute-start | bytes 393224 | tf_op jit(solution)/shard_map/ppermute | solution.py:30
  110.5 2.7 %collective-permute-start.11 = (bf16[64,1024]{1,0:T(8,128)(2,1)S(1)}, bf16[64,1024]{1,0:T(8,128)(2,1)S(1)}, u32[]{:S(2)}, u32[]{:S(2)}) collective-permute-start(bf16[64,1024]{1,0:T(8,128)(2,1)S(1)} %get-tuple-element.28), channel_id=1, source_target_pairs={{0,32},{1,33},{2,34},{3,35},{4,36},{5,37},{6,38},{7,39},{8,40},{9,... | collective-permute-start | bytes 393224 | tf_op jit(solution)/shard_map/ppermute | solution.py:30
  113.2 1.6 collective-permute-start.12
  114.8 17.7 %collective-permute-done.13 = bf16[256,1024]{1,0:T(8,128)(2,1)} collective-permute-done((bf16[256,1024]{1,0:T(8,128)(2,1)}, bf16[256,1024]{1,0:T(8,128)(2,1)}, u32[]{:S(2)}, u32[]{:S(2)}) %collective-permute-start.13) | collective-permute-done | bytes 524320 | tf_op jit(solution)/shard_map/ppermute | solution.py:30
  132.5 10.0 %collective-permute-done.14 = bf16[256,1024]{1,0:T(8,128)(2,1)} collective-permute-done((bf16[256,1024]{1,0:T(8,128)(2,1)}, bf16[256,1024]{1,0:T(8,128)(2,1)}, u32[]{:S(2)}, u32[]{:S(2)}) %collective-permute-start.14) | collective-permute-done | bytes 524320 | tf_op jit(solution)/shard_map/ppermute | solution.py:30
  142.5 2.1 %add_convert_fusion.2 = (bf16[64,1024]{1,0:T(8,128)(2,1)}, bf16[64,1024]{1,0:T(8,128)(2,1)}, bf16[64,1024]{1,0:T(8,128)(2,1)}) fusion(bf16[256,1024]{1,0:T(8,128)(2,1)} %collective-permute-done.14, bf16[256,1024]{1,0:T(8,128)(2,1)} %collective-permute-done.13, bf16[256,1024]{1,0:T(8,128)(2,1)S(1)} %copy-done.6, bf16[256,1024]{1,0:T(8,128)(2,1)S(1)} %copy-done.12), kind=kLoop, calls=%fused_computation.7 | loop fusion | flops 1572864 | bytes 1966080 | tf_op jit(solution)/shard_map/convert_element_type | solution.py:151
  144.6 1.4 collective-permute-start.15
  146.0 2.6 %collective-permute-start.16 = (bf16[64,1024]{1,0:T(8,128)(2,1)}, bf16[64,1024]{1,0:T(8,128)(2,1)}, u32[]{:S(2)}, u32[]{:S(2)}) collective-permute-start(bf16[64,1024]{1,0:T(8,128)(2,1)} %get-tuple-element.31), channel_id=1, source_target_pairs={{0,8},{1,9},{2,10},{3,11},{4,12},{5,13},{6,14},{7,15},{8,0},{9,1},... | collective-permute-start | bytes 393224 | tf_op jit(solution)/shard_map/ppermute | solution.py:30
  149.2 1.1 convert_add_fusion.1
  151.0 2.2 %collective-permute-done.16 = bf16[64,1024]{1,0:T(8,128)(2,1)} collective-permute-done((bf16[64,1024]{1,0:T(8,128)(2,1)}, bf16[64,1024]{1,0:T(8,128)(2,1)}, u32[]{:S(2)}, u32[]{:S(2)}) %collective-permute-start.16) | collective-permute-done | bytes 131104 | tf_op jit(solution)/shard_map/ppermute | solution.py:30
  153.9 1.3 convert_add_fusion
  155.2 0.8 copy.11
  156.6 2.1 %shard_map.66 = f32[64,2048]{1,0:T(8,128)} custom-call(s32[4]{0:T(128)} %pad_add_fusion.at_ref, f32[64,2048]{1,0:T(8,128)} %get-tuple-element.20.direct_ref, bf16[64,1024]{1,0:T(8,128)(2,1)} %bitcast.24, bf16[64,1024]{1,0:T(8,128)(2,1)} %copy-done.13), custom_call_target="tpu_custom_call" | custom-call | bytes 1310736 | tf_op jit(solution)/shard_map/pallas_call | solution.py:43
  158.8 3.6 %collective-permute-start.18 = (bf16[64,2048]{1,0:T(8,128)(2,1)S(1)}, bf16[64,2048]{1,0:T(8,128)(2,1)S(1)}, u32[]{:S(2)}, u32[]{:S(2)}) collective-permute-start(bf16[64,2048]{1,0:T(8,128)(2,1)S(1)} %select_convert_fusion), channel_id=1, source_target_pairs={{0,64},{1,65},{2,66},{3,67},{4,68},{5,69},{6,70},{7,71},{8,72},{9,... | collective-permute-start | bytes 786440 | tf_op jit(solution)/shard_map/ppermute | solution.py:30
  162.4 4.9 %shard_map.65 = (f32[512,256]{1,0:T(8,128)}, f32[512,256]{1,0:T(8,128)}) custom-call(s32[4]{0:T(128)} %pad_add_fusion.at_ref, bf16[16,160,256]{2,1,0:T(8,128)(2,1)} %copy-done.2, bf16[2048,512]{1,0:T(8,128)(2,1)} %shard_map.59.a_ref.own_ref, bf16[2048,512]{1,0:T(8,128)(2,1)} %collective-permute-done.1.a_ref.cross_ref), custom_call_target="tpu_custom_call" | custom-call | flops 1073741824 | bytes 6553616 | tf_op jit(solution)/shard_map/pallas_call | solution.py:43
  167.3 0.9 multiply_add_fusion
  168.2 1.2 collective-permute-done.6
  169.4 0.9 add.123
  (49 shorter events, 3.4 us)
Async XLA Ops:
  3.5 4.4 %copy-start.1 = (bf16[512,2048]{0,1:T(8,128)(2,1)}, bf16[512,2048]{0,1:T(8,128)(2,1)S(1)}, u32[]{:S(2)}) copy-start(bf16[512,2048]{0,1:T(8,128)(2,1)S(1)} %copy.8) | copy-start | bytes 6291460
  3.5 4.4 %collective-permute-start = (bf16[2048,512]{1,0:T(8,128)(2,1)S(1)}, bf16[2048,512]{1,0:T(8,128)(2,1)}, u32[]{:S(2)}, u32[]{:S(2)}) collective-permute-start(bf16[2048,512]{1,0:T(8,128)(2,1)S(1)} %bitcast.16), channel_id=1, source_target_pairs={{0,2},{1,3},{2,0},{3,1},{4,6},{5,7},{6,4},{7,5},{8,10},{9,11},{10,... | collective-permute-start | bytes 6291464 | tf_op jit(solution)/shard_map/ppermute | solution.py:30
  11.6 49.5 %collective-permute-start.1 = (bf16[2048,512]{1,0:T(8,128)(2,1)}, bf16[2048,512]{1,0:T(8,128)(2,1)}, u32[]{:S(2)}, u32[]{:S(2)}) collective-permute-start(bf16[2048,512]{1,0:T(8,128)(2,1)} %shard_map.59.a_ref.own_ref), channel_id=1, source_target_pairs={{0,1},{1,0},{2,3},{3,2},{4,5},{5,4},{6,7},{7,6},{8,9},{9,8},{10,11... | collective-permute-start | bytes 6291464 | tf_op jit(solution)/shard_map/ppermute | solution.py:30
  17.0 25.6 %all-to-all-start.1 = ((bf16[16,64,512]{2,1,0:T(8,128)(2,1)}), bf16[16,64,512]{2,1,0:T(8,128)(2,1)S(1)}, u32[]{:S(2)}, u32[]{:S(2)}) async-start(bf16[16,64,512]{2,1,0:T(8,128)(2,1)} %shard_map.61), calls=%async_computation.1 | async-start | bytes 2097152 | tf_op jit(solution)/shard_map/all_to_all | solution.py:213
  42.6 1.0 copy-start.4
  43.6 41.3 %all-to-all-start = ((bf16[16,64,1152]{2,1,0:T(8,128)(2,1)}), bf16[16,64,1152]{2,1,0:T(8,128)(2,1)S(1)}, u32[]{:S(2)}, u32[]{:S(2)}) async-start(bf16[16,64,1152]{2,1,0:T(8,128)(2,1)} %shard_map.60.after_ref), calls=%async_computation | async-start | bytes 4718592 | tf_op jit(solution)/shard_map/all_to_all | solution.py:226
  74.0 3.5 %collective-permute-start.2 = (f32[2,64,256]{2,1,0:T(8,128)}, f32[2,64,256]{2,1,0:T(8,128)S(1)}, u32[]{:S(2)}, u32[]{:S(2)}) collective-permute-start(f32[2,64,256]{2,1,0:T(8,128)} %dynamic-slice_bitcast_fusion), channel_id=1, source_target_pairs={{0,2},{1,3},{2,0},{3,1},{4,6},{5,7},{6,4},{7,5},{8,10},{9,11},{10,... | collective-permute-start | bytes 393224 | tf_op jit(solution)/shard_map/ppermute | solution.py:30
  74.0 16.2 %collective-permute-start.4 = (bf16[256,1024]{1,0:T(8,128)(2,1)}, bf16[256,1024]{1,0:T(8,128)(2,1)S(1)}, u32[]{:S(2)}, u32[]{:S(2)}) collective-permute-start(bf16[256,1024]{1,0:T(8,128)(2,1)} %get-tuple-element.15), channel_id=1, source_target_pairs={{0,4},{1,5},{2,6},{3,7},{4,8},{5,9},{6,10},{7,11},{8,12},{9,13},{1... | collective-permute-start | bytes 1572872 | tf_op jit(solution)/shard_map/ppermute | solution.py:30
  75.6 16.6 %collective-permute-start.5 = (bf16[256,1024]{1,0:T(8,128)(2,1)}, bf16[256,1024]{1,0:T(8,128)(2,1)S(1)}, u32[]{:S(2)}, u32[]{:S(2)}) collective-permute-start(bf16[256,1024]{1,0:T(8,128)(2,1)} %get-tuple-element.16), channel_id=1, source_target_pairs={{0,16},{1,17},{2,18},{3,19},{4,20},{5,21},{6,22},{7,23},{8,24},{9,... | collective-permute-start | bytes 1572872 | tf_op jit(solution)/shard_map/ppermute | solution.py:30
  78.4 5.8 %collective-permute-start.3 = (f32[2,64,256]{2,1,0:T(8,128)S(1)}, f32[2,64,256]{2,1,0:T(8,128)S(1)}, u32[]{:S(2)}, u32[]{:S(2)}) collective-permute-start(f32[2,64,256]{2,1,0:T(8,128)S(1)} %bitcast_add_fusion), channel_id=1, source_target_pairs={{0,64},{1,65},{2,66},{3,67},{4,68},{5,69},{6,70},{7,71},{8,72},{9,... | collective-permute-start | bytes 393224 | tf_op jit(solution)/shard_map/ppermute | solution.py:30
  80.1 26.3 %collective-permute-start.8 = (bf16[256,1024]{1,0:T(8,128)(2,1)}, bf16[256,1024]{1,0:T(8,128)(2,1)}, u32[]{:S(2)}, u32[]{:S(2)}) collective-permute-start(bf16[256,1024]{1,0:T(8,128)(2,1)} %get-tuple-element.21), channel_id=1, source_target_pairs={{0,8},{1,9},{2,10},{3,11},{4,12},{5,13},{6,14},{7,15},{8,0},{9,1},... | collective-permute-start | bytes 1572872 | tf_op jit(solution)/shard_map/ppermute | solution.py:30
  82.8 24.3 %collective-permute-start.9 = (bf16[256,1024]{1,0:T(8,128)(2,1)}, bf16[256,1024]{1,0:T(8,128)(2,1)}, u32[]{:S(2)}, u32[]{:S(2)}) collective-permute-start(bf16[256,1024]{1,0:T(8,128)(2,1)} %get-tuple-element.22), channel_id=1, source_target_pairs={{0,12},{1,13},{2,14},{3,15},{4,0},{5,1},{6,2},{7,3},{8,4},{9,5},{1... | collective-permute-start | bytes 1572872 | tf_op jit(solution)/shard_map/ppermute | solution.py:30
  84.9 7.3 %copy-start = (bf16[16,64,1152]{2,1,0:T(8,128)(2,1)}, bf16[16,64,1152]{2,1,0:T(8,128)(2,1)S(1)}, u32[]{:S(2)}) copy-start(bf16[16,64,1152]{2,1,0:T(8,128)(2,1)S(1)} %all-to-all-done.got_ref) | copy-start | bytes 7077892
  90.2 1.9 %copy-start.7 = (bf16[256,1024]{1,0:T(8,128)(2,1)}, bf16[256,1024]{1,0:T(8,128)(2,1)S(1)}, u32[]{:S(2)}) copy-start(bf16[256,1024]{1,0:T(8,128)(2,1)S(1)} %collective-permute-done.4.after_ref) | copy-start | bytes 1572868
  92.1 0.8 copy-start.5
  96.3 10.7 %copy-start.8 = (bf16[256,1024]{1,0:T(8,128)(2,1)S(1)}, bf16[256,1024]{1,0:T(8,128)(2,1)}, u32[]{:S(2)}) copy-start(bf16[256,1024]{1,0:T(8,128)(2,1)} %copy-done.7) | copy-start | bytes 1572868
  96.3 10.7 %copy-start.9 = (bf16[256,1024]{1,0:T(8,128)(2,1)S(1)}, bf16[256,1024]{1,0:T(8,128)(2,1)}, u32[]{:S(2)}) copy-start(bf16[256,1024]{1,0:T(8,128)(2,1)} %get-tuple-element.14.also_ref) | copy-start | bytes 1572868
  96.3 46.2 %copy-start.6 = (bf16[256,1024]{1,0:T(8,128)(2,1)S(1)}, bf16[256,1024]{1,0:T(8,128)(2,1)}, u32[]{:S(2)}) copy-start(bf16[256,1024]{1,0:T(8,128)(2,1)} %copy-done.5) | copy-start | bytes 1572868
  96.3 46.2 %copy-start.12 = (bf16[256,1024]{1,0:T(8,128)(2,1)S(1)}, bf16[256,1024]{1,0:T(8,128)(2,1)}, u32[]{:S(2)}) copy-start(bf16[256,1024]{1,0:T(8,128)(2,1)} %get-tuple-element.23) | copy-start | bytes 1572868
  96.4 53.9 %all-to-all-start.2 = ((bf16[16,160,256]{2,1,0:T(8,128)(2,1)}), bf16[16,160,256]{2,1,0:T(8,128)(2,1)S(1)}, u32[]{:S(2)}, u32[]{:S(2)}) async-start(bf16[16,160,256]{2,1,0:T(8,128)(2,1)} %get-tuple-element.17), calls=%async_computation.2 | async-start | bytes 2621440 | tf_op jit(solution)/shard_map/all_to_all | solution.py:233
  101.8 30.7 %collective-permute-start.13 = (bf16[256,1024]{1,0:T(8,128)(2,1)}, bf16[256,1024]{1,0:T(8,128)(2,1)}, u32[]{:S(2)}, u32[]{:S(2)}) collective-permute-start(bf16[256,1024]{1,0:T(8,128)(2,1)} %get-tuple-element.24), channel_id=1, source_target_pairs={{0,32},{1,33},{2,34},{3,35},{4,36},{5,37},{6,38},{7,39},{8,40},{9,... | collective-permute-start | bytes 1572872 | tf_op jit(solution)/shard_map/ppermute | solution.py:30
  105.2 37.3 %collective-permute-start.14 = (bf16[256,1024]{1,0:T(8,128)(2,1)}, bf16[256,1024]{1,0:T(8,128)(2,1)}, u32[]{:S(2)}, u32[]{:S(2)}) collective-permute-start(bf16[256,1024]{1,0:T(8,128)(2,1)} %get-tuple-element.25), channel_id=1, source_target_pairs={{0,48},{1,49},{2,50},{3,51},{4,52},{5,53},{6,54},{7,55},{8,56},{9,... | collective-permute-start | bytes 1572872 | tf_op jit(solution)/shard_map/ppermute | solution.py:30
  108.5 40.0 %collective-permute-start.10 = (bf16[64,1024]{1,0:T(8,128)(2,1)S(1)}, bf16[64,1024]{1,0:T(8,128)(2,1)S(1)}, u32[]{:S(2)}, u32[]{:S(2)}) collective-permute-start(bf16[64,1024]{1,0:T(8,128)(2,1)S(1)} %get-tuple-element.26), channel_id=1, source_target_pairs={{0,16},{1,17},{2,18},{3,19},{4,20},{5,21},{6,22},{7,23},{8,24},{9,... | collective-permute-start | bytes 393224 | tf_op jit(solution)/shard_map/ppermute | solution.py:30
  110.5 38.7 %collective-permute-start.11 = (bf16[64,1024]{1,0:T(8,128)(2,1)S(1)}, bf16[64,1024]{1,0:T(8,128)(2,1)S(1)}, u32[]{:S(2)}, u32[]{:S(2)}) collective-permute-start(bf16[64,1024]{1,0:T(8,128)(2,1)S(1)} %get-tuple-element.28), channel_id=1, source_target_pairs={{0,32},{1,33},{2,34},{3,35},{4,36},{5,37},{6,38},{7,39},{8,40},{9,... | collective-permute-start | bytes 393224 | tf_op jit(solution)/shard_map/ppermute | solution.py:30
  113.2 35.9 %collective-permute-start.12 = (bf16[64,1024]{1,0:T(8,128)(2,1)S(1)}, bf16[64,1024]{1,0:T(8,128)(2,1)S(1)}, u32[]{:S(2)}, u32[]{:S(2)}) collective-permute-start(bf16[64,1024]{1,0:T(8,128)(2,1)S(1)} %get-tuple-element.27), channel_id=1, source_target_pairs={{0,48},{1,49},{2,50},{3,51},{4,52},{5,53},{6,54},{7,55},{8,56},{9,... | collective-permute-start | bytes 393224 | tf_op jit(solution)/shard_map/ppermute | solution.py:30
  144.6 6.4 %collective-permute-start.15 = (bf16[64,1024]{1,0:T(8,128)(2,1)}, bf16[64,1024]{1,0:T(8,128)(2,1)S(1)}, u32[]{:S(2)}, u32[]{:S(2)}) collective-permute-start(bf16[64,1024]{1,0:T(8,128)(2,1)} %get-tuple-element.29), channel_id=1, source_target_pairs={{0,4},{1,5},{2,6},{3,7},{4,8},{5,9},{6,10},{7,11},{8,12},{9,13},{1... | collective-permute-start | bytes 393224 | tf_op jit(solution)/shard_map/ppermute | solution.py:30
  146.0 7.2 %collective-permute-start.16 = (bf16[64,1024]{1,0:T(8,128)(2,1)}, bf16[64,1024]{1,0:T(8,128)(2,1)}, u32[]{:S(2)}, u32[]{:S(2)}) collective-permute-start(bf16[64,1024]{1,0:T(8,128)(2,1)} %get-tuple-element.31), channel_id=1, source_target_pairs={{0,8},{1,9},{2,10},{3,11},{4,12},{5,13},{6,14},{7,15},{8,0},{9,1},... | collective-permute-start | bytes 393224 | tf_op jit(solution)/shard_map/ppermute | solution.py:30
  148.6 5.3 %collective-permute-start.17 = (bf16[64,1024]{1,0:T(8,128)(2,1)}, bf16[64,1024]{1,0:T(8,128)(2,1)}, u32[]{:S(2)}, u32[]{:S(2)}) collective-permute-start(bf16[64,1024]{1,0:T(8,128)(2,1)} %get-tuple-element.30), channel_id=1, source_target_pairs={{0,12},{1,13},{2,14},{3,15},{4,0},{5,1},{6,2},{7,3},{8,4},{9,5},{1... | collective-permute-start | bytes 393224 | tf_op jit(solution)/shard_map/ppermute | solution.py:30
  150.3 8.4 %copy-start.2 = (bf16[16,160,256]{2,1,0:T(8,128)(2,1)}, bf16[16,160,256]{2,1,0:T(8,128)(2,1)S(1)}, u32[]{:S(2)}) copy-start(bf16[16,160,256]{2,1,0:T(8,128)(2,1)S(1)} %all-to-all-done.2.pt_ref) | copy-start | bytes 3932164
  150.7 5.2 %collective-permute-start.7 = (bf16[64,1024]{1,0:T(8,128)(2,1)S(1)}, bf16[64,1024]{1,0:T(8,128)(2,1)S(1)}, u32[]{:S(2)}, u32[]{:S(2)}) collective-permute-start(bf16[64,1024]{1,0:T(8,128)(2,1)S(1)} %bitcast.26), channel_id=1, source_target_pairs={{0,2},{1,3},{2,0},{3,1},{4,6},{5,7},{6,4},{7,5},{8,10},{9,11},{10,... | collective-permute-start | bytes 393224 | tf_op jit(solution)/shard_map/ppermute | solution.py:30
  155.9 0.7 copy-start.13
  158.7 8.5 %copy-start.3 = (f32[64,2048]{1,0:T(8,128)S(1)}, f32[64,2048]{1,0:T(8,128)}, u32[]{:S(2)}) copy-start(f32[64,2048]{1,0:T(8,128)} %shard_map.66) | copy-start | bytes 1572868
  158.8 8.5 %copy-start.10 = (f32[64,2048]{1,0:T(8,128)S(1)}, f32[64,2048]{1,0:T(8,128)}, u32[]{:S(2)}) copy-start(f32[64,2048]{1,0:T(8,128)} %param.5) | copy-start | bytes 1572868
  158.8 8.5 %collective-permute-start.18 = (bf16[64,2048]{1,0:T(8,128)(2,1)S(1)}, bf16[64,2048]{1,0:T(8,128)(2,1)S(1)}, u32[]{:S(2)}, u32[]{:S(2)}) collective-permute-start(bf16[64,2048]{1,0:T(8,128)(2,1)S(1)} %select_convert_fusion), channel_id=1, source_target_pairs={{0,64},{1,65},{2,66},{3,67},{4,68},{5,69},{6,70},{7,71},{8,72},{9,... | collective-permute-start | bytes 786440 | tf_op jit(solution)/shard_map/ppermute | solution.py:30
  167.3 2.1 %copy-start.11 = (f32[512,256]{1,0:T(8,128)S(1)}, f32[512,256]{1,0:T(8,128)}, u32[]{:S(2)}) copy-start(f32[512,256]{1,0:T(8,128)} %get-tuple-element.18) | copy-start | bytes 1572868
  167.3 2.1 %collective-permute-start.6 = (f32[512,256]{1,0:T(8,128)}, f32[512,256]{1,0:T(8,128)S(1)}, u32[]{:S(2)}, u32[]{:S(2)}) collective-permute-start(f32[512,256]{1,0:T(8,128)} %get-tuple-element.19), channel_id=1, source_target_pairs={{0,2},{1,3},{2,0},{3,1},{4,6},{5,7},{6,4},{7,5},{8,10},{9,11},{10,... | collective-permute-start | bytes 1572872 | tf_op jit(solution)/shard_map/ppermute | solution.py:30

commit v10 on v9

--- a/solution.py
+++ b/solution.py
@@ -153,7 +153,8 @@
     return jnp.concatenate(sums, axis=1)
 
 
-def own_sum_kernel(at_ref, got_ref, pt_ref, after_ref, also_ref, direct_ref, slots_ref):
+def own_sum_kernel(at_ref, got_ref, pt_ref, *refs):
+    direct_ref, slots_ref = refs[-2:]
     chip = at_ref[0] * 4 + at_ref[1]
     rows = direct_ref.shape[0]
     wide, low = 2 * rows, rows // 2
@@ -227,8 +228,8 @@
     direct, slots = kernel_call(
         own_sum_kernel,
         [shape((rows, feats), f32), shape((16, 2 * rows + rows // 2, tests), bf16)],
-        [SMEM, VMEM, VMEM, ANY, ANY],
-        at, own, pt.reshape(2 * rows, tests), crossed[0][0], crossed[1][0],
+        [SMEM, VMEM, VMEM] + [ANY] * 6,
+        at, own, pt.reshape(2 * rows, tests), *crossed[0], *crossed[1],
     )
     slots = lax.all_to_all(slots, ("z", "x"), split_axis=0, concat_axis=0, tiled=True)
     mirror = slots[:, 2 * rows :]

time: 172 us -> 166 us (0.965)
  waiting for transfers between devices: 67 us -> 57.9 us
  starting transfers between devices: 48.8 us -> 53.6 us
    ppermute x19, waiting for transfers between devices: 57.1 us -> 48 us  [send(): return lax.ppermute(value, AXES, pairs)]
    all_to_all x2, starting transfers between devices: 13.3 us -> 16.8 us  [on_device(): lax.all_to_all(slots, ('z', 'x'), split_axis=0, concat_axis=0, tiled=True)]
  transfers between devices with their start and end apart: 22 -> 22, of which waited for: 12 -> 12; matrix products, arithmetic and copies ran while one was open for 7% -> 7% of each run, Pallas kernels for 17% -> 16%
where the time goes in v10:
time: 166 us; the launch traced here: 165 us
  waiting for transfers between devices  57.9 us (35%)
  starting transfers between devices  53.6 us (32%)
  Pallas kernels  35.3 us (21%)
  other arithmetic  10.2 us (6%)
  local copies, waits for them, and re-layouts  6.64 us (4%)
    ppermute x19, waiting for transfers between devices, send(): return lax.ppermute(value, AXES, pairs)  48 us
    pallas_call x8, Pallas kernels, kernel_call(): pl.pallas_call(body, out_shape=outs, in_specs=specs, out_specs=[VMEM] * l...  35.3 us
    ppermute x19, starting transfers between devices, send(): return lax.ppermute(value, AXES, pairs)  33 us
    all_to_all x2, starting transfers between devices, on_device(): lax.all_to_all(slots, ('z', 'x'), split_axis=0, concat_axis=0, tiled=True)  16.8 us
    all_to_all x2, waiting for transfers between devices, on_device(): lax.all_to_all(slots, ('z', 'x'), split_axis=0, concat_axis=0, tiled=True)  9.9 us
    unnamed x31, local copies, waits for them, and re-layouts  5.46 us
    all_to_all x1, starting transfers between devices, on_device(): lax.all_to_all(own, ('z', 'x'), split_axis=0, concat_axis=0, tiled=True)  3.72 us
    convert_element_type x2, other arithmetic, second_stage(): rs = [send(mids[k].astype(bf16), along(axis, k)) for k in (1, 2, 3)]  3.58 us
  transfers between devices with their start and end apart: 22, of which 12 were waited for; matrix products, arithmetic and copies ran while one was open for 7% of the time, Pallas kernels for 16%

profile of v10, /device:TPU:0, one launch (start us, length us, event | category | flops | bytes accessed | tf_op | source)
XLA Modules:
  0.0 164.6 jit_solution(18146819611958546224)
XLA Ops:
  0.6 2.9 %copy.8 = bf16[512,2048]{0,1:T(8,128)(2,1)S(1)} copy(bf16[512,2048]{1,0:T(8,128)(2,1)} %param.4) | data formatting | bytes 4194304 | tf_op args[0]
  3.6 0.8 pad_add_fusion.at_ref
  4.5 3.4 %collective-permute-done.sib_ref.b2_ref = bf16[2048,512]{1,0:T(8,128)(2,1)} collective-permute-done((bf16[2048,512]{1,0:T(8,128)(2,1)S(1)}, bf16[2048,512]{1,0:T(8,128)(2,1)}, u32[]{:S(2)}, u32[]{:S(2)}) %collective-permute-start) | collective-permute-done | bytes 2097184 | tf_op jit(solution)/shard_map/ppermute | solution.py:30
  7.9 3.7 %shard_map.59.a_ref.own_ref = bf16[2048,512]{1,0:T(8,128)(2,1)} custom-call(s32[4]{0:T(128)} %pad_add_fusion.at_ref, bf16[2048,512]{1,0:T(8,128)(2,1)} %bitcast.17, bf16[2048,512]{1,0:T(8,128)(2,1)} %collective-permute-done.sib_ref.b2_ref), custom_call_target="tpu_custom_call" | custom-call | bytes 6291472 | tf_op jit(solution)/shard_map/pallas_call | solution.py:43
  11.6 3.3 %collective-permute-start.1 = (bf16[2048,512]{1,0:T(8,128)(2,1)}, bf16[2048,512]{1,0:T(8,128)(2,1)}, u32[]{:S(2)}, u32[]{:S(2)}) collective-permute-start(bf16[2048,512]{1,0:T(8,128)(2,1)} %shard_map.59.a_ref.own_ref), channel_id=1, source_target_pairs={{0,1},{1,0},{2,3},{3,2},{4,5},{5,4},{6,7},{7,6},{8,9},{9,8},{10,11... | collective-permute-start | bytes 6291464 | tf_op jit(solution)/shard_map/ppermute | solution.py:30
  14.9 2.1 %shard_map.61 = bf16[16,64,512]{2,1,0:T(8,128)(2,1)} custom-call(bf16[64,4096]{1,0:T(8,128)(2,1)} %f_ref.1, bf16[64,256]{1,0:T(8,128)(2,1)} %bitcast.27), custom_call_target="tpu_custom_call" | custom-call | bytes 1605632 | tf_op jit(solution)/shard_map/pallas_call | solution.py:43
  17.0 7.9 %all-to-all-start.1 = ((bf16[16,64,512]{2,1,0:T(8,128)(2,1)}), bf16[16,64,512]{2,1,0:T(8,128)(2,1)S(1)}, u32[]{:S(2)}, u32[]{:S(2)}) async-start(bf16[16,64,512]{2,1,0:T(8,128)(2,1)} %shard_map.61), calls=%async_computation.1 | async-start | bytes 2097152 | tf_op jit(solution)/shard_map/all_to_all | solution.py:214
  24.9 7.8 %shard_map.60.after_ref = bf16[16,64,1152]{2,1,0:T(8,128)(2,1)} custom-call(bf16[2048,512]{1,0:T(8,128)(2,1)} %shard_map.59.a_ref.own_ref, bf16[2048,512]{1,0:T(8,128)(2,1)} %bitcast.18, bf16[2048,512]{1,0:T(8,128)(2,1)} %collective-permute-done.sib_ref.b2_ref), custom_call_target="tpu_custom_call" | custom-call | flops 3221225472 | bytes 8650752 | tf_op jit(solution)/shard_map/pallas_call | solution.py:43
  32.7 9.9 %all-to-all-done.1 = bf16[16,64,512]{2,1,0:T(8,128)(2,1)S(1)} async-done(((bf16[16,64,512]{2,1,0:T(8,128)(2,1)}), bf16[16,64,512]{2,1,0:T(8,128)(2,1)S(1)}, u32[]{:S(2)}, u32[]{:S(2)}) %all-to-all-start.1) | async-done | bytes 1048608 | tf_op jit(solution)/shard_map/all_to_all | solution.py:214
  42.6 1.0 copy-done.4
  43.6 3.7 %all-to-all-start = ((bf16[16,64,1152]{2,1,0:T(8,128)(2,1)}), bf16[16,64,1152]{2,1,0:T(8,128)(2,1)S(1)}, u32[]{:S(2)}, u32[]{:S(2)}) async-start(bf16[16,64,1152]{2,1,0:T(8,128)(2,1)} %shard_map.60.after_ref), calls=%async_computation | async-start | bytes 4718592 | tf_op jit(solution)/shard_map/all_to_all | solution.py:227
  47.3 13.8 %collective-permute-done.1.a_ref.cross_ref = bf16[2048,512]{1,0:T(8,128)(2,1)} collective-permute-done((bf16[2048,512]{1,0:T(8,128)(2,1)}, bf16[2048,512]{1,0:T(8,128)(2,1)}, u32[]{:S(2)}, u32[]{:S(2)}) %collective-permute-start.1) | collective-permute-done | bytes 2097184 | tf_op jit(solution)/shard_map/ppermute | solution.py:30
  61.1 9.0 %shard_map.62 = (bf16[256,1024]{1,0:T(8,128)(2,1)}, bf16[256,1024]{1,0:T(8,128)(2,1)}, bf16[256,1024]{1,0:T(8,128)(2,1)}, bf16[256,1024]{1,0:T(8,128)(2,1)}, bf1...) custom-call(s32[4]{0:T(128)} %pad_add_fusion.at_ref, ...), custom_call_target="tpu_custom_call" | custom-call | flops 4294967296 | bytes 12845072 | tf_op jit(solution)/shard_map/pallas_call | solution.py:43
  70.1 1.5 collective-permute-start.4
  71.7 2.3 %shard_map.63 = f32[256,256]{1,0:T(8,128)} custom-call(bf16[1024,512]{1,0:T(8,128)(2,1)} %bitcast.20, bf16[16,64,1152]{2,1,0:T(8,128)(2,1)} %shard_map.60.after_ref, bf16[256,1024]{1,0:T(8,128)(2,1)} %get-tuple-element.14.also_ref), custom_call_target="tpu_custom_call" | custom-call | flops 134217728 | bytes 4194304 | tf_op jit(solution)/shard_map/pallas_call | solution.py:43
  74.0 0.9 dynamic-slice_bitcast_fusion
  75.0 1.3 collective-permute-done.2
  76.3 0.9 bitcast_add_fusion
  77.2 1.7 %collective-permute-start.3 = (f32[2,64,256]{2,1,0:T(8,128)S(1)}, f32[2,64,256]{2,1,0:T(8,128)S(1)}, u32[]{:S(2)}, u32[]{:S(2)}) collective-permute-start(f32[2,64,256]{2,1,0:T(8,128)S(1)} %bitcast_add_fusion), channel_id=1, source_target_pairs={{0,64},{1,65},{2,66},{3,67},{4,68},{5,69},{6,70},{7,71},{8,72},{9,... | collective-permute-start | bytes 393224 | tf_op jit(solution)/shard_map/ppermute | solution.py:30
  78.9 2.7 %collective-permute-start.5 = (bf16[256,1024]{1,0:T(8,128)(2,1)}, bf16[256,1024]{1,0:T(8,128)(2,1)}, u32[]{:S(2)}, u32[]{:S(2)}) collective-permute-start(bf16[256,1024]{1,0:T(8,128)(2,1)} %get-tuple-element.16), channel_id=1, source_target_pairs={{0,8},{1,9},{2,10},{3,11},{4,12},{5,13},{6,14},{7,15},{8,0},{9,1},... | collective-permute-start | bytes 1572872 | tf_op jit(solution)/shard_map/ppermute | solution.py:30
  81.6 1.4 collective-permute-start.6
  83.1 1.9 %collective-permute-start.7 = (bf16[256,1024]{1,0:T(8,128)(2,1)}, bf16[256,1024]{1,0:T(8,128)(2,1)S(1)}, u32[]{:S(2)}, u32[]{:S(2)}) collective-permute-start(bf16[256,1024]{1,0:T(8,128)(2,1)} %get-tuple-element.18), channel_id=1, source_target_pairs={{0,16},{1,17},{2,18},{3,19},{4,20},{5,21},{6,22},{7,23},{8,24},{9,... | collective-permute-start | bytes 1572872 | tf_op jit(solution)/shard_map/ppermute | solution.py:30
  85.0 3.6 %collective-permute-start.8 = (bf16[256,1024]{1,0:T(8,128)(2,1)}, bf16[256,1024]{1,0:T(8,128)(2,1)}, u32[]{:S(2)}, u32[]{:S(2)}) collective-permute-start(bf16[256,1024]{1,0:T(8,128)(2,1)} %get-tuple-element.19), channel_id=1, source_target_pairs={{0,32},{1,33},{2,34},{3,35},{4,36},{5,37},{6,38},{7,39},{8,40},{9,... | collective-permute-start | bytes 1572872 | tf_op jit(solution)/shard_map/ppermute | solution.py:30
  88.8 3.2 %collective-permute-start.9 = (bf16[256,1024]{1,0:T(8,128)(2,1)}, bf16[256,1024]{1,0:T(8,128)(2,1)}, u32[]{:S(2)}, u32[]{:S(2)}) collective-permute-start(bf16[256,1024]{1,0:T(8,128)(2,1)} %get-tuple-element.20), channel_id=1, source_target_pairs={{0,48},{1,49},{2,50},{3,51},{4,52},{5,53},{6,54},{7,55},{8,56},{9,... | collective-permute-start | bytes 1572872 | tf_op jit(solution)/shard_map/ppermute | solution.py:30
  92.6 8.2 %collective-permute-done.5.refs_1_ = bf16[256,1024]{1,0:T(8,128)(2,1)} collective-permute-done((bf16[256,1024]{1,0:T(8,128)(2,1)}, bf16[256,1024]{1,0:T(8,128)(2,1)}, u32[]{:S(2)}, u32[]{:S(2)}) %collective-permute-start.5) | collective-permute-done | bytes 524320 | tf_op jit(solution)/shard_map/ppermute | solution.py:30
  100.8 3.9 %collective-permute-done.6.refs_2_ = bf16[256,1024]{1,0:T(8,128)(2,1)} collective-permute-done((bf16[256,1024]{1,0:T(8,128)(2,1)}, bf16[256,1024]{1,0:T(8,128)(2,1)}, u32[]{:S(2)}, u32[]{:S(2)}) %collective-permute-start.6) | collective-permute-done | bytes 524320 | tf_op jit(solution)/shard_map/ppermute | solution.py:30
  104.8 6.5 %collective-permute-done.8.refs_4_ = bf16[256,1024]{1,0:T(8,128)(2,1)} collective-permute-done((bf16[256,1024]{1,0:T(8,128)(2,1)}, bf16[256,1024]{1,0:T(8,128)(2,1)}, u32[]{:S(2)}, u32[]{:S(2)}) %collective-permute-start.8) | collective-permute-done | bytes 524320 | tf_op jit(solution)/shard_map/ppermute | solution.py:30
  111.2 3.4 %shard_map.64 = (f32[64,2048]{1,0:T(8,128)}, bf16[16,160,256]{2,1,0:T(8,128)(2,1)}) custom-call(s32[4]{0:T(128)} %pad_add_fusion.at_ref, bf16[16,64,1152]{2,1,0:T(8,128)(2,1)} %copy-done, bf16[128,256]{1,0:T(8,128)(2,1)} %bitcast.25, bf16[256,1024]{1,0:T(8,128)(2,1)} %copy-done.7, bf16[256,1024]{1,0:T(8,128)(2,1)} %collective-permute-done.5.refs_1_, ...), custom_call_target="tpu_custom_call" | custom-call | bytes 7405584 | tf_op jit(solution)/shard_map/pallas_call | solution.py:43
  114.6 9.0 %all-to-all-start.2 = ((bf16[16,160,256]{2,1,0:T(8,128)(2,1)}), bf16[16,160,256]{2,1,0:T(8,128)(2,1)S(1)}, u32[]{:S(2)}, u32[]{:S(2)}) async-start(bf16[16,160,256]{2,1,0:T(8,128)(2,1)} %get-tuple-element.21), calls=%async_computation.2 | async-start | bytes 2621440 | tf_op jit(solution)/shard_map/all_to_all | solution.py:234
  123.7 1.5 add_convert_fusion.5
  125.1 2.0 %collective-permute-start.12 = (bf16[64,1024]{1,0:T(8,128)(2,1)S(1)}, bf16[64,1024]{1,0:T(8,128)(2,1)S(1)}, u32[]{:S(2)}, u32[]{:S(2)}) collective-permute-start(bf16[64,1024]{1,0:T(8,128)(2,1)S(1)} %get-tuple-element.26), channel_id=1, source_target_pairs={{0,16},{1,17},{2,18},{3,19},{4,20},{5,21},{6,22},{7,23},{8,24},{9,... | collective-permute-start | bytes 393224 | tf_op jit(solution)/shard_map/ppermute | solution.py:30
  127.1 2.7 %collective-permute-start.13 = (bf16[64,1024]{1,0:T(8,128)(2,1)S(1)}, bf16[64,1024]{1,0:T(8,128)(2,1)S(1)}, u32[]{:S(2)}, u32[]{:S(2)}) collective-permute-start(bf16[64,1024]{1,0:T(8,128)(2,1)S(1)} %get-tuple-element.28), channel_id=1, source_target_pairs={{0,32},{1,33},{2,34},{3,35},{4,36},{5,37},{6,38},{7,39},{8,40},{9,... | collective-permute-start | bytes 393224 | tf_op jit(solution)/shard_map/ppermute | solution.py:30
  129.8 1.5 collective-permute-start.14
  131.2 2.1 %add_convert_fusion.2 = (bf16[64,1024]{1,0:T(8,128)(2,1)}, bf16[64,1024]{1,0:T(8,128)(2,1)}, bf16[64,1024]{1,0:T(8,128)(2,1)}) fusion(bf16[256,1024]{1,0:T(8,128)(2,1)} %collective-permute-done.9.refs_5_, bf16[256,1024]{1,0:T(8,128)(2,1)} %collective-permute-done.8.refs_4_, bf16[256,1024]{1,0:T(8,128)(2,1)S(1)} %copy-done.6, bf16[256,1024]{1,0:T(8,128)(2,1)S(1)} %copy-done.12), kind=kLoop, calls=%fused_computation.7 | loop fusion | flops 1572864 | bytes 1966080 | tf_op jit(solution)/shard_map/convert_element_type | solution.py:151
  133.4 1.5 collective-permute-start.15
  134.8 2.7 %collective-permute-start.16 = (bf16[64,1024]{1,0:T(8,128)(2,1)}, bf16[64,1024]{1,0:T(8,128)(2,1)}, u32[]{:S(2)}, u32[]{:S(2)}) collective-permute-start(bf16[64,1024]{1,0:T(8,128)(2,1)} %get-tuple-element.31), channel_id=1, source_target_pairs={{0,8},{1,9},{2,10},{3,11},{4,12},{5,13},{6,14},{7,15},{8,0},{9,1},... | collective-permute-start | bytes 393224 | tf_op jit(solution)/shard_map/ppermute | solution.py:30
  137.5 7.6 %collective-permute-done.12 = bf16[64,1024]{1,0:T(8,128)(2,1)S(1)} collective-permute-done((bf16[64,1024]{1,0:T(8,128)(2,1)S(1)}, bf16[64,1024]{1,0:T(8,128)(2,1)S(1)}, u32[]{:S(2)}, u32[]{:S(2)}) %collective-permute-start.12) | collective-permute-done | bytes 131104 | tf_op jit(solution)/shard_map/ppermute | solution.py:30
  145.1 1.8 %collective-permute-start.17 = (bf16[64,1024]{1,0:T(8,128)(2,1)}, bf16[64,1024]{1,0:T(8,128)(2,1)}, u32[]{:S(2)}, u32[]{:S(2)}) collective-permute-start(bf16[64,1024]{1,0:T(8,128)(2,1)} %get-tuple-element.30), channel_id=1, source_target_pairs={{0,12},{1,13},{2,14},{3,15},{4,0},{5,1},{6,2},{7,3},{8,4},{9,5},{1... | collective-permute-start | bytes 393224 | tf_op jit(solution)/shard_map/ppermute | solution.py:30
  146.8 1.1 convert_add_fusion.1
  148.5 1.8 %collective-permute-done.17 = bf16[64,1024]{1,0:T(8,128)(2,1)} collective-permute-done((bf16[64,1024]{1,0:T(8,128)(2,1)}, bf16[64,1024]{1,0:T(8,128)(2,1)}, u32[]{:S(2)}, u32[]{:S(2)}) %collective-permute-start.17) | collective-permute-done | bytes 131104 | tf_op jit(solution)/shard_map/ppermute | solution.py:30
  150.3 1.3 convert_add_fusion
  151.6 0.8 copy.11
  152.4 0.7 copy-done.13
  153.1 2.1 %shard_map.66 = f32[64,2048]{1,0:T(8,128)} custom-call(s32[4]{0:T(128)} %pad_add_fusion.at_ref, f32[64,2048]{1,0:T(8,128)} %get-tuple-element.24.direct_ref, bf16[64,1024]{1,0:T(8,128)(2,1)} %bitcast.24, bf16[64,1024]{1,0:T(8,128)(2,1)} %copy-done.13), custom_call_target="tpu_custom_call" | custom-call | bytes 1310736 | tf_op jit(solution)/shard_map/pallas_call | solution.py:43
  155.2 1.5 collective-permute-start.18
  156.7 4.9 %shard_map.65 = (f32[512,256]{1,0:T(8,128)}, f32[512,256]{1,0:T(8,128)}) custom-call(s32[4]{0:T(128)} %pad_add_fusion.at_ref, bf16[16,160,256]{2,1,0:T(8,128)(2,1)} %copy-done.2, bf16[2048,512]{1,0:T(8,128)(2,1)} %shard_map.59.a_ref.own_ref, bf16[2048,512]{1,0:T(8,128)(2,1)} %collective-permute-done.1.a_ref.cross_ref), custom_call_target="tpu_custom_call" | custom-call | flops 1073741824 | bytes 6553616 | tf_op jit(solution)/shard_map/pallas_call | solution.py:43
  162.2 0.9 multiply_add_fusion
  163.7 0.9 add.123
  (49 shorter events, 2.9 us)
Async XLA Ops:
  3.5 4.4 %copy-start.1 = (bf16[512,2048]{0,1:T(8,128)(2,1)}, bf16[512,2048]{0,1:T(8,128)(2,1)S(1)}, u32[]{:S(2)}) copy-start(bf16[512,2048]{0,1:T(8,128)(2,1)S(1)} %copy.8) | copy-start | bytes 6291460
  3.5 4.4 %collective-permute-start = (bf16[2048,512]{1,0:T(8,128)(2,1)S(1)}, bf16[2048,512]{1,0:T(8,128)(2,1)}, u32[]{:S(2)}, u32[]{:S(2)}) collective-permute-start(bf16[2048,512]{1,0:T(8,128)(2,1)S(1)} %bitcast.16), channel_id=1, source_target_pairs={{0,2},{1,3},{2,0},{3,1},{4,6},{5,7},{6,4},{7,5},{8,10},{9,11},{10,... | collective-permute-start | bytes 6291464 | tf_op jit(solution)/shard_map/ppermute | solution.py:30
  11.6 49.5 %collective-permute-start.1 = (bf16[2048,512]{1,0:T(8,128)(2,1)}, bf16[2048,512]{1,0:T(8,128)(2,1)}, u32[]{:S(2)}, u32[]{:S(2)}) collective-permute-start(bf16[2048,512]{1,0:T(8,128)(2,1)} %shard_map.59.a_ref.own_ref), channel_id=1, source_target_pairs={{0,1},{1,0},{2,3},{3,2},{4,5},{5,4},{6,7},{7,6},{8,9},{9,8},{10,11... | collective-permute-start | bytes 6291464 | tf_op jit(solution)/shard_map/ppermute | solution.py:30
  17.0 25.6 %all-to-all-start.1 = ((bf16[16,64,512]{2,1,0:T(8,128)(2,1)}), bf16[16,64,512]{2,1,0:T(8,128)(2,1)S(1)}, u32[]{:S(2)}, u32[]{:S(2)}) async-start(bf16[16,64,512]{2,1,0:T(8,128)(2,1)} %shard_map.61), calls=%async_computation.1 | async-start | bytes 2097152 | tf_op jit(solution)/shard_map/all_to_all | solution.py:214
  42.6 1.0 copy-start.4
  43.6 49.1 %all-to-all-start = ((bf16[16,64,1152]{2,1,0:T(8,128)(2,1)}), bf16[16,64,1152]{2,1,0:T(8,128)(2,1)S(1)}, u32[]{:S(2)}, u32[]{:S(2)}) async-start(bf16[16,64,1152]{2,1,0:T(8,128)(2,1)} %shard_map.60.after_ref), calls=%async_computation | async-start | bytes 4718592 | tf_op jit(solution)/shard_map/all_to_all | solution.py:227
  70.1 18.7 %collective-permute-start.4 = (bf16[256,1024]{1,0:T(8,128)(2,1)}, bf16[256,1024]{1,0:T(8,128)(2,1)S(1)}, u32[]{:S(2)}, u32[]{:S(2)}) collective-permute-start(bf16[256,1024]{1,0:T(8,128)(2,1)} %get-tuple-element.15), channel_id=1, source_target_pairs={{0,4},{1,5},{2,6},{3,7},{4,8},{5,9},{6,10},{7,11},{8,12},{9,13},{1... | collective-permute-start | bytes 1572872 | tf_op jit(solution)/shard_map/ppermute | solution.py:30
  74.9 1.4 collective-permute-start.2
  77.2 7.7 %collective-permute-start.3 = (f32[2,64,256]{2,1,0:T(8,128)S(1)}, f32[2,64,256]{2,1,0:T(8,128)S(1)}, u32[]{:S(2)}, u32[]{:S(2)}) collective-permute-start(f32[2,64,256]{2,1,0:T(8,128)S(1)} %bitcast_add_fusion), channel_id=1, source_target_pairs={{0,64},{1,65},{2,66},{3,67},{4,68},{5,69},{6,70},{7,71},{8,72},{9,... | collective-permute-start | bytes 393224 | tf_op jit(solution)/shard_map/ppermute | solution.py:30
  78.9 21.9 %collective-permute-start.5 = (bf16[256,1024]{1,0:T(8,128)(2,1)}, bf16[256,1024]{1,0:T(8,128)(2,1)}, u32[]{:S(2)}, u32[]{:S(2)}) collective-permute-start(bf16[256,1024]{1,0:T(8,128)(2,1)} %get-tuple-element.16), channel_id=1, source_target_pairs={{0,8},{1,9},{2,10},{3,11},{4,12},{5,13},{6,14},{7,15},{8,0},{9,1},... | collective-permute-start | bytes 1572872 | tf_op jit(solution)/shard_map/ppermute | solution.py:30
  81.6 23.1 %collective-permute-start.6 = (bf16[256,1024]{1,0:T(8,128)(2,1)}, bf16[256,1024]{1,0:T(8,128)(2,1)}, u32[]{:S(2)}, u32[]{:S(2)}) collective-permute-start(bf16[256,1024]{1,0:T(8,128)(2,1)} %get-tuple-element.17), channel_id=1, source_target_pairs={{0,12},{1,13},{2,14},{3,15},{4,0},{5,1},{6,2},{7,3},{8,4},{9,5},{1... | collective-permute-start | bytes 1572872 | tf_op jit(solution)/shard_map/ppermute | solution.py:30
  83.1 21.7 %collective-permute-start.7 = (bf16[256,1024]{1,0:T(8,128)(2,1)}, bf16[256,1024]{1,0:T(8,128)(2,1)S(1)}, u32[]{:S(2)}, u32[]{:S(2)}) collective-permute-start(bf16[256,1024]{1,0:T(8,128)(2,1)} %get-tuple-element.18), channel_id=1, source_target_pairs={{0,16},{1,17},{2,18},{3,19},{4,20},{5,21},{6,22},{7,23},{8,24},{9,... | collective-permute-start | bytes 1572872 | tf_op jit(solution)/shard_map/ppermute | solution.py:30
  85.0 26.2 %collective-permute-start.8 = (bf16[256,1024]{1,0:T(8,128)(2,1)}, bf16[256,1024]{1,0:T(8,128)(2,1)}, u32[]{:S(2)}, u32[]{:S(2)}) collective-permute-start(bf16[256,1024]{1,0:T(8,128)(2,1)} %get-tuple-element.19), channel_id=1, source_target_pairs={{0,32},{1,33},{2,34},{3,35},{4,36},{5,37},{6,38},{7,39},{8,40},{9,... | collective-permute-start | bytes 1572872 | tf_op jit(solution)/shard_map/ppermute | solution.py:30
  88.8 22.4 %copy-start.7 = (bf16[256,1024]{1,0:T(8,128)(2,1)}, bf16[256,1024]{1,0:T(8,128)(2,1)S(1)}, u32[]{:S(2)}) copy-start(bf16[256,1024]{1,0:T(8,128)(2,1)S(1)} %collective-permute-done.4.refs_0_) | copy-start | bytes 1572868
  88.8 22.4 %collective-permute-start.9 = (bf16[256,1024]{1,0:T(8,128)(2,1)}, bf16[256,1024]{1,0:T(8,128)(2,1)}, u32[]{:S(2)}, u32[]{:S(2)}) collective-permute-start(bf16[256,1024]{1,0:T(8,128)(2,1)} %get-tuple-element.20), channel_id=1, source_target_pairs={{0,48},{1,49},{2,50},{3,51},{4,52},{5,53},{6,54},{7,55},{8,56},{9,... | collective-permute-start | bytes 1572872 | tf_op jit(solution)/shard_map/ppermute | solution.py:30
  92.6 18.6 %copy-start = (bf16[16,64,1152]{2,1,0:T(8,128)(2,1)}, bf16[16,64,1152]{2,1,0:T(8,128)(2,1)S(1)}, u32[]{:S(2)}) copy-start(bf16[16,64,1152]{2,1,0:T(8,128)(2,1)S(1)} %all-to-all-done.got_ref) | copy-start | bytes 7077892
  104.8 6.5 %copy-start.5 = (bf16[256,1024]{1,0:T(8,128)(2,1)}, bf16[256,1024]{1,0:T(8,128)(2,1)S(1)}, u32[]{:S(2)}) copy-start(bf16[256,1024]{1,0:T(8,128)(2,1)S(1)} %collective-permute-done.7.refs_3_) | copy-start | bytes 1572868
  114.6 9.0 %copy-start.8 = (bf16[256,1024]{1,0:T(8,128)(2,1)S(1)}, bf16[256,1024]{1,0:T(8,128)(2,1)}, u32[]{:S(2)}) copy-start(bf16[256,1024]{1,0:T(8,128)(2,1)} %copy-done.7) | copy-start | bytes 1572868
  114.6 9.0 %copy-start.9 = (bf16[256,1024]{1,0:T(8,128)(2,1)S(1)}, bf16[256,1024]{1,0:T(8,128)(2,1)}, u32[]{:S(2)}) copy-start(bf16[256,1024]{1,0:T(8,128)(2,1)} %get-tuple-element.14.also_ref) | copy-start | bytes 1572868
  114.6 16.6 %copy-start.6 = (bf16[256,1024]{1,0:T(8,128)(2,1)S(1)}, bf16[256,1024]{1,0:T(8,128)(2,1)}, u32[]{:S(2)}) copy-start(bf16[256,1024]{1,0:T(8,128)(2,1)} %copy-done.5) | copy-start | bytes 1572868
  114.6 16.6 %copy-start.12 = (bf16[256,1024]{1,0:T(8,128)(2,1)S(1)}, bf16[256,1024]{1,0:T(8,128)(2,1)}, u32[]{:S(2)}) copy-start(bf16[256,1024]{1,0:T(8,128)(2,1)} %get-tuple-element.25) | copy-start | bytes 1572868
  114.6 33.3 %all-to-all-start.2 = ((bf16[16,160,256]{2,1,0:T(8,128)(2,1)}), bf16[16,160,256]{2,1,0:T(8,128)(2,1)S(1)}, u32[]{:S(2)}, u32[]{:S(2)}) async-start(bf16[16,160,256]{2,1,0:T(8,128)(2,1)} %get-tuple-element.21), calls=%async_computation.2 | async-start | bytes 2621440 | tf_op jit(solution)/shard_map/all_to_all | solution.py:234
  125.1 19.9 %collective-permute-start.12 = (bf16[64,1024]{1,0:T(8,128)(2,1)S(1)}, bf16[64,1024]{1,0:T(8,128)(2,1)S(1)}, u32[]{:S(2)}, u32[]{:S(2)}) collective-permute-start(bf16[64,1024]{1,0:T(8,128)(2,1)S(1)} %get-tuple-element.26), channel_id=1, source_target_pairs={{0,16},{1,17},{2,18},{3,19},{4,20},{5,21},{6,22},{7,23},{8,24},{9,... | collective-permute-start | bytes 393224 | tf_op jit(solution)/shard_map/ppermute | solution.py:30
  127.1 19.7 %collective-permute-start.13 = (bf16[64,1024]{1,0:T(8,128)(2,1)S(1)}, bf16[64,1024]{1,0:T(8,128)(2,1)S(1)}, u32[]{:S(2)}, u32[]{:S(2)}) collective-permute-start(bf16[64,1024]{1,0:T(8,128)(2,1)S(1)} %get-tuple-element.28), channel_id=1, source_target_pairs={{0,32},{1,33},{2,34},{3,35},{4,36},{5,37},{6,38},{7,39},{8,40},{9,... | collective-permute-start | bytes 393224 | tf_op jit(solution)/shard_map/ppermute | solution.py:30
  129.8 17.1 %collective-permute-start.14 = (bf16[64,1024]{1,0:T(8,128)(2,1)S(1)}, bf16[64,1024]{1,0:T(8,128)(2,1)S(1)}, u32[]{:S(2)}, u32[]{:S(2)}) collective-permute-start(bf16[64,1024]{1,0:T(8,128)(2,1)S(1)} %get-tuple-element.27), channel_id=1, source_target_pairs={{0,48},{1,49},{2,50},{3,51},{4,52},{5,53},{6,54},{7,55},{8,56},{9,... | collective-permute-start | bytes 393224 | tf_op jit(solution)/shard_map/ppermute | solution.py:30
  133.4 15.1 %collective-permute-start.15 = (bf16[64,1024]{1,0:T(8,128)(2,1)}, bf16[64,1024]{1,0:T(8,128)(2,1)S(1)}, u32[]{:S(2)}, u32[]{:S(2)}) collective-permute-start(bf16[64,1024]{1,0:T(8,128)(2,1)} %get-tuple-element.29), channel_id=1, source_target_pairs={{0,4},{1,5},{2,6},{3,7},{4,8},{5,9},{6,10},{7,11},{8,12},{9,13},{1... | collective-permute-start | bytes 393224 | tf_op jit(solution)/shard_map/ppermute | solution.py:30
  134.8 13.7 %collective-permute-start.16 = (bf16[64,1024]{1,0:T(8,128)(2,1)}, bf16[64,1024]{1,0:T(8,128)(2,1)}, u32[]{:S(2)}, u32[]{:S(2)}) collective-permute-start(bf16[64,1024]{1,0:T(8,128)(2,1)} %get-tuple-element.31), channel_id=1, source_target_pairs={{0,8},{1,9},{2,10},{3,11},{4,12},{5,13},{6,14},{7,15},{8,0},{9,1},... | collective-permute-start | bytes 393224 | tf_op jit(solution)/shard_map/ppermute | solution.py:30
  145.1 5.3 %collective-permute-start.17 = (bf16[64,1024]{1,0:T(8,128)(2,1)}, bf16[64,1024]{1,0:T(8,128)(2,1)}, u32[]{:S(2)}, u32[]{:S(2)}) collective-permute-start(bf16[64,1024]{1,0:T(8,128)(2,1)} %get-tuple-element.30), channel_id=1, source_target_pairs={{0,12},{1,13},{2,14},{3,15},{4,0},{5,1},{6,2},{7,3},{8,4},{9,5},{1... | collective-permute-start | bytes 393224 | tf_op jit(solution)/shard_map/ppermute | solution.py:30
  147.9 7.2 %copy-start.2 = (bf16[16,160,256]{2,1,0:T(8,128)(2,1)}, bf16[16,160,256]{2,1,0:T(8,128)(2,1)S(1)}, u32[]{:S(2)}) copy-start(bf16[16,160,256]{2,1,0:T(8,128)(2,1)S(1)} %all-to-all-done.2.pt_ref) | copy-start | bytes 3932164
  148.4 4.0 %collective-permute-start.11 = (bf16[64,1024]{1,0:T(8,128)(2,1)S(1)}, bf16[64,1024]{1,0:T(8,128)(2,1)S(1)}, u32[]{:S(2)}, u32[]{:S(2)}) collective-permute-start(bf16[64,1024]{1,0:T(8,128)(2,1)S(1)} %bitcast.26), channel_id=1, source_target_pairs={{0,2},{1,3},{2,0},{3,1},{4,6},{5,7},{6,4},{7,5},{8,10},{9,11},{10,... | collective-permute-start | bytes 393224 | tf_op jit(solution)/shard_map/ppermute | solution.py:30
  152.4 0.7 copy-start.13
  155.2 7.0 %copy-start.3 = (f32[64,2048]{1,0:T(8,128)S(1)}, f32[64,2048]{1,0:T(8,128)}, u32[]{:S(2)}) copy-start(f32[64,2048]{1,0:T(8,128)} %shard_map.66) | copy-start | bytes 1572868
  155.2 7.0 %copy-start.10 = (f32[64,2048]{1,0:T(8,128)S(1)}, f32[64,2048]{1,0:T(8,128)}, u32[]{:S(2)}) copy-start(f32[64,2048]{1,0:T(8,128)} %param.5) | copy-start | bytes 1572868
  155.2 6.9 %collective-permute-start.18 = (bf16[64,2048]{1,0:T(8,128)(2,1)S(1)}, bf16[64,2048]{1,0:T(8,128)(2,1)S(1)}, u32[]{:S(2)}, u32[]{:S(2)}) collective-permute-start(bf16[64,2048]{1,0:T(8,128)(2,1)S(1)} %select_convert_fusion), channel_id=1, source_target_pairs={{0,64},{1,65},{2,66},{3,67},{4,68},{5,69},{6,70},{7,71},{8,72},{9,... | collective-permute-start | bytes 786440 | tf_op jit(solution)/shard_map/ppermute | solution.py:30
  161.6 2.1 %copy-start.11 = (f32[512,256]{1,0:T(8,128)S(1)}, f32[512,256]{1,0:T(8,128)}, u32[]{:S(2)}) copy-start(f32[512,256]{1,0:T(8,128)} %get-tuple-element.22) | copy-start | bytes 1572868
  161.6 2.1 %collective-permute-start.10 = (f32[512,256]{1,0:T(8,128)}, f32[512,256]{1,0:T(8,128)S(1)}, u32[]{:S(2)}, u32[]{:S(2)}) collective-permute-start(f32[512,256]{1,0:T(8,128)} %get-tuple-element.23), channel_id=1, source_target_pairs={{0,2},{1,3},{2,0},{3,1},{4,6},{5,7},{6,4},{7,5},{8,10},{9,11},{10,... | collective-permute-start | bytes 1572872 | tf_op jit(solution)/shard_map/ppermute | solution.py:30

commit v11 on v10

--- a/solution.py
+++ b/solution.py
@@ -202,8 +202,6 @@
         picked, gt, sib,
         flops=3 * 16 * rows * feats * tokens,
     )
-    cross = gram(at, arrived, gt, sib, own)
-    crossed = first_stage(cross)
 
     (slots,) = kernel_call(
         slots_kernel,
@@ -216,13 +214,15 @@
         functools.partial(factor_kernel, 4 * rows),
         [shape((4 * rows, tests), f32)],
         [VMEM, ANY, ANY],
-        slots.reshape(16 * rows, -1), own, cross[0],
+        slots.reshape(16 * rows, -1), own, picked,
         flops=2 * 16 * rows * 4 * rows * tests,
     )
     pt = pt.reshape(2, 2, rows, tests)
     half = lambda i: lax.dynamic_index_in_dim(pt, i, 1, keepdims=False)
     pt = half(c) + send(half(1 - c), flip("c"))
     pt = (pt + send(pt, flip("yl"))).astype(bf16)
+    cross = gram(at, arrived, gt, sib, pt)
+    crossed = first_stage(cross)
 
     own = lax.all_to_all(own, ("z", "x"), split_axis=0, concat_axis=0, tiled=True)
     direct, slots = kernel_call(

time: 166 us -> 163 us (0.982)
  the two profiles are of different devices: /device:TPU:0 before, /device:TPU:17 now
where the time goes in v11:
time: 163 us; the launch traced here: 162 us
  starting transfers between devices  58.3 us (36%)
  waiting for transfers between devices  48.4 us (30%)
  Pallas kernels  35.3 us (22%)
  other arithmetic  11.1 us (7%)
  local copies, waits for them, and re-layouts  8.25 us (5%)
    ppermute x19, starting transfers between devices, send(): return lax.ppermute(value, AXES, pairs)  42.6 us
    ppermute x19, waiting for transfers between devices, send(): return lax.ppermute(value, AXES, pairs)  40.2 us
    pallas_call x8, Pallas kernels, kernel_call(): pl.pallas_call(body, out_shape=outs, in_specs=specs, out_specs=[VMEM] * l...  35.3 us
    all_to_all x2, starting transfers between devices, on_device(): lax.all_to_all(slots, ('z', 'x'), split_axis=0, concat_axis=0, tiled=True)  11.6 us
    all_to_all x2, waiting for transfers between devices, on_device(): lax.all_to_all(slots, ('z', 'x'), split_axis=0, concat_axis=0, tiled=True)  8.25 us
    unnamed x33, local copies, waits for them, and re-layouts  7.07 us
    all_to_all x1, starting transfers between devices, on_device(): lax.all_to_all(own, ('z', 'x'), split_axis=0, concat_axis=0, tiled=True)  4.19 us
    convert_element_type x2, other arithmetic, second_stage(): rs = [send(mids[k].astype(bf16), along(axis, k)) for k in (1, 2, 3)]  3.55 us
  transfers between devices with their start and end apart: 22, of which 11 were waited for; matrix products, arithmetic and copies ran while one was open for 7% of the time, Pallas kernels for 16%

profile of v11, /device:TPU:17, one launch (start us, length us, event | category | flops | bytes accessed | tf_op | source)
XLA Modules:
  0.0 162.2 jit_solution(1234121549504552361)
XLA Ops:
  0.6 2.9 %copy.10 = bf16[512,2048]{0,1:T(8,128)(2,1)S(1)} copy(bf16[512,2048]{1,0:T(8,128)(2,1)} %param.4) | data formatting | bytes 4194304 | tf_op args[0]
  4.9 3.2 %collective-permute-done.sib_ref.b2_ref = bf16[2048,512]{1,0:T(8,128)(2,1)} collective-permute-done((bf16[2048,512]{1,0:T(8,128)(2,1)S(1)}, bf16[2048,512]{1,0:T(8,128)(2,1)}, u32[]{:S(2)}, u32[]{:S(2)}) %collective-permute-start) | collective-permute-done | bytes 2097184 | tf_op jit(solution)/shard_map/ppermute | solution.py:30
  8.2 3.7 %shard_map.59.a_ref.also_ref.own_ref = bf16[2048,512]{1,0:T(8,128)(2,1)} custom-call(s32[4]{0:T(128)} %pad_add_fusion.at_ref, bf16[2048,512]{1,0:T(8,128)(2,1)} %bitcast.21, bf16[2048,512]{1,0:T(8,128)(2,1)} %collective-permute-done.sib_ref.b2_ref), custom_call_target="tpu_custom_call" | custom-call | bytes 6291472 | tf_op jit(solution)/shard_map/pallas_call | solution.py:43
  11.9 2.1 %shard_map.61 = bf16[16,64,512]{2,1,0:T(8,128)(2,1)} custom-call(bf16[64,4096]{1,0:T(8,128)(2,1)} %f_ref.1, bf16[64,256]{1,0:T(8,128)(2,1)} %bitcast.31), custom_call_target="tpu_custom_call" | custom-call | bytes 1605632 | tf_op jit(solution)/shard_map/pallas_call | solution.py:43
  14.1 7.7 %all-to-all-start.1 = ((bf16[16,64,512]{2,1,0:T(8,128)(2,1)}), bf16[16,64,512]{2,1,0:T(8,128)(2,1)S(1)}, u32[]{:S(2)}, u32[]{:S(2)}) async-start(bf16[16,64,512]{2,1,0:T(8,128)(2,1)} %shard_map.61), calls=%async_computation.1 | async-start | bytes 2097152 | tf_op jit(solution)/shard_map/all_to_all | solution.py:212
  21.7 7.8 %shard_map.60.after_ref = bf16[16,64,1152]{2,1,0:T(8,128)(2,1)} custom-call(bf16[2048,512]{1,0:T(8,128)(2,1)} %shard_map.59.a_ref.also_ref.own_ref, bf16[2048,512]{1,0:T(8,128)(2,1)} %bitcast.22, bf16[2048,512]{1,0:T(8,128)(2,1)} %collective-permute-done.sib_ref.b2_ref), custom_call_target="tpu_custom_call" | custom-call | flops 3221225472 | bytes 8650752 | tf_op jit(solution)/shard_map/pallas_call | solution.py:43
  29.5 8.2 %all-to-all-done.1 = bf16[16,64,512]{2,1,0:T(8,128)(2,1)S(1)} async-done(((bf16[16,64,512]{2,1,0:T(8,128)(2,1)}), bf16[16,64,512]{2,1,0:T(8,128)(2,1)S(1)}, u32[]{:S(2)}, u32[]{:S(2)}) %all-to-all-start.1) | async-done | bytes 1048608 | tf_op jit(solution)/shard_map/all_to_all | solution.py:212
  37.7 1.0 copy-done.4
  38.7 4.2 %all-to-all-start = ((bf16[16,64,1152]{2,1,0:T(8,128)(2,1)}), bf16[16,64,1152]{2,1,0:T(8,128)(2,1)S(1)}, u32[]{:S(2)}, u32[]{:S(2)}) async-start(bf16[16,64,1152]{2,1,0:T(8,128)(2,1)} %shard_map.60.after_ref), calls=%async_computation | async-start | bytes 4718592 | tf_op jit(solution)/shard_map/all_to_all | solution.py:227
  42.9 2.3 %shard_map.62 = f32[256,256]{1,0:T(8,128)} custom-call(bf16[1024,512]{1,0:T(8,128)(2,1)} %bitcast.24, bf16[16,64,1152]{2,1,0:T(8,128)(2,1)} %shard_map.60.after_ref, bf16[2048,512]{1,0:T(8,128)(2,1)} %shard_map.59.a_ref.also_ref.own_ref), custom_call_target="tpu_custom_call" | custom-call | flops 134217728 | bytes 5767168 | tf_op jit(solution)/shard_map/pallas_call | solution.py:43
  45.2 0.9 dynamic-slice_bitcast_fusion
  46.1 2.2 %collective-permute-start.1 = (f32[2,64,256]{2,1,0:T(8,128)S(1)}, f32[2,64,256]{2,1,0:T(8,128)S(1)}, u32[]{:S(2)}, u32[]{:S(2)}) collective-permute-start(f32[2,64,256]{2,1,0:T(8,128)S(1)} %dynamic-slice_bitcast_fusion), channel_id=1, source_target_pairs={{0,2},{1,3},{2,0},{3,1},{4,6},{5,7},{6,4},{7,5},{8,10},{9,11},{10,... | collective-permute-start | bytes 393224 | tf_op jit(solution)/shard_map/ppermute | solution.py:30
  48.3 1.0 collective-permute-done.1
  49.3 0.9 bitcast_add_fusion
  50.2 2.0 %collective-permute-start.2 = (f32[2,64,256]{2,1,0:T(8,128)S(1)}, f32[2,64,256]{2,1,0:T(8,128)S(1)}, u32[]{:S(2)}, u32[]{:S(2)}) collective-permute-start(f32[2,64,256]{2,1,0:T(8,128)S(1)} %bitcast_add_fusion), channel_id=1, source_target_pairs={{0,64},{1,65},{2,66},{3,67},{4,68},{5,69},{6,70},{7,71},{8,72},{9,... | collective-permute-start | bytes 393224 | tf_op jit(solution)/shard_map/ppermute | solution.py:30
  52.2 10.1 %collective-permute-done.2 = f32[2,64,256]{2,1,0:T(8,128)S(1)} collective-permute-done((f32[2,64,256]{2,1,0:T(8,128)S(1)}, f32[2,64,256]{2,1,0:T(8,128)S(1)}, u32[]{:S(2)}, u32[]{:S(2)}) %collective-permute-start.2) | collective-permute-done | bytes 131104 | tf_op jit(solution)/shard_map/ppermute | solution.py:30
  62.9 9.0 %shard_map.63 = (bf16[256,1024]{1,0:T(8,128)(2,1)}, bf16[256,1024]{1,0:T(8,128)(2,1)}, bf16[256,1024]{1,0:T(8,128)(2,1)}, bf16[256,1024]{1,0:T(8,128)(2,1)}, bf1...) custom-call(s32[4]{0:T(128)} %pad_add_fusion.at_ref, ...), custom_call_target="tpu_custom_call" | custom-call | flops 4294967296 | bytes 10551312 | tf_op jit(solution)/shard_map/pallas_call | solution.py:43
  72.0 1.2 collective-permute-start.4
  73.2 2.5 %collective-permute-start.5 = (bf16[256,1024]{1,0:T(8,128)(2,1)}, bf16[256,1024]{1,0:T(8,128)(2,1)}, u32[]{:S(2)}, u32[]{:S(2)}) collective-permute-start(bf16[256,1024]{1,0:T(8,128)(2,1)} %get-tuple-element.15), channel_id=1, source_target_pairs={{0,8},{1,9},{2,10},{3,11},{4,12},{5,13},{6,14},{7,15},{8,0},{9,1},... | collective-permute-start | bytes 1572872 | tf_op jit(solution)/shard_map/ppermute | solution.py:30
  75.6 1.2 collective-permute-start.6
  76.8 1.6 %collective-permute-start.7 = (bf16[256,1024]{1,0:T(8,128)(2,1)}, bf16[256,1024]{1,0:T(8,128)(2,1)S(1)}, u32[]{:S(2)}, u32[]{:S(2)}) collective-permute-start(bf16[256,1024]{1,0:T(8,128)(2,1)} %get-tuple-element.17), channel_id=1, source_target_pairs={{0,16},{1,17},{2,18},{3,19},{4,20},{5,21},{6,22},{7,23},{8,24},{9,... | collective-permute-start | bytes 1572872 | tf_op jit(solution)/shard_map/ppermute | solution.py:30
  78.4 3.3 %collective-permute-start.8 = (bf16[256,1024]{1,0:T(8,128)(2,1)}, bf16[256,1024]{1,0:T(8,128)(2,1)S(1)}, u32[]{:S(2)}, u32[]{:S(2)}) collective-permute-start(bf16[256,1024]{1,0:T(8,128)(2,1)} %get-tuple-element.18), channel_id=1, source_target_pairs={{0,32},{1,33},{2,34},{3,35},{4,36},{5,37},{6,38},{7,39},{8,40},{9,... | collective-permute-start | bytes 1572872 | tf_op jit(solution)/shard_map/ppermute | solution.py:30
  81.7 4.3 %collective-permute-done.4.refs_0_ = bf16[256,1024]{1,0:T(8,128)(2,1)S(1)} collective-permute-done((bf16[256,1024]{1,0:T(8,128)(2,1)}, bf16[256,1024]{1,0:T(8,128)(2,1)S(1)}, u32[]{:S(2)}, u32[]{:S(2)}) %collective-permute-start.4) | collective-permute-done | bytes 524320 | tf_op jit(solution)/shard_map/ppermute | solution.py:30
  86.8 3.3 %collective-permute-start.9 = (bf16[256,1024]{1,0:T(8,128)(2,1)}, bf16[256,1024]{1,0:T(8,128)(2,1)}, u32[]{:S(2)}, u32[]{:S(2)}) collective-permute-start(bf16[256,1024]{1,0:T(8,128)(2,1)} %get-tuple-element.19), channel_id=1, source_target_pairs={{0,48},{1,49},{2,50},{3,51},{4,52},{5,53},{6,54},{7,55},{8,56},{9,... | collective-permute-start | bytes 1572872 | tf_op jit(solution)/shard_map/ppermute | solution.py:30
  90.2 7.8 %collective-permute-done.5.refs_1_ = bf16[256,1024]{1,0:T(8,128)(2,1)} collective-permute-done((bf16[256,1024]{1,0:T(8,128)(2,1)}, bf16[256,1024]{1,0:T(8,128)(2,1)}, u32[]{:S(2)}, u32[]{:S(2)}) %collective-permute-start.5) | collective-permute-done | bytes 524320 | tf_op jit(solution)/shard_map/ppermute | solution.py:30
  98.1 4.9 %collective-permute-done.8.refs_4_ = bf16[256,1024]{1,0:T(8,128)(2,1)S(1)} collective-permute-done((bf16[256,1024]{1,0:T(8,128)(2,1)}, bf16[256,1024]{1,0:T(8,128)(2,1)S(1)}, u32[]{:S(2)}, u32[]{:S(2)}) %collective-permute-start.8) | collective-permute-done | bytes 524320 | tf_op jit(solution)/shard_map/ppermute | solution.py:30
  103.1 0.8 copy-done.7
  103.9 3.4 %shard_map.64 = (f32[64,2048]{1,0:T(8,128)}, bf16[16,160,256]{2,1,0:T(8,128)(2,1)}) custom-call(s32[4]{0:T(128)} %pad_add_fusion.at_ref, bf16[16,64,1152]{2,1,0:T(8,128)(2,1)} %copy-done, bf16[128,256]{1,0:T(8,128)(2,1)} %bitcast.29, bf16[256,1024]{1,0:T(8,128)(2,1)} %copy-done.9, bf16[256,1024]{1,0:T(8,128)(2,1)} %collective-permute-done.5.refs_1_, ...), custom_call_target="tpu_custom_call" | custom-call | bytes 7405584 | tf_op jit(solution)/shard_map/pallas_call | solution.py:43
  107.3 3.9 %all-to-all-start.2 = ((bf16[16,160,256]{2,1,0:T(8,128)(2,1)}), bf16[16,160,256]{2,1,0:T(8,128)(2,1)S(1)}, u32[]{:S(2)}, u32[]{:S(2)}) async-start(bf16[16,160,256]{2,1,0:T(8,128)(2,1)} %get-tuple-element.20), calls=%async_computation.2 | async-start | bytes 2621440 | tf_op jit(solution)/shard_map/all_to_all | solution.py:234
  111.2 1.6 add_convert_fusion.5
  112.8 2.3 %collective-permute-start.12 = (bf16[64,1024]{1,0:T(8,128)(2,1)S(1)}, bf16[64,1024]{1,0:T(8,128)(2,1)S(1)}, u32[]{:S(2)}, u32[]{:S(2)}) collective-permute-start(bf16[64,1024]{1,0:T(8,128)(2,1)S(1)} %get-tuple-element.26), channel_id=1, source_target_pairs={{0,16},{1,17},{2,18},{3,19},{4,20},{5,21},{6,22},{7,23},{8,24},{9,... | collective-permute-start | bytes 393224 | tf_op jit(solution)/shard_map/ppermute | solution.py:30
  115.7 1.5 collective-permute-start.13
  117.2 2.0 %add_convert_fusion.2 = (bf16[64,1024]{1,0:T(8,128)(2,1)}, bf16[64,1024]{1,0:T(8,128)(2,1)}, bf16[64,1024]{1,0:T(8,128)(2,1)}) fusion(bf16[256,1024]{1,0:T(8,128)(2,1)} %collective-permute-done.9.refs_5_, bf16[256,1024]{1,0:T(8,128)(2,1)S(1)} %copy-done.8, bf16[256,1024]{1,0:T(8,128)(2,1)S(1)} %copy-done.6, bf16[256,1024]{1,0:T(8,128)(2,1)S(1)} %copy-done.13), kind=kLoop, calls=%fused_computation.7 | loop fusion | flops 1572864 | bytes 1966080 | tf_op jit(solution)/shard_map/convert_element_type | solution.py:151
  119.2 1.2 collective-permute-start.15
  120.4 1.5 collective-permute-start.17
  121.9 7.5 %collective-permute-done.12 = bf16[64,1024]{1,0:T(8,128)(2,1)S(1)} collective-permute-done((bf16[64,1024]{1,0:T(8,128)(2,1)S(1)}, bf16[64,1024]{1,0:T(8,128)(2,1)S(1)}, u32[]{:S(2)}, u32[]{:S(2)}) %collective-permute-start.12) | collective-permute-done | bytes 131104 | tf_op jit(solution)/shard_map/ppermute | solution.py:30
  129.4 3.8 %collective-permute-start.16 = (bf16[64,1024]{1,0:T(8,128)(2,1)}, bf16[64,1024]{1,0:T(8,128)(2,1)}, u32[]{:S(2)}, u32[]{:S(2)}) collective-permute-start(bf16[64,1024]{1,0:T(8,128)(2,1)} %get-tuple-element.31), channel_id=1, source_target_pairs={{0,8},{1,9},{2,10},{3,11},{4,12},{5,13},{6,14},{7,15},{8,0},{9,1},... | collective-permute-start | bytes 393224 | tf_op jit(solution)/shard_map/ppermute | solution.py:30
  133.4 1.2 convert_add_fusion.1
  135.0 3.5 %collective-permute-start.11 = (bf16[64,1024]{1,0:T(8,128)(2,1)S(1)}, bf16[64,1024]{1,0:T(8,128)(2,1)S(1)}, u32[]{:S(2)}, u32[]{:S(2)}) collective-permute-start(bf16[64,1024]{1,0:T(8,128)(2,1)S(1)} %bitcast.30), channel_id=1, source_target_pairs={{0,2},{1,3},{2,0},{3,1},{4,6},{5,7},{6,4},{7,5},{8,10},{9,11},{10,... | collective-permute-start | bytes 393224 | tf_op jit(solution)/shard_map/ppermute | solution.py:30
  138.5 1.2 convert_add_fusion
  141.2 2.1 %shard_map.66 = f32[64,2048]{1,0:T(8,128)} custom-call(s32[4]{0:T(128)} %pad_add_fusion.at_ref, f32[64,2048]{1,0:T(8,128)} %get-tuple-element.23.direct_ref, bf16[64,1024]{1,0:T(8,128)(2,1)} %bitcast.28, bf16[64,1024]{1,0:T(8,128)(2,1)} %copy-done.14), custom_call_target="tpu_custom_call" | custom-call | bytes 1310736 | tf_op jit(solution)/shard_map/pallas_call | solution.py:43
  143.3 1.1 select_convert_fusion
  144.4 6.7 %collective-permute-start.18 = (bf16[64,2048]{1,0:T(8,128)(2,1)S(1)}, bf16[64,2048]{1,0:T(8,128)(2,1)S(1)}, u32[]{:S(2)}, u32[]{:S(2)}) collective-permute-start(bf16[64,2048]{1,0:T(8,128)(2,1)S(1)} %select_convert_fusion), channel_id=1, source_target_pairs={{0,64},{1,65},{2,66},{3,67},{4,68},{5,69},{6,70},{7,71},{8,72},{9,... | collective-permute-start | bytes 786440 | tf_op jit(solution)/shard_map/ppermute | solution.py:30
  151.1 4.9 %shard_map.65 = (f32[512,256]{1,0:T(8,128)}, f32[512,256]{1,0:T(8,128)}) custom-call(s32[4]{0:T(128)} %pad_add_fusion.at_ref, bf16[16,160,256]{2,1,0:T(8,128)(2,1)} %copy-done.2, bf16[2048,512]{1,0:T(8,128)(2,1)} %shard_map.59.a_ref.also_ref.own_ref, bf16[2048,512]{1,0:T(8,128)(2,1)} %collective-permute-done.3.a_ref.cross_ref), custom_call_target="tpu_custom_call" | custom-call | flops 1073741824 | bytes 6553616 | tf_op jit(solution)/shard_map/pallas_call | solution.py:43
  156.0 3.6 %collective-permute-start.10 = (f32[512,256]{1,0:T(8,128)}, f32[512,256]{1,0:T(8,128)S(1)}, u32[]{:S(2)}, u32[]{:S(2)}) collective-permute-start(f32[512,256]{1,0:T(8,128)} %get-tuple-element.22), channel_id=1, source_target_pairs={{0,2},{1,3},{2,0},{3,1},{4,6},{5,7},{6,4},{7,5},{8,10},{9,11},{10,... | collective-permute-start | bytes 1572872 | tf_op jit(solution)/shard_map/ppermute | solution.py:30
  159.6 0.9 multiply_add_fusion
  160.5 0.8 collective-permute-done.10
  161.3 0.9 add.123
  (51 shorter events, 5.9 us)
Async XLA Ops:
  3.5 4.7 %copy-start.1 = (bf16[512,2048]{0,1:T(8,128)(2,1)}, bf16[512,2048]{0,1:T(8,128)(2,1)S(1)}, u32[]{:S(2)}) copy-start(bf16[512,2048]{0,1:T(8,128)(2,1)S(1)} %copy.10) | copy-start | bytes 6291460
  3.5 4.7 %collective-permute-start = (bf16[2048,512]{1,0:T(8,128)(2,1)S(1)}, bf16[2048,512]{1,0:T(8,128)(2,1)}, u32[]{:S(2)}, u32[]{:S(2)}) collective-permute-start(bf16[2048,512]{1,0:T(8,128)(2,1)S(1)} %bitcast.20), channel_id=1, source_target_pairs={{0,2},{1,3},{2,0},{3,1},{4,6},{5,7},{6,4},{7,5},{8,10},{9,11},{10,... | collective-permute-start | bytes 6291464 | tf_op jit(solution)/shard_map/ppermute | solution.py:30
  11.9 51.0 %collective-permute-start.3 = (bf16[2048,512]{1,0:T(8,128)(2,1)}, bf16[2048,512]{1,0:T(8,128)(2,1)}, u32[]{:S(2)}, u32[]{:S(2)}) collective-permute-start(bf16[2048,512]{1,0:T(8,128)(2,1)} %shard_map.59.a_ref.also_ref.own_ref), channel_id=1, source_target_pairs={{0,1},{1,0},{2,3},{3,2},{4,5},{5,4},{6,7},{7,6},{8,9},{9,8},{10,11... | collective-permute-start | bytes 6291464 | tf_op jit(solution)/shard_map/ppermute | solution.py:30
  14.1 23.7 %all-to-all-start.1 = ((bf16[16,64,512]{2,1,0:T(8,128)(2,1)}), bf16[16,64,512]{2,1,0:T(8,128)(2,1)S(1)}, u32[]{:S(2)}, u32[]{:S(2)}) async-start(bf16[16,64,512]{2,1,0:T(8,128)(2,1)} %shard_map.61), calls=%async_computation.1 | async-start | bytes 2097152 | tf_op jit(solution)/shard_map/all_to_all | solution.py:212
  37.7 1.0 copy-start.4
  38.7 51.4 %all-to-all-start = ((bf16[16,64,1152]{2,1,0:T(8,128)(2,1)}), bf16[16,64,1152]{2,1,0:T(8,128)(2,1)S(1)}, u32[]{:S(2)}, u32[]{:S(2)}) async-start(bf16[16,64,1152]{2,1,0:T(8,128)(2,1)} %shard_map.60.after_ref), calls=%async_computation | async-start | bytes 4718592 | tf_op jit(solution)/shard_map/all_to_all | solution.py:227
  46.1 3.2 %collective-permute-start.1 = (f32[2,64,256]{2,1,0:T(8,128)S(1)}, f32[2,64,256]{2,1,0:T(8,128)S(1)}, u32[]{:S(2)}, u32[]{:S(2)}) collective-permute-start(f32[2,64,256]{2,1,0:T(8,128)S(1)} %dynamic-slice_bitcast_fusion), channel_id=1, source_target_pairs={{0,2},{1,3},{2,0},{3,1},{4,6},{5,7},{6,4},{7,5},{8,10},{9,11},{10,... | collective-permute-start | bytes 393224 | tf_op jit(solution)/shard_map/ppermute | solution.py:30
  50.2 12.1 %collective-permute-start.2 = (f32[2,64,256]{2,1,0:T(8,128)S(1)}, f32[2,64,256]{2,1,0:T(8,128)S(1)}, u32[]{:S(2)}, u32[]{:S(2)}) collective-permute-start(f32[2,64,256]{2,1,0:T(8,128)S(1)} %bitcast_add_fusion), channel_id=1, source_target_pairs={{0,64},{1,65},{2,66},{3,67},{4,68},{5,69},{6,70},{7,71},{8,72},{9,... | collective-permute-start | bytes 393224 | tf_op jit(solution)/shard_map/ppermute | solution.py:30
  72.0 14.1 %collective-permute-start.4 = (bf16[256,1024]{1,0:T(8,128)(2,1)}, bf16[256,1024]{1,0:T(8,128)(2,1)S(1)}, u32[]{:S(2)}, u32[]{:S(2)}) collective-permute-start(bf16[256,1024]{1,0:T(8,128)(2,1)} %get-tuple-element.14), channel_id=1, source_target_pairs={{0,4},{1,5},{2,6},{3,7},{4,8},{5,9},{6,10},{7,11},{8,12},{9,13},{1... | collective-permute-start | bytes 1572872 | tf_op jit(solution)/shard_map/ppermute | solution.py:30
  73.2 24.8 %collective-permute-start.5 = (bf16[256,1024]{1,0:T(8,128)(2,1)}, bf16[256,1024]{1,0:T(8,128)(2,1)}, u32[]{:S(2)}, u32[]{:S(2)}) collective-permute-start(bf16[256,1024]{1,0:T(8,128)(2,1)} %get-tuple-element.15), channel_id=1, source_target_pairs={{0,8},{1,9},{2,10},{3,11},{4,12},{5,13},{6,14},{7,15},{8,0},{9,1},... | collective-permute-start | bytes 1572872 | tf_op jit(solution)/shard_map/ppermute | solution.py:30
  75.6 22.5 %collective-permute-start.6 = (bf16[256,1024]{1,0:T(8,128)(2,1)}, bf16[256,1024]{1,0:T(8,128)(2,1)}, u32[]{:S(2)}, u32[]{:S(2)}) collective-permute-start(bf16[256,1024]{1,0:T(8,128)(2,1)} %get-tuple-element.16), channel_id=1, source_target_pairs={{0,12},{1,13},{2,14},{3,15},{4,0},{5,1},{6,2},{7,3},{8,4},{9,5},{1... | collective-permute-start | bytes 1572872 | tf_op jit(solution)/shard_map/ppermute | solution.py:30
  76.8 21.4 %collective-permute-start.7 = (bf16[256,1024]{1,0:T(8,128)(2,1)}, bf16[256,1024]{1,0:T(8,128)(2,1)S(1)}, u32[]{:S(2)}, u32[]{:S(2)}) collective-permute-start(bf16[256,1024]{1,0:T(8,128)(2,1)} %get-tuple-element.17), channel_id=1, source_target_pairs={{0,16},{1,17},{2,18},{3,19},{4,20},{5,21},{6,22},{7,23},{8,24},{9,... | collective-permute-start | bytes 1572872 | tf_op jit(solution)/shard_map/ppermute | solution.py:30
  78.4 24.7 %collective-permute-start.8 = (bf16[256,1024]{1,0:T(8,128)(2,1)}, bf16[256,1024]{1,0:T(8,128)(2,1)S(1)}, u32[]{:S(2)}, u32[]{:S(2)}) collective-permute-start(bf16[256,1024]{1,0:T(8,128)(2,1)} %get-tuple-element.18), channel_id=1, source_target_pairs={{0,32},{1,33},{2,34},{3,35},{4,36},{5,37},{6,38},{7,39},{8,40},{9,... | collective-permute-start | bytes 1572872 | tf_op jit(solution)/shard_map/ppermute | solution.py:30
  86.0 0.8 copy-start.9
  86.8 16.2 %collective-permute-start.9 = (bf16[256,1024]{1,0:T(8,128)(2,1)}, bf16[256,1024]{1,0:T(8,128)(2,1)}, u32[]{:S(2)}, u32[]{:S(2)}) collective-permute-start(bf16[256,1024]{1,0:T(8,128)(2,1)} %get-tuple-element.19), channel_id=1, source_target_pairs={{0,48},{1,49},{2,50},{3,51},{4,52},{5,53},{6,54},{7,55},{8,56},{9,... | collective-permute-start | bytes 1572872 | tf_op jit(solution)/shard_map/ppermute | solution.py:30
  90.2 12.9 %copy-start = (bf16[16,64,1152]{2,1,0:T(8,128)(2,1)}, bf16[16,64,1152]{2,1,0:T(8,128)(2,1)S(1)}, u32[]{:S(2)}) copy-start(bf16[16,64,1152]{2,1,0:T(8,128)(2,1)S(1)} %all-to-all-done.got_ref) | copy-start | bytes 7077892
  98.1 5.0 %copy-start.5 = (bf16[256,1024]{1,0:T(8,128)(2,1)}, bf16[256,1024]{1,0:T(8,128)(2,1)S(1)}, u32[]{:S(2)}) copy-start(bf16[256,1024]{1,0:T(8,128)(2,1)S(1)} %collective-permute-done.7.refs_3_) | copy-start | bytes 1572868
  103.1 0.8 copy-start.7
  107.3 3.9 %copy-start.10 = (bf16[256,1024]{1,0:T(8,128)(2,1)S(1)}, bf16[256,1024]{1,0:T(8,128)(2,1)}, u32[]{:S(2)}) copy-start(bf16[256,1024]{1,0:T(8,128)(2,1)} %copy-done.9) | copy-start | bytes 1572868
  107.3 9.9 %copy-start.6 = (bf16[256,1024]{1,0:T(8,128)(2,1)S(1)}, bf16[256,1024]{1,0:T(8,128)(2,1)}, u32[]{:S(2)}) copy-start(bf16[256,1024]{1,0:T(8,128)(2,1)} %copy-done.5) | copy-start | bytes 1572868
  107.3 9.9 %copy-start.8 = (bf16[256,1024]{1,0:T(8,128)(2,1)S(1)}, bf16[256,1024]{1,0:T(8,128)(2,1)}, u32[]{:S(2)}) copy-start(bf16[256,1024]{1,0:T(8,128)(2,1)} %copy-done.7) | copy-start | bytes 1572868
  107.3 9.9 %copy-start.13 = (bf16[256,1024]{1,0:T(8,128)(2,1)S(1)}, bf16[256,1024]{1,0:T(8,128)(2,1)}, u32[]{:S(2)}) copy-start(bf16[256,1024]{1,0:T(8,128)(2,1)} %get-tuple-element.25) | copy-start | bytes 1572868
  107.3 27.3 %all-to-all-start.2 = ((bf16[16,160,256]{2,1,0:T(8,128)(2,1)}), bf16[16,160,256]{2,1,0:T(8,128)(2,1)S(1)}, u32[]{:S(2)}, u32[]{:S(2)}) async-start(bf16[16,160,256]{2,1,0:T(8,128)(2,1)} %get-tuple-element.20), calls=%async_computation.2 | async-start | bytes 2621440 | tf_op jit(solution)/shard_map/all_to_all | solution.py:234
  112.8 16.5 %collective-permute-start.12 = (bf16[64,1024]{1,0:T(8,128)(2,1)S(1)}, bf16[64,1024]{1,0:T(8,128)(2,1)S(1)}, u32[]{:S(2)}, u32[]{:S(2)}) collective-permute-start(bf16[64,1024]{1,0:T(8,128)(2,1)S(1)} %get-tuple-element.26), channel_id=1, source_target_pairs={{0,16},{1,17},{2,18},{3,19},{4,20},{5,21},{6,22},{7,23},{8,24},{9,... | collective-permute-start | bytes 393224 | tf_op jit(solution)/shard_map/ppermute | solution.py:30
  115.1 18.0 %collective-permute-start.14 = (bf16[64,1024]{1,0:T(8,128)(2,1)S(1)}, bf16[64,1024]{1,0:T(8,128)(2,1)S(1)}, u32[]{:S(2)}, u32[]{:S(2)}) collective-permute-start(bf16[64,1024]{1,0:T(8,128)(2,1)S(1)} %get-tuple-element.27), channel_id=1, source_target_pairs={{0,48},{1,49},{2,50},{3,51},{4,52},{5,53},{6,54},{7,55},{8,56},{9,... | collective-permute-start | bytes 393224 | tf_op jit(solution)/shard_map/ppermute | solution.py:30
  115.7 17.7 %collective-permute-start.13 = (bf16[64,1024]{1,0:T(8,128)(2,1)S(1)}, bf16[64,1024]{1,0:T(8,128)(2,1)S(1)}, u32[]{:S(2)}, u32[]{:S(2)}) collective-permute-start(bf16[64,1024]{1,0:T(8,128)(2,1)S(1)} %get-tuple-element.28), channel_id=1, source_target_pairs={{0,32},{1,33},{2,34},{3,35},{4,36},{5,37},{6,38},{7,39},{8,40},{9,... | collective-permute-start | bytes 393224 | tf_op jit(solution)/shard_map/ppermute | solution.py:30
  119.2 19.3 %collective-permute-start.15 = (bf16[64,1024]{1,0:T(8,128)(2,1)}, bf16[64,1024]{1,0:T(8,128)(2,1)S(1)}, u32[]{:S(2)}, u32[]{:S(2)}) collective-permute-start(bf16[64,1024]{1,0:T(8,128)(2,1)} %get-tuple-element.29), channel_id=1, source_target_pairs={{0,4},{1,5},{2,6},{3,7},{4,8},{5,9},{6,10},{7,11},{8,12},{9,13},{1... | collective-permute-start | bytes 393224 | tf_op jit(solution)/shard_map/ppermute | solution.py:30
  120.4 18.1 %collective-permute-start.17 = (bf16[64,1024]{1,0:T(8,128)(2,1)}, bf16[64,1024]{1,0:T(8,128)(2,1)}, u32[]{:S(2)}, u32[]{:S(2)}) collective-permute-start(bf16[64,1024]{1,0:T(8,128)(2,1)} %get-tuple-element.30), channel_id=1, source_target_pairs={{0,12},{1,13},{2,14},{3,15},{4,0},{5,1},{6,2},{7,3},{8,4},{9,5},{1... | collective-permute-start | bytes 393224 | tf_op jit(solution)/shard_map/ppermute | solution.py:30
  129.4 9.1 %collective-permute-start.16 = (bf16[64,1024]{1,0:T(8,128)(2,1)}, bf16[64,1024]{1,0:T(8,128)(2,1)}, u32[]{:S(2)}, u32[]{:S(2)}) collective-permute-start(bf16[64,1024]{1,0:T(8,128)(2,1)} %get-tuple-element.31), channel_id=1, source_target_pairs={{0,8},{1,9},{2,10},{3,11},{4,12},{5,13},{6,14},{7,15},{8,0},{9,1},... | collective-permute-start | bytes 393224 | tf_op jit(solution)/shard_map/ppermute | solution.py:30
  134.6 8.7 %copy-start.2 = (bf16[16,160,256]{2,1,0:T(8,128)(2,1)}, bf16[16,160,256]{2,1,0:T(8,128)(2,1)S(1)}, u32[]{:S(2)}) copy-start(bf16[16,160,256]{2,1,0:T(8,128)(2,1)S(1)} %all-to-all-done.2.pt_ref) | copy-start | bytes 3932164
  135.0 5.5 %collective-permute-start.11 = (bf16[64,1024]{1,0:T(8,128)(2,1)S(1)}, bf16[64,1024]{1,0:T(8,128)(2,1)S(1)}, u32[]{:S(2)}, u32[]{:S(2)}) collective-permute-start(bf16[64,1024]{1,0:T(8,128)(2,1)S(1)} %bitcast.30), channel_id=1, source_target_pairs={{0,2},{1,3},{2,0},{3,1},{4,6},{5,7},{6,4},{7,5},{8,10},{9,11},{10,... | collective-permute-start | bytes 393224 | tf_op jit(solution)/shard_map/ppermute | solution.py:30
  140.5 0.7 copy-start.14
  144.4 15.2 %copy-start.3 = (f32[64,2048]{1,0:T(8,128)S(1)}, f32[64,2048]{1,0:T(8,128)}, u32[]{:S(2)}) copy-start(f32[64,2048]{1,0:T(8,128)} %shard_map.66) | copy-start | bytes 1572868
  144.4 15.2 %copy-start.11 = (f32[64,2048]{1,0:T(8,128)S(1)}, f32[64,2048]{1,0:T(8,128)}, u32[]{:S(2)}) copy-start(f32[64,2048]{1,0:T(8,128)} %param.5) | copy-start | bytes 1572868
  144.4 15.2 %collective-permute-start.18 = (bf16[64,2048]{1,0:T(8,128)(2,1)S(1)}, bf16[64,2048]{1,0:T(8,128)(2,1)S(1)}, u32[]{:S(2)}, u32[]{:S(2)}) collective-permute-start(bf16[64,2048]{1,0:T(8,128)(2,1)S(1)} %select_convert_fusion), channel_id=1, source_target_pairs={{0,64},{1,65},{2,66},{3,67},{4,68},{5,69},{6,70},{7,71},{8,72},{9,... | collective-permute-start | bytes 786440 | tf_op jit(solution)/shard_map/ppermute | solution.py:30
  156.0 5.3 %copy-start.12 = (f32[512,256]{1,0:T(8,128)S(1)}, f32[512,256]{1,0:T(8,128)}, u32[]{:S(2)}) copy-start(f32[512,256]{1,0:T(8,128)} %get-tuple-element.21) | copy-start | bytes 1572868
  156.0 5.3 %collective-permute-start.10 = (f32[512,256]{1,0:T(8,128)}, f32[512,256]{1,0:T(8,128)S(1)}, u32[]{:S(2)}, u32[]{:S(2)}) collective-permute-start(f32[512,256]{1,0:T(8,128)} %get-tuple-element.22), channel_id=1, source_target_pairs={{0,2},{1,3},{2,0},{3,1},{4,6},{5,7},{6,4},{7,5},{8,10},{9,11},{10,... | collective-permute-start | bytes 1572872 | tf_op jit(solution)/shard_map/ppermute | solution.py:30

commit v12 on v11

--- a/solution.py
+++ b/solution.py
@@ -63,19 +63,12 @@
     )
 
 
-def pick_kernel(at_ref, gt_ref, sib_ref, out_ref):
-    for i, ref in enumerate((gt_ref, sib_ref)):
-        for b in range(16):
-            start = pl.ds(pl.multiple_of(b * 128 + at_ref[2], 64), 64)
-            out_ref[(16 * i + b) * 64 : (16 * i + b + 1) * 64, :] = ref[start, :]
-
-
-def own_kernel(a_ref, b1_ref, b2_ref, out_ref):
+def own_kernel(a1_ref, a2_ref, b1_ref, b2_ref, out_ref):
     rows = out_ref.shape[1]
     wide = 2 * rows
     for g in range(4):
-        left1 = a_ref[4 * g * rows : 4 * (g + 1) * rows, :]
-        left2 = a_ref[(16 + 4 * g) * rows : (20 + 4 * g) * rows, :]
+        left1 = a1_ref[4 * g * rows : 4 * (g + 1) * rows, :]
+        left2 = a2_ref[4 * g * rows : 4 * (g + 1) * rows, :]
         for q in range(3):
             cols = pl.ds((g + q) % 4 * 4 * wide, 4 * wide)
             acc = lax.dot_general(left1, b1_ref[cols, :], NT, preferred_element_type=f32)
@@ -88,17 +81,17 @@
                     out_ref[4 * g + i, :, (lo - i) * wide : (hi - i) * wide] = piece
 
 
-def gram_kernel(at_ref, a_ref, b1_ref, b2_ref, after_ref, *outs):
+def gram_kernel(at_ref, a1_ref, a2_ref, b1_ref, b2_ref, after_ref, *outs):
     z, x = at_ref[0], at_ref[1]
-    rows, m, n, tile = 64, a_ref.shape[0] // 2, b1_ref.shape[0] // 2, 256
+    rows, n, tile = 64, b1_ref.shape[0] // 2, 256
     for half in range(2):
         left1, left2 = [], []
         for k in range(4):
             for j in range(4):
                 dx, dz = (k, j) if half == 0 else (j, k)
                 block = (lax.rem(z + dz, 4) * 4 + lax.rem(x + dx, 4)) * rows
-                left1.append(a_ref[pl.ds(pl.multiple_of(block, rows), rows), :])
-                left2.append(a_ref[pl.ds(pl.multiple_of(block + m, rows), rows), :])
+                left1.append(a1_ref[pl.ds(pl.multiple_of(block, rows), rows), :])
+                left2.append(a2_ref[pl.ds(pl.multiple_of(block, rows), rows), :])
         left1, left2 = jnp.concatenate(left1), jnp.concatenate(left2)
         for t in range(n // tile):
             cols = pl.ds(half * n + t * tile, tile)
@@ -109,26 +102,25 @@
                 outs[4 * half + k][:, t * tile : (t + 1) * tile] = part
 
 
-def gram(at, a, b1, b2, after):
+def gram(at, a1, a2, b1, b2, after):
     n = b1.shape[0]
     return kernel_call(
         gram_kernel,
         [jax.ShapeDtypeStruct((256, n // 2), bf16)] * 8,
-        [SMEM] + [VMEM] * 3 + [ANY],
-        at, a, b1, b2, after,
-        flops=2 * a.shape[0] * n * b1.shape[1],
-    )
-
-
-def scores_kernel(at_ref, pt_ref, own_ref, cross_ref, keep_ref, give_ref):
+        [SMEM] + [VMEM] * 4 + [ANY],
+        at, a1, a2, b1, b2, after,
+        flops=4 * a1.shape[0] * n * b1.shape[1],
+    )
+
+
+def scores_kernel(at_ref, pt_ref, own1_ref, own2_ref, cross1_ref, cross2_ref, keep_ref, give_ref):
     h = at_ref[3]
-    m = own_ref.shape[0] // 2
+    m = own1_ref.shape[0]
     p_own = pt_ref[:, pl.ds(pl.multiple_of(h * 64, 64), 64), :].reshape(m, pt_ref.shape[-1])
     p_cross = pt_ref[:, pl.ds(pl.multiple_of((1 - h) * 64, 64), 64), :].reshape(m, pt_ref.shape[-1])
-    for side, out_ref in enumerate((keep_ref, give_ref)):
-        s = slice(side * m, (side + 1) * m)
-        acc = lax.dot_general(own_ref[s, :], p_own, TN, preferred_element_type=f32)
-        out_ref[...] = acc + lax.dot_general(cross_ref[s, :], p_cross, TN, preferred_element_type=f32)
+    for own, cross, out_ref in ((own1_ref, cross1_ref, keep_ref), (own2_ref, cross2_ref, give_ref)):
+        acc = lax.dot_general(own[...], p_own, TN, preferred_element_type=f32)
+        out_ref[...] = acc + lax.dot_general(cross[...], p_cross, TN, preferred_element_type=f32)
 
 
 def first_stage(parts):
@@ -193,13 +185,16 @@
     gt = grads.T
     sib = send(gt, flip("c"))
 
-    (picked,) = kernel_call(pick_kernel, [shape((feats, tokens), bf16)], [SMEM, VMEM, VMEM], at, gt, sib)
-    arrived = send(picked, flip("yh"))
+    pick = lambda v: lax.dynamic_index_in_dim(v.reshape(16, 2, rows, tokens), c, 1, keepdims=False)
+    mine = pick(gt).reshape(feats // 2, tokens)
+    far1 = send(mine, flip("yh"))
+    sib_mine = pick(sib).reshape(feats // 2, tokens)
+    far2 = send(sib_mine, flip("yh"))
     (own,) = kernel_call(
         own_kernel,
         [shape((16, rows, 18 * rows), bf16)],
-        [VMEM] * 3,
-        picked, gt, sib,
+        [VMEM] * 4,
+        mine, sib_mine, gt, sib,
         flops=3 * 16 * rows * feats * tokens,
     )
 
@@ -214,14 +209,14 @@
         functools.partial(factor_kernel, 4 * rows),
         [shape((4 * rows, tests), f32)],
         [VMEM, ANY, ANY],
-        slots.reshape(16 * rows, -1), own, picked,
+        slots.reshape(16 * rows, -1), own, mine,
         flops=2 * 16 * rows * 4 * rows * tests,
     )
     pt = pt.reshape(2, 2, rows, tests)
     half = lambda i: lax.dynamic_index_in_dim(pt, i, 1, keepdims=False)
     pt = half(c) + send(half(1 - c), flip("c"))
     pt = (pt + send(pt, flip("yl"))).astype(bf16)
-    cross = gram(at, arrived, gt, sib, pt)
+    cross = gram(at, far1, far2, gt, sib, pt)
     crossed = first_stage(cross)
 
     own = lax.all_to_all(own, ("z", "x"), split_axis=0, concat_axis=0, tiled=True)
@@ -238,8 +233,8 @@
     keep, give = kernel_call(
         scores_kernel,
         [shape((tokens, tests), f32)] * 2,
-        [SMEM] + [VMEM] * 3,
-        at, slots, picked, arrived,
+        [SMEM] + [VMEM] * 5,
+        at, slots, mine, sib_mine, far1, far2,
         flops=8 * 16 * rows * tokens * tests,
     )
     scores = keep + send(give, flip("c"))

time: 163 us -> 161 us (0.988)
  the two profiles are of different devices: /device:TPU:17 before, /device:TPU:0 now
where the time goes in v12:
time: 161 us; the launch traced here: 159 us
  waiting for transfers between devices  58.9 us (37%)
  starting transfers between devices  47.1 us (29%)
  Pallas kernels  31.8 us (20%)
  other arithmetic  10.8 us (7%)
  local copies, waits for them, and re-layouts  9.69 us (6%)
    ppermute x20, waiting for transfers between devices, send(): return lax.ppermute(value, AXES, pairs)  54.9 us
    pallas_call x7, Pallas kernels, kernel_call(): pl.pallas_call(body, out_shape=outs, in_specs=specs, out_specs=[VMEM] * l...  31.8 us
    ppermute x20, starting transfers between devices, send(): return lax.ppermute(value, AXES, pairs)  31.1 us
    all_to_all x2, starting transfers between devices, on_device(): lax.all_to_all(slots, ('z', 'x'), split_axis=0, concat_axis=0, tiled=True)  12.3 us
    unnamed x39, local copies, waits for them, and re-layouts  6.05 us
    all_to_all x2, waiting for transfers between devices, on_device(): lax.all_to_all(slots, ('z', 'x'), split_axis=0, concat_axis=0, tiled=True)  3.99 us
    all_to_all x1, starting transfers between devices, on_device(): lax.all_to_all(own, ('z', 'x'), split_axis=0, concat_axis=0, tiled=True)  3.72 us
    convert_element_type x2, other arithmetic, second_stage(): rs = [send(mids[k].astype(bf16), along(axis, k)) for k in (1, 2, 3)]  3.45 us
  transfers between devices with their start and end apart: 23, of which 9 were waited for; matrix products, arithmetic and copies ran while one was open for 9% of the time, Pallas kernels for 17%

profile of v12, /device:TPU:0, one launch (start us, length us, event | category | flops | bytes accessed | tf_op | source)
XLA Modules:
  0.0 159.3 jit_solution(17398283506419751833)
XLA Ops:
  0.6 2.9 %copy.12 = bf16[512,2048]{0,1:T(8,128)(2,1)S(1)} copy(bf16[512,2048]{1,0:T(8,128)(2,1)} %param.4) | data formatting | bytes 4194304 | tf_op args[0]
  3.6 2.6 %shard_map.60 = bf16[16,64,512]{2,1,0:T(8,128)(2,1)} custom-call(bf16[64,4096]{1,0:T(8,128)(2,1)} %f_ref.1, bf16[64,256]{1,0:T(8,128)(2,1)} %bitcast.43), custom_call_target="tpu_custom_call" | custom-call | bytes 1605632 | tf_op jit(solution)/shard_map/pallas_call | solution.py:43
  6.2 8.0 %all-to-all-start.1 = ((bf16[16,64,512]{2,1,0:T(8,128)(2,1)}), bf16[16,64,512]{2,1,0:T(8,128)(2,1)}, u32[]{:S(2)}, u32[]{:S(2)}) async-start(bf16[16,64,512]{2,1,0:T(8,128)(2,1)} %shard_map.60), calls=%async_computation.1 | async-start | bytes 2097152 | tf_op jit(solution)/shard_map/all_to_all | solution.py:207
  14.3 3.3 %collective-permute-start.3 = (bf16[1024,512]{1,0:T(8,128)(2,1)S(1)}, bf16[1024,512]{1,0:T(8,128)(2,1)}, u32[]{:S(2)}, u32[]{:S(2)}) collective-permute-start(bf16[1024,512]{1,0:T(8,128)(2,1)S(1)} %bitcast.29), channel_id=1, source_target_pairs={{0,1},{1,0},{2,3},{3,2},{4,5},{5,4},{6,7},{7,6},{8,9},{9,8},{10,11... | collective-permute-start | bytes 3145736 | tf_op jit(solution)/shard_map/ppermute | solution.py:30
  17.6 2.4 %constant_dynamic-slice_fusion.2 = bf16[16,1,64,512]{3,2,1,0:T(8,128)(2,1)} fusion(bf16[16,2,64,512]{3,2,1,0:T(8,128)(2,1)} %bitcast.7, s32[]{:T(128)S(6)} %select_n.28), kind=kLoop, calls=%fused_computation.17 | loop fusion | bytes 2097156 | tf_op jit(solution)/shard_map/jit(dynamic_index_in_dim)/dynamic_slice | solution.py:188
  20.3 7.7 %shard_map.59.after_ref = bf16[16,64,1152]{2,1,0:T(8,128)(2,1)} custom-call(bf16[1024,512]{1,0:T(8,128)(2,1)} %bitcast.30, bf16[1024,512]{1,0:T(8,128)(2,1)} %bitcast.8.a2_ref.own2_ref, bf16[2048,512]{1,0:T(8,128)(2,1)} %bitcast.35, bf16[2048,512]{1,0:T(8,128)(2,1)} %collective-permute-done.b2_ref), custom_call_target="tpu_custom_call" | custom-call | flops 3221225472 | bytes 8650752 | tf_op jit(solution)/shard_map/pallas_call | solution.py:43
  28.1 4.0 %all-to-all-done.1 = bf16[16,64,512]{2,1,0:T(8,128)(2,1)} async-done(((bf16[16,64,512]{2,1,0:T(8,128)(2,1)}), bf16[16,64,512]{2,1,0:T(8,128)(2,1)}, u32[]{:S(2)}, u32[]{:S(2)}) %all-to-all-start.1) | async-done | bytes 1048608 | tf_op jit(solution)/shard_map/all_to_all | solution.py:207
  32.1 3.7 %all-to-all-start = ((bf16[16,64,1152]{2,1,0:T(8,128)(2,1)}), bf16[16,64,1152]{2,1,0:T(8,128)(2,1)S(1)}, u32[]{:S(2)}, u32[]{:S(2)}) async-start(bf16[16,64,1152]{2,1,0:T(8,128)(2,1)} %shard_map.59.after_ref), calls=%async_computation | async-start | bytes 4718592 | tf_op jit(solution)/shard_map/all_to_all | solution.py:222
  35.8 2.3 %shard_map.61 = f32[256,256]{1,0:T(8,128)} custom-call(bf16[1024,512]{1,0:T(8,128)(2,1)} %bitcast.10.slots_ref, bf16[16,64,1152]{2,1,0:T(8,128)(2,1)} %shard_map.59.after_ref, bf16[1024,512]{1,0:T(8,128)(2,1)} %bitcast.31), custom_call_target="tpu_custom_call" | custom-call | flops 134217728 | bytes 4718592 | tf_op jit(solution)/shard_map/pallas_call | solution.py:43
  38.1 0.9 dynamic-slice_bitcast_fusion
  39.1 1.3 collective-permute-done.1
  40.4 0.9 bitcast_add_fusion
  41.3 1.7 %collective-permute-start.2 = (f32[2,64,256]{2,1,0:T(8,128)S(1)}, f32[2,64,256]{2,1,0:T(8,128)}, u32[]{:S(2)}, u32[]{:S(2)}) collective-permute-start(f32[2,64,256]{2,1,0:T(8,128)S(1)} %bitcast_add_fusion), channel_id=1, source_target_pairs={{0,64},{1,65},{2,66},{3,67},{4,68},{5,69},{6,70},{7,71},{8,72},{9,... | collective-permute-start | bytes 393224 | tf_op jit(solution)/shard_map/ppermute | solution.py:30
  43.6 22.9 %collective-permute-done.2 = f32[2,64,256]{2,1,0:T(8,128)} collective-permute-done((f32[2,64,256]{2,1,0:T(8,128)S(1)}, f32[2,64,256]{2,1,0:T(8,128)}, u32[]{:S(2)}, u32[]{:S(2)}) %collective-permute-start.2) | collective-permute-done | bytes 131104 | tf_op jit(solution)/shard_map/ppermute | solution.py:30
  66.6 1.5 add_convert_fusion.6.after_ref
  68.1 8.8 %shard_map.62 = (bf16[256,1024]{1,0:T(8,128)(2,1)}, bf16[256,1024]{1,0:T(8,128)(2,1)}, bf16[256,1024]{1,0:T(8,128)(2,1)}, bf16[256,1024]{1,0:T(8,128)(2,1)}, bf1...) custom-call(s32[4]{0:T(128)} %pad_add_fusion.at_ref, ...), custom_call_target="tpu_custom_call" | custom-call | flops 4294967296 | bytes 10551312 | tf_op jit(solution)/shard_map/pallas_call | solution.py:43
  76.9 1.6 collective-permute-start.5
  78.5 2.7 %collective-permute-start.6 = (bf16[256,1024]{1,0:T(8,128)(2,1)}, bf16[256,1024]{1,0:T(8,128)(2,1)S(1)}, u32[]{:S(2)}, u32[]{:S(2)}) collective-permute-start(bf16[256,1024]{1,0:T(8,128)(2,1)} %get-tuple-element.15), channel_id=1, source_target_pairs={{0,8},{1,9},{2,10},{3,11},{4,12},{5,13},{6,14},{7,15},{8,0},{9,1},... | collective-permute-start | bytes 1572872 | tf_op jit(solution)/shard_map/ppermute | solution.py:30
  81.2 1.5 collective-permute-start.7
  82.7 1.5 collective-permute-start.8
  84.1 2.7 %collective-permute-start.9 = (bf16[256,1024]{1,0:T(8,128)(2,1)}, bf16[256,1024]{1,0:T(8,128)(2,1)S(1)}, u32[]{:S(2)}, u32[]{:S(2)}) collective-permute-start(bf16[256,1024]{1,0:T(8,128)(2,1)} %get-tuple-element.18), channel_id=1, source_target_pairs={{0,32},{1,33},{2,34},{3,35},{4,36},{5,37},{6,38},{7,39},{8,40},{9,... | collective-permute-start | bytes 1572872 | tf_op jit(solution)/shard_map/ppermute | solution.py:30
  86.8 6.2 %collective-permute-done.5.refs_0_ = bf16[256,1024]{1,0:T(8,128)(2,1)S(1)} collective-permute-done((bf16[256,1024]{1,0:T(8,128)(2,1)}, bf16[256,1024]{1,0:T(8,128)(2,1)S(1)}, u32[]{:S(2)}, u32[]{:S(2)}) %collective-permute-start.5) | collective-permute-done | bytes 524320 | tf_op jit(solution)/shard_map/ppermute | solution.py:30
  93.1 1.7 %collective-permute-start.10 = (bf16[256,1024]{1,0:T(8,128)(2,1)}, bf16[256,1024]{1,0:T(8,128)(2,1)}, u32[]{:S(2)}, u32[]{:S(2)}) collective-permute-start(bf16[256,1024]{1,0:T(8,128)(2,1)} %get-tuple-element.19), channel_id=1, source_target_pairs={{0,48},{1,49},{2,50},{3,51},{4,52},{5,53},{6,54},{7,55},{8,56},{9,... | collective-permute-start | bytes 1572872 | tf_op jit(solution)/shard_map/ppermute | solution.py:30
  94.8 8.2 %collective-permute-done.6.refs_1_ = bf16[256,1024]{1,0:T(8,128)(2,1)S(1)} collective-permute-done((bf16[256,1024]{1,0:T(8,128)(2,1)}, bf16[256,1024]{1,0:T(8,128)(2,1)S(1)}, u32[]{:S(2)}, u32[]{:S(2)}) %collective-permute-start.6) | collective-permute-done | bytes 524320 | tf_op jit(solution)/shard_map/ppermute | solution.py:30
  103.0 4.7 %collective-permute-done.9.refs_4_ = bf16[256,1024]{1,0:T(8,128)(2,1)S(1)} collective-permute-done((bf16[256,1024]{1,0:T(8,128)(2,1)}, bf16[256,1024]{1,0:T(8,128)(2,1)S(1)}, u32[]{:S(2)}, u32[]{:S(2)}) %collective-permute-start.9) | collective-permute-done | bytes 524320 | tf_op jit(solution)/shard_map/ppermute | solution.py:30
  107.8 0.8 copy-done.7
  108.6 0.8 copy-done
  109.3 3.4 %shard_map.63 = (f32[64,2048]{1,0:T(8,128)}, bf16[16,160,256]{2,1,0:T(8,128)(2,1)}) custom-call(s32[4]{0:T(128)} %pad_add_fusion.at_ref, bf16[16,64,1152]{2,1,0:T(8,128)(2,1)} %copy-done, bf16[128,256]{1,0:T(8,128)(2,1)} %bitcast.41, bf16[256,1024]{1,0:T(8,128)(2,1)} %copy-done.9, bf16[256,1024]{1,0:T(8,128)(2,1)} %copy-done.11, ...), custom_call_target="tpu_custom_call" | custom-call | bytes 7405584 | tf_op jit(solution)/shard_map/pallas_call | solution.py:43
  112.7 4.3 %all-to-all-start.2 = ((bf16[16,160,256]{2,1,0:T(8,128)(2,1)}), bf16[16,160,256]{2,1,0:T(8,128)(2,1)S(1)}, u32[]{:S(2)}, u32[]{:S(2)}) async-start(bf16[16,160,256]{2,1,0:T(8,128)(2,1)} %get-tuple-element.20), calls=%async_computation.2 | async-start | bytes 2621440 | tf_op jit(solution)/shard_map/all_to_all | solution.py:229
  117.1 1.5 add_convert_fusion.5
  118.6 2.2 %collective-permute-start.13 = (bf16[64,1024]{1,0:T(8,128)(2,1)S(1)}, bf16[64,1024]{1,0:T(8,128)(2,1)S(1)}, u32[]{:S(2)}, u32[]{:S(2)}) collective-permute-start(bf16[64,1024]{1,0:T(8,128)(2,1)S(1)} %get-tuple-element.26), channel_id=1, source_target_pairs={{0,16},{1,17},{2,18},{3,19},{4,20},{5,21},{6,22},{7,23},{8,24},{9,... | collective-permute-start | bytes 393224 | tf_op jit(solution)/shard_map/ppermute | solution.py:30
  120.8 1.3 collective-permute-start.15
  122.1 2.2 %collective-permute-start.14 = (bf16[64,1024]{1,0:T(8,128)(2,1)S(1)}, bf16[64,1024]{1,0:T(8,128)(2,1)S(1)}, u32[]{:S(2)}, u32[]{:S(2)}) collective-permute-start(bf16[64,1024]{1,0:T(8,128)(2,1)S(1)} %get-tuple-element.28), channel_id=1, source_target_pairs={{0,32},{1,33},{2,34},{3,35},{4,36},{5,37},{6,38},{7,39},{8,40},{9,... | collective-permute-start | bytes 393224 | tf_op jit(solution)/shard_map/ppermute | solution.py:30
  124.3 1.9 %add_convert_fusion.2 = (bf16[64,1024]{1,0:T(8,128)(2,1)}, bf16[64,1024]{1,0:T(8,128)(2,1)}, bf16[64,1024]{1,0:T(8,128)(2,1)}) fusion(bf16[256,1024]{1,0:T(8,128)(2,1)} %collective-permute-done.10.refs_5_, bf16[256,1024]{1,0:T(8,128)(2,1)S(1)} %copy-done.8, bf16[256,1024]{1,0:T(8,128)(2,1)S(1)} %copy-done.6, bf16[256,1024]{1,0:T(8,128)(2,1)S(1)} %copy-done.16), kind=kLoop, calls=%fused_computation.7 | loop fusion | flops 1572864 | bytes 1966080 | tf_op jit(solution)/shard_map/convert_element_type | solution.py:143
  126.2 1.5 collective-permute-start.16
  127.7 1.8 %collective-permute-start.18 = (bf16[64,1024]{1,0:T(8,128)(2,1)}, bf16[64,1024]{1,0:T(8,128)(2,1)}, u32[]{:S(2)}, u32[]{:S(2)}) collective-permute-start(bf16[64,1024]{1,0:T(8,128)(2,1)} %get-tuple-element.30), channel_id=1, source_target_pairs={{0,12},{1,13},{2,14},{3,15},{4,0},{5,1},{6,2},{7,3},{8,4},{9,5},{1... | collective-permute-start | bytes 393224 | tf_op jit(solution)/shard_map/ppermute | solution.py:30
  129.5 7.8 %collective-permute-done.13 = bf16[64,1024]{1,0:T(8,128)(2,1)S(1)} collective-permute-done((bf16[64,1024]{1,0:T(8,128)(2,1)S(1)}, bf16[64,1024]{1,0:T(8,128)(2,1)S(1)}, u32[]{:S(2)}, u32[]{:S(2)}) %collective-permute-start.13) | collective-permute-done | bytes 131104 | tf_op jit(solution)/shard_map/ppermute | solution.py:30
  137.3 2.5 %collective-permute-start.17 = (bf16[64,1024]{1,0:T(8,128)(2,1)}, bf16[64,1024]{1,0:T(8,128)(2,1)}, u32[]{:S(2)}, u32[]{:S(2)}) collective-permute-start(bf16[64,1024]{1,0:T(8,128)(2,1)} %get-tuple-element.31), channel_id=1, source_target_pairs={{0,8},{1,9},{2,10},{3,11},{4,12},{5,13},{6,14},{7,15},{8,0},{9,1},... | collective-permute-start | bytes 393224 | tf_op jit(solution)/shard_map/ppermute | solution.py:30
  139.8 1.2 convert_add_fusion.1
  141.5 2.5 %collective-permute-done.17 = bf16[64,1024]{1,0:T(8,128)(2,1)} collective-permute-done((bf16[64,1024]{1,0:T(8,128)(2,1)}, bf16[64,1024]{1,0:T(8,128)(2,1)}, u32[]{:S(2)}, u32[]{:S(2)}) %collective-permute-start.17) | collective-permute-done | bytes 131104 | tf_op jit(solution)/shard_map/ppermute | solution.py:30
  144.0 1.2 convert_add_fusion
  145.3 0.8 copy.23
  146.7 2.1 %shard_map.65 = f32[64,2048]{1,0:T(8,128)} custom-call(s32[4]{0:T(128)} %pad_add_fusion.at_ref, f32[64,2048]{1,0:T(8,128)} %get-tuple-element.23.direct_ref, bf16[64,1024]{1,0:T(8,128)(2,1)} %bitcast.40, bf16[64,1024]{1,0:T(8,128)(2,1)} %copy-done.17), custom_call_target="tpu_custom_call" | custom-call | bytes 1310736 | tf_op jit(solution)/shard_map/pallas_call | solution.py:43
  148.9 2.5 %collective-permute-start.19 = (bf16[64,2048]{1,0:T(8,128)(2,1)S(1)}, bf16[64,2048]{1,0:T(8,128)(2,1)S(1)}, u32[]{:S(2)}, u32[]{:S(2)}) collective-permute-start(bf16[64,2048]{1,0:T(8,128)(2,1)S(1)} %select_convert_fusion), channel_id=1, source_target_pairs={{0,64},{1,65},{2,66},{3,67},{4,68},{5,69},{6,70},{7,71},{8,72},{9,... | collective-permute-start | bytes 786440 | tf_op jit(solution)/shard_map/ppermute | solution.py:30
  151.4 4.8 %shard_map.64 = (f32[512,256]{1,0:T(8,128)}, f32[512,256]{1,0:T(8,128)}) custom-call(s32[4]{0:T(128)} %pad_add_fusion.at_ref, bf16[16,160,256]{2,1,0:T(8,128)(2,1)} %copy-done.2, bf16[1024,512]{1,0:T(8,128)(2,1)} %bitcast.32, bf16[1024,512]{1,0:T(8,128)(2,1)} %bitcast.8.a2_ref.own2_ref, bf16[1024,512]{1,0:T(8,128)(2,1)} %collective-permute-done.3.a1_ref.cross1_ref, ...), custom_call_target="tpu_custom_call" | custom-call | flops 1073741824 | bytes 6553616 | tf_op jit(solution)/shard_map/pallas_call | solution.py:43
  156.3 0.9 multiply_add_fusion
  157.2 1.2 collective-permute-done.11
  158.4 0.9 add.126
  (60 shorter events, 2.6 us)
Async XLA Ops:
  3.5 10.8 %copy-start.4 = (bf16[512,2048]{0,1:T(8,128)(2,1)}, bf16[512,2048]{0,1:T(8,128)(2,1)S(1)}, u32[]{:S(2)}) copy-start(bf16[512,2048]{0,1:T(8,128)(2,1)S(1)} %copy.12) | copy-start | bytes 6291460
  3.5 14.1 %collective-permute-start = (bf16[2048,512]{1,0:T(8,128)(2,1)S(1)}, bf16[2048,512]{1,0:T(8,128)(2,1)}, u32[]{:S(2)}, u32[]{:S(2)}) collective-permute-start(bf16[2048,512]{1,0:T(8,128)(2,1)S(1)} %bitcast.33), channel_id=1, source_target_pairs={{0,2},{1,3},{2,0},{3,1},{4,6},{5,7},{6,4},{7,5},{8,10},{9,11},{10,... | collective-permute-start | bytes 6291464 | tf_op jit(solution)/shard_map/ppermute | solution.py:30
  6.2 25.9 %all-to-all-start.1 = ((bf16[16,64,512]{2,1,0:T(8,128)(2,1)}), bf16[16,64,512]{2,1,0:T(8,128)(2,1)}, u32[]{:S(2)}, u32[]{:S(2)}) async-start(bf16[16,64,512]{2,1,0:T(8,128)(2,1)} %shard_map.60), calls=%async_computation.1 | async-start | bytes 2097152 | tf_op jit(solution)/shard_map/all_to_all | solution.py:207
  14.3 6.0 %copy-start.1 = (bf16[16,1,64,512]{3,2,1,0:T(8,128)(2,1)}, bf16[16,1,64,512]{3,2,1,0:T(8,128)(2,1)S(1)}, u32[]{:S(2)}) copy-start(bf16[16,1,64,512]{3,2,1,0:T(8,128)(2,1)S(1)} %constant_dynamic-slice_fusion.3) | copy-start | bytes 3145732
  14.3 53.7 %collective-permute-start.3 = (bf16[1024,512]{1,0:T(8,128)(2,1)S(1)}, bf16[1024,512]{1,0:T(8,128)(2,1)}, u32[]{:S(2)}, u32[]{:S(2)}) collective-permute-start(bf16[1024,512]{1,0:T(8,128)(2,1)S(1)} %bitcast.29), channel_id=1, source_target_pairs={{0,1},{1,0},{2,3},{3,2},{4,5},{5,4},{6,7},{7,6},{8,9},{9,8},{10,11... | collective-permute-start | bytes 3145736 | tf_op jit(solution)/shard_map/ppermute | solution.py:30
  20.0 48.1 %collective-permute-start.4 = (bf16[1024,512]{1,0:T(8,128)(2,1)}, bf16[1024,512]{1,0:T(8,128)(2,1)}, u32[]{:S(2)}, u32[]{:S(2)}) collective-permute-start(bf16[1024,512]{1,0:T(8,128)(2,1)} %bitcast.8.a2_ref.own2_ref), channel_id=1, source_target_pairs={{0,1},{1,0},{2,3},{3,2},{4,5},{5,4},{6,7},{7,6},{8,9},{9,8},{10,11... | collective-permute-start | bytes 3145736 | tf_op jit(solution)/shard_map/ppermute | solution.py:30
  32.1 75.7 %all-to-all-start = ((bf16[16,64,1152]{2,1,0:T(8,128)(2,1)}), bf16[16,64,1152]{2,1,0:T(8,128)(2,1)S(1)}, u32[]{:S(2)}, u32[]{:S(2)}) async-start(bf16[16,64,1152]{2,1,0:T(8,128)(2,1)} %shard_map.59.after_ref), calls=%async_computation | async-start | bytes 4718592 | tf_op jit(solution)/shard_map/all_to_all | solution.py:222
  39.0 1.4 collective-permute-start.1
  41.3 25.2 %collective-permute-start.2 = (f32[2,64,256]{2,1,0:T(8,128)S(1)}, f32[2,64,256]{2,1,0:T(8,128)}, u32[]{:S(2)}, u32[]{:S(2)}) collective-permute-start(f32[2,64,256]{2,1,0:T(8,128)S(1)} %bitcast_add_fusion), channel_id=1, source_target_pairs={{0,64},{1,65},{2,66},{3,67},{4,68},{5,69},{6,70},{7,71},{8,72},{9,... | collective-permute-start | bytes 393224 | tf_op jit(solution)/shard_map/ppermute | solution.py:30
  76.9 16.1 %collective-permute-start.5 = (bf16[256,1024]{1,0:T(8,128)(2,1)}, bf16[256,1024]{1,0:T(8,128)(2,1)S(1)}, u32[]{:S(2)}, u32[]{:S(2)}) collective-permute-start(bf16[256,1024]{1,0:T(8,128)(2,1)} %get-tuple-element.14), channel_id=1, source_target_pairs={{0,4},{1,5},{2,6},{3,7},{4,8},{5,9},{6,10},{7,11},{8,12},{9,13},{1... | collective-permute-start | bytes 1572872 | tf_op jit(solution)/shard_map/ppermute | solution.py:30
  78.5 24.5 %collective-permute-start.6 = (bf16[256,1024]{1,0:T(8,128)(2,1)}, bf16[256,1024]{1,0:T(8,128)(2,1)S(1)}, u32[]{:S(2)}, u32[]{:S(2)}) collective-permute-start(bf16[256,1024]{1,0:T(8,128)(2,1)} %get-tuple-element.15), channel_id=1, source_target_pairs={{0,8},{1,9},{2,10},{3,11},{4,12},{5,13},{6,14},{7,15},{8,0},{9,1},... | collective-permute-start | bytes 1572872 | tf_op jit(solution)/shard_map/ppermute | solution.py:30
  81.2 21.8 %collective-permute-start.7 = (bf16[256,1024]{1,0:T(8,128)(2,1)}, bf16[256,1024]{1,0:T(8,128)(2,1)S(1)}, u32[]{:S(2)}, u32[]{:S(2)}) collective-permute-start(bf16[256,1024]{1,0:T(8,128)(2,1)} %get-tuple-element.16), channel_id=1, source_target_pairs={{0,12},{1,13},{2,14},{3,15},{4,0},{5,1},{6,2},{7,3},{8,4},{9,5},{1... | collective-permute-start | bytes 1572872 | tf_op jit(solution)/shard_map/ppermute | solution.py:30
  82.7 20.3 %collective-permute-start.8 = (bf16[256,1024]{1,0:T(8,128)(2,1)}, bf16[256,1024]{1,0:T(8,128)(2,1)S(1)}, u32[]{:S(2)}, u32[]{:S(2)}) collective-permute-start(bf16[256,1024]{1,0:T(8,128)(2,1)} %get-tuple-element.17), channel_id=1, source_target_pairs={{0,16},{1,17},{2,18},{3,19},{4,20},{5,21},{6,22},{7,23},{8,24},{9,... | collective-permute-start | bytes 1572872 | tf_op jit(solution)/shard_map/ppermute | solution.py:30
  84.1 23.6 %collective-permute-start.9 = (bf16[256,1024]{1,0:T(8,128)(2,1)}, bf16[256,1024]{1,0:T(8,128)(2,1)S(1)}, u32[]{:S(2)}, u32[]{:S(2)}) collective-permute-start(bf16[256,1024]{1,0:T(8,128)(2,1)} %get-tuple-element.18), channel_id=1, source_target_pairs={{0,32},{1,33},{2,34},{3,35},{4,36},{5,37},{6,38},{7,39},{8,40},{9,... | collective-permute-start | bytes 1572872 | tf_op jit(solution)/shard_map/ppermute | solution.py:30
  93.1 14.7 %copy-start.9 = (bf16[256,1024]{1,0:T(8,128)(2,1)}, bf16[256,1024]{1,0:T(8,128)(2,1)S(1)}, u32[]{:S(2)}) copy-start(bf16[256,1024]{1,0:T(8,128)(2,1)S(1)} %collective-permute-done.5.refs_0_) | copy-start | bytes 1572868
  93.1 14.7 %collective-permute-start.10 = (bf16[256,1024]{1,0:T(8,128)(2,1)}, bf16[256,1024]{1,0:T(8,128)(2,1)}, u32[]{:S(2)}, u32[]{:S(2)}) collective-permute-start(bf16[256,1024]{1,0:T(8,128)(2,1)} %get-tuple-element.19), channel_id=1, source_target_pairs={{0,48},{1,49},{2,50},{3,51},{4,52},{5,53},{6,54},{7,55},{8,56},{9,... | collective-permute-start | bytes 1572872 | tf_op jit(solution)/shard_map/ppermute | solution.py:30
  103.0 4.8 %copy-start.11 = (bf16[256,1024]{1,0:T(8,128)(2,1)}, bf16[256,1024]{1,0:T(8,128)(2,1)S(1)}, u32[]{:S(2)}) copy-start(bf16[256,1024]{1,0:T(8,128)(2,1)S(1)} %collective-permute-done.6.refs_1_) | copy-start | bytes 1572868
  103.0 4.7 %copy-start.13 = (bf16[256,1024]{1,0:T(8,128)(2,1)}, bf16[256,1024]{1,0:T(8,128)(2,1)S(1)}, u32[]{:S(2)}) copy-start(bf16[256,1024]{1,0:T(8,128)(2,1)S(1)} %collective-permute-done.7.refs_2_) | copy-start | bytes 1572868
  103.0 4.8 %copy-start.5 = (bf16[256,1024]{1,0:T(8,128)(2,1)}, bf16[256,1024]{1,0:T(8,128)(2,1)S(1)}, u32[]{:S(2)}) copy-start(bf16[256,1024]{1,0:T(8,128)(2,1)S(1)} %collective-permute-done.8.refs_3_) | copy-start | bytes 1572868
  107.8 0.8 copy-start.7
  107.8 1.5 copy-start
  112.7 4.4 %copy-start.10 = (bf16[256,1024]{1,0:T(8,128)(2,1)S(1)}, bf16[256,1024]{1,0:T(8,128)(2,1)}, u32[]{:S(2)}) copy-start(bf16[256,1024]{1,0:T(8,128)(2,1)} %copy-done.9) | copy-start | bytes 1572868
  112.7 4.4 %copy-start.12 = (bf16[256,1024]{1,0:T(8,128)(2,1)S(1)}, bf16[256,1024]{1,0:T(8,128)(2,1)}, u32[]{:S(2)}) copy-start(bf16[256,1024]{1,0:T(8,128)(2,1)} %copy-done.11) | copy-start | bytes 1572868
  112.7 11.6 %copy-start.6 = (bf16[256,1024]{1,0:T(8,128)(2,1)S(1)}, bf16[256,1024]{1,0:T(8,128)(2,1)}, u32[]{:S(2)}) copy-start(bf16[256,1024]{1,0:T(8,128)(2,1)} %copy-done.5) | copy-start | bytes 1572868
  112.7 11.6 %copy-start.8 = (bf16[256,1024]{1,0:T(8,128)(2,1)S(1)}, bf16[256,1024]{1,0:T(8,128)(2,1)}, u32[]{:S(2)}) copy-start(bf16[256,1024]{1,0:T(8,128)(2,1)} %copy-done.7) | copy-start | bytes 1572868
  112.7 28.2 %all-to-all-start.2 = ((bf16[16,160,256]{2,1,0:T(8,128)(2,1)}), bf16[16,160,256]{2,1,0:T(8,128)(2,1)S(1)}, u32[]{:S(2)}, u32[]{:S(2)}) async-start(bf16[16,160,256]{2,1,0:T(8,128)(2,1)} %get-tuple-element.20), calls=%async_computation.2 | async-start | bytes 2621440 | tf_op jit(solution)/shard_map/all_to_all | solution.py:229
  117.1 7.2 %copy-start.16 = (bf16[256,1024]{1,0:T(8,128)(2,1)S(1)}, bf16[256,1024]{1,0:T(8,128)(2,1)}, u32[]{:S(2)}) copy-start(bf16[256,1024]{1,0:T(8,128)(2,1)} %get-tuple-element.25) | copy-start | bytes 1572868
  118.6 18.7 %collective-permute-start.13 = (bf16[64,1024]{1,0:T(8,128)(2,1)S(1)}, bf16[64,1024]{1,0:T(8,128)(2,1)S(1)}, u32[]{:S(2)}, u32[]{:S(2)}) collective-permute-start(bf16[64,1024]{1,0:T(8,128)(2,1)S(1)} %get-tuple-element.26), channel_id=1, source_target_pairs={{0,16},{1,17},{2,18},{3,19},{4,20},{5,21},{6,22},{7,23},{8,24},{9,... | collective-permute-start | bytes 393224 | tf_op jit(solution)/shard_map/ppermute | solution.py:30
  120.8 19.0 %collective-permute-start.15 = (bf16[64,1024]{1,0:T(8,128)(2,1)S(1)}, bf16[64,1024]{1,0:T(8,128)(2,1)S(1)}, u32[]{:S(2)}, u32[]{:S(2)}) collective-permute-start(bf16[64,1024]{1,0:T(8,128)(2,1)S(1)} %get-tuple-element.27), channel_id=1, source_target_pairs={{0,48},{1,49},{2,50},{3,51},{4,52},{5,53},{6,54},{7,55},{8,56},{9,... | collective-permute-start | bytes 393224 | tf_op jit(solution)/shard_map/ppermute | solution.py:30
  122.1 17.7 %collective-permute-start.14 = (bf16[64,1024]{1,0:T(8,128)(2,1)S(1)}, bf16[64,1024]{1,0:T(8,128)(2,1)S(1)}, u32[]{:S(2)}, u32[]{:S(2)}) collective-permute-start(bf16[64,1024]{1,0:T(8,128)(2,1)S(1)} %get-tuple-element.28), channel_id=1, source_target_pairs={{0,32},{1,33},{2,34},{3,35},{4,36},{5,37},{6,38},{7,39},{8,40},{9,... | collective-permute-start | bytes 393224 | tf_op jit(solution)/shard_map/ppermute | solution.py:30
  126.2 15.2 %collective-permute-start.16 = (bf16[64,1024]{1,0:T(8,128)(2,1)}, bf16[64,1024]{1,0:T(8,128)(2,1)S(1)}, u32[]{:S(2)}, u32[]{:S(2)}) collective-permute-start(bf16[64,1024]{1,0:T(8,128)(2,1)} %get-tuple-element.29), channel_id=1, source_target_pairs={{0,4},{1,5},{2,6},{3,7},{4,8},{5,9},{6,10},{7,11},{8,12},{9,13},{1... | collective-permute-start | bytes 393224 | tf_op jit(solution)/shard_map/ppermute | solution.py:30
  127.7 13.8 %collective-permute-start.18 = (bf16[64,1024]{1,0:T(8,128)(2,1)}, bf16[64,1024]{1,0:T(8,128)(2,1)}, u32[]{:S(2)}, u32[]{:S(2)}) collective-permute-start(bf16[64,1024]{1,0:T(8,128)(2,1)} %get-tuple-element.30), channel_id=1, source_target_pairs={{0,12},{1,13},{2,14},{3,15},{4,0},{5,1},{6,2},{7,3},{8,4},{9,5},{1... | collective-permute-start | bytes 393224 | tf_op jit(solution)/shard_map/ppermute | solution.py:30
  137.3 6.8 %collective-permute-start.17 = (bf16[64,1024]{1,0:T(8,128)(2,1)}, bf16[64,1024]{1,0:T(8,128)(2,1)}, u32[]{:S(2)}, u32[]{:S(2)}) collective-permute-start(bf16[64,1024]{1,0:T(8,128)(2,1)} %get-tuple-element.31), channel_id=1, source_target_pairs={{0,8},{1,9},{2,10},{3,11},{4,12},{5,13},{6,14},{7,15},{8,0},{9,1},... | collective-permute-start | bytes 393224 | tf_op jit(solution)/shard_map/ppermute | solution.py:30
  140.9 7.9 %copy-start.2 = (bf16[16,160,256]{2,1,0:T(8,128)(2,1)}, bf16[16,160,256]{2,1,0:T(8,128)(2,1)S(1)}, u32[]{:S(2)}) copy-start(bf16[16,160,256]{2,1,0:T(8,128)(2,1)S(1)} %all-to-all-done.2.pt_ref) | copy-start | bytes 3932164
  141.4 4.7 %collective-permute-start.12 = (bf16[64,1024]{1,0:T(8,128)(2,1)S(1)}, bf16[64,1024]{1,0:T(8,128)(2,1)S(1)}, u32[]{:S(2)}, u32[]{:S(2)}) collective-permute-start(bf16[64,1024]{1,0:T(8,128)(2,1)S(1)} %bitcast.42), channel_id=1, source_target_pairs={{0,2},{1,3},{2,0},{3,1},{4,6},{5,7},{6,4},{7,5},{8,10},{9,11},{10,... | collective-permute-start | bytes 393224 | tf_op jit(solution)/shard_map/ppermute | solution.py:30
  146.1 0.7 copy-start.17
  148.9 7.4 %copy-start.3 = (f32[64,2048]{1,0:T(8,128)S(1)}, f32[64,2048]{1,0:T(8,128)}, u32[]{:S(2)}) copy-start(f32[64,2048]{1,0:T(8,128)} %shard_map.65) | copy-start | bytes 1572868
  148.9 7.4 %copy-start.14 = (f32[64,2048]{1,0:T(8,128)S(1)}, f32[64,2048]{1,0:T(8,128)}, u32[]{:S(2)}) copy-start(f32[64,2048]{1,0:T(8,128)} %param.5) | copy-start | bytes 1572868
  148.9 7.4 %collective-permute-start.19 = (bf16[64,2048]{1,0:T(8,128)(2,1)S(1)}, bf16[64,2048]{1,0:T(8,128)(2,1)S(1)}, u32[]{:S(2)}, u32[]{:S(2)}) collective-permute-start(bf16[64,2048]{1,0:T(8,128)(2,1)S(1)} %select_convert_fusion), channel_id=1, source_target_pairs={{0,64},{1,65},{2,66},{3,67},{4,68},{5,69},{6,70},{7,71},{8,72},{9,... | collective-permute-start | bytes 786440 | tf_op jit(solution)/shard_map/ppermute | solution.py:30
  156.3 2.1 %copy-start.15 = (f32[512,256]{1,0:T(8,128)S(1)}, f32[512,256]{1,0:T(8,128)}, u32[]{:S(2)}) copy-start(f32[512,256]{1,0:T(8,128)} %get-tuple-element.21) | copy-start | bytes 1572868
  156.3 2.1 %collective-permute-start.11 = (f32[512,256]{1,0:T(8,128)}, f32[512,256]{1,0:T(8,128)S(1)}, u32[]{:S(2)}, u32[]{:S(2)}) collective-permute-start(f32[512,256]{1,0:T(8,128)} %get-tuple-element.22), channel_id=1, source_target_pairs={{0,2},{1,3},{2,0},{3,1},{4,6},{5,7},{6,4},{7,5},{8,10},{9,11},{10,... | collective-permute-start | bytes 1572872 | tf_op jit(solution)/shard_map/ppermute | solution.py:30

commit v13 on v12

--- a/solution.py
+++ b/solution.py
@@ -223,8 +223,8 @@
     direct, slots = kernel_call(
         own_sum_kernel,
         [shape((rows, feats), f32), shape((16, 2 * rows + rows // 2, tests), bf16)],
-        [SMEM, VMEM, VMEM] + [ANY] * 6,
-        at, own, pt.reshape(2 * rows, tests), *crossed[0], *crossed[1],
+        [SMEM, VMEM, VMEM] + [ANY] * 5,
+        at, own, pt.reshape(2 * rows, tests), *crossed[0], *crossed[1][:2],
     )
     slots = lax.all_to_all(slots, ("z", "x"), split_axis=0, concat_axis=0, tiled=True)
     mirror = slots[:, 2 * rows :]

time: 161 us -> 195 us (1.21)
  waiting for transfers between devices: 58.9 us -> 94.1 us
  starting transfers between devices: 47.1 us -> 43.8 us
  local copies, waits for them, and re-layouts: 9.69 us -> 11.7 us
    ppermute x20, waiting for transfers between devices: 54.9 us -> 87.5 us  [send(): return lax.ppermute(value, AXES, pairs)]
    ppermute x20, starting transfers between devices: 31.1 us -> 28.2 us  [send(): return lax.ppermute(value, AXES, pairs)]
    all_to_all x2, waiting for transfers between devices: 3.99 us -> 6.61 us  [on_device(): lax.all_to_all(slots, ('z', 'x'), split_axis=0, concat_axis=0, tiled=True)]
  transfers between devices with their start and end apart: 23 -> 23, of which waited for: 9 -> 10; matrix products, arithmetic and copies ran while one was open for 9% -> 8% of each run, Pallas kernels for 17% -> 14%
where the time goes in v13:
time: 195 us; the launch traced here: 193 us
  waiting for transfers between devices  94.1 us (48%)
  starting transfers between devices  43.8 us (22%)
  Pallas kernels  31.7 us (16%)
  local copies, waits for them, and re-layouts  11.7 us (6%)
  other arithmetic  10.8 us (6%)
    ppermute x20, waiting for transfers between devices, send(): return lax.ppermute(value, AXES, pairs)  87.5 us
    pallas_call x7, Pallas kernels, kernel_call(): pl.pallas_call(body, out_shape=outs, in_specs=specs, out_specs=[VMEM] * l...  31.7 us
    ppermute x20, starting transfers between devices, send(): return lax.ppermute(value, AXES, pairs)  28.2 us
    all_to_all x2, starting transfers between devices, on_device(): lax.all_to_all(slots, ('z', 'x'), split_axis=0, concat_axis=0, tiled=True)  11.9 us
    unnamed x39, local copies, waits for them, and re-layouts  7.04 us
    all_to_all x2, waiting for transfers between devices, on_device(): lax.all_to_all(slots, ('z', 'x'), split_axis=0, concat_axis=0, tiled=True)  6.61 us
  transfers between devices with their start and end apart: 23, of which 10 were waited for; matrix products, arithmetic and copies ran while one was open for 8% of the time, Pallas kernels for 14%

profile of v13, /device:TPU:0, one launch (start us, length us, event | category | flops | bytes accessed | tf_op | source)
XLA Modules:
  0.0 192.9 jit_solution(10578544084388421646)
XLA Ops:
  0.6 2.9 %copy.12 = bf16[512,2048]{0,1:T(8,128)(2,1)S(1)} copy(bf16[512,2048]{1,0:T(8,128)(2,1)} %param.4) | data formatting | bytes 4194304 | tf_op args[0]
  3.6 2.5 %shard_map.60 = bf16[16,64,512]{2,1,0:T(8,128)(2,1)} custom-call(bf16[64,4096]{1,0:T(8,128)(2,1)} %f_ref.1, bf16[64,256]{1,0:T(8,128)(2,1)} %bitcast.46), custom_call_target="tpu_custom_call" | custom-call | bytes 1605632 | tf_op jit(solution)/shard_map/pallas_call | solution.py:43
  6.1 8.0 %all-to-all-start.1 = ((bf16[16,64,512]{2,1,0:T(8,128)(2,1)}), bf16[16,64,512]{2,1,0:T(8,128)(2,1)}, u32[]{:S(2)}, u32[]{:S(2)}) async-start(bf16[16,64,512]{2,1,0:T(8,128)(2,1)} %shard_map.60), calls=%async_computation.1 | async-start | bytes 2097152 | tf_op jit(solution)/shard_map/all_to_all | solution.py:207
  14.1 1.1 constant_dynamic-slice_fusion.3
  15.2 2.4 %constant_dynamic-slice_fusion.2 = bf16[16,1,64,512]{3,2,1,0:T(8,128)(2,1)} fusion(bf16[16,2,64,512]{3,2,1,0:T(8,128)(2,1)} %bitcast.7, s32[]{:T(128)S(6)} %select_n.28), kind=kLoop, calls=%fused_computation.17 | loop fusion | bytes 2097156 | tf_op jit(solution)/shard_map/jit(dynamic_index_in_dim)/dynamic_slice | solution.py:188
  17.6 7.8 %shard_map.59.after_ref = bf16[16,64,1152]{2,1,0:T(8,128)(2,1)} custom-call(bf16[1024,512]{1,0:T(8,128)(2,1)} %bitcast.29, bf16[1024,512]{1,0:T(8,128)(2,1)} %bitcast.37, bf16[2048,512]{1,0:T(8,128)(2,1)} %bitcast.35, bf16[2048,512]{1,0:T(8,128)(2,1)} %collective-permute-done.b2_ref), custom_call_target="tpu_custom_call" | custom-call | flops 3221225472 | bytes 8650752 | tf_op jit(solution)/shard_map/pallas_call | solution.py:43
  25.4 6.6 %all-to-all-done.1 = bf16[16,64,512]{2,1,0:T(8,128)(2,1)} async-done(((bf16[16,64,512]{2,1,0:T(8,128)(2,1)}), bf16[16,64,512]{2,1,0:T(8,128)(2,1)}, u32[]{:S(2)}, u32[]{:S(2)}) %all-to-all-start.1) | async-done | bytes 1048608 | tf_op jit(solution)/shard_map/all_to_all | solution.py:207
  32.0 3.7 %all-to-all-start = ((bf16[16,64,1152]{2,1,0:T(8,128)(2,1)}), bf16[16,64,1152]{2,1,0:T(8,128)(2,1)S(1)}, u32[]{:S(2)}, u32[]{:S(2)}) async-start(bf16[16,64,1152]{2,1,0:T(8,128)(2,1)} %shard_map.59.after_ref), calls=%async_computation | async-start | bytes 4718592 | tf_op jit(solution)/shard_map/all_to_all | solution.py:222
  35.7 3.3 %collective-permute-start.3 = (bf16[1024,512]{1,0:T(8,128)(2,1)S(1)}, bf16[1024,512]{1,0:T(8,128)(2,1)}, u32[]{:S(2)}, u32[]{:S(2)}) collective-permute-start(bf16[1024,512]{1,0:T(8,128)(2,1)S(1)} %bitcast.32), channel_id=1, source_target_pairs={{0,1},{1,0},{2,3},{3,2},{4,5},{5,4},{6,7},{7,6},{8,9},{9,8},{10,11... | collective-permute-start | bytes 3145736 | tf_op jit(solution)/shard_map/ppermute | solution.py:30
  39.3 2.3 %shard_map.61 = f32[256,256]{1,0:T(8,128)} custom-call(bf16[1024,512]{1,0:T(8,128)(2,1)} %bitcast.10.slots_ref, bf16[16,64,1152]{2,1,0:T(8,128)(2,1)} %shard_map.59.after_ref, bf16[1024,512]{1,0:T(8,128)(2,1)} %bitcast.30), custom_call_target="tpu_custom_call" | custom-call | flops 134217728 | bytes 4718592 | tf_op jit(solution)/shard_map/pallas_call | solution.py:43
  41.6 0.9 dynamic-slice_bitcast_fusion
  42.6 1.3 collective-permute-done.1
  44.0 0.9 bitcast_add_fusion
  44.9 1.7 collective-permute-start.2
  47.2 40.0 %collective-permute-done.2 = f32[2,64,256]{2,1,0:T(8,128)} collective-permute-done((f32[2,64,256]{2,1,0:T(8,128)S(1)}, f32[2,64,256]{2,1,0:T(8,128)}, u32[]{:S(2)}, u32[]{:S(2)}) %collective-permute-start.2) | collective-permute-done | bytes 131104 | tf_op jit(solution)/shard_map/ppermute | solution.py:30
  87.2 1.5 add_convert_fusion.6.after_ref
  88.8 8.8 %shard_map.62 = (bf16[256,1024]{1,0:T(8,128)(2,1)}, bf16[256,1024]{1,0:T(8,128)(2,1)}, bf16[256,1024]{1,0:T(8,128)(2,1)}, bf16[256,1024]{1,0:T(8,128)(2,1)}, bf1...) custom-call(s32[4]{0:T(128)} %pad_add_fusion.at_ref, ...), custom_call_target="tpu_custom_call" | custom-call | flops 4294967296 | bytes 10551312 | tf_op jit(solution)/shard_map/pallas_call | solution.py:43
  97.6 1.6 collective-permute-start.5
  99.3 2.7 %collective-permute-start.6 = (bf16[256,1024]{1,0:T(8,128)(2,1)}, bf16[256,1024]{1,0:T(8,128)(2,1)S(1)}, u32[]{:S(2)}, u32[]{:S(2)}) collective-permute-start(bf16[256,1024]{1,0:T(8,128)(2,1)} %get-tuple-element.15), channel_id=1, source_target_pairs={{0,8},{1,9},{2,10},{3,11},{4,12},{5,13},{6,14},{7,15},{8,0},{9,1},... | collective-permute-start | bytes 1572872 | tf_op jit(solution)/shard_map/ppermute | solution.py:30
  101.9 1.5 collective-permute-start.7
  103.4 1.5 collective-permute-start.8
  104.9 2.7 %collective-permute-start.9 = (bf16[256,1024]{1,0:T(8,128)(2,1)}, bf16[256,1024]{1,0:T(8,128)(2,1)S(1)}, u32[]{:S(2)}, u32[]{:S(2)}) collective-permute-start(bf16[256,1024]{1,0:T(8,128)(2,1)} %get-tuple-element.18), channel_id=1, source_target_pairs={{0,32},{1,33},{2,34},{3,35},{4,36},{5,37},{6,38},{7,39},{8,40},{9,... | collective-permute-start | bytes 1572872 | tf_op jit(solution)/shard_map/ppermute | solution.py:30
  107.5 5.6 %collective-permute-done.5.refs_0_ = bf16[256,1024]{1,0:T(8,128)(2,1)S(1)} collective-permute-done((bf16[256,1024]{1,0:T(8,128)(2,1)}, bf16[256,1024]{1,0:T(8,128)(2,1)S(1)}, u32[]{:S(2)}, u32[]{:S(2)}) %collective-permute-start.5) | collective-permute-done | bytes 524320 | tf_op jit(solution)/shard_map/ppermute | solution.py:30
  113.2 10.0 %collective-permute-done.6.refs_1_ = bf16[256,1024]{1,0:T(8,128)(2,1)S(1)} collective-permute-done((bf16[256,1024]{1,0:T(8,128)(2,1)}, bf16[256,1024]{1,0:T(8,128)(2,1)S(1)}, u32[]{:S(2)}, u32[]{:S(2)}) %collective-permute-start.6) | collective-permute-done | bytes 524320 | tf_op jit(solution)/shard_map/ppermute | solution.py:30
  123.2 0.8 copy-done.11
  124.2 3.7 %collective-permute-done.9.refs_4_ = bf16[256,1024]{1,0:T(8,128)(2,1)S(1)} collective-permute-done((bf16[256,1024]{1,0:T(8,128)(2,1)}, bf16[256,1024]{1,0:T(8,128)(2,1)S(1)}, u32[]{:S(2)}, u32[]{:S(2)}) %collective-permute-start.9) | collective-permute-done | bytes 524320 | tf_op jit(solution)/shard_map/ppermute | solution.py:30
  127.9 0.8 copy-done.7
  128.7 0.8 copy-done
  129.5 3.4 %shard_map.63 = (f32[64,2048]{1,0:T(8,128)}, bf16[16,160,256]{2,1,0:T(8,128)(2,1)}) custom-call(s32[4]{0:T(128)} %pad_add_fusion.at_ref, bf16[16,64,1152]{2,1,0:T(8,128)(2,1)} %copy-done, bf16[128,256]{1,0:T(8,128)(2,1)} %bitcast.44, bf16[256,1024]{1,0:T(8,128)(2,1)} %copy-done.9, bf16[256,1024]{1,0:T(8,128)(2,1)} %copy-done.11, ...), custom_call_target="tpu_custom_call" | custom-call | bytes 6881296 | tf_op jit(solution)/shard_map/pallas_call | solution.py:43
  132.9 3.8 %all-to-all-start.2 = ((bf16[16,160,256]{2,1,0:T(8,128)(2,1)}), bf16[16,160,256]{2,1,0:T(8,128)(2,1)S(1)}, u32[]{:S(2)}, u32[]{:S(2)}) async-start(bf16[16,160,256]{2,1,0:T(8,128)(2,1)} %get-tuple-element.19), calls=%async_computation.2 | async-start | bytes 2621440 | tf_op jit(solution)/shard_map/all_to_all | solution.py:229
  136.7 3.1 %collective-permute-start.15 = (bf16[256,1024]{1,0:T(8,128)(2,1)}, bf16[256,1024]{1,0:T(8,128)(2,1)}, u32[]{:S(2)}, u32[]{:S(2)}) collective-permute-start(bf16[256,1024]{1,0:T(8,128)(2,1)} %get-tuple-element.25), channel_id=1, source_target_pairs={{0,48},{1,49},{2,50},{3,51},{4,52},{5,53},{6,54},{7,55},{8,56},{9,... | collective-permute-start | bytes 1572872 | tf_op jit(solution)/shard_map/ppermute | solution.py:30
  139.8 1.5 add_convert_fusion.5
  141.6 3.2 %collective-permute-start.14 = (bf16[64,1024]{1,0:T(8,128)(2,1)S(1)}, bf16[64,1024]{1,0:T(8,128)(2,1)S(1)}, u32[]{:S(2)}, u32[]{:S(2)}) collective-permute-start(bf16[64,1024]{1,0:T(8,128)(2,1)S(1)} %get-tuple-element.27), channel_id=1, source_target_pairs={{0,48},{1,49},{2,50},{3,51},{4,52},{5,53},{6,54},{7,55},{8,56},{9,... | collective-permute-start | bytes 393224 | tf_op jit(solution)/shard_map/ppermute | solution.py:30
  144.8 20.9 %collective-permute-done.15 = bf16[256,1024]{1,0:T(8,128)(2,1)} collective-permute-done((bf16[256,1024]{1,0:T(8,128)(2,1)}, bf16[256,1024]{1,0:T(8,128)(2,1)}, u32[]{:S(2)}, u32[]{:S(2)}) %collective-permute-start.15) | collective-permute-done | bytes 524320 | tf_op jit(solution)/shard_map/ppermute | solution.py:30
  165.7 2.0 %add_convert_fusion.2 = (bf16[64,1024]{1,0:T(8,128)(2,1)}, bf16[64,1024]{1,0:T(8,128)(2,1)}, bf16[64,1024]{1,0:T(8,128)(2,1)}) fusion(bf16[256,1024]{1,0:T(8,128)(2,1)} %collective-permute-done.15, bf16[256,1024]{1,0:T(8,128)(2,1)S(1)} %copy-done.8, bf16[256,1024]{1,0:T(8,128)(2,1)S(1)} %copy-done.6, bf16[256,1024]{1,0:T(8,128)(2,1)S(1)} %copy-done.16), kind=kLoop, calls=%fused_computation.7 | loop fusion | flops 1572864 | bytes 1966080 | tf_op jit(solution)/shard_map/convert_element_type | solution.py:143
  167.7 0.7 collective-permute-start.16
  168.4 2.5 %collective-permute-start.18 = (bf16[64,1024]{1,0:T(8,128)(2,1)}, bf16[64,1024]{1,0:T(8,128)(2,1)}, u32[]{:S(2)}, u32[]{:S(2)}) collective-permute-start(bf16[64,1024]{1,0:T(8,128)(2,1)} %get-tuple-element.30), channel_id=1, source_target_pairs={{0,12},{1,13},{2,14},{3,15},{4,0},{5,1},{6,2},{7,3},{8,4},{9,5},{1... | collective-permute-start | bytes 393224 | tf_op jit(solution)/shard_map/ppermute | solution.py:30
  171.4 1.2 convert_add_fusion.1
  173.1 1.0 collective-permute-done.16
  174.1 3.6 %collective-permute-done.17 = bf16[64,1024]{1,0:T(8,128)(2,1)} collective-permute-done((bf16[64,1024]{1,0:T(8,128)(2,1)}, bf16[64,1024]{1,0:T(8,128)(2,1)}, u32[]{:S(2)}, u32[]{:S(2)}) %collective-permute-start.17) | collective-permute-done | bytes 131104 | tf_op jit(solution)/shard_map/ppermute | solution.py:30
  177.7 1.2 convert_add_fusion
  179.0 0.8 copy.23
  180.4 2.1 %shard_map.65 = f32[64,2048]{1,0:T(8,128)} custom-call(s32[4]{0:T(128)} %pad_add_fusion.at_ref, f32[64,2048]{1,0:T(8,128)} %get-tuple-element.22.direct_ref, bf16[64,1024]{1,0:T(8,128)(2,1)} %bitcast.43, bf16[64,1024]{1,0:T(8,128)(2,1)} %copy-done.17), custom_call_target="tpu_custom_call" | custom-call | bytes 1310736 | tf_op jit(solution)/shard_map/pallas_call | solution.py:43
  182.6 2.5 %collective-permute-start.19 = (bf16[64,2048]{1,0:T(8,128)(2,1)S(1)}, bf16[64,2048]{1,0:T(8,128)(2,1)S(1)}, u32[]{:S(2)}, u32[]{:S(2)}) collective-permute-start(bf16[64,2048]{1,0:T(8,128)(2,1)S(1)} %select_convert_fusion), channel_id=1, source_target_pairs={{0,64},{1,65},{2,66},{3,67},{4,68},{5,69},{6,70},{7,71},{8,72},{9,... | collective-permute-start | bytes 786440 | tf_op jit(solution)/shard_map/ppermute | solution.py:30
  185.1 4.8 %shard_map.64 = (f32[512,256]{1,0:T(8,128)}, f32[512,256]{1,0:T(8,128)}) custom-call(s32[4]{0:T(128)} %pad_add_fusion.at_ref, bf16[16,160,256]{2,1,0:T(8,128)(2,1)} %copy-done.2, bf16[1024,512]{1,0:T(8,128)(2,1)} %bitcast.31, bf16[1024,512]{1,0:T(8,128)(2,1)} %bitcast.39, bf16[1024,512]{1,0:T(8,128)(2,1)} %collective-permute-done.3.a1_ref.cross1_ref, ...), custom_call_target="tpu_custom_call" | custom-call | flops 1073741824 | bytes 6553616 | tf_op jit(solution)/shard_map/pallas_call | solution.py:43
  189.9 0.9 multiply_add_fusion
  190.8 1.2 collective-permute-done.10
  192.0 0.9 add.126
  (60 shorter events, 3.4 us)
Async XLA Ops:
  3.5 11.7 %copy-start.4 = (bf16[512,2048]{0,1:T(8,128)(2,1)}, bf16[512,2048]{0,1:T(8,128)(2,1)S(1)}, u32[]{:S(2)}) copy-start(bf16[512,2048]{0,1:T(8,128)(2,1)S(1)} %copy.12) | copy-start | bytes 6291460
  3.5 11.7 %collective-permute-start = (bf16[2048,512]{1,0:T(8,128)(2,1)S(1)}, bf16[2048,512]{1,0:T(8,128)(2,1)}, u32[]{:S(2)}, u32[]{:S(2)}) collective-permute-start(bf16[2048,512]{1,0:T(8,128)(2,1)S(1)} %bitcast.33), channel_id=1, source_target_pairs={{0,2},{1,3},{2,0},{3,1},{4,6},{5,7},{6,4},{7,5},{8,10},{9,11},{10,... | collective-permute-start | bytes 6291464 | tf_op jit(solution)/shard_map/ppermute | solution.py:30
  6.1 25.9 %all-to-all-start.1 = ((bf16[16,64,512]{2,1,0:T(8,128)(2,1)}), bf16[16,64,512]{2,1,0:T(8,128)(2,1)}, u32[]{:S(2)}, u32[]{:S(2)}) async-start(bf16[16,64,512]{2,1,0:T(8,128)(2,1)} %shard_map.60), calls=%async_computation.1 | async-start | bytes 2097152 | tf_op jit(solution)/shard_map/all_to_all | solution.py:207
  25.4 10.3 %copy-start.1 = (bf16[16,1,64,512]{3,2,1,0:T(8,128)(2,1)S(1)}, bf16[16,1,64,512]{3,2,1,0:T(8,128)(2,1)}, u32[]{:S(2)}) copy-start(bf16[16,1,64,512]{3,2,1,0:T(8,128)(2,1)} %constant_dynamic-slice_fusion.3) | copy-start | bytes 3145732
  32.0 95.9 %all-to-all-start = ((bf16[16,64,1152]{2,1,0:T(8,128)(2,1)}), bf16[16,64,1152]{2,1,0:T(8,128)(2,1)S(1)}, u32[]{:S(2)}, u32[]{:S(2)}) async-start(bf16[16,64,1152]{2,1,0:T(8,128)(2,1)} %shard_map.59.after_ref), calls=%async_computation | async-start | bytes 4718592 | tf_op jit(solution)/shard_map/all_to_all | solution.py:222
  35.7 53.0 %collective-permute-start.3 = (bf16[1024,512]{1,0:T(8,128)(2,1)S(1)}, bf16[1024,512]{1,0:T(8,128)(2,1)}, u32[]{:S(2)}, u32[]{:S(2)}) collective-permute-start(bf16[1024,512]{1,0:T(8,128)(2,1)S(1)} %bitcast.32), channel_id=1, source_target_pairs={{0,1},{1,0},{2,3},{3,2},{4,5},{5,4},{6,7},{7,6},{8,9},{9,8},{10,11... | collective-permute-start | bytes 3145736 | tf_op jit(solution)/shard_map/ppermute | solution.py:30
  39.0 49.8 %collective-permute-start.4 = (bf16[1024,512]{1,0:T(8,128)(2,1)}, bf16[1024,512]{1,0:T(8,128)(2,1)}, u32[]{:S(2)}, u32[]{:S(2)}) collective-permute-start(bf16[1024,512]{1,0:T(8,128)(2,1)} %bitcast.38), channel_id=1, source_target_pairs={{0,1},{1,0},{2,3},{3,2},{4,5},{5,4},{6,7},{7,6},{8,9},{9,8},{10,11... | collective-permute-start | bytes 3145736 | tf_op jit(solution)/shard_map/ppermute | solution.py:30
  42.5 1.4 collective-permute-start.1
  44.9 42.3 %collective-permute-start.2 = (f32[2,64,256]{2,1,0:T(8,128)S(1)}, f32[2,64,256]{2,1,0:T(8,128)}, u32[]{:S(2)}, u32[]{:S(2)}) collective-permute-start(f32[2,64,256]{2,1,0:T(8,128)S(1)} %bitcast_add_fusion), channel_id=1, source_target_pairs={{0,64},{1,65},{2,66},{3,67},{4,68},{5,69},{6,70},{7,71},{8,72},{9,... | collective-permute-start | bytes 393224 | tf_op jit(solution)/shard_map/ppermute | solution.py:30
  97.6 15.6 %collective-permute-start.5 = (bf16[256,1024]{1,0:T(8,128)(2,1)}, bf16[256,1024]{1,0:T(8,128)(2,1)S(1)}, u32[]{:S(2)}, u32[]{:S(2)}) collective-permute-start(bf16[256,1024]{1,0:T(8,128)(2,1)} %get-tuple-element.14), channel_id=1, source_target_pairs={{0,4},{1,5},{2,6},{3,7},{4,8},{5,9},{6,10},{7,11},{8,12},{9,13},{1... | collective-permute-start | bytes 1572872 | tf_op jit(solution)/shard_map/ppermute | solution.py:30
  99.3 23.9 %collective-permute-start.6 = (bf16[256,1024]{1,0:T(8,128)(2,1)}, bf16[256,1024]{1,0:T(8,128)(2,1)S(1)}, u32[]{:S(2)}, u32[]{:S(2)}) collective-permute-start(bf16[256,1024]{1,0:T(8,128)(2,1)} %get-tuple-element.15), channel_id=1, source_target_pairs={{0,8},{1,9},{2,10},{3,11},{4,12},{5,13},{6,14},{7,15},{8,0},{9,1},... | collective-permute-start | bytes 1572872 | tf_op jit(solution)/shard_map/ppermute | solution.py:30
  101.9 21.3 %collective-permute-start.7 = (bf16[256,1024]{1,0:T(8,128)(2,1)}, bf16[256,1024]{1,0:T(8,128)(2,1)S(1)}, u32[]{:S(2)}, u32[]{:S(2)}) collective-permute-start(bf16[256,1024]{1,0:T(8,128)(2,1)} %get-tuple-element.16), channel_id=1, source_target_pairs={{0,12},{1,13},{2,14},{3,15},{4,0},{5,1},{6,2},{7,3},{8,4},{9,5},{1... | collective-permute-start | bytes 1572872 | tf_op jit(solution)/shard_map/ppermute | solution.py:30
  103.4 19.8 %collective-permute-start.8 = (bf16[256,1024]{1,0:T(8,128)(2,1)}, bf16[256,1024]{1,0:T(8,128)(2,1)S(1)}, u32[]{:S(2)}, u32[]{:S(2)}) collective-permute-start(bf16[256,1024]{1,0:T(8,128)(2,1)} %get-tuple-element.17), channel_id=1, source_target_pairs={{0,16},{1,17},{2,18},{3,19},{4,20},{5,21},{6,22},{7,23},{8,24},{9,... | collective-permute-start | bytes 1572872 | tf_op jit(solution)/shard_map/ppermute | solution.py:30
  104.9 23.0 %collective-permute-start.9 = (bf16[256,1024]{1,0:T(8,128)(2,1)}, bf16[256,1024]{1,0:T(8,128)(2,1)S(1)}, u32[]{:S(2)}, u32[]{:S(2)}) collective-permute-start(bf16[256,1024]{1,0:T(8,128)(2,1)} %get-tuple-element.18), channel_id=1, source_target_pairs={{0,32},{1,33},{2,34},{3,35},{4,36},{5,37},{6,38},{7,39},{8,40},{9,... | collective-permute-start | bytes 1572872 | tf_op jit(solution)/shard_map/ppermute | solution.py:30
  113.2 10.1 %copy-start.9 = (bf16[256,1024]{1,0:T(8,128)(2,1)}, bf16[256,1024]{1,0:T(8,128)(2,1)S(1)}, u32[]{:S(2)}) copy-start(bf16[256,1024]{1,0:T(8,128)(2,1)S(1)} %collective-permute-done.5.refs_0_) | copy-start | bytes 1572868
  123.2 0.8 copy-start.11
  123.2 1.0 copy-start.13
  124.2 3.7 %copy-start.5 = (bf16[256,1024]{1,0:T(8,128)(2,1)}, bf16[256,1024]{1,0:T(8,128)(2,1)S(1)}, u32[]{:S(2)}) copy-start(bf16[256,1024]{1,0:T(8,128)(2,1)S(1)} %collective-permute-done.8.refs_3_) | copy-start | bytes 1572868
  127.9 0.8 copy-start.7
  127.9 1.6 copy-start
  132.9 7.0 %copy-start.10 = (bf16[256,1024]{1,0:T(8,128)(2,1)S(1)}, bf16[256,1024]{1,0:T(8,128)(2,1)}, u32[]{:S(2)}) copy-start(bf16[256,1024]{1,0:T(8,128)(2,1)} %copy-done.9) | copy-start | bytes 1572868
  132.9 7.0 %copy-start.12 = (bf16[256,1024]{1,0:T(8,128)(2,1)S(1)}, bf16[256,1024]{1,0:T(8,128)(2,1)}, u32[]{:S(2)}) copy-start(bf16[256,1024]{1,0:T(8,128)(2,1)} %copy-done.11) | copy-start | bytes 1572868
  132.9 32.9 %copy-start.6 = (bf16[256,1024]{1,0:T(8,128)(2,1)S(1)}, bf16[256,1024]{1,0:T(8,128)(2,1)}, u32[]{:S(2)}) copy-start(bf16[256,1024]{1,0:T(8,128)(2,1)} %copy-done.5) | copy-start | bytes 1572868
  132.9 32.9 %copy-start.8 = (bf16[256,1024]{1,0:T(8,128)(2,1)S(1)}, bf16[256,1024]{1,0:T(8,128)(2,1)}, u32[]{:S(2)}) copy-start(bf16[256,1024]{1,0:T(8,128)(2,1)} %copy-done.7) | copy-start | bytes 1572868
  132.9 39.7 %all-to-all-start.2 = ((bf16[16,160,256]{2,1,0:T(8,128)(2,1)}), bf16[16,160,256]{2,1,0:T(8,128)(2,1)S(1)}, u32[]{:S(2)}, u32[]{:S(2)}) async-start(bf16[16,160,256]{2,1,0:T(8,128)(2,1)} %get-tuple-element.19), calls=%async_computation.2 | async-start | bytes 2621440 | tf_op jit(solution)/shard_map/all_to_all | solution.py:229
  136.7 29.0 %collective-permute-start.15 = (bf16[256,1024]{1,0:T(8,128)(2,1)}, bf16[256,1024]{1,0:T(8,128)(2,1)}, u32[]{:S(2)}, u32[]{:S(2)}) collective-permute-start(bf16[256,1024]{1,0:T(8,128)(2,1)} %get-tuple-element.25), channel_id=1, source_target_pairs={{0,48},{1,49},{2,50},{3,51},{4,52},{5,53},{6,54},{7,55},{8,56},{9,... | collective-permute-start | bytes 1572872 | tf_op jit(solution)/shard_map/ppermute | solution.py:30
  139.8 25.9 %copy-start.16 = (bf16[256,1024]{1,0:T(8,128)(2,1)S(1)}, bf16[256,1024]{1,0:T(8,128)(2,1)}, u32[]{:S(2)}) copy-start(bf16[256,1024]{1,0:T(8,128)(2,1)} %get-tuple-element.24) | copy-start | bytes 1572868
  141.3 29.6 %collective-permute-start.12 = (bf16[64,1024]{1,0:T(8,128)(2,1)S(1)}, bf16[64,1024]{1,0:T(8,128)(2,1)S(1)}, u32[]{:S(2)}, u32[]{:S(2)}) collective-permute-start(bf16[64,1024]{1,0:T(8,128)(2,1)S(1)} %get-tuple-element.26), channel_id=1, source_target_pairs={{0,16},{1,17},{2,18},{3,19},{4,20},{5,21},{6,22},{7,23},{8,24},{9,... | collective-permute-start | bytes 393224 | tf_op jit(solution)/shard_map/ppermute | solution.py:30
  141.6 29.8 %collective-permute-start.14 = (bf16[64,1024]{1,0:T(8,128)(2,1)S(1)}, bf16[64,1024]{1,0:T(8,128)(2,1)S(1)}, u32[]{:S(2)}, u32[]{:S(2)}) collective-permute-start(bf16[64,1024]{1,0:T(8,128)(2,1)S(1)} %get-tuple-element.27), channel_id=1, source_target_pairs={{0,48},{1,49},{2,50},{3,51},{4,52},{5,53},{6,54},{7,55},{8,56},{9,... | collective-permute-start | bytes 393224 | tf_op jit(solution)/shard_map/ppermute | solution.py:30
  144.8 26.6 %collective-permute-start.13 = (bf16[64,1024]{1,0:T(8,128)(2,1)S(1)}, bf16[64,1024]{1,0:T(8,128)(2,1)S(1)}, u32[]{:S(2)}, u32[]{:S(2)}) collective-permute-start(bf16[64,1024]{1,0:T(8,128)(2,1)S(1)} %get-tuple-element.28), channel_id=1, source_target_pairs={{0,32},{1,33},{2,34},{3,35},{4,36},{5,37},{6,38},{7,39},{8,40},{9,... | collective-permute-start | bytes 393224 | tf_op jit(solution)/shard_map/ppermute | solution.py:30
  167.7 6.4 %collective-permute-start.16 = (bf16[64,1024]{1,0:T(8,128)(2,1)}, bf16[64,1024]{1,0:T(8,128)(2,1)S(1)}, u32[]{:S(2)}, u32[]{:S(2)}) collective-permute-start(bf16[64,1024]{1,0:T(8,128)(2,1)} %get-tuple-element.29), channel_id=1, source_target_pairs={{0,4},{1,5},{2,6},{3,7},{4,8},{5,9},{6,10},{7,11},{8,12},{9,13},{1... | collective-permute-start | bytes 393224 | tf_op jit(solution)/shard_map/ppermute | solution.py:30
  168.4 5.7 %collective-permute-start.18 = (bf16[64,1024]{1,0:T(8,128)(2,1)}, bf16[64,1024]{1,0:T(8,128)(2,1)}, u32[]{:S(2)}, u32[]{:S(2)}) collective-permute-start(bf16[64,1024]{1,0:T(8,128)(2,1)} %get-tuple-element.30), channel_id=1, source_target_pairs={{0,12},{1,13},{2,14},{3,15},{4,0},{5,1},{6,2},{7,3},{8,4},{9,5},{1... | collective-permute-start | bytes 393224 | tf_op jit(solution)/shard_map/ppermute | solution.py:30
  170.9 6.8 %collective-permute-start.17 = (bf16[64,1024]{1,0:T(8,128)(2,1)}, bf16[64,1024]{1,0:T(8,128)(2,1)}, u32[]{:S(2)}, u32[]{:S(2)}) collective-permute-start(bf16[64,1024]{1,0:T(8,128)(2,1)} %get-tuple-element.31), channel_id=1, source_target_pairs={{0,8},{1,9},{2,10},{3,11},{4,12},{5,13},{6,14},{7,15},{8,0},{9,1},... | collective-permute-start | bytes 393224 | tf_op jit(solution)/shard_map/ppermute | solution.py:30
  172.6 9.9 %copy-start.2 = (bf16[16,160,256]{2,1,0:T(8,128)(2,1)}, bf16[16,160,256]{2,1,0:T(8,128)(2,1)S(1)}, u32[]{:S(2)}) copy-start(bf16[16,160,256]{2,1,0:T(8,128)(2,1)S(1)} %all-to-all-done.2.pt_ref) | copy-start | bytes 3932164
  173.0 6.7 %collective-permute-start.11 = (bf16[64,1024]{1,0:T(8,128)(2,1)S(1)}, bf16[64,1024]{1,0:T(8,128)(2,1)S(1)}, u32[]{:S(2)}, u32[]{:S(2)}) collective-permute-start(bf16[64,1024]{1,0:T(8,128)(2,1)S(1)} %bitcast.45), channel_id=1, source_target_pairs={{0,2},{1,3},{2,0},{3,1},{4,6},{5,7},{6,4},{7,5},{8,10},{9,11},{10,... | collective-permute-start | bytes 393224 | tf_op jit(solution)/shard_map/ppermute | solution.py:30
  179.8 0.7 copy-start.17
  182.6 7.3 %copy-start.3 = (f32[64,2048]{1,0:T(8,128)S(1)}, f32[64,2048]{1,0:T(8,128)}, u32[]{:S(2)}) copy-start(f32[64,2048]{1,0:T(8,128)} %shard_map.65) | copy-start | bytes 1572868
  182.6 7.3 %copy-start.14 = (f32[64,2048]{1,0:T(8,128)S(1)}, f32[64,2048]{1,0:T(8,128)}, u32[]{:S(2)}) copy-start(f32[64,2048]{1,0:T(8,128)} %param.5) | copy-start | bytes 1572868
  182.6 7.3 %collective-permute-start.19 = (bf16[64,2048]{1,0:T(8,128)(2,1)S(1)}, bf16[64,2048]{1,0:T(8,128)(2,1)S(1)}, u32[]{:S(2)}, u32[]{:S(2)}) collective-permute-start(bf16[64,2048]{1,0:T(8,128)(2,1)S(1)} %select_convert_fusion), channel_id=1, source_target_pairs={{0,64},{1,65},{2,66},{3,67},{4,68},{5,69},{6,70},{7,71},{8,72},{9,... | collective-permute-start | bytes 786440 | tf_op jit(solution)/shard_map/ppermute | solution.py:30
  189.9 2.1 %copy-start.15 = (f32[512,256]{1,0:T(8,128)S(1)}, f32[512,256]{1,0:T(8,128)}, u32[]{:S(2)}) copy-start(f32[512,256]{1,0:T(8,128)} %get-tuple-element.20) | copy-start | bytes 1572868
  189.9 2.1 %collective-permute-start.10 = (f32[512,256]{1,0:T(8,128)}, f32[512,256]{1,0:T(8,128)S(1)}, u32[]{:S(2)}, u32[]{:S(2)}) collective-permute-start(f32[512,256]{1,0:T(8,128)} %get-tuple-element.21), channel_id=1, source_target_pairs={{0,2},{1,3},{2,0},{3,1},{4,6},{5,7},{6,4},{7,5},{8,10},{9,11},{10,... | collective-permute-start | bytes 1572872 | tf_op jit(solution)/shard_map/ppermute | solution.py:30
